TPU v7x, 32 devices: a whole 2x2x4 slice. The times are simulated.
32 devices in a mesh: groups: 1, seq: 32 (over z, y, x, core).
Axes of the slice: x: 2, y: 2, z: 4, core: 2. Of those that a mesh axis runs over, the one named last changes fastest.
Arguments:
- features: bfloat16 [2, 4096, 1536], P('groups', 'seq'), may hold values from -6 to 6
- cotangent: bfloat16 [2, 4096, 1536], P('groups', 'seq'), may hold values from -6 to 6
- dilated_kernel_weight: bfloat16 [1536, 3, 768], P('seq'), may hold values from -0.09375 to 0.09375
- project_weight: bfloat16 [1536, 768], P('seq'), may hold values from -0.21875 to 0.21875
- outer_gain: float32 [1536], replicated, may hold values from 0.1 to 1.9
- inner_gain: float32 [768], replicated, may hold values from 0.1 to 1.9
Outputs:
- block_out: bfloat16 [2, 4096, 1536], P('groups', 'seq')
- grad_features: bfloat16 [2, 4096, 1536], P('groups', 'seq')
- grad_dilated: float32 [1536, 3, 768], P(('groups', 'seq'))
- grad_project: float32 [1536, 768], P(('groups', 'seq'))
- grad_outer_gain: float32 [1536], P(('groups', 'seq'))
- grad_inner_gain: float32 [768], P(('groups', 'seq'))
All inputs are finite; a program needn't handle non-finite values.
Results may differ from a plain program's by a relative error of at most 0.0056.
Values may be sent and summed in bfloat16 or wider, within the bound.
No kernel may reach another device: no remote copies, remote signals or barrier semaphores. Data moves between devices by JAX's collectives and lax.ppermute only.
A program may use at most 128 MiB of HBM per device.

v0:
```python
import math

import jax
import jax.numpy as jnp
from jax import lax
from jax.sharding import PartitionSpec as P

KERNEL_TAPS = 3
DILATION_STEP = 32


eps = 1e-06


def padded(block, sides, width):
    for axis, dim in sides:
        count = lax.axis_size(axis)
        forward = [(i, i + 1) for i in range(count - 1)]
        backward = [(target, source) for source, target in forward]
        low = lax.ppermute(
            lax.slice_in_dim(block, block.shape[dim] - width, None, axis=dim), axis, forward
        )
        high = lax.ppermute(lax.slice_in_dim(block, 0, width, axis=dim), axis, backward)
        block = jnp.concatenate([low, block, high], axis=dim)
    return block


def act_norm(values, gain):
    meansq = jnp.mean(values * values, axis=-1, keepdims=True)
    return jax.nn.gelu(values * lax.rsqrt(meansq + eps) * gain, approximate=True)


def reduce_dilated(padded_input, conv_output_gradient, factor):
    bin_count = conv_output_gradient.shape[1]
    tap_slices = [
        jnp.einsum(
            "btc,bti->ci",
            padded_input[:, tap_index * DILATION_STEP : tap_index * DILATION_STEP + bin_count],
            conv_output_gradient,
            preferred_element_type=jnp.float32,
        )
        for tap_index in range(KERNEL_TAPS)
    ]
    return lax.psum_scatter(
        jnp.stack(tap_slices, axis=1) * factor, "seq", scatter_dimension=0, tiled=True
    )


def body(features, cotangent, dilated_kernel_weight, project_weight, outer_gain, inner_gain):
    bin_count = features.shape[1]
    factor = 1.0 / math.sqrt(features.shape[0] * bin_count * lax.axis_size("seq"))
    full_dilated = lax.all_gather(dilated_kernel_weight, "seq", axis=0, tiled=True)
    full_project = lax.all_gather(project_weight, "seq", axis=0, tiled=True)
    as_float = features.astype(jnp.float32)
    active_features = act_norm(as_float, outer_gain).astype(jnp.bfloat16)
    padded_input = padded(active_features, (("seq", 1),), DILATION_STEP)
    conv_output = jnp.einsum(
        "btc,ci->bti",
        padded_input[:, 0:bin_count],
        full_dilated[:, 0, :],
        preferred_element_type=jnp.float32,
    )
    for tap_index in range(1, KERNEL_TAPS):
        conv_output = conv_output + jnp.einsum(
            "btc,ci->bti",
            padded_input[:, tap_index * DILATION_STEP : tap_index * DILATION_STEP + bin_count],
            full_dilated[:, tap_index, :],
            preferred_element_type=jnp.float32,
        )
    hidden = act_norm(conv_output, inner_gain).astype(jnp.bfloat16)
    block_out = (
        as_float
        + jnp.einsum("bti,ci->btc", hidden, full_project, preferred_element_type=jnp.float32)
    ).astype(jnp.bfloat16)
    grad_hidden = jnp.einsum(
        "btc,ci->bti", cotangent, full_project, preferred_element_type=jnp.float32
    )
    unused, pull_inner = jax.vjp(act_norm, conv_output, inner_gain)
    conv_output_gradient, grad_gain_inner = pull_inner(grad_hidden)
    conv_output_gradient = conv_output_gradient.astype(jnp.bfloat16)
    padded_input_gradient = padded(conv_output_gradient, (("seq", 1),), DILATION_STEP)
    grad_active = jnp.zeros(features.shape, jnp.float32)
    for tap_index in range(KERNEL_TAPS):
        tap_shift = (KERNEL_TAPS - 1 - tap_index) * DILATION_STEP
        grad_active = grad_active + jnp.einsum(
            "bti,ci->btc",
            padded_input_gradient[:, tap_shift : tap_shift + bin_count],
            full_dilated[:, tap_index, :],
            preferred_element_type=jnp.float32,
        )
    unused_two, pull_outer = jax.vjp(act_norm, as_float, outer_gain)
    grad_branch, grad_gain_outer = pull_outer(grad_active)
    grad_features = (cotangent.astype(jnp.float32) + grad_branch).astype(jnp.bfloat16)
    grad_dilated = reduce_dilated(padded_input, conv_output_gradient, factor)
    grad_project = lax.psum_scatter(
        jnp.einsum("btc,bti->ci", cotangent, hidden, preferred_element_type=jnp.float32) * factor,
        "seq",
        scatter_dimension=0,
        tiled=True,
    )
    grad_outer_gain, grad_inner_gain = (
        lax.psum_scatter(grad_gain_outer * factor, "seq", scatter_dimension=0, tiled=True),
        lax.psum_scatter(grad_gain_inner * factor, "seq", scatter_dimension=0, tiled=True),
    )
    return (block_out, grad_features, grad_dilated, grad_project, grad_outer_gain, grad_inner_gain)


def solution(mesh):
    return jax.shard_map(
        body,
        mesh=mesh,
        in_specs=(
            P("groups", "seq", None),
            P("groups", "seq", None),
            P("seq", None, None),
            P("seq", None),
            P(),
            P(),
        ),
        out_specs=(
            P("groups", "seq", None),
            P("groups", "seq", None),
            P(("groups", "seq"), None, None),
            P(("groups", "seq"), None),
            P(("groups", "seq")),
            P(("groups", "seq")),
        ),
        check_vma=False,
    )
```

profile of v0, /device:TPU:0, one launch (start us, length us, event | category | flops | bytes accessed | tf_op | source)
XLA Modules:
  0.0 433.5 jit_solution(2068119754786179202)
XLA Ops:
  7.2 0.0 all-gather.3.cloned.1.call-start
  7.2 0.7 all-gather.3.cloned.1.call-update
  7.9 0.0 all-gather.5.cloned.1.call-start
  8.0 0.7 all-gather.5.cloned.1.call-update
  8.7 0.0 reduce-scatter.7.cloned.1.call-start
  8.7 1.4 fusion.27
  10.1 1.4 fusion.18
  11.5 2.4 collective-permute-start
  13.9 1.3 collective-permute-start.1
  15.2 71.3 %all-gather.3.cloned.1.call-done = bf16[1536,3,768]{2,0,1:T(8,128)(2,1)} async-done(((bf16[48,3,768]{2,0,1:T(8,128)(2,1)}), bf16[1536,3,768]{2,0,1:T(8,128)(2,1)}) %all-gather.3.cloned.1.call-update) | async-done | bytes 7077904 | tf_op jit(solution)/shard_map/all_gather | solution.py:52
  86.5 2.4 fusion.8
  89.0 0.0 collective-permute-done.1
  89.0 0.0 copy-start.4
  89.0 2.5 fusion.10
  91.5 0.0 copy-start.1
  91.5 0.0 copy-start.6
  91.5 0.0 collective-permute-done
  91.5 0.0 copy-start.2
  91.6 2.6 multiply_reduce_fusion.2
  94.2 3.2 fusion
  97.4 6.1 %copy.26 = f32[1536,768]{1,0:T(8,128)} copy(f32[1536,768]{0,1:T(8,128)} %fusion) | data formatting | bytes 9437184
  103.5 0.0 reduce-scatter.7.cloned.1.call-update
  103.5 0.0 reduce-scatter.5.cloned.1.call-start
  103.6 41.6 %all-gather.5.cloned.1.call-done = bf16[1536,768]{1,0:T(8,128)(2,1)} async-done(((bf16[48,768]{1,0:T(8,128)(2,1)}), bf16[1536,768]{1,0:T(8,128)(2,1)}) %all-gather.5.cloned.1.call-update) | async-done | bytes 2359312 | tf_op jit(solution)/shard_map/all_gather | solution.py:53
  145.2 3.6 multiply_reduce_fusion
  148.9 0.2 fusion.37
  149.1 0.7 copy-done.3
  149.8 0.8 convolution_bitcast_fusion.2
  150.6 0.1 copy-done.5
  150.7 0.8 convolution_bitcast_fusion
  151.5 0.8 convolution_bitcast_fusion.1
  152.4 5.5 %maximum_multiply_fusion = f32[1536,3,768]{2,0,1:T(8,128)} fusion(f32[1536,1,768]{2,0,1:T(8,128)S(1)} %convolution_bitcast_fusion, f32[1536,1,768]{2,0,1:T(8,128)S(1)} %convolution_bitcast_fusion.1, f32[1536,1,768]{2,0,1:T(8,128)S(1)} %convolution_bitcast_fusion.2), kind=kLoop, calls=%fused_computation | loop fusion | flops 10616832 | bytes 28311552 | tf_op jit(solution)/shard_map/mul | solution.py:45
  157.8 0.0 reduce-scatter.5.cloned.1.call-update
  157.9 2.3 collective-permute-start.3
  160.2 2.5 fusion.7
  162.8 1.9 fusion.2
  164.6 1.6 collective-permute-start.2
  166.3 0.0 collective-permute-done.3
  166.3 2.5 fusion.9
  168.8 0.0 collective-permute-done.2
  168.9 4.4 %fusion.21 = (f32[1536]{0:T(1024)S(1)}, f32[2,128]{1,0:T(2,128)}, f32[2,128,1536]{2,1,0:T(8,128)S(1)}) fusion(bf16[2,128,1536]{2,1,0:T(8,128)(2,1)S(1)} %copy-done, f32[2,128]{1,0:T(2,128)S(1)} %copy-done.9, f32[1536]{0:T(1024)S(1)} %copy-done.7, f32[2,128,1536]{2,1,0:T(8,128)S(1)} %fusion.9, f32[2,128,1536]{2,1,0:T(8,128)S(1)} %fusion.7, ...), kind=kOutput, calls=%fused_computation.38 | convolution fusion | flops 616167680 | bytes 8370176 | tf_op jit(solution)/shard_map/bti,ci->btc/dot_general | solution.py:85
  173.3 42.5 %all-reduce.2 = (f32[1536]{0:T(1024)S(1)}, f32[768]{0:T(1024)S(1)}) all-reduce(f32[1536]{0:T(1024)S(1)} %broadcast_multiply_fusion, f32[768]{0:T(1024)S(1)} %broadcast_multiply_fusion.1), channel_id=4, replica_groups=mesh['groups'=1,'seq'=32] {'seq'}, use_global_device_ids=true, to_apply=%region_7.0.clone | all-reduce | flops 2304 | bytes 18432
  215.8 0.6 dynamic-slice
  216.4 0.6 dynamic-slice.1
  217.0 0.7 multiply_multiply_fusion.5
  217.7 2.1 fusion.26
  219.8 37.8 %reduce-scatter.7.cloned.1.call-done = f32[48,768]{1,0:T(8,128)} async-done(((f32[1536,768]{1,0:T(8,128)}), f32[48,768]{1,0:T(8,128)}) %reduce-scatter.7.cloned.1.call-update) | async-done | bytes 147472
  257.5 169.5 %reduce-scatter.5.cloned.1.call-done = f32[48,3,768]{2,0,1:T(8,128)} async-done(((f32[1536,3,768]{2,0,1:T(8,128)}), f32[48,3,768]{2,0,1:T(8,128)}) %reduce-scatter.5.cloned.1.call-update) | async-done | bytes 442384 | tf_op jit(solution)/shard_map/reduce_scatter | solution.py:44
  (25 shorter events, 0.1 us)
Async XLA Ops:
  7.2 2.9 copy-start
  7.2 79.3 %all-gather.3.cloned.1.call-start = ((), (), s32[]{:S(2)}) async-start(), calls=%async_computation.2 | async-start | bytes 7299072 | tf_op jit(solution)/shard_map/all_gather | solution.py:52
  7.9 137.3 %all-gather.5.cloned.1.call-start = ((), (), s32[]{:S(2)}) async-start(), calls=%async_computation.3 | async-start | bytes 2433024 | tf_op jit(solution)/shard_map/all_gather | solution.py:53
  8.7 248.9 %reduce-scatter.7.cloned.1.call-start = ((), (), s32[]{:S(2)}) async-start(), calls=%async_computation.5 | async-start | bytes 4866048
  10.1 78.9 %copy-start.8 = (f32[2,128]{1,0:T(2,128)}, f32[2,128]{1,0:T(2,128)S(1)}, u32[]{:S(2)}) copy-start(f32[2,128]{1,0:T(2,128)S(1)} %fusion.42) | copy-start | bytes 3076
  11.5 80.0 %collective-permute-start = (bf16[2,32,1536]{2,1,0:T(8,128)(2,1)S(1)}, bf16[2,32,1536]{2,1,0:T(8,128)(2,1)S(1)}, u32[]{:S(2)}, u32[]{:S(2)}) collective-permute-start(bf16[2,32,1536]{2,1,0:T(8,128)(2,1)S(1)} %get-tuple-element.24), channel_id=1, source_target_pairs={{0,1},{1,2},{2,3},{3,4},{4,5},{5,6},{6,7},{7,8},{8,9},{9,10},{10,1... | collective-permute-start | bytes 589832 | tf_op jit(solution)/shard_map/ppermute | solution.py:20
  13.9 75.0 %collective-permute-start.1 = (bf16[2,32,1536]{2,1,0:T(8,128)(2,1)S(1)}, bf16[2,32,1536]{2,1,0:T(8,128)(2,1)S(1)}, u32[]{:S(2)}, u32[]{:S(2)}) collective-permute-start(bf16[2,32,1536]{2,1,0:T(8,128)(2,1)S(1)} %get-tuple-element.25), channel_id=1, source_target_pairs={{1,0},{2,1},{3,2},{4,3},{5,4},{6,5},{7,6},{8,7},{9,8},{10,9},{11,1... | collective-permute-start | bytes 589832 | tf_op jit(solution)/shard_map/ppermute | solution.py:23
  89.0 2.5 copy-start.4
  91.5 2.7 copy-start.1
  91.5 2.7 copy-start.6
  91.5 2.7 copy-start.2
  103.5 323.5 %reduce-scatter.5.cloned.1.call-start = ((), (), s32[]{:S(2)}) async-start(), calls=%async_computation.4 | async-start | bytes 14598144 | tf_op jit(solution)/shard_map/reduce_scatter | solution.py:44
  148.8 0.9 copy-start.3
  149.8 0.9 copy-start.5
  157.9 4.9 %copy-start.11 = (bf16[1536,768]{1,0:T(8,128)(2,1)S(1)}, bf16[1536,768]{1,0:T(8,128)(2,1)}, u32[]{:S(2)}) copy-start(bf16[1536,768]{1,0:T(8,128)(2,1)} %all-gather.5.cloned.1.call-done) | copy-start | bytes 7077892
  157.9 8.4 %collective-permute-start.3 = (bf16[2,32,768]{2,1,0:T(8,128)(2,1)S(1)}, bf16[2,32,768]{2,1,0:T(8,128)(2,1)S(1)}, u32[]{:S(2)}, u32[]{:S(2)}) collective-permute-start(bf16[2,32,768]{2,1,0:T(8,128)(2,1)S(1)} %get-tuple-element.27), channel_id=1, source_target_pairs={{0,1},{1,2},{2,3},{3,4},{4,5},{5,6},{6,7},{7,8},{8,9},{9,10},{10,1... | collective-permute-start | bytes 294920 | tf_op jit(solution)/shard_map/ppermute | solution.py:20
  162.8 1.9 copy-start.10
  164.6 4.2 copy-start.7
  164.6 4.2 copy-start.9
  164.6 4.2 collective-permute-start.2
Sparse Core Ops, SparseCore 0:
  11.0 75.5 all-gather.2
  89.4 55.7 all-gather.4
  151.3 106.2 reduce-scatter.6
  265.0 161.9 reduce-scatter.4
where the time goes:
time: 434 us
  waiting for transfers between devices  322 us (74%)
  blocking collectives  42.5 us (10%)
  matrix products  28.2 us (6%)
  between operations  14.1 us (3%)
  other arithmetic  11.2 us (3%)
  local copies, waits for them, and re-layouts  8.18 us (2%)
  starting transfers between devices  7.73 us (2%)
    reduce_scatter x1, waiting for transfers between devices, reduce_dilated(): lax.psum_scatter(jnp.stack(tap_slices, axis=1) * factor, 'seq', scatter_d...  169 us
    all_gather x1, waiting for transfers between devices, body(): lax.all_gather(dilated_kernel_weight, 'seq', axis=0, tiled=True)  71.3 us
    unnamed x1, blocking collectives  42.5 us
    all_gather x1, waiting for transfers between devices, body(): full_project = lax.all_gather(project_weight, 'seq', axis=0, tiled=True)  41.6 us
    unnamed x5, waiting for transfers between devices  39.2 us
    dot_general x3, matrix products, body(): jnp.einsum('bti,ci->btc', padded_input_gradient[:, tap_shift:tap_shift +...  9.53 us
  transfers between devices with their start and end apart: 8, of which 4 were waited for; matrix products, arithmetic and copies ran while one was open for 11% of the time, Pallas kernels for 0%

commit v1 on v0

--- a/solution.py
+++ b/solution.py
@@ -3,10 +3,13 @@
 import jax
 import jax.numpy as jnp
 from jax import lax
+from jax.experimental import pallas as pl
+from jax.experimental.pallas import tpu as pltpu
 from jax.sharding import PartitionSpec as P
 
 KERNEL_TAPS = 3
 DILATION_STEP = 32
+TORUS_DEVICES = 32
 
 
 eps = 1e-06
@@ -46,7 +49,7 @@
     )
 
 
-def body(features, cotangent, dilated_kernel_weight, project_weight, outer_gain, inner_gain):
+def body_any(features, cotangent, dilated_kernel_weight, project_weight, outer_gain, inner_gain):
     bin_count = features.shape[1]
     factor = 1.0 / math.sqrt(features.shape[0] * bin_count * lax.axis_size("seq"))
     full_dilated = lax.all_gather(dilated_kernel_weight, "seq", axis=0, tiled=True)
@@ -103,6 +106,267 @@
         lax.psum_scatter(grad_gain_inner * factor, "seq", scatter_dimension=0, tiled=True),
     )
     return (block_out, grad_features, grad_dilated, grad_project, grad_outer_gain, grad_inner_gain)
+
+
+def links(move):
+    return [(i, move(i)) for i in range(TORUS_DEVICES)]
+
+
+CORE = links(lambda i: i ^ 1)
+FIRST = links(lambda i: i ^ (4 if i & 1 else 2))
+SECOND = links(lambda i: i ^ (2 if i & 1 else 4))
+UP = links(lambda i: (i + 8) % TORUS_DEVICES)
+DOWN = links(lambda i: (i - 8) % TORUS_DEVICES)
+
+
+def send(block, pairs):
+    return lax.ppermute(block, "seq", pairs)
+
+
+def cat(*parts):
+    return jnp.concatenate(parts, axis=0)
+
+
+def gather_z(block):
+    half = block.shape[0] // 2
+    below = send(block, UP)
+    above = send(block, DOWN)
+    far_low = send(below[:half], UP)
+    far_high = send(above[half:], DOWN)
+    return cat(block, above, far_low, far_high, below)
+
+
+def scatter_z(total):
+    n = total.shape[0] // 4
+    half = n // 2
+    message = total[2 * n : 3 * n].astype(jnp.bfloat16)
+    low = send(message[:half], UP).astype(jnp.float32)
+    high = send(message[half:], DOWN).astype(jnp.float32)
+    to_up = cat(total[n : n + half] + low, total[n + half : 2 * n]).astype(jnp.bfloat16)
+    to_down = cat(total[3 * n : 3 * n + half], total[3 * n + half :] + high).astype(jnp.bfloat16)
+    from_below = send(to_up, UP).astype(jnp.float32)
+    from_above = send(to_down, DOWN).astype(jnp.float32)
+    return total[:n] + from_below + from_above
+
+
+def scatter_pair(total, pairs):
+    n = total.shape[0] // 2
+    return total[:n] + send(total[n:].astype(jnp.bfloat16), pairs).astype(jnp.float32)
+
+
+def block_orders():
+    both = [(m, r2, r1, k) for r2 in (0, 1) for r1 in (0, 1) for k in range(4) for m in (0, 1)]
+    last = [(2, r2, r1, k) for r2 in (0, 1) for k in range(4) for r1 in (0, 1)]
+    proj = [(3, r2, r1, k) for k in range(4) for r2 in (0, 1) for r1 in (0, 1)]
+    return both + last + proj
+
+
+def order_kernel(index_ref, source_ref, own_ref, other_ref):
+    device = index_ref[0]
+    core = device & 1
+    x = (device >> 1) & 1
+    y = (device >> 2) & 1
+    z = device >> 3
+    for at, (matrix, r2, r1, k) in enumerate(block_orders()):
+        zk = (z + k) & 3
+        for target, parity in ((own_ref, core), (other_ref, 1 - core)):
+            dx = r1 + parity * (r2 - r1)
+            dy = r2 + parity * (r1 - r2)
+            block = zk * 8 + (y ^ dy) * 4 + (x ^ dx) * 2 + parity
+            target[at] = source_ref[matrix, block]
+
+
+def in_arrival_order(source):
+    shape = jax.ShapeDtypeStruct((64,) + source.shape[2:], source.dtype)
+    index = lax.axis_index("seq").astype(jnp.int32).reshape(1)
+    return pl.pallas_call(
+        order_kernel,
+        out_shape=(shape, shape),
+        in_specs=[
+            pl.BlockSpec(memory_space=pltpu.SMEM),
+            pl.BlockSpec(memory_space=pltpu.VMEM),
+        ],
+        out_specs=[
+            pl.BlockSpec(memory_space=pltpu.VMEM),
+            pl.BlockSpec(memory_space=pltpu.VMEM),
+        ],
+        compiler_params=pltpu.CompilerParams(vmem_limit_bytes=32 << 20),
+        name="order",
+    )(index, source)
+
+
+def natural_kernel(index_ref, own0, other0, own2, other2, own3, other3, *rest):
+    targets, sems = rest[:4], rest[4]
+    device = index_ref[0]
+    core = device & 1
+    x = (device >> 1) & 1
+    y = (device >> 2) & 1
+    z = device >> 3
+    copies = []
+    for at, (matrix, r2, r1, k) in enumerate(block_orders()):
+        zk = (z + k) & 3
+        if at < 32:
+            pair, local = (own0, other0), at
+        elif at < 48:
+            pair, local = (own2, other2), at - 32
+        else:
+            pair, local = (own3, other3), at - 48
+        for side, (source, parity) in enumerate(zip(pair, (core, 1 - core))):
+            dx = r1 + parity * (r2 - r1)
+            dy = r2 + parity * (r1 - r2)
+            block = zk * 8 + (y ^ dy) * 4 + (x ^ dx) * 2 + parity
+            copies.append(
+                pltpu.make_async_copy(
+                    source.at[local], targets[matrix].at[block], sems.at[2 * at + side]
+                )
+            )
+    for copy in copies:
+        copy.start()
+    for copy in copies:
+        copy.wait()
+
+
+def in_natural_order(own0, other0, own2, other2, own3, other3):
+    rows, inner = own0.shape[1:]
+    shape = jax.ShapeDtypeStruct((32, rows, inner), own0.dtype)
+    index = lax.axis_index("seq").astype(jnp.int32).reshape(1)
+    whole = pl.pallas_call(
+        natural_kernel,
+        out_shape=(shape,) * 4,
+        in_specs=[pl.BlockSpec(memory_space=pltpu.SMEM)]
+        + [pl.BlockSpec(memory_space=pl.ANY)] * 6,
+        out_specs=[pl.BlockSpec(memory_space=pl.ANY)] * 4,
+        scratch_shapes=[pltpu.SemaphoreType.DMA((128,))],
+        name="natural",
+    )(index, own0, other0, own2, other2, own3, other3)
+    return [array.reshape(32 * rows, inner) for array in whole]
+
+
+def rows_dot(left, right):
+    return jnp.einsum("nrt,ti->nri", left, right, preferred_element_type=jnp.float32)
+
+
+def contract(left, right):
+    n, rows, tokens = left.shape
+    return jnp.einsum(
+        "ct,ci->ti",
+        left.reshape(n * rows, tokens),
+        right.reshape(n * rows, right.shape[2]),
+        preferred_element_type=jnp.float32,
+    )
+
+
+def body_torus(features, cotangent, dilated_kernel_weight, project_weight, outer_gain, inner_gain):
+    batch, bin_count, channels = features.shape
+    inner = project_weight.shape[1]
+    rows = project_weight.shape[0]
+    tokens = batch * bin_count
+    factor = 1.0 / math.sqrt(tokens * TORUS_DEVICES)
+
+    taps01 = jnp.stack([dilated_kernel_weight[:, 0, :], dilated_kernel_weight[:, 1, :]])
+    tail = jnp.stack([dilated_kernel_weight[:, 2, :], project_weight])
+    tail_first = send(tail, FIRST)
+    plane0 = gather_z(taps01)
+    tap2 = cat(tail[:1], tail_first[:1])
+    proj = cat(tail[1:], tail_first[1:])
+    proj = cat(proj, send(proj, SECOND))
+    near2 = gather_z(tap2)
+    near0 = cat(plane0, send(plane0, FIRST))
+    far0 = send(near0, SECOND)
+    far2 = send(near2, SECOND)
+    own3 = gather_z(proj)
+    own0 = cat(near0, far0)
+    own2 = cat(near2, far2)
+    other0 = cat(send(near0, CORE), send(far0, CORE))
+    other2 = cat(send(near2, CORE), send(far2, CORE))
+    other3 = send(own3, CORE)
+
+    features_padded = padded(features, (("seq", 1),), DILATION_STEP)
+    active = act_norm(features_padded.astype(jnp.float32), outer_gain).astype(jnp.bfloat16)
+    turned = [
+        active[:, tap * DILATION_STEP : tap * DILATION_STEP + bin_count]
+        .reshape(tokens, channels)
+        .T.reshape(32, rows, tokens)
+        for tap in range(KERNEL_TAPS)
+    ]
+    turned.append(cotangent.reshape(tokens, channels).T.reshape(32, rows, tokens))
+    act_own, act_other = in_arrival_order(jnp.stack(turned))
+
+    conv_output = (
+        contract(act_own[:32], own0)
+        + contract(act_other[:32], other0)
+        + contract(act_own[32:48], own2)
+        + contract(act_other[32:48], other2)
+    )
+    hidden32, pull_inner = jax.vjp(act_norm, conv_output, inner_gain)
+    hidden = hidden32.astype(jnp.bfloat16)
+
+    keep3 = rows_dot(act_own[48:], hidden)
+    give3 = rows_dot(act_other[48:], hidden).astype(jnp.bfloat16)
+    sum3 = keep3 + send(give3, CORE).astype(jnp.float32)
+    sum3 = scatter_z(sum3)
+    sum3 = scatter_pair(sum3, SECOND)
+    sum3 = scatter_pair(sum3, FIRST)
+    grad_project = sum3[0] * factor
+
+    grad_hidden = contract(act_own[48:], own3) + contract(act_other[48:], other3)
+    grad_conv, grad_gain_inner = pull_inner(grad_hidden)
+    grad_conv = grad_conv.astype(jnp.bfloat16)
+
+    keep0 = rows_dot(act_own[:32], grad_conv)
+    give0 = rows_dot(act_other[:32], grad_conv).astype(jnp.bfloat16)
+    keep2 = rows_dot(act_own[32:48], grad_conv)
+    give2 = rows_dot(act_other[32:48], grad_conv).astype(jnp.bfloat16)
+    sum0 = keep0 + send(give0, CORE).astype(jnp.float32)
+    sum2 = keep2 + send(give2, CORE).astype(jnp.float32)
+    sum2 = scatter_pair(sum2, SECOND)
+    sum0 = scatter_pair(sum0, SECOND)
+    sum2 = scatter_z(sum2)
+    sum0 = scatter_pair(sum0, FIRST)
+    sum2 = scatter_pair(sum2, FIRST)
+    sum0 = scatter_z(sum0)
+    grad_dilated = jnp.stack([sum0[0], sum0[1], sum2[0]], axis=1) * factor
+
+    weights = in_natural_order(own0, other0, own2, other2, own3, other3)
+    block_out = (
+        features.astype(jnp.float32)
+        + jnp.einsum(
+            "bti,ci->btc",
+            hidden.reshape(batch, bin_count, inner),
+            weights[3],
+            preferred_element_type=jnp.float32,
+        )
+    ).astype(jnp.bfloat16)
+    grad_padded = padded(
+        grad_conv.reshape(batch, bin_count, inner), (("seq", 1),), DILATION_STEP
+    )
+    grad_active = jnp.zeros(features.shape, jnp.float32)
+    for tap in range(KERNEL_TAPS):
+        shift = (KERNEL_TAPS - 1 - tap) * DILATION_STEP
+        grad_active = grad_active + jnp.einsum(
+            "bti,ci->btc",
+            grad_padded[:, shift : shift + bin_count],
+            weights[tap],
+            preferred_element_type=jnp.float32,
+        )
+    unused, pull_outer = jax.vjp(act_norm, features.astype(jnp.float32), outer_gain)
+    grad_branch, grad_gain_outer = pull_outer(grad_active)
+    grad_features = (cotangent.astype(jnp.float32) + grad_branch).astype(jnp.bfloat16)
+
+    gains = jnp.concatenate([grad_gain_outer, grad_gain_inner]) * factor
+    for distance in (1, 2, 4, 8, 16):
+        gains = gains + send(gains, links(lambda i: i ^ distance))
+    device = lax.axis_index("seq")
+    grad_outer_gain = lax.dynamic_slice(gains, (device * rows,), (rows,))
+    part = inner // TORUS_DEVICES
+    grad_inner_gain = lax.dynamic_slice(gains, (channels + device * part,), (part,))
+    return (block_out, grad_features, grad_dilated, grad_project, grad_outer_gain, grad_inner_gain)
+
+
+def body(*operands):
+    if lax.axis_size("seq") == TORUS_DEVICES:
+        return body_torus(*operands)
+    return body_any(*operands)
 
 
 def solution(mesh):

time: 434 us -> 488 us (1.12)
  Pallas kernels: 0 us -> 288 us
  waiting for transfers between devices: 322 us -> 46.1 us
  starting transfers between devices: 7.73 us -> 81.6 us
  blocking collectives: 42.5 us -> 0 us
  local copies, waits for them, and re-layouts: 8.18 us -> 31.4 us
  between operations: 14.1 us -> 1.42 us
    pallas_call x0 -> x2, Pallas kernels: none -> 288 us  [the longest x1 288 us: in_natural_order(): pl.pallas_call(natural_kernel, out_shape=(shape,) * 4, in_specs=[pl.Block...]
    reduce_scatter x1 -> x0, waiting for transfers between devices: 169 us -> none  [reduce_dilated(): lax.psum_scatter(jnp.stack(tap_slices, axis=1) * factor, 'seq', scatter_d...]
    all_gather x2 -> x0, waiting for transfers between devices: 113 us -> none  [the longest x1 71.3 us: body(): lax.all_gather(dilated_kernel_weight, 'seq', axis=0, tiled=True)]
    ppermute x0 -> x48, starting transfers between devices: none -> 72.7 us  [send(): return lax.ppermute(block, 'seq', pairs)]
    ppermute x0 -> x48, waiting for transfers between devices: none -> 46.1 us  [send(): return lax.ppermute(block, 'seq', pairs)]
    unnamed x1 -> x0, blocking collectives: 42.5 us -> none
    unnamed x5 -> x0, waiting for transfers between devices: 39.2 us -> none
    unnamed x27 -> x73, local copies, waits for them, and re-layouts: 8.13 us -> 16 us
  transfers between devices with their start and end apart: 8 -> 52, of which waited for: 4 -> 15; matrix products, arithmetic and copies ran while one was open for 11% -> 12% of each run, Pallas kernels for 0% -> 59%
where the time goes in v1:
time: 488 us; the launch traced here: 487 us
  Pallas kernels  288 us (59%)
  starting transfers between devices  81.6 us (17%)
  waiting for transfers between devices  46.1 us (9%)
  local copies, waits for them, and re-layouts  31.4 us (6%)
  matrix products  27.7 us (6%)
  other arithmetic  10.6 us (2%)
    pallas_call x1, Pallas kernels, in_natural_order(): pl.pallas_call(natural_kernel, out_shape=(shape,) * 4, in_specs=[pl.Block...  288 us
    ppermute x48, starting transfers between devices, send(): return lax.ppermute(block, 'seq', pairs)  72.7 us
    ppermute x48, waiting for transfers between devices, send(): return lax.ppermute(block, 'seq', pairs)  46.1 us
    unnamed x73, local copies, waits for them, and re-layouts  16 us
    dot_general x6, matrix products, rows_dot(): jnp.einsum('nrt,ti->nri', left, right, preferred_element_type=jnp.float32)  10 us
  transfers between devices with their start and end apart: 52, of which 15 were waited for; matrix products, arithmetic and copies ran while one was open for 12% of the time, Pallas kernels for 59%

profile of v1, /device:TPU:0, one launch (start us, length us, event | category | flops | bytes accessed | tf_op | source)
XLA Modules:
  0.0 487.1 jit_solution(7326280792239964178)
XLA Ops:
  2.5 5.0 %collective-permute-start.2 = (bf16[2,48,768]{2,1,0:T(8,128)(2,1)}, bf16[2,48,768]{2,1,0:T(8,128)(2,1)}, u32[]{:S(2)}, u32[]{:S(2)}) collective-permute-start(bf16[2,48,768]{2,1,0:T(8,128)(2,1)} %pad_maximum_fusion.11), channel_id=1, source_target_pairs={{0,24},{1,25},{2,26},{3,27},{4,28},{5,29},{6,30},{7,31},{8,0},{9,1... | collective-permute-start | bytes 442376 | tf_op jit(solution)/shard_map/ppermute | solution.py:123
  7.5 1.8 fusion.78
  10.6 3.0 collective-permute-start
  19.0 2.4 collective-permute-done.10
  21.4 1.6 fusion.82
  23.7 3.7 collective-permute-start.11
  29.7 1.7 constant_dynamic-update-slice_fusion.10
  31.4 3.8 collective-permute-start.5
  40.8 1.7 constant_dynamic-update-slice_fusion.9
  44.1 1.7 constant_dynamic-update-slice_fusion.7
  46.5 2.0 collective-permute-start.19
  50.4 3.8 collective-permute-start.14
  55.8 7.1 %collective-permute-done.13 = bf16[1,48,768]{2,1,0:T(8,128)(2,1)S(1)} collective-permute-done((bf16[1,48,768]{2,1,0:T(8,128)(2,1)S(1)}, bf16[1,48,768]{2,1,0:T(8,128)(2,1)S(1)}, u32[]{:S(2)}, u32[]{:S(2)}) %collective-permute-start.13) | collective-permute-done | bytes 73760 | tf_op jit(solution)/shard_map/ppermute | solution.py:123
  64.2 1.6 collective-permute-start.21
  68.4 2.3 collective-permute-start.22
  73.1 2.0 collective-permute-done.22
  75.4 1.9 collective-permute-done.15
  80.4 1.8 convolution_bitcast_fusion.3
  82.3 7.7 %collective-permute-done.7 = bf16[16,48,768]{2,1,0:T(8,128)(2,1)S(1)} collective-permute-done((bf16[16,48,768]{2,1,0:T(8,128)(2,1)}, bf16[16,48,768]{2,1,0:T(8,128)(2,1)S(1)}, u32[]{:S(2)}, u32[]{:S(2)}) %collective-permute-start.7) | collective-permute-done | bytes 1179680 | tf_op jit(solution)/shard_map/ppermute | solution.py:123
  97.0 2.2 convolution_convert_fusion
  99.9 3.2 collective-permute-start.25
  103.1 288.2 %natural.1 = (bf16[32,48,768]{2,1,0:T(8,128)(2,1)}, bf16[32,48,768]{2,1,0:T(8,128)(2,1)}, bf16[32,48,768]{2,1,0:T(8,128)(2,1)}, bf16[32,48,768]{2,1,0:T(8,128)(2,1)}) custom-call(s32[1]{0:T(128)} %bitcast.index_ref, bf16[32,48,768]{2,1,0:T(8,128)(2,1)} %copy-done.10, bf16[32,48,768]{2,1,0:T(8,128)(2,1)} %copy-done.3, ...), custom_call_target="tpu_custom_call" | custom-call | tf_op jit(solution)/shard_map/natural/pallas_call | solution.py:233
  391.3 2.6 fusion.84
  398.2 1.9 fusion.40
  400.2 3.8 fusion.20
  406.0 2.2 collective-permute-start.48
  408.2 1.7 collective-permute-done.48
  409.9 2.1 collective-permute-start.49
  412.0 3.7 fusion.1
  415.7 2.0 collective-permute-start.50
  417.7 1.7 collective-permute-done.50
  419.5 2.6 collective-permute-start.51
  422.1 1.7 fusion.83
  424.1 3.6 collective-permute-start.43
  428.3 2.1 collective-permute-start.34
  431.1 3.9 collective-permute-start.44
  435.1 2.6 convert_add_fusion
  437.8 2.1 collective-permute-start.27
  442.5 3.5 collective-permute-done.42
  447.9 1.9 collective-permute-start.35
  449.8 2.0 collective-permute-start.37
  451.8 4.9 %collective-permute-done.45 = bf16[2,48,768]{2,1,0:T(8,128)(2,1)S(1)} collective-permute-done((bf16[2,48,768]{2,1,0:T(8,128)(2,1)S(1)}, bf16[2,48,768]{2,1,0:T(8,128)(2,1)S(1)}, u32[]{:S(2)}, u32[]{:S(2)}) %collective-permute-start.45) | collective-permute-done | bytes 147488 | tf_op jit(solution)/shard_map/ppermute | solution.py:123
  459.3 4.1 collective-permute-start.38
  464.2 3.5 collective-permute-done.28
  469.2 2.9 collective-permute-start.31
  475.2 4.0 collective-permute-start.32
  479.3 2.6 collective-permute-done.32
  481.9 4.3 collective-permute-done.30
  (221 shorter events, 61.4 us)
Async XLA Ops:
  2.5 25.7 %collective-permute-start.2 = (bf16[2,48,768]{2,1,0:T(8,128)(2,1)}, bf16[2,48,768]{2,1,0:T(8,128)(2,1)}, u32[]{:S(2)}, u32[]{:S(2)}) collective-permute-start(bf16[2,48,768]{2,1,0:T(8,128)(2,1)} %pad_maximum_fusion.11), channel_id=1, source_target_pairs={{0,24},{1,25},{2,26},{3,27},{4,28},{5,29},{6,30},{7,31},{8,0},{9,1... | collective-permute-start | bytes 442376 | tf_op jit(solution)/shard_map/ppermute | solution.py:123
  7.5 19.9 %collective-permute-start.3 = (bf16[2,48,768]{2,1,0:T(8,128)(2,1)}, bf16[2,48,768]{2,1,0:T(8,128)(2,1)S(1)}, u32[]{:S(2)}, u32[]{:S(2)}) collective-permute-start(bf16[2,48,768]{2,1,0:T(8,128)(2,1)} %pad_maximum_fusion.11), channel_id=1, source_target_pairs={{0,8},{1,9},{2,10},{3,11},{4,12},{5,13},{6,14},{7,15},{8,16},{9,17... | collective-permute-start | bytes 442376 | tf_op jit(solution)/shard_map/ppermute | solution.py:123
  9.3 22.1 %collective-permute-start.1 = (bf16[2,32,1536]{2,1,0:T(8,128)(2,1)}, bf16[2,32,1536]{2,1,0:T(8,128)(2,1)S(1)}, u32[]{:S(2)}, u32[]{:S(2)}) collective-permute-start(bf16[2,32,1536]{2,1,0:T(8,128)(2,1)} %get-tuple-element.42), channel_id=1, source_target_pairs={{1,0},{2,1},{3,2},{4,3},{5,4},{6,5},{7,6},{8,7},{9,8},{10,9},{11,1... | collective-permute-start | bytes 589832 | tf_op jit(solution)/shard_map/ppermute | solution.py:26
  10.6 24.6 %collective-permute-start = (bf16[2,32,1536]{2,1,0:T(8,128)(2,1)}, bf16[2,32,1536]{2,1,0:T(8,128)(2,1)S(1)}, u32[]{:S(2)}, u32[]{:S(2)}) collective-permute-start(bf16[2,32,1536]{2,1,0:T(8,128)(2,1)} %get-tuple-element.41), channel_id=1, source_target_pairs={{0,1},{1,2},{2,3},{3,4},{4,5},{5,6},{6,7},{7,8},{8,9},{9,10},{10,1... | collective-permute-start | bytes 589832 | tf_op jit(solution)/shard_map/ppermute | solution.py:23
  14.3 7.0 %collective-permute-start.10 = (bf16[2,48,768]{2,1,0:T(8,128)(2,1)}, bf16[2,48,768]{2,1,0:T(8,128)(2,1)}, u32[]{:S(2)}, u32[]{:S(2)}) collective-permute-start(bf16[2,48,768]{2,1,0:T(8,128)(2,1)} %pad_maximum_fusion.10), channel_id=1, source_target_pairs={{0,2},{1,5},{2,0},{3,7},{4,6},{5,1},{6,4},{7,3},{8,10},{9,13},{10,... | collective-permute-start | bytes 442376 | tf_op jit(solution)/shard_map/ppermute | solution.py:123
  23.7 25.8 %collective-permute-start.11 = (bf16[2,48,768]{2,1,0:T(8,128)(2,1)}, bf16[2,48,768]{2,1,0:T(8,128)(2,1)}, u32[]{:S(2)}, u32[]{:S(2)}) collective-permute-start(bf16[2,48,768]{2,1,0:T(8,128)(2,1)} %pad_maximum_fusion.9), channel_id=1, source_target_pairs={{0,24},{1,25},{2,26},{3,27},{4,28},{5,29},{6,30},{7,31},{8,0},{9,1... | collective-permute-start | bytes 442376 | tf_op jit(solution)/shard_map/ppermute | solution.py:123
  27.4 21.2 %collective-permute-start.12 = (bf16[2,48,768]{2,1,0:T(8,128)(2,1)}, bf16[2,48,768]{2,1,0:T(8,128)(2,1)}, u32[]{:S(2)}, u32[]{:S(2)}) collective-permute-start(bf16[2,48,768]{2,1,0:T(8,128)(2,1)} %pad_maximum_fusion.9), channel_id=1, source_target_pairs={{0,8},{1,9},{2,10},{3,11},{4,12},{5,13},{6,14},{7,15},{8,16},{9,17... | collective-permute-start | bytes 442376 | tf_op jit(solution)/shard_map/ppermute | solution.py:123
  28.1 12.7 %collective-permute-start.4 = (bf16[1,48,768]{2,1,0:T(8,128)(2,1)}, bf16[1,48,768]{2,1,0:T(8,128)(2,1)}, u32[]{:S(2)}, u32[]{:S(2)}) collective-permute-start(bf16[1,48,768]{2,1,0:T(8,128)(2,1)} %slice.279), channel_id=1, source_target_pairs={{0,8},{1,9},{2,10},{3,11},{4,12},{5,13},{6,14},{7,15},{8,16},{9,17... | collective-permute-start | bytes 221192 | tf_op jit(solution)/shard_map/ppermute | solution.py:123
  31.4 11.2 %collective-permute-start.5 = (bf16[1,48,768]{2,1,0:T(8,128)(2,1)S(1)}, bf16[1,48,768]{2,1,0:T(8,128)(2,1)}, u32[]{:S(2)}, u32[]{:S(2)}) collective-permute-start(bf16[1,48,768]{2,1,0:T(8,128)(2,1)S(1)} %slice.280), channel_id=1, source_target_pairs={{0,24},{1,25},{2,26},{3,27},{4,28},{5,29},{6,30},{7,31},{8,0},{9,1... | collective-permute-start | bytes 221192 | tf_op jit(solution)/shard_map/ppermute | solution.py:123
  35.2 11.3 %collective-permute-start.18 = (bf16[2,48,768]{2,1,0:T(8,128)(2,1)}, bf16[2,48,768]{2,1,0:T(8,128)(2,1)S(1)}, u32[]{:S(2)}, u32[]{:S(2)}) collective-permute-start(bf16[2,48,768]{2,1,0:T(8,128)(2,1)} %pad_maximum_fusion.12), channel_id=1, source_target_pairs={{0,4},{1,3},{2,6},{3,1},{4,0},{5,7},{6,2},{7,5},{8,12},{9,11},{10,... | collective-permute-start | bytes 442376 | tf_op jit(solution)/shard_map/ppermute | solution.py:123
  45.8 25.4 %collective-permute-start.6 = (bf16[8,48,768]{2,1,0:T(8,128)(2,1)}, bf16[8,48,768]{2,1,0:T(8,128)(2,1)S(1)}, u32[]{:S(2)}, u32[]{:S(2)}) collective-permute-start(bf16[8,48,768]{2,1,0:T(8,128)(2,1)} %get-tuple-element.75), channel_id=1, source_target_pairs={{0,2},{1,5},{2,0},{3,7},{4,6},{5,1},{6,4},{7,3},{8,10},{9,13},{10,... | collective-permute-start | bytes 1769480 | tf_op jit(solution)/shard_map/ppermute | solution.py:123
  46.5 21.9 %collective-permute-start.19 = (bf16[4,48,768]{2,1,0:T(8,128)(2,1)S(1)}, bf16[4,48,768]{2,1,0:T(8,128)(2,1)S(1)}, u32[]{:S(2)}, u32[]{:S(2)}) collective-permute-start(bf16[4,48,768]{2,1,0:T(8,128)(2,1)S(1)} %pad_maximum_fusion.6), channel_id=1, source_target_pairs={{0,24},{1,25},{2,26},{3,27},{4,28},{5,29},{6,30},{7,31},{8,0},{9,1... | collective-permute-start | bytes 884744 | tf_op jit(solution)/shard_map/ppermute | solution.py:123
  48.5 15.7 %collective-permute-start.20 = (bf16[4,48,768]{2,1,0:T(8,128)(2,1)S(1)}, bf16[4,48,768]{2,1,0:T(8,128)(2,1)S(1)}, u32[]{:S(2)}, u32[]{:S(2)}) collective-permute-start(bf16[4,48,768]{2,1,0:T(8,128)(2,1)S(1)} %pad_maximum_fusion.6), channel_id=1, source_target_pairs={{0,8},{1,9},{2,10},{3,11},{4,12},{5,13},{6,14},{7,15},{8,16},{9,17... | collective-permute-start | bytes 884744 | tf_op jit(solution)/shard_map/ppermute | solution.py:123
  49.5 13.4 %collective-permute-start.13 = (bf16[1,48,768]{2,1,0:T(8,128)(2,1)S(1)}, bf16[1,48,768]{2,1,0:T(8,128)(2,1)S(1)}, u32[]{:S(2)}, u32[]{:S(2)}) collective-permute-start(bf16[1,48,768]{2,1,0:T(8,128)(2,1)S(1)} %slice.282), channel_id=1, source_target_pairs={{0,8},{1,9},{2,10},{3,11},{4,12},{5,13},{6,14},{7,15},{8,16},{9,17... | collective-permute-start | bytes 221192 | tf_op jit(solution)/shard_map/ppermute | solution.py:123
  50.4 13.2 %collective-permute-start.14 = (bf16[1,48,768]{2,1,0:T(8,128)(2,1)S(1)}, bf16[1,48,768]{2,1,0:T(8,128)(2,1)S(1)}, u32[]{:S(2)}, u32[]{:S(2)}) collective-permute-start(bf16[1,48,768]{2,1,0:T(8,128)(2,1)S(1)} %slice.283), channel_id=1, source_target_pairs={{0,24},{1,25},{2,26},{3,27},{4,28},{5,29},{6,30},{7,31},{8,0},{9,1... | collective-permute-start | bytes 221192 | tf_op jit(solution)/shard_map/ppermute | solution.py:123
  64.2 7.0 %collective-permute-start.21 = (bf16[2,48,768]{2,1,0:T(8,128)(2,1)S(1)}, bf16[2,48,768]{2,1,0:T(8,128)(2,1)S(1)}, u32[]{:S(2)}, u32[]{:S(2)}) collective-permute-start(bf16[2,48,768]{2,1,0:T(8,128)(2,1)S(1)} %slice.285), channel_id=1, source_target_pairs={{0,8},{1,9},{2,10},{3,11},{4,12},{5,13},{6,14},{7,15},{8,16},{9,17... | collective-permute-start | bytes 442376 | tf_op jit(solution)/shard_map/ppermute | solution.py:123
  67.4 12.1 %collective-permute-start.16 = (bf16[8,48,768]{2,1,0:T(8,128)(2,1)S(1)}, bf16[8,48,768]{2,1,0:T(8,128)(2,1)S(1)}, u32[]{:S(2)}, u32[]{:S(2)}) collective-permute-start(bf16[8,48,768]{2,1,0:T(8,128)(2,1)S(1)} %get-tuple-element.80), channel_id=1, source_target_pairs={{0,1},{1,0},{2,3},{3,2},{4,5},{5,4},{6,7},{7,6},{8,9},{9,8},{10,11... | collective-permute-start | bytes 1769480 | tf_op jit(solution)/shard_map/ppermute | solution.py:123
  67.4 9.9 %collective-permute-start.15 = (bf16[8,48,768]{2,1,0:T(8,128)(2,1)S(1)}, bf16[8,48,768]{2,1,0:T(8,128)(2,1)S(1)}, u32[]{:S(2)}, u32[]{:S(2)}) collective-permute-start(bf16[8,48,768]{2,1,0:T(8,128)(2,1)S(1)} %get-tuple-element.80), channel_id=1, source_target_pairs={{0,4},{1,3},{2,6},{3,1},{4,0},{5,7},{6,2},{7,5},{8,12},{9,11},{10,... | collective-permute-start | bytes 1769480 | tf_op jit(solution)/shard_map/ppermute | solution.py:123
  68.4 6.7 %collective-permute-start.22 = (bf16[2,48,768]{2,1,0:T(8,128)(2,1)S(1)}, bf16[2,48,768]{2,1,0:T(8,128)(2,1)S(1)}, u32[]{:S(2)}, u32[]{:S(2)}) collective-permute-start(bf16[2,48,768]{2,1,0:T(8,128)(2,1)S(1)} %slice.286), channel_id=1, source_target_pairs={{0,24},{1,25},{2,26},{3,27},{4,28},{5,29},{6,30},{7,31},{8,0},{9,1... | collective-permute-start | bytes 442376 | tf_op jit(solution)/shard_map/ppermute | solution.py:123
  72.1 17.8 %collective-permute-start.7 = (bf16[16,48,768]{2,1,0:T(8,128)(2,1)}, bf16[16,48,768]{2,1,0:T(8,128)(2,1)S(1)}, u32[]{:S(2)}, u32[]{:S(2)}) collective-permute-start(bf16[16,48,768]{2,1,0:T(8,128)(2,1)} %get-tuple-element.51), channel_id=1, source_target_pairs={{0,4},{1,3},{2,6},{3,1},{4,0},{5,7},{6,2},{7,5},{8,12},{9,11},{10,... | collective-permute-start | bytes 3538952 | tf_op jit(solution)/shard_map/ppermute | solution.py:123
  75.1 15.4 %collective-permute-start.23 = (bf16[16,48,768]{2,1,0:T(8,128)(2,1)S(1)}, bf16[16,48,768]{2,1,0:T(8,128)(2,1)S(1)}, u32[]{:S(2)}, u32[]{:S(2)}) collective-permute-start(bf16[16,48,768]{2,1,0:T(8,128)(2,1)S(1)} %constant_dynamic-update-slice_fusion.38.own3), channel_id=1, source_target_pairs={{0,1},{1,0},{2,3},{3,2},{4,5},{5,4},{6,7},{7,6},{8,9},{9,8},{10,11... | collective-permute-start | bytes 3538952 | tf_op jit(solution)/shard_map/ppermute | solution.py:123
  77.3 4.9 %collective-permute-start.17 = (bf16[8,48,768]{2,1,0:T(8,128)(2,1)S(1)}, bf16[8,48,768]{2,1,0:T(8,128)(2,1)S(1)}, u32[]{:S(2)}, u32[]{:S(2)}) collective-permute-start(bf16[8,48,768]{2,1,0:T(8,128)(2,1)S(1)} %collective-permute-done.15), channel_id=1, source_target_pairs={{0,1},{1,0},{2,3},{3,2},{4,5},{5,4},{6,7},{7,6},{8,9},{9,8},{10,11... | collective-permute-start | bytes 1769480 | tf_op jit(solution)/shard_map/ppermute | solution.py:123
  79.0 12.6 %collective-permute-start.8 = (bf16[16,48,768]{2,1,0:T(8,128)(2,1)S(1)}, bf16[16,48,768]{2,1,0:T(8,128)(2,1)S(1)}, u32[]{:S(2)}, u32[]{:S(2)}) collective-permute-start(bf16[16,48,768]{2,1,0:T(8,128)(2,1)S(1)} %copy-done.22), channel_id=1, source_target_pairs={{0,1},{1,0},{2,3},{3,2},{4,5},{5,4},{6,7},{7,6},{8,9},{9,8},{10,11... | collective-permute-start | bytes 3538952 | tf_op jit(solution)/shard_map/ppermute | solution.py:123
  99.9 298.3 %collective-permute-start.25 = (bf16[2,32,768]{2,1,0:T(8,128)(2,1)}, bf16[2,32,768]{2,1,0:T(8,128)(2,1)}, u32[]{:S(2)}, u32[]{:S(2)}) collective-permute-start(bf16[2,32,768]{2,1,0:T(8,128)(2,1)} %get-tuple-element.54), channel_id=1, source_target_pairs={{0,1},{1,2},{2,3},{3,4},{4,5},{5,6},{6,7},{7,8},{8,9},{9,10},{10,1... | collective-permute-start | bytes 294920 | tf_op jit(solution)/shard_map/ppermute | solution.py:23
  393.9 6.1 %collective-permute-start.24 = (bf16[2,32,768]{2,1,0:T(8,128)(2,1)S(1)}, bf16[2,32,768]{2,1,0:T(8,128)(2,1)S(1)}, u32[]{:S(2)}, u32[]{:S(2)}) collective-permute-start(bf16[2,32,768]{2,1,0:T(8,128)(2,1)S(1)} %copy-done.19), channel_id=1, source_target_pairs={{1,0},{2,1},{3,2},{4,3},{5,4},{6,5},{7,6},{8,7},{9,8},{10,9},{11,1... | collective-permute-start | bytes 294920 | tf_op jit(solution)/shard_map/ppermute | solution.py:26
  395.2 39.8 %collective-permute-start.26 = (bf16[32,48,768]{2,1,0:T(8,128)(2,1)}, bf16[32,48,768]{2,1,0:T(8,128)(2,1)}, u32[]{:S(2)}, u32[]{:S(2)}) collective-permute-start(bf16[32,48,768]{2,1,0:T(8,128)(2,1)} %convolution_convert_fusion), channel_id=1, source_target_pairs={{0,1},{1,0},{2,3},{3,2},{4,5},{5,4},{6,7},{7,6},{8,9},{9,8},{10,11... | collective-permute-start | bytes 7077896 | tf_op jit(solution)/shard_map/ppermute | solution.py:123
  398.2 23.9 %collective-permute-start.40 = (bf16[16,48,768]{2,1,0:T(8,128)(2,1)}, bf16[16,48,768]{2,1,0:T(8,128)(2,1)}, u32[]{:S(2)}, u32[]{:S(2)}) collective-permute-start(bf16[16,48,768]{2,1,0:T(8,128)(2,1)} %convolution_convert_fusion.1), channel_id=1, source_target_pairs={{0,1},{1,0},{2,3},{3,2},{4,5},{5,4},{6,7},{7,6},{8,9},{9,8},{10,11... | collective-permute-start | bytes 3538952 | tf_op jit(solution)/shard_map/ppermute | solution.py:123
  406.0 21.8 %collective-permute-start.33 = (bf16[16,48,768]{2,1,0:T(8,128)(2,1)}, bf16[16,48,768]{2,1,0:T(8,128)(2,1)S(1)}, u32[]{:S(2)}, u32[]{:S(2)}) collective-permute-start(bf16[16,48,768]{2,1,0:T(8,128)(2,1)} %convolution_convert_fusion.2), channel_id=1, source_target_pairs={{0,1},{1,0},{2,3},{3,2},{4,5},{5,4},{6,7},{7,6},{8,9},{9,8},{10,11... | collective-permute-start | bytes 3538952 | tf_op jit(solution)/shard_map/ppermute | solution.py:123
  409.9 5.8 %collective-permute-start.49 = (f32[2304]{0:T(1024)S(1)}, f32[2304]{0:T(1024)S(1)}, u32[]{:S(2)}, u32[]{:S(2)}) collective-permute-start(f32[2304]{0:T(1024)S(1)} %add.213), channel_id=1, source_target_pairs={{0,4},{1,5},{2,6},{3,7},{4,0},{5,1},{6,2},{7,3},{8,12},{9,13},{10,... | collective-permute-start | bytes 27656 | tf_op jit(solution)/shard_map/ppermute | solution.py:123
  419.5 21.9 %collective-permute-start.51 = (f32[2304]{0:T(1024)S(1)}, f32[2304]{0:T(1024)S(1)}, u32[]{:S(2)}, u32[]{:S(2)}) collective-permute-start(f32[2304]{0:T(1024)S(1)} %add.215), channel_id=1, source_target_pairs={{0,16},{1,17},{2,18},{3,19},{4,20},{5,21},{6,22},{7,23},{8,24},{9,... | collective-permute-start | bytes 27656 | tf_op jit(solution)/shard_map/ppermute | solution.py:123
  423.9 7.1 %collective-permute-start.41 = (bf16[2,48,768]{2,1,0:T(8,128)(2,1)S(1)}, bf16[2,48,768]{2,1,0:T(8,128)(2,1)S(1)}, u32[]{:S(2)}, u32[]{:S(2)}) collective-permute-start(bf16[2,48,768]{2,1,0:T(8,128)(2,1)S(1)} %get-tuple-element.28), channel_id=1, source_target_pairs={{0,8},{1,9},{2,10},{3,11},{4,12},{5,13},{6,14},{7,15},{8,16},{9,17... | collective-permute-start | bytes 442376 | tf_op jit(solution)/shard_map/ppermute | solution.py:123
  424.1 6.9 %collective-permute-start.43 = (bf16[2,48,768]{2,1,0:T(8,128)(2,1)S(1)}, bf16[2,48,768]{2,1,0:T(8,128)(2,1)S(1)}, u32[]{:S(2)}, u32[]{:S(2)}) collective-permute-start(bf16[2,48,768]{2,1,0:T(8,128)(2,1)S(1)} %get-tuple-element.29), channel_id=1, source_target_pairs={{0,24},{1,25},{2,26},{3,27},{4,28},{5,29},{6,30},{7,31},{8,0},{9,1... | collective-permute-start | bytes 442376 | tf_op jit(solution)/shard_map/ppermute | solution.py:123
  428.3 19.4 %collective-permute-start.34 = (bf16[8,48,768]{2,1,0:T(8,128)(2,1)S(1)}, bf16[8,48,768]{2,1,0:T(8,128)(2,1)S(1)}, u32[]{:S(2)}, u32[]{:S(2)}) collective-permute-start(bf16[8,48,768]{2,1,0:T(8,128)(2,1)S(1)} %slice.394), channel_id=1, source_target_pairs={{0,4},{1,3},{2,6},{3,1},{4,0},{5,7},{6,2},{7,5},{8,12},{9,11},{10,... | collective-permute-start | bytes 1769480 | tf_op jit(solution)/shard_map/ppermute | solution.py:123
  431.1 11.4 %collective-permute-start.44 = (bf16[4,48,768]{2,1,0:T(8,128)(2,1)S(1)}, bf16[4,48,768]{2,1,0:T(8,128)(2,1)S(1)}, u32[]{:S(2)}, u32[]{:S(2)}) collective-permute-start(bf16[4,48,768]{2,1,0:T(8,128)(2,1)S(1)} %pad_maximum_fusion.8), channel_id=1, source_target_pairs={{0,24},{1,25},{2,26},{3,27},{4,28},{5,29},{6,30},{7,31},{8,0},{9,1... | collective-permute-start | bytes 884744 | tf_op jit(solution)/shard_map/ppermute | solution.py:123
  435.0 11.0 %collective-permute-start.42 = (bf16[4,48,768]{2,1,0:T(8,128)(2,1)S(1)}, bf16[4,48,768]{2,1,0:T(8,128)(2,1)S(1)}, u32[]{:S(2)}, u32[]{:S(2)}) collective-permute-start(bf16[4,48,768]{2,1,0:T(8,128)(2,1)S(1)} %pad_maximum_fusion.7), channel_id=1, source_target_pairs={{0,8},{1,9},{2,10},{3,11},{4,12},{5,13},{6,14},{7,15},{8,16},{9,17... | collective-permute-start | bytes 884744 | tf_op jit(solution)/shard_map/ppermute | solution.py:123
  437.8 19.6 %collective-permute-start.27 = (bf16[16,48,768]{2,1,0:T(8,128)(2,1)S(1)}, bf16[16,48,768]{2,1,0:T(8,128)(2,1)S(1)}, u32[]{:S(2)}, u32[]{:S(2)}) collective-permute-start(bf16[16,48,768]{2,1,0:T(8,128)(2,1)S(1)} %slice.393), channel_id=1, source_target_pairs={{0,4},{1,3},{2,6},{3,1},{4,0},{5,7},{6,2},{7,5},{8,12},{9,11},{10,... | collective-permute-start | bytes 3538952 | tf_op jit(solution)/shard_map/ppermute | solution.py:123
  446.1 10.6 %collective-permute-start.45 = (bf16[2,48,768]{2,1,0:T(8,128)(2,1)S(1)}, bf16[2,48,768]{2,1,0:T(8,128)(2,1)S(1)}, u32[]{:S(2)}, u32[]{:S(2)}) collective-permute-start(bf16[2,48,768]{2,1,0:T(8,128)(2,1)S(1)} %slice.396), channel_id=1, source_target_pairs={{0,4},{1,3},{2,6},{3,1},{4,0},{5,7},{6,2},{7,5},{8,12},{9,11},{10,... | collective-permute-start | bytes 442376 | tf_op jit(solution)/shard_map/ppermute | solution.py:123
  447.9 11.3 %collective-permute-start.35 = (bf16[1,48,768]{2,1,0:T(8,128)(2,1)S(1)}, bf16[1,48,768]{2,1,0:T(8,128)(2,1)S(1)}, u32[]{:S(2)}, u32[]{:S(2)}) collective-permute-start(bf16[1,48,768]{2,1,0:T(8,128)(2,1)S(1)} %get-tuple-element.47), channel_id=1, source_target_pairs={{0,8},{1,9},{2,10},{3,11},{4,12},{5,13},{6,14},{7,15},{8,16},{9,17... | collective-permute-start | bytes 221192 | tf_op jit(solution)/shard_map/ppermute | solution.py:123
  449.8 9.4 %collective-permute-start.37 = (bf16[1,48,768]{2,1,0:T(8,128)(2,1)S(1)}, bf16[1,48,768]{2,1,0:T(8,128)(2,1)S(1)}, u32[]{:S(2)}, u32[]{:S(2)}) collective-permute-start(bf16[1,48,768]{2,1,0:T(8,128)(2,1)S(1)} %get-tuple-element.48), channel_id=1, source_target_pairs={{0,24},{1,25},{2,26},{3,27},{4,28},{5,29},{6,30},{7,31},{8,0},{9,1... | collective-permute-start | bytes 221192 | tf_op jit(solution)/shard_map/ppermute | solution.py:123
  456.7 6.8 %collective-permute-start.46 = (bf16[1,48,768]{2,1,0:T(8,128)(2,1)S(1)}, bf16[1,48,768]{2,1,0:T(8,128)(2,1)S(1)}, u32[]{:S(2)}, u32[]{:S(2)}) collective-permute-start(bf16[1,48,768]{2,1,0:T(8,128)(2,1)S(1)} %slice.397), channel_id=1, source_target_pairs={{0,2},{1,5},{2,0},{3,7},{4,6},{5,1},{6,4},{7,3},{8,10},{9,13},{10,... | collective-permute-start | bytes 221192 | tf_op jit(solution)/shard_map/ppermute | solution.py:123
  457.8 9.9 %collective-permute-start.28 = (bf16[8,48,768]{2,1,0:T(8,128)(2,1)S(1)}, bf16[8,48,768]{2,1,0:T(8,128)(2,1)S(1)}, u32[]{:S(2)}, u32[]{:S(2)}) collective-permute-start(bf16[8,48,768]{2,1,0:T(8,128)(2,1)S(1)} %slice.395), channel_id=1, source_target_pairs={{0,2},{1,5},{2,0},{3,7},{4,6},{5,1},{6,4},{7,3},{8,10},{9,13},{10,... | collective-permute-start | bytes 1769480 | tf_op jit(solution)/shard_map/ppermute | solution.py:123
  459.3 12.8 %collective-permute-start.38 = (bf16[2,48,768]{2,1,0:T(8,128)(2,1)S(1)}, bf16[2,48,768]{2,1,0:T(8,128)(2,1)S(1)}, u32[]{:S(2)}, u32[]{:S(2)}) collective-permute-start(bf16[2,48,768]{2,1,0:T(8,128)(2,1)S(1)} %pad_maximum_fusion.16), channel_id=1, source_target_pairs={{0,24},{1,25},{2,26},{3,27},{4,28},{5,29},{6,30},{7,31},{8,0},{9,1... | collective-permute-start | bytes 442376 | tf_op jit(solution)/shard_map/ppermute | solution.py:123
  463.4 8.7 %collective-permute-start.36 = (bf16[2,48,768]{2,1,0:T(8,128)(2,1)S(1)}, bf16[2,48,768]{2,1,0:T(8,128)(2,1)S(1)}, u32[]{:S(2)}, u32[]{:S(2)}) collective-permute-start(bf16[2,48,768]{2,1,0:T(8,128)(2,1)S(1)} %pad_maximum_fusion.15), channel_id=1, source_target_pairs={{0,8},{1,9},{2,10},{3,11},{4,12},{5,13},{6,14},{7,15},{8,16},{9,17... | collective-permute-start | bytes 442376 | tf_op jit(solution)/shard_map/ppermute | solution.py:123
  467.9 7.2 %collective-permute-start.29 = (bf16[1,48,768]{2,1,0:T(8,128)(2,1)S(1)}, bf16[1,48,768]{2,1,0:T(8,128)(2,1)S(1)}, u32[]{:S(2)}, u32[]{:S(2)}) collective-permute-start(bf16[1,48,768]{2,1,0:T(8,128)(2,1)S(1)} %get-tuple-element.43), channel_id=1, source_target_pairs={{0,8},{1,9},{2,10},{3,11},{4,12},{5,13},{6,14},{7,15},{8,16},{9,17... | collective-permute-start | bytes 221192 | tf_op jit(solution)/shard_map/ppermute | solution.py:123
  469.2 6.0 %collective-permute-start.31 = (bf16[1,48,768]{2,1,0:T(8,128)(2,1)S(1)}, bf16[1,48,768]{2,1,0:T(8,128)(2,1)S(1)}, u32[]{:S(2)}, u32[]{:S(2)}) collective-permute-start(bf16[1,48,768]{2,1,0:T(8,128)(2,1)S(1)} %get-tuple-element.44), channel_id=1, source_target_pairs={{0,24},{1,25},{2,26},{3,27},{4,28},{5,29},{6,30},{7,31},{8,0},{9,1... | collective-permute-start | bytes 221192 | tf_op jit(solution)/shard_map/ppermute | solution.py:123
  472.2 7.1 %collective-permute-start.39 = (bf16[1,48,768]{2,1,0:T(8,128)(2,1)S(1)}, bf16[1,48,768]{2,1,0:T(8,128)(2,1)S(1)}, u32[]{:S(2)}, u32[]{:S(2)}) collective-permute-start(bf16[1,48,768]{2,1,0:T(8,128)(2,1)S(1)} %slice.398), channel_id=1, source_target_pairs={{0,2},{1,5},{2,0},{3,7},{4,6},{5,1},{6,4},{7,3},{8,10},{9,13},{10,... | collective-permute-start | bytes 221192 | tf_op jit(solution)/shard_map/ppermute | solution.py:123
  475.2 6.7 %collective-permute-start.32 = (bf16[2,48,768]{2,1,0:T(8,128)(2,1)S(1)}, bf16[2,48,768]{2,1,0:T(8,128)(2,1)S(1)}, u32[]{:S(2)}, u32[]{:S(2)}) collective-permute-start(bf16[2,48,768]{2,1,0:T(8,128)(2,1)S(1)} %pad_maximum_fusion.14), channel_id=1, source_target_pairs={{0,24},{1,25},{2,26},{3,27},{4,28},{5,29},{6,30},{7,31},{8,0},{9,1... | collective-permute-start | bytes 442376 | tf_op jit(solution)/shard_map/ppermute | solution.py:123
  479.2 7.0 %collective-permute-start.30 = (bf16[2,48,768]{2,1,0:T(8,128)(2,1)S(1)}, bf16[2,48,768]{2,1,0:T(8,128)(2,1)S(1)}, u32[]{:S(2)}, u32[]{:S(2)}) collective-permute-start(bf16[2,48,768]{2,1,0:T(8,128)(2,1)S(1)} %pad_maximum_fusion.13), channel_id=1, source_target_pairs={{0,8},{1,9},{2,10},{3,11},{4,12},{5,13},{6,14},{7,15},{8,16},{9,17... | collective-permute-start | bytes 442376 | tf_op jit(solution)/shard_map/ppermute | solution.py:123
  (32 other events, 228.8 us)

commit v2 on v0

--- a/solution.py
+++ b/solution.py
@@ -3,10 +3,13 @@
 import jax
 import jax.numpy as jnp
 from jax import lax
+from jax.experimental import pallas as pl
+from jax.experimental.pallas import tpu as pltpu
 from jax.sharding import PartitionSpec as P
 
 KERNEL_TAPS = 3
 DILATION_STEP = 32
+TORUS_DEVICES = 32
 
 
 eps = 1e-06
@@ -46,7 +49,7 @@
     )
 
 
-def body(features, cotangent, dilated_kernel_weight, project_weight, outer_gain, inner_gain):
+def body_any(features, cotangent, dilated_kernel_weight, project_weight, outer_gain, inner_gain):
     bin_count = features.shape[1]
     factor = 1.0 / math.sqrt(features.shape[0] * bin_count * lax.axis_size("seq"))
     full_dilated = lax.all_gather(dilated_kernel_weight, "seq", axis=0, tiled=True)
@@ -105,6 +108,325 @@
     return (block_out, grad_features, grad_dilated, grad_project, grad_outer_gain, grad_inner_gain)
 
 
+def links(move):
+    return [(i, move(i)) for i in range(TORUS_DEVICES)]
+
+
+CORE = links(lambda i: i ^ 1)
+FIRST = links(lambda i: i ^ (4 if i & 1 else 2))
+SECOND = links(lambda i: i ^ (2 if i & 1 else 4))
+UP = links(lambda i: (i + 8) % TORUS_DEVICES)
+DOWN = links(lambda i: (i - 8) % TORUS_DEVICES)
+ACROSS = links(lambda i: (i + 16) % TORUS_DEVICES)
+
+
+def send(block, pairs):
+    return lax.ppermute(block, "seq", pairs)
+
+
+def cat(*parts):
+    return jnp.concatenate(parts, axis=0)
+
+
+def gather_z(block):
+    return cat(block, send(block, DOWN), send(block, ACROSS), send(block, UP))
+
+
+def scatter_z(total):
+    n = total.shape[0] // 4
+    message = total[n:].astype(jnp.bfloat16)
+    up = send(message[:n], UP).astype(jnp.float32)
+    across = send(message[n : 2 * n], ACROSS).astype(jnp.float32)
+    down = send(message[2 * n :], DOWN).astype(jnp.float32)
+    return total[:n] + up + across + down
+
+
+def scatter_pair(total, pairs):
+    n = total.shape[0] // 2
+    return total[:n] + send(total[n:].astype(jnp.bfloat16), pairs).astype(jnp.float32)
+
+
+TAP_ORDER = [
+    (tap, r2, r1, k) for r2 in (0, 1) for r1 in (0, 1) for k in range(4) for tap in range(3)
+]
+PROJECT_ORDER = [(3, r2, r1, k) for k in range(4) for r2 in (0, 1) for r1 in (0, 1)]
+
+
+def placing(device):
+    core = device & 1
+    x = (device >> 1) & 1
+    y = (device >> 2) & 1
+    z = device >> 3
+
+    def block_of(r2, r1, k, other):
+        parity = 1 - core if other else core
+        dx = r1 + parity * (r2 - r1)
+        dy = r2 + parity * (r1 - r2)
+        return ((z + k) & 3) * 8 + (y ^ dy) * 4 + (x ^ dx) * 2 + parity
+
+    return block_of
+
+
+def device_index():
+    return lax.axis_index("seq").astype(jnp.int32).reshape(1)
+
+
+def order_kernel(index_ref, source_ref, own_ref, other_ref):
+    block_of = placing(index_ref[0])
+    for at, (matrix, r2, r1, k) in enumerate(TAP_ORDER + PROJECT_ORDER):
+        own_ref[at] = source_ref[matrix, block_of(r2, r1, k, False)]
+        other_ref[at] = source_ref[matrix, block_of(r2, r1, k, True)]
+
+
+def in_arrival_order(source):
+    shape = jax.ShapeDtypeStruct((64,) + source.shape[2:], source.dtype)
+    return pl.pallas_call(
+        order_kernel,
+        out_shape=(shape, shape),
+        in_specs=[
+            pl.BlockSpec(memory_space=pltpu.SMEM),
+            pl.BlockSpec(memory_space=pltpu.VMEM),
+        ],
+        out_specs=[pl.BlockSpec(memory_space=pltpu.VMEM)] * 2,
+        compiler_params=pltpu.CompilerParams(vmem_limit_bytes=32 << 20),
+        name="order",
+    )(device_index(), source)
+
+
+def fetch_blocks(order, block_of, own_ref, other_ref, target_of, sems):
+    copies = []
+    for at, (matrix, r2, r1, k) in enumerate(order):
+        for side, source in enumerate((own_ref, other_ref)):
+            copies.append(
+                pltpu.make_async_copy(
+                    source.at[at],
+                    target_of(matrix).at[block_of(r2, r1, k, bool(side))],
+                    sems.at[2 * at + side],
+                )
+            )
+    for copy in copies:
+        copy.start()
+    for copy in copies:
+        copy.wait()
+
+
+def block_out_kernel(index_ref, features_ref, hidden_ref, own_ref, other_ref, out_ref, weight, sems):
+    block_of = placing(index_ref[0])
+    fetch_blocks(PROJECT_ORDER, block_of, own_ref, other_ref, lambda m: weight, sems)
+    count, rows, inner = weight.shape
+    product = lax.dot_general(
+        hidden_ref[...],
+        weight[...].reshape(count * rows, inner),
+        (((1,), (1,)), ((), ())),
+        preferred_element_type=jnp.float32,
+    )
+    out_ref[...] = (features_ref[...].astype(jnp.float32) + product).astype(jnp.bfloat16)
+
+
+def project_back(features, hidden, own, other):
+    rows, inner = own.shape[1:]
+    vmem = pl.BlockSpec(memory_space=pltpu.VMEM)
+    hbm = pl.BlockSpec(memory_space=pl.ANY)
+    return pl.pallas_call(
+        block_out_kernel,
+        out_shape=jax.ShapeDtypeStruct(features.shape, features.dtype),
+        in_specs=[pl.BlockSpec(memory_space=pltpu.SMEM), vmem, vmem, hbm, hbm],
+        out_specs=vmem,
+        scratch_shapes=[
+            pltpu.VMEM((32, rows, inner), own.dtype),
+            pltpu.SemaphoreType.DMA((2 * len(PROJECT_ORDER),)),
+        ],
+        compiler_params=pltpu.CompilerParams(vmem_limit_bytes=32 << 20),
+        name="project_back",
+    )(device_index(), features, hidden, own, other)
+
+
+GELU_SCALE = math.sqrt(2.0 / math.pi)
+GELU_CUBE = 0.044715
+
+
+def stream_grad_kernel(
+    index_ref,
+    features_ref,
+    cotangent_ref,
+    grad_ref,
+    gain_ref,
+    own_ref,
+    other_ref,
+    out_ref,
+    gain_grad_ref,
+    weight,
+    total,
+    sems,
+):
+    block_of = placing(index_ref[0])
+    fetch_blocks(TAP_ORDER, block_of, own_ref, other_ref, lambda m: weight.at[m], sems)
+    taps, count, rows, inner = weight.shape
+    batch, padded_bins, _ = grad_ref.shape
+    bins = padded_bins - 2 * DILATION_STEP
+    for b in range(batch):
+        rows_sum = None
+        for tap in range(taps):
+            shift = (taps - 1 - tap) * DILATION_STEP
+            part = lax.dot_general(
+                grad_ref[b, shift : shift + bins, :],
+                weight[tap].reshape(count * rows, inner),
+                (((1,), (1,)), ((), ())),
+                preferred_element_type=jnp.float32,
+            )
+            rows_sum = part if rows_sum is None else rows_sum + part
+        total[b * bins : (b + 1) * bins, :] = rows_sum
+    channels = count * rows
+    step = 32
+    gain = gain_ref[...]
+
+    def some_rows(i, gain_sum):
+        at = pl.ds(pl.multiple_of(i * step, step), step)
+        x = features_ref[at, :].astype(jnp.float32)
+        inverse = lax.rsqrt(jnp.sum(x * x, axis=-1, keepdims=True) * (1.0 / channels) + eps)
+        scaled = x * inverse
+        v = scaled * gain
+        square = v * v
+        t = jnp.tanh(GELU_SCALE * (v + GELU_CUBE * (v * square)))
+        slope = 0.5 * (1.0 + t) + 0.5 * v * (1.0 - t * t) * (
+            GELU_SCALE * (1.0 + (3.0 * GELU_CUBE) * square)
+        )
+        dv = total[at, :] * slope
+        dn = dv * gain
+        mean = jnp.sum(dn * scaled, axis=-1, keepdims=True) * (1.0 / channels)
+        dx = inverse * (dn - scaled * mean)
+        out_ref[at, :] = (cotangent_ref[at, :].astype(jnp.float32) + dx).astype(jnp.bfloat16)
+        return gain_sum + jnp.sum(dv * scaled, axis=0, keepdims=True)
+
+    gain_grad_ref[...] = lax.fori_loop(
+        0, batch * bins // step, some_rows, jnp.zeros((1, channels), jnp.float32)
+    )
+
+
+def stream_grad(features, cotangent, grad_padded, gain, own, other):
+    rows, inner = own.shape[1:]
+    tokens, channels = features.shape
+    vmem = pl.BlockSpec(memory_space=pltpu.VMEM)
+    hbm = pl.BlockSpec(memory_space=pl.ANY)
+    return pl.pallas_call(
+        stream_grad_kernel,
+        out_shape=(
+            jax.ShapeDtypeStruct(features.shape, features.dtype),
+            jax.ShapeDtypeStruct((1, channels), jnp.float32),
+        ),
+        in_specs=[pl.BlockSpec(memory_space=pltpu.SMEM), vmem, vmem, vmem, vmem, hbm, hbm],
+        out_specs=[vmem, vmem],
+        scratch_shapes=[
+            pltpu.VMEM((KERNEL_TAPS, 32, rows, inner), own.dtype),
+            pltpu.VMEM((tokens, channels), jnp.float32),
+            pltpu.SemaphoreType.DMA((2 * len(TAP_ORDER),)),
+        ],
+        compiler_params=pltpu.CompilerParams(vmem_limit_bytes=40 << 20),
+        name="stream_grad",
+    )(device_index(), features, cotangent, grad_padded, gain.reshape(1, channels), own, other)
+
+
+def rows_dot(left, right):
+    return jnp.einsum("nrt,ti->nri", left, right, preferred_element_type=jnp.float32)
+
+
+def contract(left, right):
+    n, rows, tokens = left.shape
+    return jnp.einsum(
+        "ct,ci->ti",
+        left.reshape(n * rows, tokens),
+        right.reshape(n * rows, right.shape[2]),
+        preferred_element_type=jnp.float32,
+    )
+
+
+def body_torus(features, cotangent, dilated_kernel_weight, project_weight, outer_gain, inner_gain):
+    batch, bin_count, channels = features.shape
+    inner = project_weight.shape[1]
+    rows = project_weight.shape[0]
+    tokens = batch * bin_count
+    factor = 1.0 / math.sqrt(tokens * TORUS_DEVICES)
+
+    taps = jnp.moveaxis(dilated_kernel_weight, 1, 0)
+    plane = gather_z(taps)
+    proj = project_weight[None]
+    proj = cat(proj, send(proj, FIRST))
+    proj = cat(proj, send(proj, SECOND))
+    near = cat(plane, send(plane, FIRST))
+    far = send(near, SECOND)
+    own_project = gather_z(proj)
+    own_taps = cat(near, far)
+    near_other = send(near, CORE)
+    far_other = send(far, CORE)
+    other_project = send(own_project, CORE)
+    other_taps = cat(near_other, far_other)
+
+    features_padded = padded(features, (("seq", 1),), DILATION_STEP)
+    active = act_norm(features_padded.astype(jnp.float32), outer_gain).astype(jnp.bfloat16)
+    turned = [
+        active[:, tap * DILATION_STEP : tap * DILATION_STEP + bin_count]
+        .reshape(tokens, channels)
+        .T.reshape(32, rows, tokens)
+        for tap in range(KERNEL_TAPS)
+    ]
+    turned.append(cotangent.reshape(tokens, channels).T.reshape(32, rows, tokens))
+    act_own, act_other = in_arrival_order(jnp.stack(turned))
+
+    conv_output = (
+        contract(act_own[:24], near)
+        + contract(act_other[:24], near_other)
+        + contract(act_own[24:48], far)
+        + contract(act_other[24:48], far_other)
+    )
+    hidden32, pull_inner = jax.vjp(act_norm, conv_output, inner_gain)
+    hidden = hidden32.astype(jnp.bfloat16)
+
+    keep3 = rows_dot(act_own[48:], hidden)
+    give3 = rows_dot(act_other[48:], hidden).astype(jnp.bfloat16)
+    sum3 = keep3 + send(give3, CORE).astype(jnp.float32)
+    sum3 = scatter_z(sum3)
+    sum3 = scatter_pair(sum3, SECOND)
+    sum3 = scatter_pair(sum3, FIRST)
+    grad_project = sum3[0] * factor
+
+    grad_hidden = contract(act_own[48:], own_project) + contract(act_other[48:], other_project)
+    grad_conv, grad_gain_inner = pull_inner(grad_hidden)
+    grad_conv = grad_conv.astype(jnp.bfloat16)
+
+    keep = rows_dot(act_own[:48], grad_conv)
+    give = rows_dot(act_other[:48], grad_conv).astype(jnp.bfloat16)
+    sums = keep + send(give, CORE).astype(jnp.float32)
+    sums = scatter_pair(sums, SECOND)
+    sums = scatter_pair(sums, FIRST)
+    sums = scatter_z(sums)
+    grad_dilated = jnp.moveaxis(sums, 0, 1) * factor
+
+    flat = features.reshape(tokens, channels)
+    block_out = project_back(flat, hidden, own_project, other_project).reshape(features.shape)
+    grad_padded = padded(
+        grad_conv.reshape(batch, bin_count, inner), (("seq", 1),), DILATION_STEP
+    )
+    grad_features, grad_gain_outer = stream_grad(
+        flat, cotangent.reshape(tokens, channels), grad_padded, outer_gain, own_taps, other_taps
+    )
+    grad_features = grad_features.reshape(features.shape)
+
+    gains = jnp.concatenate([grad_gain_outer[0], grad_gain_inner]) * factor
+    for distance in (1, 2, 4, 8, 16):
+        gains = gains + send(gains, links(lambda i: i ^ distance))
+    device = lax.axis_index("seq")
+    grad_outer_gain = lax.dynamic_slice(gains, (device * rows,), (rows,))
+    part = inner // TORUS_DEVICES
+    grad_inner_gain = lax.dynamic_slice(gains, (channels + device * part,), (part,))
+    return (block_out, grad_features, grad_dilated, grad_project, grad_outer_gain, grad_inner_gain)
+
+
+def body(*operands):
+    if lax.axis_size("seq") == TORUS_DEVICES:
+        return body_torus(*operands)
+    return body_any(*operands)
+
+
 def solution(mesh):
     return jax.shard_map(
         body,

time: 434 us -> 224 us (0.52)
  waiting for transfers between devices: 322 us -> 74.6 us
  starting transfers between devices: 7.73 us -> 62.5 us
  blocking collectives: 42.5 us -> 0 us
  Pallas kernels: 0 us -> 22.5 us
  local copies, waits for them, and re-layouts: 8.18 us -> 28.5 us
  between operations: 14.1 us -> 1.09 us
  matrix products: 28.2 us -> 16.9 us
  other arithmetic: 11.2 us -> 16.4 us
    reduce_scatter x1 -> x0, waiting for transfers between devices: 169 us -> none  [reduce_dilated(): lax.psum_scatter(jnp.stack(tap_slices, axis=1) * factor, 'seq', scatter_d...]
    all_gather x2 -> x0, waiting for transfers between devices: 113 us -> none  [the longest x1 71.3 us: body(): lax.all_gather(dilated_kernel_weight, 'seq', axis=0, tiled=True)]
    ppermute x0 -> x30, waiting for transfers between devices: none -> 74.6 us  [send(): return lax.ppermute(block, 'seq', pairs)]
    ppermute x0 -> x30, starting transfers between devices: none -> 52.9 us  [send(): return lax.ppermute(block, 'seq', pairs)]
    unnamed x1 -> x0, blocking collectives: 42.5 us -> none
    unnamed x5 -> x0, waiting for transfers between devices: 39.2 us -> none
    pallas_call x0 -> x3, Pallas kernels: none -> 22.5 us  [the longest x1 18.5 us: stream_grad(): pl.pallas_call(stream_grad_kernel, out_shape=(jax.ShapeDtypeStruct(featur...]
    dot_general x12 -> x10, matrix products: 28.2 us -> 16.9 us  [the longest x6 11.5 us: contract(): jnp.einsum('ct,ci->ti', left.reshape(n * rows, tokens), right.reshape(n *...]
  transfers between devices with their start and end apart: 8 -> 34, of which waited for: 4 -> 11; matrix products, arithmetic and copies ran while one was open for 11% -> 24% of each run, Pallas kernels for 0% -> 10%
where the time goes in v2:
time: 224 us; the launch traced here: 223 us
  waiting for transfers between devices  74.6 us (33%)
  starting transfers between devices  62.5 us (28%)
  local copies, waits for them, and re-layouts  28.5 us (13%)
  Pallas kernels  22.5 us (10%)
  matrix products  16.9 us (8%)
  other arithmetic  16.4 us (7%)
    ppermute x30, waiting for transfers between devices, send(): return lax.ppermute(block, 'seq', pairs)  74.6 us
    ppermute x30, starting transfers between devices, send(): return lax.ppermute(block, 'seq', pairs)  52.9 us
    pallas_call x1, Pallas kernels, stream_grad(): pl.pallas_call(stream_grad_kernel, out_shape=(jax.ShapeDtypeStruct(featur...  18.5 us
    unnamed x36, local copies, waits for them, and re-layouts  13.9 us
    dot_general x6, matrix products, contract(): jnp.einsum('ct,ci->ti', left.reshape(n * rows, tokens), right.reshape(n *...  11.5 us
    ppermute x2, starting transfers between devices, padded(): lax.ppermute(lax.slice_in_dim(block, block.shape[dim] - width, None, axis...  6.98 us
    reshape x3, local copies, waits for them, and re-layouts, body_torus(): turned = [active[:, tap * DILATION_STEP:tap * DILATION_STEP + bin_count]....  5.97 us
    dot_general x4, matrix products, rows_dot(): jnp.einsum('nrt,ti->nri', left, right, preferred_element_type=jnp.float32)  5.42 us
  transfers between devices with their start and end apart: 34, of which 11 were waited for; matrix products, arithmetic and copies ran while one was open for 24% of the time, Pallas kernels for 10%

profile of v2, /device:TPU:0, one launch (start us, length us, event | category | flops | bytes accessed | tf_op | source)
XLA Modules:
  0.0 222.6 jit_solution(1311199326634281596)
XLA Ops:
  0.7 5.1 %collective-permute-start.2 = (bf16[3,48,768]{2,1,0:T(8,128)(2,1)}, bf16[3,48,768]{2,1,0:T(8,128)(2,1)S(1)}, u32[]{:S(2)}, u32[]{:S(2)}) collective-permute-start(bf16[3,48,768]{2,1,0:T(8,128)(2,1)} %bitcast.97), channel_id=1, source_target_pairs={{0,24},{1,25},{2,26},{3,27},{4,28},{5,29},{6,30},{7,31},{8,0},{9,1... | collective-permute-start | bytes 663560 | tf_op jit(solution)/shard_map/ppermute | solution.py:124
  6.8 1.8 fusion.45
  9.8 3.7 %collective-permute-start = (bf16[2,32,1536]{2,1,0:T(8,128)(2,1)}, bf16[2,32,1536]{2,1,0:T(8,128)(2,1)}, u32[]{:S(2)}, u32[]{:S(2)}) collective-permute-start(bf16[2,32,1536]{2,1,0:T(8,128)(2,1)} %get-tuple-element.31), channel_id=1, source_target_pairs={{0,1},{1,2},{2,3},{3,4},{4,5},{5,6},{6,7},{7,8},{8,9},{9,10},{10,1... | collective-permute-start | bytes 589832 | tf_op jit(solution)/shard_map/ppermute | solution.py:23
  13.6 1.7 constant_dynamic-update-slice_fusion.16
  16.2 8.6 %collective-permute-done.3 = bf16[3,48,768]{2,1,0:T(8,128)(2,1)S(1)} collective-permute-done((bf16[3,48,768]{2,1,0:T(8,128)(2,1)}, bf16[3,48,768]{2,1,0:T(8,128)(2,1)S(1)}, u32[]{:S(2)}, u32[]{:S(2)}) %collective-permute-start.3) | collective-permute-done | bytes 221216 | tf_op jit(solution)/shard_map/ppermute | solution.py:124
  26.0 1.5 collective-permute-start.5
  29.4 1.6 collective-permute-start.10
  30.9 1.5 constant_dynamic-update-slice_fusion.9
  36.3 4.5 %collective-permute-done.5 = bf16[12,48,768]{2,1,0:T(8,128)(2,1)} collective-permute-done((bf16[12,48,768]{2,1,0:T(8,128)(2,1)S(1)}, bf16[12,48,768]{2,1,0:T(8,128)(2,1)}, u32[]{:S(2)}, u32[]{:S(2)}) %collective-permute-start.5) | collective-permute-done | bytes 884768 | tf_op jit(solution)/shard_map/ppermute | solution.py:124
  40.8 2.6 %constant_dynamic-update-slice_fusion.12 = (bf16[48,48,768]{2,1,0:T(8,128)(2,1)}, bf16[24,48,768]{2,1,0:T(8,128)(2,1)}) fusion(bf16[48,48,768]{2,1,0:T(8,128)(2,1)} %get-tuple-element.35, bf16[12,48,768]{2,1,0:T(8,128)(2,1)} %collective-permute-done.5, bf16[24,48,768]{2,1,0:T(8,128)(2,1)} %get-tuple-element.36), kind=kLoop, calls=%fused_computation.85 | loop fusion | bytes 2654208
  43.4 1.4 collective-permute-start.7
  45.8 3.2 %collective-permute-start.12 = (bf16[4,48,768]{2,1,0:T(8,128)(2,1)S(1)}, bf16[4,48,768]{2,1,0:T(8,128)(2,1)S(1)}, u32[]{:S(2)}, u32[]{:S(2)}) collective-permute-start(bf16[4,48,768]{2,1,0:T(8,128)(2,1)S(1)} %pad_maximum_fusion.5), channel_id=1, source_target_pairs={{0,16},{1,17},{2,18},{3,19},{4,20},{5,21},{6,22},{7,23},{8,24},{9,... | collective-permute-start | bytes 884744 | tf_op jit(solution)/shard_map/ppermute | solution.py:124
  49.0 2.0 collective-permute-start.13
  51.6 1.8 collective-permute-done.11
  54.2 18.5 %collective-permute-done.12 = bf16[4,48,768]{2,1,0:T(8,128)(2,1)S(1)} collective-permute-done((bf16[4,48,768]{2,1,0:T(8,128)(2,1)S(1)}, bf16[4,48,768]{2,1,0:T(8,128)(2,1)S(1)}, u32[]{:S(2)}, u32[]{:S(2)}) %collective-permute-start.12) | collective-permute-done | bytes 294944 | tf_op jit(solution)/shard_map/ppermute | solution.py:124
  74.7 2.1 fusion.4
  76.8 1.4 fusion.43
  79.6 2.3 %copy.17 = bf16[256,1536]{0,1:T(8,128)(2,1)} copy(bf16[256,1536]{1,0:T(8,128)(2,1)} %bitcast.95) | data formatting | bytes 1572864 | tf_op jit(solution)/shard_map/reshape | solution.py:368
  81.9 2.3 %copy.16 = bf16[256,1536]{0,1:T(8,128)(2,1)} copy(bf16[256,1536]{1,0:T(8,128)(2,1)} %bitcast.94) | data formatting | bytes 1572864 | tf_op jit(solution)/shard_map/reshape | solution.py:368
  84.2 1.6 pad_maximum_fusion.1.source_ref
  86.0 1.8 convolution_bitcast_fusion
  87.8 2.2 convolution_bitcast_fusion.3
  90.0 2.2 convolution_bitcast_fusion.4
  92.2 2.2 fusion.11
  95.2 2.4 %multiply_reduce_fusion = (f32[768]{0:T(1024)S(1)}, f32[256]{0:T(256)S(1)}, f32[256,768]{1,0:T(8,128)S(1)}) fusion(f32[256,768]{1,0:T(8,128)S(1)} %get-tuple-element.44, f32[256]{0:T(256)S(1)} %fusion.39, f32[768]{0:T(1024)S(1)} %copy-done.12, f32[256,768]{1,0:T(8,128)S(1)} %convolution_bitcast_fusion, bf16[64,48,256]{2,1,0:T(8,128)(2,1)S(1)} %get-tuple-element.10, ...), kind=kOutput, calls=%fused_computation.45 | convolution fusion | flops 307297280 | bytes 5120000 | tf_op jit(solution)/shard_map/ct,ci->ti/dot_general | solution.py:335
  99.8 1.5 convolution_convert_fusion.1
  101.3 4.3 %collective-permute-done.17 = bf16[48,48,768]{2,1,0:T(8,128)(2,1)S(1)} collective-permute-done((bf16[48,48,768]{2,1,0:T(8,128)(2,1)S(1)}, bf16[48,48,768]{2,1,0:T(8,128)(2,1)S(1)}, u32[]{:S(2)}, u32[]{:S(2)}) %collective-permute-start.17) | collective-permute-done | bytes 3538976 | tf_op jit(solution)/shard_map/ppermute | solution.py:124
  108.2 2.8 %copy-done.3 = f32[48,48,768]{2,1,0:T(8,128)} copy-done((f32[48,48,768]{2,1,0:T(8,128)}, f32[48,48,768]{2,1,0:T(8,128)S(1)}, u32[]{:S(2)}) %copy-start.3) | copy-done | bytes 7077912
  110.9 1.6 collective-permute-start.18
  112.5 1.6 constant_dynamic-update-slice_fusion.11.own_ref
  115.4 3.3 %collective-permute-start.15 = (bf16[2,32,768]{2,1,0:T(8,128)(2,1)S(1)}, bf16[2,32,768]{2,1,0:T(8,128)(2,1)S(1)}, u32[]{:S(2)}, u32[]{:S(2)}) collective-permute-start(bf16[2,32,768]{2,1,0:T(8,128)(2,1)S(1)} %get-tuple-element.33), channel_id=1, source_target_pairs={{0,1},{1,2},{2,3},{3,4},{4,5},{5,6},{6,7},{7,8},{8,9},{9,10},{10,1... | collective-permute-start | bytes 294920 | tf_op jit(solution)/shard_map/ppermute | solution.py:23
  118.7 1.8 pad_maximum_fusion.other_ref
  120.5 18.5 %stream_grad.1 = (bf16[256,1536]{1,0:T(8,128)(2,1)}, f32[1,1536]{1,0:T(1,128)S(1)}) custom-call(s32[1]{0:T(128)} %bitcast.index_ref, bf16[256,1536]{1,0:T(8,128)(2,1)S(1)} %bitcast.84, bf16[256,1536]{1,0:T(8,128)(2,1)S(1)} %bitcast.87, bf16[2,192,768]{2,1,0:T(8,128)(2,1)S(1)} %pad_maximum_fusion.4.grad_ref, f32[1,1536]{1,0:T(1,128)S(1)} %reshape.96.gain_ref, ...), custom_call_target="tpu_custom_call" | custom-call | tf_op jit(solution)/shard_map/stream_grad/pallas_call | solution.py:311
  139.1 1.7 fusion.47
  140.9 5.1 %collective-permute-start.26 = (bf16[4,48,768]{2,1,0:T(8,128)(2,1)S(1)}, bf16[4,48,768]{2,1,0:T(8,128)(2,1)S(1)}, u32[]{:S(2)}, u32[]{:S(2)}) collective-permute-start(bf16[4,48,768]{2,1,0:T(8,128)(2,1)S(1)} %get-tuple-element.19), channel_id=1, source_target_pairs={{0,24},{1,25},{2,26},{3,27},{4,28},{5,29},{6,30},{7,31},{8,0},{9,1... | collective-permute-start | bytes 884744 | tf_op jit(solution)/shard_map/ppermute | solution.py:124
  146.0 2.5 %collective-permute-start.25 = (bf16[4,48,768]{2,1,0:T(8,128)(2,1)S(1)}, bf16[4,48,768]{2,1,0:T(8,128)(2,1)S(1)}, u32[]{:S(2)}, u32[]{:S(2)}) collective-permute-start(bf16[4,48,768]{2,1,0:T(8,128)(2,1)S(1)} %get-tuple-element.20), channel_id=1, source_target_pairs={{0,16},{1,17},{2,18},{3,19},{4,20},{5,21},{6,22},{7,23},{8,24},{9,... | collective-permute-start | bytes 884744 | tf_op jit(solution)/shard_map/ppermute | solution.py:124
  148.5 2.9 %slice_add_fusion = f32[24,48,768]{2,1,0:T(8,128)S(1)} fusion(f32[48,48,768]{2,1,0:T(8,128)} %copy-done.3, bf16[24,48,768]{2,1,0:T(8,128)(2,1)} %collective-permute-done.18), kind=kLoop, calls=%fused_computation.2 | loop fusion | flops 1769472 | bytes 8847360 | tf_op jit(solution)/shard_map/add | solution.py:146
  151.5 10.9 %collective-permute-start.19 = (bf16[12,48,768]{2,1,0:T(8,128)(2,1)S(1)}, bf16[12,48,768]{2,1,0:T(8,128)(2,1)}, u32[]{:S(2)}, u32[]{:S(2)}) collective-permute-start(bf16[12,48,768]{2,1,0:T(8,128)(2,1)S(1)} %slice.188), channel_id=1, source_target_pairs={{0,2},{1,5},{2,0},{3,7},{4,6},{5,1},{6,4},{7,3},{8,10},{9,13},{10,... | collective-permute-start | bytes 2654216 | tf_op jit(solution)/shard_map/ppermute | solution.py:124
  162.5 11.7 %collective-permute-done.25 = bf16[4,48,768]{2,1,0:T(8,128)(2,1)S(1)} collective-permute-done((bf16[4,48,768]{2,1,0:T(8,128)(2,1)S(1)}, bf16[4,48,768]{2,1,0:T(8,128)(2,1)S(1)}, u32[]{:S(2)}, u32[]{:S(2)}) %collective-permute-start.25) | collective-permute-done | bytes 294944 | tf_op jit(solution)/shard_map/ppermute | solution.py:124
  174.3 6.9 %collective-permute-start.27 = (bf16[2,48,768]{2,1,0:T(8,128)(2,1)S(1)}, bf16[2,48,768]{2,1,0:T(8,128)(2,1)S(1)}, u32[]{:S(2)}, u32[]{:S(2)}) collective-permute-start(bf16[2,48,768]{2,1,0:T(8,128)(2,1)S(1)} %slice.189), channel_id=1, source_target_pairs={{0,4},{1,3},{2,6},{3,1},{4,0},{5,7},{6,2},{7,5},{8,12},{9,11},{10,... | collective-permute-start | bytes 442376 | tf_op jit(solution)/shard_map/ppermute | solution.py:124
  181.3 3.7 %collective-permute-done.30 = f32[2304]{0:T(1024)S(1)} collective-permute-done((f32[2304]{0:T(1024)S(1)}, f32[2304]{0:T(1024)S(1)}, u32[]{:S(2)}, u32[]{:S(2)}) %collective-permute-start.30) | collective-permute-done | bytes 9248 | tf_op jit(solution)/shard_map/ppermute | solution.py:124
  185.0 3.7 %collective-permute-done.31 = f32[2304]{0:T(1024)S(1)} collective-permute-done((f32[2304]{0:T(1024)S(1)}, f32[2304]{0:T(1024)S(1)}, u32[]{:S(2)}, u32[]{:S(2)}) %collective-permute-start.31) | collective-permute-done | bytes 9248 | tf_op jit(solution)/shard_map/ppermute | solution.py:124
  188.7 1.5 collective-permute-start.32
  190.2 2.2 collective-permute-done.32
  192.4 3.4 %collective-permute-start.33 = (f32[2304]{0:T(1024)S(1)}, f32[2304]{0:T(1024)S(1)}, u32[]{:S(2)}, u32[]{:S(2)}) collective-permute-start(f32[2304]{0:T(1024)S(1)} %add.139), channel_id=1, source_target_pairs={{0,16},{1,17},{2,18},{3,19},{4,20},{5,21},{6,22},{7,23},{8,24},{9,... | collective-permute-start | bytes 27656 | tf_op jit(solution)/shard_map/ppermute | solution.py:124
  195.8 3.8 %project_back.1 = bf16[256,1536]{1,0:T(8,128)(2,1)} custom-call(s32[1]{0:T(128)} %bitcast.index_ref, bf16[256,1536]{1,0:T(8,128)(2,1)S(1)} %bitcast.85, bf16[256,768]{1,0:T(8,128)(2,1)S(1)} %get-tuple-element.30.hidden_ref, bf16[16,48,768]{2,1,0:T(8,128)(2,1)} %constant_dynamic-update-slice_fusion.5.own_ref, ...), custom_call_target="tpu_custom_call" | custom-call | tf_op jit(solution)/shard_map/project_back/pallas_call | solution.py:230
  206.2 4.9 %collective-permute-done.22 = bf16[3,48,768]{2,1,0:T(8,128)(2,1)S(1)} collective-permute-done((bf16[3,48,768]{2,1,0:T(8,128)(2,1)S(1)}, bf16[3,48,768]{2,1,0:T(8,128)(2,1)S(1)}, u32[]{:S(2)}, u32[]{:S(2)}) %collective-permute-start.22) | collective-permute-done | bytes 221216 | tf_op jit(solution)/shard_map/ppermute | solution.py:124
  211.1 10.6 %collective-permute-done.21 = bf16[3,48,768]{2,1,0:T(8,128)(2,1)S(1)} collective-permute-done((bf16[3,48,768]{2,1,0:T(8,128)(2,1)S(1)}, bf16[3,48,768]{2,1,0:T(8,128)(2,1)S(1)}, u32[]{:S(2)}, u32[]{:S(2)}) %collective-permute-start.21) | collective-permute-done | bytes 221216 | tf_op jit(solution)/shard_map/ppermute | solution.py:124
  (112 shorter events, 30.7 us)
Async XLA Ops:
  0.6 26.8 %copy-start.10 = (bf16[48,768]{1,0:T(8,128)(2,1)S(1)}, bf16[48,768]{1,0:T(8,128)(2,1)}, u32[]{:S(2)}) copy-start(bf16[48,768]{1,0:T(8,128)(2,1)} %param.9) | copy-start | bytes 221188
  0.6 27.5 %copy-start.2 = (bf16[2,128,1536]{2,1,0:T(8,128)(2,1)S(1)}, bf16[2,128,1536]{2,1,0:T(8,128)(2,1)}, u32[]{:S(2)}) copy-start(bf16[2,128,1536]{2,1,0:T(8,128)(2,1)} %param.7) | copy-start | bytes 2359300
  0.7 14.7 %collective-permute-start.2 = (bf16[3,48,768]{2,1,0:T(8,128)(2,1)}, bf16[3,48,768]{2,1,0:T(8,128)(2,1)S(1)}, u32[]{:S(2)}, u32[]{:S(2)}) collective-permute-start(bf16[3,48,768]{2,1,0:T(8,128)(2,1)} %bitcast.97), channel_id=1, source_target_pairs={{0,24},{1,25},{2,26},{3,27},{4,28},{5,29},{6,30},{7,31},{8,0},{9,1... | collective-permute-start | bytes 663560 | tf_op jit(solution)/shard_map/ppermute | solution.py:124
  5.8 19.1 %collective-permute-start.3 = (bf16[3,48,768]{2,1,0:T(8,128)(2,1)}, bf16[3,48,768]{2,1,0:T(8,128)(2,1)S(1)}, u32[]{:S(2)}, u32[]{:S(2)}) collective-permute-start(bf16[3,48,768]{2,1,0:T(8,128)(2,1)} %bitcast.98), channel_id=1, source_target_pairs={{0,16},{1,17},{2,18},{3,19},{4,20},{5,21},{6,22},{7,23},{8,24},{9,... | collective-permute-start | bytes 663560 | tf_op jit(solution)/shard_map/ppermute | solution.py:124
  5.8 19.1 %collective-permute-start.4 = (bf16[3,48,768]{2,1,0:T(8,128)(2,1)}, bf16[3,48,768]{2,1,0:T(8,128)(2,1)S(1)}, u32[]{:S(2)}, u32[]{:S(2)}) collective-permute-start(bf16[3,48,768]{2,1,0:T(8,128)(2,1)} %bitcast.99), channel_id=1, source_target_pairs={{0,8},{1,9},{2,10},{3,11},{4,12},{5,13},{6,14},{7,15},{8,16},{9,17... | collective-permute-start | bytes 663560 | tf_op jit(solution)/shard_map/ppermute | solution.py:124
  8.6 23.9 %collective-permute-start.1 = (bf16[2,32,1536]{2,1,0:T(8,128)(2,1)}, bf16[2,32,1536]{2,1,0:T(8,128)(2,1)}, u32[]{:S(2)}, u32[]{:S(2)}) collective-permute-start(bf16[2,32,1536]{2,1,0:T(8,128)(2,1)} %get-tuple-element.32), channel_id=1, source_target_pairs={{1,0},{2,1},{3,2},{4,3},{5,4},{6,5},{7,6},{8,7},{9,8},{10,9},{11,1... | collective-permute-start | bytes 589832 | tf_op jit(solution)/shard_map/ppermute | solution.py:26
  9.8 22.6 %collective-permute-start = (bf16[2,32,1536]{2,1,0:T(8,128)(2,1)}, bf16[2,32,1536]{2,1,0:T(8,128)(2,1)}, u32[]{:S(2)}, u32[]{:S(2)}) collective-permute-start(bf16[2,32,1536]{2,1,0:T(8,128)(2,1)} %get-tuple-element.31), channel_id=1, source_target_pairs={{0,1},{1,2},{2,3},{3,4},{4,5},{5,6},{6,7},{7,8},{8,9},{9,10},{10,1... | collective-permute-start | bytes 589832 | tf_op jit(solution)/shard_map/ppermute | solution.py:23
  15.3 12.8 %copy-start.8 = (bf16[3,48,768]{2,1,0:T(8,128)(2,1)}, bf16[3,48,768]{2,1,0:T(8,128)(2,1)S(1)}, u32[]{:S(2)}) copy-start(bf16[3,48,768]{2,1,0:T(8,128)(2,1)S(1)} %collective-permute-done.2) | copy-start | bytes 663556
  15.3 17.1 %copy-start = (bf16[2,128,1536]{2,1,0:T(8,128)(2,1)S(1)}, bf16[2,128,1536]{2,1,0:T(8,128)(2,1)}, u32[]{:S(2)}) copy-start(bf16[2,128,1536]{2,1,0:T(8,128)(2,1)} %param.6) | copy-start | bytes 2359300
  15.3 13.1 %collective-permute-start.9 = (bf16[1,48,768]{2,1,0:T(8,128)(2,1)}, bf16[1,48,768]{2,1,0:T(8,128)(2,1)}, u32[]{:S(2)}, u32[]{:S(2)}) collective-permute-start(bf16[1,48,768]{2,1,0:T(8,128)(2,1)} %bitcast.102), channel_id=1, source_target_pairs={{0,2},{1,5},{2,0},{3,7},{4,6},{5,1},{6,4},{7,3},{8,10},{9,13},{10,... | collective-permute-start | bytes 221192 | tf_op jit(solution)/shard_map/ppermute | solution.py:124
  24.9 2.6 %copy-start.6 = (bf16[3,48,768]{2,1,0:T(8,128)(2,1)}, bf16[3,48,768]{2,1,0:T(8,128)(2,1)S(1)}, u32[]{:S(2)}) copy-start(bf16[3,48,768]{2,1,0:T(8,128)(2,1)S(1)} %collective-permute-done.3) | copy-start | bytes 663556
  26.0 14.8 %collective-permute-start.5 = (bf16[12,48,768]{2,1,0:T(8,128)(2,1)S(1)}, bf16[12,48,768]{2,1,0:T(8,128)(2,1)}, u32[]{:S(2)}, u32[]{:S(2)}) collective-permute-start(bf16[12,48,768]{2,1,0:T(8,128)(2,1)S(1)} %pad_maximum_fusion.3), channel_id=1, source_target_pairs={{0,2},{1,5},{2,0},{3,7},{4,6},{5,1},{6,4},{7,3},{8,10},{9,13},{10,... | collective-permute-start | bytes 2654216 | tf_op jit(solution)/shard_map/ppermute | solution.py:124
  28.4 5.4 %copy-start.9 = (bf16[3,48,768]{2,1,0:T(8,128)(2,1)S(1)}, bf16[3,48,768]{2,1,0:T(8,128)(2,1)}, u32[]{:S(2)}) copy-start(bf16[3,48,768]{2,1,0:T(8,128)(2,1)} %copy-done.8) | copy-start | bytes 663556
  28.4 6.2 %copy-start.7 = (bf16[3,48,768]{2,1,0:T(8,128)(2,1)S(1)}, bf16[3,48,768]{2,1,0:T(8,128)(2,1)}, u32[]{:S(2)}) copy-start(bf16[3,48,768]{2,1,0:T(8,128)(2,1)} %copy-done.6) | copy-start | bytes 663556
  29.4 15.5 %collective-permute-start.10 = (bf16[2,48,768]{2,1,0:T(8,128)(2,1)S(1)}, bf16[2,48,768]{2,1,0:T(8,128)(2,1)S(1)}, u32[]{:S(2)}, u32[]{:S(2)}) collective-permute-start(bf16[2,48,768]{2,1,0:T(8,128)(2,1)S(1)} %pad_maximum_fusion.6), channel_id=1, source_target_pairs={{0,4},{1,3},{2,6},{3,1},{4,0},{5,7},{6,2},{7,5},{8,12},{9,11},{10,... | collective-permute-start | bytes 442376 | tf_op jit(solution)/shard_map/ppermute | solution.py:124
  43.4 31.3 %copy-start.11 = (f32[1536]{0:T(1024)S(1)}, f32[1536]{0:T(1024)}, u32[]{:S(2)}) copy-start(f32[1536]{0:T(1024)} %param.10) | copy-start | bytes 18436
  43.4 40.8 %collective-permute-start.7 = (bf16[24,48,768]{2,1,0:T(8,128)(2,1)}, bf16[24,48,768]{2,1,0:T(8,128)(2,1)}, u32[]{:S(2)}, u32[]{:S(2)}) collective-permute-start(bf16[24,48,768]{2,1,0:T(8,128)(2,1)} %get-tuple-element.28), channel_id=1, source_target_pairs={{0,4},{1,3},{2,6},{3,1},{4,0},{5,7},{6,2},{7,5},{8,12},{9,11},{10,... | collective-permute-start | bytes 5308424 | tf_op jit(solution)/shard_map/ppermute | solution.py:124
  45.7 7.7 %collective-permute-start.11 = (bf16[4,48,768]{2,1,0:T(8,128)(2,1)S(1)}, bf16[4,48,768]{2,1,0:T(8,128)(2,1)S(1)}, u32[]{:S(2)}, u32[]{:S(2)}) collective-permute-start(bf16[4,48,768]{2,1,0:T(8,128)(2,1)S(1)} %pad_maximum_fusion.5), channel_id=1, source_target_pairs={{0,24},{1,25},{2,26},{3,27},{4,28},{5,29},{6,30},{7,31},{8,0},{9,1... | collective-permute-start | bytes 884744 | tf_op jit(solution)/shard_map/ppermute | solution.py:124
  45.8 26.9 %collective-permute-start.12 = (bf16[4,48,768]{2,1,0:T(8,128)(2,1)S(1)}, bf16[4,48,768]{2,1,0:T(8,128)(2,1)S(1)}, u32[]{:S(2)}, u32[]{:S(2)}) collective-permute-start(bf16[4,48,768]{2,1,0:T(8,128)(2,1)S(1)} %pad_maximum_fusion.5), channel_id=1, source_target_pairs={{0,16},{1,17},{2,18},{3,19},{4,20},{5,21},{6,22},{7,23},{8,24},{9,... | collective-permute-start | bytes 884744 | tf_op jit(solution)/shard_map/ppermute | solution.py:124
  49.0 24.5 %collective-permute-start.13 = (bf16[4,48,768]{2,1,0:T(8,128)(2,1)S(1)}, bf16[4,48,768]{2,1,0:T(8,128)(2,1)S(1)}, u32[]{:S(2)}, u32[]{:S(2)}) collective-permute-start(bf16[4,48,768]{2,1,0:T(8,128)(2,1)S(1)} %pad_maximum_fusion.5), channel_id=1, source_target_pairs={{0,8},{1,9},{2,10},{3,11},{4,12},{5,13},{6,14},{7,15},{8,16},{9,17... | collective-permute-start | bytes 884744 | tf_op jit(solution)/shard_map/ppermute | solution.py:124
  74.2 11.8 %collective-permute-start.14 = (bf16[16,48,768]{2,1,0:T(8,128)(2,1)}, bf16[16,48,768]{2,1,0:T(8,128)(2,1)}, u32[]{:S(2)}, u32[]{:S(2)}) collective-permute-start(bf16[16,48,768]{2,1,0:T(8,128)(2,1)} %constant_dynamic-update-slice_fusion.5.own_ref), channel_id=1, source_target_pairs={{0,1},{1,0},{2,3},{3,2},{4,5},{5,4},{6,7},{7,6},{8,9},{9,8},{10,11... | collective-permute-start | bytes 3538952 | tf_op jit(solution)/shard_map/ppermute | solution.py:124
  74.2 15.8 %collective-permute-start.6 = (bf16[24,48,768]{2,1,0:T(8,128)(2,1)}, bf16[24,48,768]{2,1,0:T(8,128)(2,1)}, u32[]{:S(2)}, u32[]{:S(2)}) collective-permute-start(bf16[24,48,768]{2,1,0:T(8,128)(2,1)} %get-tuple-element.28), channel_id=1, source_target_pairs={{0,1},{1,0},{2,3},{3,2},{4,5},{5,4},{6,7},{7,6},{8,9},{9,8},{10,11... | collective-permute-start | bytes 5308424 | tf_op jit(solution)/shard_map/ppermute | solution.py:124
  84.2 10.2 %collective-permute-start.8 = (bf16[24,48,768]{2,1,0:T(8,128)(2,1)}, bf16[24,48,768]{2,1,0:T(8,128)(2,1)S(1)}, u32[]{:S(2)}, u32[]{:S(2)}) collective-permute-start(bf16[24,48,768]{2,1,0:T(8,128)(2,1)} %collective-permute-done.7), channel_id=1, source_target_pairs={{0,1},{1,0},{2,3},{3,2},{4,5},{5,4},{6,7},{7,6},{8,9},{9,8},{10,11... | collective-permute-start | bytes 5308424 | tf_op jit(solution)/shard_map/ppermute | solution.py:124
  94.4 0.8 copy-start.12
  99.2 6.4 %collective-permute-start.17 = (bf16[48,48,768]{2,1,0:T(8,128)(2,1)S(1)}, bf16[48,48,768]{2,1,0:T(8,128)(2,1)S(1)}, u32[]{:S(2)}, u32[]{:S(2)}) collective-permute-start(bf16[48,48,768]{2,1,0:T(8,128)(2,1)S(1)} %convolution_convert_fusion), channel_id=1, source_target_pairs={{0,1},{1,0},{2,3},{3,2},{4,5},{5,4},{6,7},{7,6},{8,9},{9,8},{10,11... | collective-permute-start | bytes 10616840 | tf_op jit(solution)/shard_map/ppermute | solution.py:124
  101.3 37.8 %collective-permute-start.23 = (bf16[16,48,768]{2,1,0:T(8,128)(2,1)}, bf16[16,48,768]{2,1,0:T(8,128)(2,1)}, u32[]{:S(2)}, u32[]{:S(2)}) collective-permute-start(bf16[16,48,768]{2,1,0:T(8,128)(2,1)} %convolution_convert_fusion.1), channel_id=1, source_target_pairs={{0,1},{1,0},{2,3},{3,2},{4,5},{5,4},{6,7},{7,6},{8,9},{9,8},{10,11... | collective-permute-start | bytes 3538952 | tf_op jit(solution)/shard_map/ppermute | solution.py:124
  106.7 4.2 %copy-start.3 = (f32[48,48,768]{2,1,0:T(8,128)}, f32[48,48,768]{2,1,0:T(8,128)S(1)}, u32[]{:S(2)}) copy-start(f32[48,48,768]{2,1,0:T(8,128)S(1)} %convert_add_fusion) | copy-start | bytes 21233668
  106.7 5.8 %copy-start.1 = (bf16[48,48,768]{2,1,0:T(8,128)(2,1)S(1)}, bf16[48,48,768]{2,1,0:T(8,128)(2,1)}, u32[]{:S(2)}) copy-start(bf16[48,48,768]{2,1,0:T(8,128)(2,1)} %get-tuple-element.27) | copy-start | bytes 10616836
  110.9 37.6 %collective-permute-start.18 = (bf16[24,48,768]{2,1,0:T(8,128)(2,1)}, bf16[24,48,768]{2,1,0:T(8,128)(2,1)}, u32[]{:S(2)}, u32[]{:S(2)}) collective-permute-start(bf16[24,48,768]{2,1,0:T(8,128)(2,1)} %slice.187), channel_id=1, source_target_pairs={{0,4},{1,3},{2,6},{3,1},{4,0},{5,7},{6,2},{7,5},{8,12},{9,11},{10,... | collective-permute-start | bytes 5308424 | tf_op jit(solution)/shard_map/ppermute | solution.py:124
  114.1 6.4 %collective-permute-start.16 = (bf16[2,32,768]{2,1,0:T(8,128)(2,1)S(1)}, bf16[2,32,768]{2,1,0:T(8,128)(2,1)S(1)}, u32[]{:S(2)}, u32[]{:S(2)}) collective-permute-start(bf16[2,32,768]{2,1,0:T(8,128)(2,1)S(1)} %get-tuple-element.34), channel_id=1, source_target_pairs={{1,0},{2,1},{3,2},{4,3},{5,4},{6,5},{7,6},{8,7},{9,8},{10,9},{11,1... | collective-permute-start | bytes 294920 | tf_op jit(solution)/shard_map/ppermute | solution.py:26
  115.4 5.1 %collective-permute-start.15 = (bf16[2,32,768]{2,1,0:T(8,128)(2,1)S(1)}, bf16[2,32,768]{2,1,0:T(8,128)(2,1)S(1)}, u32[]{:S(2)}, u32[]{:S(2)}) collective-permute-start(bf16[2,32,768]{2,1,0:T(8,128)(2,1)S(1)} %get-tuple-element.33), channel_id=1, source_target_pairs={{0,1},{1,2},{2,3},{3,4},{4,5},{5,6},{6,7},{7,8},{8,9},{9,10},{10,1... | collective-permute-start | bytes 294920 | tf_op jit(solution)/shard_map/ppermute | solution.py:23
  140.9 21.5 %collective-permute-start.26 = (bf16[4,48,768]{2,1,0:T(8,128)(2,1)S(1)}, bf16[4,48,768]{2,1,0:T(8,128)(2,1)S(1)}, u32[]{:S(2)}, u32[]{:S(2)}) collective-permute-start(bf16[4,48,768]{2,1,0:T(8,128)(2,1)S(1)} %get-tuple-element.19), channel_id=1, source_target_pairs={{0,24},{1,25},{2,26},{3,27},{4,28},{5,29},{6,30},{7,31},{8,0},{9,1... | collective-permute-start | bytes 884744 | tf_op jit(solution)/shard_map/ppermute | solution.py:124
  146.0 28.2 %collective-permute-start.25 = (bf16[4,48,768]{2,1,0:T(8,128)(2,1)S(1)}, bf16[4,48,768]{2,1,0:T(8,128)(2,1)S(1)}, u32[]{:S(2)}, u32[]{:S(2)}) collective-permute-start(bf16[4,48,768]{2,1,0:T(8,128)(2,1)S(1)} %get-tuple-element.20), channel_id=1, source_target_pairs={{0,16},{1,17},{2,18},{3,19},{4,20},{5,21},{6,22},{7,23},{8,24},{9,... | collective-permute-start | bytes 884744 | tf_op jit(solution)/shard_map/ppermute | solution.py:124
  148.5 25.7 %collective-permute-start.24 = (bf16[4,48,768]{2,1,0:T(8,128)(2,1)S(1)}, bf16[4,48,768]{2,1,0:T(8,128)(2,1)S(1)}, u32[]{:S(2)}, u32[]{:S(2)}) collective-permute-start(bf16[4,48,768]{2,1,0:T(8,128)(2,1)S(1)} %get-tuple-element.18), channel_id=1, source_target_pairs={{0,8},{1,9},{2,10},{3,11},{4,12},{5,13},{6,14},{7,15},{8,16},{9,17... | collective-permute-start | bytes 884744 | tf_op jit(solution)/shard_map/ppermute | solution.py:124
  151.4 22.8 %copy-start.4 = (f32[24,48,768]{2,1,0:T(8,128)}, f32[24,48,768]{2,1,0:T(8,128)S(1)}, u32[]{:S(2)}) copy-start(f32[24,48,768]{2,1,0:T(8,128)S(1)} %slice_add_fusion) | copy-start | bytes 10616836
  151.5 49.7 %collective-permute-start.19 = (bf16[12,48,768]{2,1,0:T(8,128)(2,1)S(1)}, bf16[12,48,768]{2,1,0:T(8,128)(2,1)}, u32[]{:S(2)}, u32[]{:S(2)}) collective-permute-start(bf16[12,48,768]{2,1,0:T(8,128)(2,1)S(1)} %slice.188), channel_id=1, source_target_pairs={{0,2},{1,5},{2,0},{3,7},{4,6},{5,1},{6,4},{7,3},{8,10},{9,13},{10,... | collective-permute-start | bytes 2654216 | tf_op jit(solution)/shard_map/ppermute | solution.py:124
  162.4 18.8 %collective-permute-start.29 = (f32[2304]{0:T(1024)S(1)}, f32[2304]{0:T(1024)S(1)}, u32[]{:S(2)}, u32[]{:S(2)}) collective-permute-start(f32[2304]{0:T(1024)S(1)} %maximum_multiply_fusion), channel_id=1, source_target_pairs={{0,1},{1,0},{2,3},{3,2},{4,5},{5,4},{6,7},{7,6},{8,9},{9,8},{10,11... | collective-permute-start | bytes 27656 | tf_op jit(solution)/shard_map/ppermute | solution.py:124
  174.3 26.5 %collective-permute-start.27 = (bf16[2,48,768]{2,1,0:T(8,128)(2,1)S(1)}, bf16[2,48,768]{2,1,0:T(8,128)(2,1)S(1)}, u32[]{:S(2)}, u32[]{:S(2)}) collective-permute-start(bf16[2,48,768]{2,1,0:T(8,128)(2,1)S(1)} %slice.189), channel_id=1, source_target_pairs={{0,4},{1,3},{2,6},{3,1},{4,0},{5,7},{6,2},{7,5},{8,12},{9,11},{10,... | collective-permute-start | bytes 442376 | tf_op jit(solution)/shard_map/ppermute | solution.py:124
  181.2 3.8 %collective-permute-start.30 = (f32[2304]{0:T(1024)S(1)}, f32[2304]{0:T(1024)S(1)}, u32[]{:S(2)}, u32[]{:S(2)}) collective-permute-start(f32[2304]{0:T(1024)S(1)} %fusion.40), channel_id=1, source_target_pairs={{0,2},{1,3},{2,0},{3,1},{4,6},{5,7},{6,4},{7,5},{8,10},{9,11},{10,... | collective-permute-start | bytes 27656 | tf_op jit(solution)/shard_map/ppermute | solution.py:124
  185.0 3.7 %collective-permute-start.31 = (f32[2304]{0:T(1024)S(1)}, f32[2304]{0:T(1024)S(1)}, u32[]{:S(2)}, u32[]{:S(2)}) collective-permute-start(f32[2304]{0:T(1024)S(1)} %add.137), channel_id=1, source_target_pairs={{0,4},{1,5},{2,6},{3,7},{4,0},{5,1},{6,2},{7,3},{8,12},{9,13},{10,... | collective-permute-start | bytes 27656 | tf_op jit(solution)/shard_map/ppermute | solution.py:124
  188.7 3.7 %collective-permute-start.32 = (f32[2304]{0:T(1024)S(1)}, f32[2304]{0:T(1024)S(1)}, u32[]{:S(2)}, u32[]{:S(2)}) collective-permute-start(f32[2304]{0:T(1024)S(1)} %add.138), channel_id=1, source_target_pairs={{0,8},{1,9},{2,10},{3,11},{4,12},{5,13},{6,14},{7,15},{8,0},{9,1},... | collective-permute-start | bytes 27656 | tf_op jit(solution)/shard_map/ppermute | solution.py:124
  192.4 7.2 %collective-permute-start.33 = (f32[2304]{0:T(1024)S(1)}, f32[2304]{0:T(1024)S(1)}, u32[]{:S(2)}, u32[]{:S(2)}) collective-permute-start(f32[2304]{0:T(1024)S(1)} %add.139), channel_id=1, source_target_pairs={{0,16},{1,17},{2,18},{3,19},{4,20},{5,21},{6,22},{7,23},{8,24},{9,... | collective-permute-start | bytes 27656 | tf_op jit(solution)/shard_map/ppermute | solution.py:124
  195.8 5.4 %copy-start.5 = (f32[24,48,768]{2,1,0:T(8,128)S(1)}, f32[24,48,768]{2,1,0:T(8,128)}, u32[]{:S(2)}) copy-start(f32[24,48,768]{2,1,0:T(8,128)} %copy-done.4) | copy-start | bytes 10616836
  200.9 4.6 %collective-permute-start.28 = (bf16[1,48,768]{2,1,0:T(8,128)(2,1)S(1)}, bf16[1,48,768]{2,1,0:T(8,128)(2,1)S(1)}, u32[]{:S(2)}, u32[]{:S(2)}) collective-permute-start(bf16[1,48,768]{2,1,0:T(8,128)(2,1)S(1)} %slice.190), channel_id=1, source_target_pairs={{0,2},{1,5},{2,0},{3,7},{4,6},{5,1},{6,4},{7,3},{8,10},{9,13},{10,... | collective-permute-start | bytes 221192 | tf_op jit(solution)/shard_map/ppermute | solution.py:124
  202.7 8.4 %collective-permute-start.22 = (bf16[3,48,768]{2,1,0:T(8,128)(2,1)S(1)}, bf16[3,48,768]{2,1,0:T(8,128)(2,1)S(1)}, u32[]{:S(2)}, u32[]{:S(2)}) collective-permute-start(bf16[3,48,768]{2,1,0:T(8,128)(2,1)S(1)} %get-tuple-element.25), channel_id=1, source_target_pairs={{0,24},{1,25},{2,26},{3,27},{4,28},{5,29},{6,30},{7,31},{8,0},{9,1... | collective-permute-start | bytes 663560 | tf_op jit(solution)/shard_map/ppermute | solution.py:124
  203.1 18.6 %collective-permute-start.21 = (bf16[3,48,768]{2,1,0:T(8,128)(2,1)S(1)}, bf16[3,48,768]{2,1,0:T(8,128)(2,1)S(1)}, u32[]{:S(2)}, u32[]{:S(2)}) collective-permute-start(bf16[3,48,768]{2,1,0:T(8,128)(2,1)S(1)} %get-tuple-element.26), channel_id=1, source_target_pairs={{0,16},{1,17},{2,18},{3,19},{4,20},{5,21},{6,22},{7,23},{8,24},{9,... | collective-permute-start | bytes 663560 | tf_op jit(solution)/shard_map/ppermute | solution.py:124
  204.1 17.6 %collective-permute-start.20 = (bf16[3,48,768]{2,1,0:T(8,128)(2,1)S(1)}, bf16[3,48,768]{2,1,0:T(8,128)(2,1)S(1)}, u32[]{:S(2)}, u32[]{:S(2)}) collective-permute-start(bf16[3,48,768]{2,1,0:T(8,128)(2,1)S(1)} %get-tuple-element.24), channel_id=1, source_target_pairs={{0,8},{1,9},{2,10},{3,11},{4,12},{5,13},{6,14},{7,15},{8,16},{9,17... | collective-permute-start | bytes 663560 | tf_op jit(solution)/shard_map/ppermute | solution.py:124

commit v3 on v0

--- a/solution.py
+++ b/solution.py
@@ -1,12 +1,16 @@
+import functools
 import math
 
 import jax
 import jax.numpy as jnp
 from jax import lax
+from jax.experimental import pallas as pl
+from jax.experimental.pallas import tpu as pltpu
 from jax.sharding import PartitionSpec as P
 
 KERNEL_TAPS = 3
 DILATION_STEP = 32
+TORUS_DEVICES = 32
 
 
 eps = 1e-06
@@ -46,7 +50,7 @@
     )
 
 
-def body(features, cotangent, dilated_kernel_weight, project_weight, outer_gain, inner_gain):
+def body_any(features, cotangent, dilated_kernel_weight, project_weight, outer_gain, inner_gain):
     bin_count = features.shape[1]
     factor = 1.0 / math.sqrt(features.shape[0] * bin_count * lax.axis_size("seq"))
     full_dilated = lax.all_gather(dilated_kernel_weight, "seq", axis=0, tiled=True)
@@ -105,6 +109,342 @@
     return (block_out, grad_features, grad_dilated, grad_project, grad_outer_gain, grad_inner_gain)
 
 
+def links(move):
+    return [(i, move(i)) for i in range(TORUS_DEVICES)]
+
+
+CORE = links(lambda i: i ^ 1)
+FIRST = links(lambda i: i ^ (4 if i & 1 else 2))
+SECOND = links(lambda i: i ^ (2 if i & 1 else 4))
+Z_NEAR = links(lambda i: i ^ 8)
+Z_FAR = links(lambda i: i ^ 16)
+
+BITS = (0, 1)
+PAIR_ORDER = [(r2, r1, low, high) for r2 in BITS for r1 in BITS for low in BITS for high in BITS]
+LAST_ORDER = [(r2, r1, low, high) for r2 in BITS for low in BITS for high in BITS for r1 in BITS]
+TAP_ORDERS = [PAIR_ORDER, PAIR_ORDER, LAST_ORDER]
+PROJECT_ORDER = [(r2, r1, low, high) for low in BITS for high in BITS for r2 in BITS for r1 in BITS]
+BLOCKS = 16
+HALF = 8
+
+VMEM = pl.BlockSpec(memory_space=pltpu.VMEM)
+SMEM = pl.BlockSpec(memory_space=pltpu.SMEM)
+
+
+def send(block, pairs):
+    return lax.ppermute(block, "seq", pairs)
+
+
+def after(value, *events):
+    return lax.optimization_barrier((value,) + events)[0]
+
+
+def device_index():
+    return lax.axis_index("seq").astype(jnp.int32).reshape(1)
+
+
+def block_of(device, place, other):
+    r2, r1, low, high = place
+    owner = device ^ other
+    parity = owner & 1
+    dx = r1 + parity * (r2 - r1)
+    dy = r2 + parity * (r1 - r2)
+    return owner ^ (16 * high + 8 * low + 4 * dy + 2 * dx)
+
+
+def assemble(inputs, outputs):
+    def kernel(*refs):
+        sources, targets = refs[: len(inputs)], refs[len(inputs) :]
+        for target, (_, _, pieces) in zip(targets, outputs):
+            for source, start, count, to_m, to_n in pieces:
+                n = sources[source].shape[1]
+                target[to_m : to_m + count, to_n : to_n + n] = sources[source][
+                    start : start + count
+                ]
+
+    tail = inputs[0].shape[2:]
+    return pl.pallas_call(
+        kernel,
+        out_shape=[
+            jax.ShapeDtypeStruct((m, n) + tail, inputs[0].dtype) for m, n, pieces in outputs
+        ],
+        in_specs=[VMEM] * len(inputs),
+        out_specs=[VMEM] * len(outputs),
+        compiler_params=pltpu.CompilerParams(vmem_limit_bytes=24 << 20),
+        name="assemble",
+    )(*inputs)
+
+
+def upper(kept, received, pick=slice(None)):
+    n = kept.shape[1] // 2
+    total = kept[pick, n:] + received[pick, n:].astype(jnp.float32)
+    return total.astype(jnp.bfloat16)
+
+
+def lower(kept, received, pick=slice(None)):
+    n = kept.shape[1] // 2
+    return kept[pick, :n] + received[pick, :n].astype(jnp.float32)
+
+
+GELU_SCALE = math.sqrt(2.0 / math.pi)
+GELU_CUBE = 0.044715
+
+
+def prepare_kernel(
+    index_ref, features_ref, cotangent_ref, gain_ref, taps_ref, project_ref, active, turned
+):
+    device = index_ref[0]
+    batch, padded_bins, channels = features_ref.shape
+    bins = padded_bins - 2 * DILATION_STEP
+    rows = taps_ref.shape[4]
+    step = 32
+    gain = gain_ref[...]
+    for b in range(batch):
+
+        def some_rows(i, carry):
+            at = pl.multiple_of(i * step, step)
+            x = features_ref[b, pl.ds(at, step), :].astype(jnp.float32)
+            inverse = lax.rsqrt(jnp.sum(x * x, axis=-1, keepdims=True) * (1.0 / channels) + eps)
+            v = x * inverse * gain
+            t = jnp.tanh(GELU_SCALE * (v + GELU_CUBE * (v * v * v)))
+            active[b, pl.ds(at, step), :] = (0.5 * v * (1.0 + t)).astype(jnp.bfloat16)
+            return carry
+
+        lax.fori_loop(0, padded_bins // step, some_rows, 0)
+
+    def blocks(order):
+        for other in BITS:
+            for at, where in enumerate(order):
+                start = pl.multiple_of(block_of(device, where, other) * rows, 16)
+                yield other, at, turned[pl.ds(start, rows), :]
+
+    for tap in range(KERNEL_TAPS):
+        for b in range(batch):
+            turned[:, b * bins : (b + 1) * bins] = active[
+                b, tap * DILATION_STEP : tap * DILATION_STEP + bins, :
+            ].T
+        for other, at, block in blocks(TAP_ORDERS[tap]):
+            taps_ref[other, at // HALF, tap, at % HALF] = block
+    turned[...] = cotangent_ref[...].T
+    for other, at, block in blocks(PROJECT_ORDER):
+        project_ref[other, at // HALF, 0, at % HALF] = block
+
+
+def prepare(features_padded, cotangent, gain, rows):
+    tokens, channels = cotangent.shape
+    shape = lambda count: jax.ShapeDtypeStruct((2, 2, count, HALF, rows, tokens), cotangent.dtype)
+    return pl.pallas_call(
+        prepare_kernel,
+        out_shape=[shape(KERNEL_TAPS), shape(1)],
+        in_specs=[SMEM, VMEM, VMEM, VMEM],
+        out_specs=[VMEM] * 2,
+        scratch_shapes=[
+            pltpu.VMEM(features_padded.shape, jnp.bfloat16),
+            pltpu.VMEM((channels, tokens), jnp.bfloat16),
+        ],
+        compiler_params=pltpu.CompilerParams(vmem_limit_bytes=32 << 20),
+        name="prepare",
+    )(device_index(), features_padded, cotangent, gain.reshape(1, channels))
+
+
+def back_kernel(order_of, index_ref, turned_ref, *refs):
+    parts, out_ref, placed = refs[:4], refs[4], refs[5]
+    device = index_ref[0]
+    matrices, inner, tokens = turned_ref.shape
+    rows = parts[0].shape[2]
+    for other in BITS:
+        for which in BITS:
+            part = parts[2 * other + which]
+            for matrix in range(matrices):
+                product = jnp.dot(
+                    part[matrix].reshape(HALF * rows, inner),
+                    turned_ref[matrix],
+                    preferred_element_type=jnp.float32,
+                )
+                for at in range(HALF):
+                    block = block_of(device, order_of[matrix][which * HALF + at], other)
+                    target = pl.ds(pl.multiple_of(block * rows, 16), rows)
+                    rows_of = product[at * rows : (at + 1) * rows]
+                    if matrix == 0:
+                        placed[target, :] = rows_of
+                    else:
+                        placed[target, :] += rows_of
+    out_ref[...] = placed[...].T
+
+
+def back(turned, parts, order_of):
+    rows = parts[0].shape[2]
+    tokens = turned.shape[2]
+    channels = 2 * BLOCKS * rows
+    return pl.pallas_call(
+        functools.partial(back_kernel, order_of),
+        out_shape=jax.ShapeDtypeStruct((tokens, channels), jnp.float32),
+        in_specs=[SMEM] + [VMEM] * 5,
+        out_specs=VMEM,
+        scratch_shapes=[pltpu.VMEM((channels, tokens), jnp.float32)],
+        compiler_params=pltpu.CompilerParams(vmem_limit_bytes=40 << 20),
+        name="back",
+    )(device_index(), turned, *parts)
+
+
+def rows_dot(left, right):
+    return jnp.einsum("mnrt,ti->mnri", left, right, preferred_element_type=jnp.float32)
+
+
+def contract(left, right):
+    return jnp.einsum(
+        "ct,ci->ti",
+        left.reshape(-1, left.shape[-1]),
+        right.reshape(-1, right.shape[-1]),
+        preferred_element_type=jnp.float32,
+    )
+
+
+def body_torus(features, cotangent, dilated_kernel_weight, project_weight, outer_gain, inner_gain):
+    batch, bin_count, channels = features.shape
+    inner = project_weight.shape[1]
+    rows = project_weight.shape[0]
+    tokens = batch * bin_count
+    factor = 1.0 / math.sqrt(tokens * TORUS_DEVICES)
+    as_bf16 = lambda value: value.astype(jnp.bfloat16)
+    as_f32 = lambda value: value.astype(jnp.float32)
+
+    taps = jnp.moveaxis(dilated_kernel_weight, 1, 0)[:, None]
+    pair = taps[:2]
+    rest = jnp.concatenate([taps[2:], project_weight[None, None]])
+    pair_in, rest_in = send(pair, Z_FAR), send(rest, FIRST)
+    pair, last, proj = assemble(
+        (pair, pair_in, rest, rest_in),
+        (
+            (2, 2, ((0, 0, 2, 0, 0), (1, 0, 2, 0, 1))),
+            (1, 2, ((2, 0, 1, 0, 0), (3, 0, 1, 0, 1))),
+            (1, 2, ((2, 1, 1, 0, 0), (3, 1, 1, 0, 1))),
+        ),
+    )
+    pair_in, last_in, proj_in = send(pair, Z_NEAR), send(last, Z_FAR), send(proj, SECOND)
+    features_padded = padded(after(features, pair), (("seq", 1),), DILATION_STEP)
+    grow = lambda m, n, a: (m, 2 * n, ((a, 0, m, 0, 0), (a + 1, 0, m, 0, n)))
+    pair, last, proj = assemble(
+        (pair, pair_in, last, last_in, proj, proj_in),
+        (grow(2, 2, 0), grow(1, 2, 2), grow(1, 2, 4)),
+    )
+    pair_in, last_in, proj_in = send(pair, FIRST), send(last, Z_NEAR), send(proj, Z_FAR)
+    (near,) = assemble(
+        after((pair, pair_in, last, last_in), features_padded),
+        (
+            (
+                3,
+                8,
+                ((0, 0, 2, 0, 0), (1, 0, 2, 0, 4), (2, 0, 1, 2, 0), (3, 0, 1, 2, 4)),
+            ),
+        ),
+    )
+    far, near_other = send(near, SECOND), send(near, CORE)
+    flat_cotangent = cotangent.reshape(tokens, channels)
+    act, act_p = prepare(after(features_padded, near), flat_cotangent, outer_gain, rows)
+    (proj,) = assemble((proj, after(proj_in, act)), (grow(1, 4, 0),))
+    proj_far, proj_other = send(proj, Z_NEAR), send(proj, CORE)
+    conv_output = contract(act[0, 0], after(near, proj)) + contract(act[1, 0], near_other)
+    far = after(far, conv_output)
+    far_other = send(far, CORE)
+    conv_output = conv_output + contract(act[0, 1], far) + contract(act[1, 1], far_other)
+    grad_hidden = contract(act_p[0, 0], after(proj, conv_output)) + contract(
+        act_p[1, 0], proj_other
+    )
+    hidden32, pull_inner = jax.vjp(act_norm, conv_output, inner_gain)
+    hidden = as_bf16(hidden32)
+    give_p = as_bf16(rows_dot(act_p[1].reshape(2, HALF, rows, tokens), hidden))
+    recv_p = send(give_p, CORE)
+    proj_far = after(proj_far, give_p)
+    proj_far_other = send(proj_far, CORE)
+    grad_hidden = (
+        grad_hidden + contract(act_p[0, 1], proj_far) + contract(act_p[1, 1], proj_far_other)
+    )
+    grad_conv, grad_gain_inner = pull_inner(grad_hidden)
+    grad_conv = as_bf16(grad_conv)
+    grad_padded = padded(
+        grad_conv.reshape(batch, bin_count, inner), (("seq", 1),), DILATION_STEP
+    )
+
+    give = as_bf16(rows_dot(act[1, 1], grad_conv))
+    recv_far = send(give, CORE)
+    give = as_bf16(rows_dot(act[1, 0], after(grad_conv, give)))
+    recv_near = send(give, CORE)
+    message_p = as_bf16(rows_dot(act_p[0, 1], after(hidden, give)) + as_f32(recv_p[1:]))
+    far_p = send(message_p, Z_NEAR)
+    message = as_bf16(
+        rows_dot(act[0, 1], after(grad_conv, message_p)) + as_f32(recv_far)
+    )
+    recv = send(message, SECOND)
+    kept = rows_dot(act[0, 0], after(grad_conv, message)) + as_f32(recv_near)
+    kept_p = rows_dot(act_p[0, 0], after(hidden, message)) + as_f32(recv_p[:1])
+
+    grad_padded = after(grad_padded, kept, kept_p)
+    turned = jnp.stack(
+        [
+            grad_padded[:, shift : shift + bin_count].reshape(tokens, inner).T
+            for shift in (2 * DILATION_STEP, DILATION_STEP, 0)
+        ]
+    )
+    grad_active = back(turned, (near, far, near_other, far_other), TAP_ORDERS)
+    far_p = after(far_p, grad_active)
+    message_p = upper(kept_p, far_p)
+    kept_p, recv_p = lower(kept_p, far_p), send(message_p, Z_FAR)
+    unused, pull_outer = jax.vjp(act_norm, as_f32(after(features, message_p)), outer_gain)
+    grad_branch, grad_gain_outer = pull_outer(grad_active.reshape(features.shape))
+    grad_features = as_bf16(as_f32(cotangent) + grad_branch)
+    gains = jnp.concatenate([grad_gain_outer, grad_gain_inner]) * factor
+    gains = gains + send(gains, CORE)
+    gains = gains + send(gains, links(lambda i: i ^ 2))
+    projected = back(
+        after(hidden, gains).T[None],
+        (proj, proj_far, proj_other, proj_far_other),
+        [PROJECT_ORDER],
+    )
+    block_out = as_bf16(as_f32(features) + projected.reshape(features.shape))
+
+    recv = after(recv, gains, block_out)
+    pair, last = slice(0, 2), slice(2, 3)
+    message, message_l = upper(kept, recv, pair), upper(kept, recv, last)
+    kept, kept_l = lower(kept, recv, pair), lower(kept, recv, last)
+    recv, recv_l = send(message, FIRST), send(message_l, Z_NEAR)
+    gains = after(gains, message, message_l)
+    gains = gains + send(gains, links(lambda i: i ^ 4))
+
+    recv, recv_l, recv_p, _ = lax.optimization_barrier((recv, recv_l, recv_p, gains))
+    message, message_l, message_p = upper(kept, recv), upper(kept_l, recv_l), upper(kept_p, recv_p)
+    kept, kept_l, kept_p = lower(kept, recv), lower(kept_l, recv_l), lower(kept_p, recv_p)
+    recv, recv_l, recv_p = send(message, Z_NEAR), send(message_l, Z_FAR), send(message_p, SECOND)
+    gains = after(gains, message, message_l, message_p)
+    gains = gains + send(gains, Z_NEAR)
+
+    recv, recv_l, recv_p, _ = lax.optimization_barrier((recv, recv_l, recv_p, gains))
+    message = upper(kept, recv)
+    message_r = jnp.concatenate([upper(kept_l, recv_l), upper(kept_p, recv_p)])
+    kept, kept_l, kept_p = lower(kept, recv), lower(kept_l, recv_l), lower(kept_p, recv_p)
+    recv, recv_r = send(message, Z_FAR), send(message_r, FIRST)
+    gains = after(gains, message, message_r)
+    gains = gains + send(gains, Z_FAR)
+
+    grad_project = (kept_p[0, 0] + as_f32(recv_r[1, 0])) * factor
+    sums = kept + as_f32(recv)
+    grad_dilated = (
+        jnp.stack([sums[0, 0], sums[1, 0], kept_l[0, 0] + as_f32(recv_r[0, 0])], axis=1) * factor
+    )
+
+    device = lax.axis_index("seq")
+    grad_outer_gain = lax.dynamic_slice(gains, (device * rows,), (rows,))
+    part = inner // TORUS_DEVICES
+    grad_inner_gain = lax.dynamic_slice(gains, (channels + device * part,), (part,))
+    return (block_out, grad_features, grad_dilated, grad_project, grad_outer_gain, grad_inner_gain)
+
+
+def body(*operands):
+    if lax.axis_size("seq") == TORUS_DEVICES:
+        return body_torus(*operands)
+    return body_any(*operands)
+
+
 def solution(mesh):
     return jax.shard_map(
         body,

time: 434 us -> 176 us (0.41)
  waiting for transfers between devices: 322 us -> 58.7 us
  starting transfers between devices: 7.73 us -> 55.1 us
  blocking collectives: 42.5 us -> 0 us
  between operations: 14.1 us -> 1.23 us
  Pallas kernels: 0 us -> 10.6 us
  matrix products: 28.2 us -> 19.7 us
  local copies, waits for them, and re-layouts: 8.18 us -> 14.9 us
    reduce_scatter x1 -> x0, waiting for transfers between devices: 169 us -> none  [reduce_dilated(): lax.psum_scatter(jnp.stack(tap_slices, axis=1) * factor, 'seq', scatter_d...]
    all_gather x2 -> x0, waiting for transfers between devices: 113 us -> none  [the longest x1 71.3 us: body(): lax.all_gather(dilated_kernel_weight, 'seq', axis=0, tiled=True)]
    ppermute x0 -> x32, waiting for transfers between devices: none -> 57.6 us  [send(): return lax.ppermute(block, 'seq', pairs)]
    ppermute x0 -> x32, starting transfers between devices: none -> 47.7 us  [send(): return lax.ppermute(block, 'seq', pairs)]
    unnamed x1 -> x0, blocking collectives: 42.5 us -> none
    unnamed x5 -> x0, waiting for transfers between devices: 39.2 us -> none
    pallas_call x0 -> x7, Pallas kernels: none -> 10.6 us  [the longest x2 5.32 us: back(): pl.pallas_call(functools.partial(back_kernel, order_of), out_shape=jax.Sh...]
    dot_general x12 -> x15, matrix products: 28.2 us -> 19.7 us  [the longest x7 12.5 us: rows_dot(): jnp.einsum('mnrt,ti->mnri', left, right, preferred_element_type=jnp.float32)]
  transfers between devices with their start and end apart: 8 -> 36, of which waited for: 4 -> 18; matrix products, arithmetic and copies ran while one was open for 11% -> 21% of each run, Pallas kernels for 0% -> 6%
where the time goes in v3:
time: 176 us; the launch traced here: 175 us
  waiting for transfers between devices  58.7 us (33%)
  starting transfers between devices  55.1 us (31%)
  matrix products  19.7 us (11%)
  local copies, waits for them, and re-layouts  14.9 us (8%)
  other arithmetic  14.9 us (8%)
  Pallas kernels  10.6 us (6%)
    ppermute x32, waiting for transfers between devices, send(): return lax.ppermute(block, 'seq', pairs)  57.6 us
    ppermute x32, starting transfers between devices, send(): return lax.ppermute(block, 'seq', pairs)  47.7 us
    dot_general x7, matrix products, rows_dot(): jnp.einsum('mnrt,ti->mnri', left, right, preferred_element_type=jnp.float32)  12.5 us
    dot_general x8, matrix products, contract(): jnp.einsum('ct,ci->ti', left.reshape(-1, left.shape[-1]), right.reshape(-...  7.23 us
    unnamed x53, local copies, waits for them, and re-layouts  6.58 us
    pallas_call x2, Pallas kernels, back(): pl.pallas_call(functools.partial(back_kernel, order_of), out_shape=jax.Sh...  5.32 us
    ppermute x2, starting transfers between devices, padded(): lax.ppermute(lax.slice_in_dim(block, block.shape[dim] - width, None, axis...  4.8 us
  transfers between devices with their start and end apart: 36, of which 18 were waited for; matrix products, arithmetic and copies ran while one was open for 21% of the time, Pallas kernels for 6%

profile of v3, /device:TPU:0, one launch (start us, length us, event | category | flops | bytes accessed | tf_op | source)
XLA Modules:
  0.0 175.2 jit_solution(316567348145361367)
XLA Ops:
  1.6 4.1 %collective-permute-start = (bf16[2,1,48,768]{3,2,0,1:T(8,128)(2,1)S(1)}, bf16[2,1,48,768]{3,2,0,1:T(8,128)(2,1)S(1)}, u32[]{:S(2)}, u32[]{:S(2)}) collective-permute-start(bf16[2,1,48,768]{3,2,0,1:T(8,128)(2,1)S(1)} %get-tuple-element.116), channel_id=1, source_target_pairs={{0,16},{1,17},{2,18},{3,19},{4,20},{5,21},{6,22},{7,23},{8,24},{9,... | collective-permute-start | bytes 442376 | tf_op jit(solution)/shard_map/ppermute | solution.py:135
  7.5 1.6 collective-permute-start.1
  9.1 3.7 %collective-permute-done = bf16[2,1,48,768]{3,2,0,1:T(8,128)(2,1)S(1)} collective-permute-done((bf16[2,1,48,768]{3,2,0,1:T(8,128)(2,1)S(1)}, bf16[2,1,48,768]{3,2,0,1:T(8,128)(2,1)S(1)}, u32[]{:S(2)}, u32[]{:S(2)}) %collective-permute-start) | collective-permute-done | bytes 147488 | tf_op jit(solution)/shard_map/ppermute | solution.py:135
  12.8 1.6 collective-permute-start.4
  14.5 1.3 collective-permute-start.2
  15.8 3.2 %collective-permute-start.5 = (bf16[1,2,48,768]{3,2,1,0:T(8,128)(2,1)S(1)}, bf16[1,2,48,768]{3,2,1,0:T(8,128)(2,1)S(1)}, u32[]{:S(2)}, u32[]{:S(2)}) collective-permute-start(bf16[1,2,48,768]{3,2,1,0:T(8,128)(2,1)S(1)} %get-tuple-element.46.refs_2_), channel_id=1, source_target_pairs={{0,16},{1,17},{2,18},{3,19},{4,20},{5,21},{6,22},{7,23},{8,24},{9,... | collective-permute-start | bytes 442376 | tf_op jit(solution)/shard_map/ppermute | solution.py:135
  19.0 1.5 collective-permute-start.6
  20.5 1.3 collective-permute-start.3
  22.8 1.3 collective-permute-done.6.refs_5_
  24.9 1.5 collective-permute-start.7
  26.5 3.4 %collective-permute-start.8 = (bf16[1,4,48,768]{3,2,1,0:T(8,128)(2,1)S(1)}, bf16[1,4,48,768]{3,2,1,0:T(8,128)(2,1)S(1)}, u32[]{:S(2)}, u32[]{:S(2)}) collective-permute-start(bf16[1,4,48,768]{3,2,1,0:T(8,128)(2,1)S(1)} %get-tuple-element.52.refs_2_), channel_id=1, source_target_pairs={{0,8},{1,9},{2,10},{3,11},{4,12},{5,13},{6,14},{7,15},{8,0},{9,1},... | collective-permute-start | bytes 884744 | tf_op jit(solution)/shard_map/ppermute | solution.py:135
  31.0 6.3 %collective-permute-done.8.refs_3_ = bf16[1,4,48,768]{3,2,1,0:T(8,128)(2,1)S(1)} collective-permute-done((bf16[1,4,48,768]{3,2,1,0:T(8,128)(2,1)S(1)}, bf16[1,4,48,768]{3,2,1,0:T(8,128)(2,1)S(1)}, u32[]{:S(2)}, u32[]{:S(2)}) %collective-permute-start.8) | collective-permute-done | bytes 294944 | tf_op jit(solution)/shard_map/ppermute | solution.py:135
  38.7 1.8 %collective-permute-start.9 = (bf16[1,4,48,768]{3,2,1,0:T(8,128)(2,1)}, bf16[1,4,48,768]{3,2,1,0:T(8,128)(2,1)}, u32[]{:S(2)}, u32[]{:S(2)}) collective-permute-start(bf16[1,4,48,768]{3,2,1,0:T(8,128)(2,1)} %get-tuple-element.56.refs_0_), channel_id=1, source_target_pairs={{0,16},{1,17},{2,18},{3,19},{4,20},{5,21},{6,22},{7,23},{8,24},{9,... | collective-permute-start | bytes 884744 | tf_op jit(solution)/shard_map/ppermute | solution.py:135
  41.6 1.3 copy-done.13
  42.9 3.3 %prepare.1 = (bf16[2,2,3,8,48,256]{5,4,3,2,1,0:T(8,128)(2,1)S(1)}, bf16[2,2,1,8,48,256]{5,4,3,2,1,0:T(8,128)(2,1)S(1)}) custom-call(s32[1]{0:T(128)} %bitcast.index_ref, bf16[2,192,1536]{2,1,0:T(8,128)(2,1)S(1)} %copy-done.13, bf16[256,1536]{1,0:T(8,128)(2,1)S(1)} %bitcast.153, f32[1,1536]{1,0:T(1,128)S(1)} %reshape.145.gain_ref), custom_call_target="tpu_custom_call" | custom-call | tf_op jit(solution)/shard_map/prepare/pallas_call | solution.py:236
  46.2 8.3 %collective-permute-done.9.refs_1_ = bf16[1,4,48,768]{3,2,1,0:T(8,128)(2,1)} collective-permute-done((bf16[1,4,48,768]{3,2,1,0:T(8,128)(2,1)}, bf16[1,4,48,768]{3,2,1,0:T(8,128)(2,1)}, u32[]{:S(2)}, u32[]{:S(2)}) %collective-permute-start.9) | collective-permute-done | bytes 294944 | tf_op jit(solution)/shard_map/ppermute | solution.py:135
  57.9 2.4 %collective-permute-done.11.refs_1_ = bf16[3,8,48,768]{3,2,1,0:T(8,128)(2,1)} collective-permute-done((bf16[3,8,48,768]{3,2,1,0:T(8,128)(2,1)S(1)}, bf16[3,8,48,768]{3,2,1,0:T(8,128)(2,1)}, u32[]{:S(2)}, u32[]{:S(2)}) %collective-permute-start.11) | collective-permute-done | bytes 1769504 | tf_op jit(solution)/shard_map/ppermute | solution.py:135
  61.9 2.3 %convolution_add_fusion.4 = f32[256,768]{0,1:T(8,128)S(1)} fusion(f32[256,768]{0,1:T(8,128)S(1)} %convolution_add_fusion.5, bf16[1152,256]{1,0:T(8,128)(2,1)S(1)} %bitcast.159, bf16[1152,768]{1,0:T(8,128)(2,1)} %bitcast.13), kind=kOutput, calls=%fused_computation.35 | convolution fusion | flops 453181440 | bytes 3932160 | tf_op jit(solution)/shard_map/ct,ci->ti/dot_general | solution.py:295
  66.7 1.5 convolution_convert_fusion.2
  68.2 7.8 %collective-permute-done.14.refs_1_ = bf16[1,8,48,768]{3,2,1,0:T(8,128)(2,1)S(1)} collective-permute-done((bf16[1,8,48,768]{3,2,1,0:T(8,128)(2,1)S(1)}, bf16[1,8,48,768]{3,2,1,0:T(8,128)(2,1)S(1)}, u32[]{:S(2)}, u32[]{:S(2)}) %collective-permute-start.14) | collective-permute-done | bytes 589856 | tf_op jit(solution)/shard_map/ppermute | solution.py:135
  79.4 1.9 %convolution_convert_fusion.1 = bf16[3,8,48,768]{3,2,1,0:T(8,128)(2,1)} fusion(bf16[256,768]{0,1:T(8,128)(2,1)S(1)} %fusion.23, bf16[2,2,3,8,48,256]{5,4,3,2,1,0:T(8,128)(2,1)S(1)} %get-tuple-element.55), kind=kOutput, calls=%fused_computation.14 | convolution fusion | flops 453869568 | bytes 2752512 | tf_op jit(solution)/shard_map/mnrt,ti->mnri/dot_general | solution.py:291
  81.8 1.9 %convolution_convert_fusion = bf16[3,8,48,768]{3,2,1,0:T(8,128)(2,1)} fusion(bf16[256,768]{0,1:T(8,128)(2,1)S(1)} %fusion.23, bf16[2,2,3,8,48,256]{5,4,3,2,1,0:T(8,128)(2,1)S(1)} %get-tuple-element.55), kind=kOutput, calls=%fused_computation.13 | convolution fusion | flops 453869568 | bytes 2752512 | tf_op jit(solution)/shard_map/mnrt,ti->mnri/dot_general | solution.py:291
  83.9 1.9 %reshape.156 = bf16[2,128,768]{1,0,2:T(2,128)(2,1)} reshape(bf16[256,768]{0,1:T(8,128)(2,1)} %copy-done.18) | data formatting | bytes 786432 | tf_op jit(solution)/shard_map/reshape | solution.py:366
  85.8 1.9 %fusion.77 = (bf16[2,32,768]{1,0,2:T(2,128)(2,1)S(1)}, bf16[2,32,768]{1,0,2:T(2,128)(2,1)S(1)}) fusion(bf16[2,128,768]{1,0,2:T(2,128)(2,1)} %reshape.156), kind=kLoop, calls=%fused_computation.138 | loop fusion | bytes 393216 | tf_op jit(solution)/shard_map/slice | solution.py:25
  87.7 1.3 collective-permute-start.20
  89.0 3.5 %collective-permute-start.19 = (bf16[2,32,768]{1,0,2:T(2,128)(2,1)S(1)}, bf16[2,32,768]{1,0,2:T(2,128)(2,1)S(1)}, u32[]{:S(2)}, u32[]{:S(2)}) collective-permute-start(bf16[2,32,768]{1,0,2:T(2,128)(2,1)S(1)} %get-tuple-element.112), channel_id=1, source_target_pairs={{0,1},{1,2},{2,3},{3,4},{4,5},{5,6},{6,7},{7,8},{8,9},{9,10},{10,1... | collective-permute-start | bytes 294920 | tf_op jit(solution)/shard_map/ppermute | solution.py:24
  93.7 2.1 %pad_maximum_fusion.1 = bf16[2,192,768]{1,0,2:T(2,128)(2,1)S(1)} fusion(bf16[2,32,768]{1,0,2:T(2,128)(2,1)S(1)} %collective-permute-done.20, bf16[2,128,768]{1,0,2:T(2,128)(2,1)S(1)} %copy-done.21, bf16[2,32,768]{1,0,2:T(2,128)(2,1)S(1)} %collective-permute-done.19), kind=kLoop, calls=%fused_computation.53 | loop fusion | flops 1769472 | bytes 1179648 | tf_op jit(solution)/shard_map/concatenate | solution.py:28
  95.8 1.4 add_convert_fusion.2
  97.2 10.2 %collective-permute-start.18 = (bf16[1,8,48,768]{3,2,1,0:T(8,128)(2,1)S(1)}, bf16[1,8,48,768]{3,2,1,0:T(8,128)(2,1)S(1)}, u32[]{:S(2)}, u32[]{:S(2)}) collective-permute-start(bf16[1,8,48,768]{3,2,1,0:T(8,128)(2,1)S(1)} %add_convert_fusion.2), channel_id=1, source_target_pairs={{0,8},{1,9},{2,10},{3,11},{4,12},{5,13},{6,14},{7,15},{8,0},{9,1},... | collective-permute-start | bytes 1769480 | tf_op jit(solution)/shard_map/ppermute | solution.py:135
  107.4 2.1 %add_convert_fusion = bf16[3,8,48,768]{3,2,1,0:T(8,128)(2,1)S(1)} fusion(bf16[3,8,48,768]{3,2,1,0:T(8,128)(2,1)} %collective-permute-done.17, bf16[256,768]{0,1:T(8,128)(2,1)S(1)} %copy-done.19, bf16[2,2,3,8,48,256]{5,4,3,2,1,0:T(8,128)(2,1)S(1)} %copy-done.1), kind=kOutput, calls=%fused_computation.1 | convolution fusion | flops 455639040 | bytes 4521984 | tf_op jit(solution)/shard_map/mnrt,ti->mnri/dot_general | solution.py:291
  109.8 1.4 convert_add_fusion.1
  111.2 2.1 %convert_add_fusion = f32[3,8,48,768]{3,2,1,0:T(8,128)S(1)} fusion(bf16[3,8,48,768]{3,2,1,0:T(8,128)(2,1)} %collective-permute-done.21, bf16[256,768]{0,1:T(8,128)(2,1)S(1)} %copy-done.19, bf16[2,2,3,8,48,256]{5,4,3,2,1,0:T(8,128)(2,1)S(1)} %copy-done.1), kind=kOutput, calls=%fused_computation | convolution fusion | flops 454754304 | bytes 6291456 | tf_op jit(solution)/shard_map/mnrt,ti->mnri/dot_general | solution.py:291
  116.6 4.0 %back.2 = f32[256,1536]{1,0:T(8,128)S(1)} custom-call(s32[1]{0:T(128)} %bitcast.index_ref, bf16[3,768,256]{2,1,0:T(8,128)(2,1)S(1)} %pad_maximum_fusion.turned_ref, bf16[3,8,48,768]{3,2,1,0:T(8,128)(2,1)S(1)} %assemble.6.refs_0_, bf16[3,8,48,768]{3,2,1,0:T(8,128)(2,1)} %collective-permute-done.11.refs_1_, bf16[3,8,48,768]{3,2,1,0:T(8,128)(2,1)S(1)} %copy-done.5, ...), custom_call_target="tpu_custom_call" | custom-call | tf_op jit(solution)/shard_map/back/pallas_call | solution.py:279
  122.3 2.7 %fusion.15 = (f32[2,128]{1,0:T(2,128)S(1)}, f32[1536]{0:T(1024)S(1)}, f32[2,128,1536]{2,1,0:T(8,128)}) fusion(bf16[2,128,1536]{2,1,0:T(8,128)(2,1)S(1)} %copy-done.17, f32[1536]{0:T(1024)S(1)} %copy-done.23, f32[2,128]{1,0:T(2,128)S(1)} %fusion.64, f32[2,128,1536]{2,1,0:T(8,128)S(1)} %bitcast.150), kind=kLoop, calls=%fused_computation.26 | loop fusion | flops 10615040 | bytes 3946496 | tf_op jit(solution)/shard_map/transpose(jvp())/reduce_sum | solution.py:34
  126.2 1.8 %collective-permute-start.23 = (f32[2304]{0:T(1024)S(1)}, f32[2304]{0:T(1024)S(1)}, u32[]{:S(2)}, u32[]{:S(2)}) collective-permute-start(f32[2304]{0:T(1024)S(1)} %fusion.65), channel_id=1, source_target_pairs={{0,2},{1,3},{2,0},{3,1},{4,6},{5,7},{6,4},{7,5},{8,10},{9,11},{10,... | collective-permute-start | bytes 27656 | tf_op jit(solution)/shard_map/ppermute | solution.py:135
  127.9 2.2 %collective-permute-done.23 = f32[2304]{0:T(1024)S(1)} collective-permute-done((f32[2304]{0:T(1024)S(1)}, f32[2304]{0:T(1024)S(1)}, u32[]{:S(2)}, u32[]{:S(2)}) %collective-permute-start.23) | collective-permute-done | bytes 9248 | tf_op jit(solution)/shard_map/ppermute | solution.py:135
  130.1 1.3 back.3
  133.6 1.6 collective-permute-start.25
  135.1 2.1 %collective-permute-start.27 = (bf16[1,4,48,768]{3,2,1,0:T(8,128)(2,1)}, bf16[1,4,48,768]{3,2,1,0:T(8,128)(2,1)S(1)}, u32[]{:S(2)}, u32[]{:S(2)}) collective-permute-start(bf16[1,4,48,768]{3,2,1,0:T(8,128)(2,1)} %get-tuple-element.98), channel_id=1, source_target_pairs={{0,16},{1,17},{2,18},{3,19},{4,20},{5,21},{6,22},{7,23},{8,24},{9,... | collective-permute-start | bytes 884744 | tf_op jit(solution)/shard_map/ppermute | solution.py:135
  139.0 2.0 %collective-permute-start.28 = (f32[2304]{0:T(1024)S(1)}, f32[2304]{0:T(1024)S(1)}, u32[]{:S(2)}, u32[]{:S(2)}) collective-permute-start(f32[2304]{0:T(1024)S(1)} %add.193), channel_id=1, source_target_pairs={{0,4},{1,5},{2,6},{3,7},{4,0},{5,1},{6,2},{7,3},{8,12},{9,13},{10,... | collective-permute-start | bytes 27656 | tf_op jit(solution)/shard_map/ppermute | solution.py:135
  141.0 1.9 %collective-permute-done.28 = f32[2304]{0:T(1024)S(1)} collective-permute-done((f32[2304]{0:T(1024)S(1)}, f32[2304]{0:T(1024)S(1)}, u32[]{:S(2)}, u32[]{:S(2)}) %collective-permute-start.28) | collective-permute-done | bytes 9248 | tf_op jit(solution)/shard_map/ppermute | solution.py:135
  142.9 7.7 %collective-permute-done.27 = bf16[1,4,48,768]{3,2,1,0:T(8,128)(2,1)S(1)} collective-permute-done((bf16[1,4,48,768]{3,2,1,0:T(8,128)(2,1)}, bf16[1,4,48,768]{3,2,1,0:T(8,128)(2,1)S(1)}, u32[]{:S(2)}, u32[]{:S(2)}) %collective-permute-start.27) | collective-permute-done | bytes 294944 | tf_op jit(solution)/shard_map/ppermute | solution.py:135
  150.7 2.3 %collective-permute-done.26 = bf16[1,4,48,768]{3,2,1,0:T(8,128)(2,1)} collective-permute-done((bf16[1,4,48,768]{3,2,1,0:T(8,128)(2,1)}, bf16[1,4,48,768]{3,2,1,0:T(8,128)(2,1)}, u32[]{:S(2)}, u32[]{:S(2)}) %collective-permute-start.26) | collective-permute-done | bytes 294944 | tf_op jit(solution)/shard_map/ppermute | solution.py:135
  155.1 1.8 %collective-permute-start.31 = (bf16[1,2,48,768]{3,2,1,0:T(8,128)(2,1)S(1)}, bf16[1,2,48,768]{3,2,1,0:T(8,128)(2,1)S(1)}, u32[]{:S(2)}, u32[]{:S(2)}) collective-permute-start(bf16[1,2,48,768]{3,2,1,0:T(8,128)(2,1)S(1)} %get-tuple-element.99), channel_id=1, source_target_pairs={{0,4},{1,3},{2,6},{3,1},{4,0},{5,7},{6,2},{7,5},{8,12},{9,11},{10,... | collective-permute-start | bytes 442376 | tf_op jit(solution)/shard_map/ppermute | solution.py:135
  156.9 7.0 %collective-permute-done.32 = f32[2304]{0:T(1024)S(1)} collective-permute-done((f32[2304]{0:T(1024)S(1)}, f32[2304]{0:T(1024)S(1)}, u32[]{:S(2)}, u32[]{:S(2)}) %collective-permute-start.32) | collective-permute-done | bytes 9248 | tf_op jit(solution)/shard_map/ppermute | solution.py:135
  165.2 2.0 %collective-permute-start.35 = (f32[2304]{0:T(1024)S(1)}, f32[2304]{0:T(1024)S(1)}, u32[]{:S(2)}, u32[]{:S(2)}) collective-permute-start(f32[2304]{0:T(1024)S(1)} %add.206), channel_id=1, source_target_pairs={{0,16},{1,17},{2,18},{3,19},{4,20},{5,21},{6,22},{7,23},{8,24},{9,... | collective-permute-start | bytes 27656 | tf_op jit(solution)/shard_map/ppermute | solution.py:135
  167.1 1.4 fusion.13
  169.5 2.4 %collective-permute-done.35 = f32[2304]{0:T(1024)S(1)} collective-permute-done((f32[2304]{0:T(1024)S(1)}, f32[2304]{0:T(1024)S(1)}, u32[]{:S(2)}, u32[]{:S(2)}) %collective-permute-start.35) | collective-permute-done | bytes 9248 | tf_op jit(solution)/shard_map/ppermute | solution.py:135
  (145 shorter events, 38.7 us)
Async XLA Ops:
  0.6 13.8 %copy-start.16 = (bf16[2,128,1536]{2,1,0:T(8,128)(2,1)S(1)}, bf16[2,128,1536]{2,1,0:T(8,128)(2,1)}, u32[]{:S(2)}) copy-start(bf16[2,128,1536]{2,1,0:T(8,128)(2,1)} %param.6) | copy-start | bytes 2359300
  1.6 11.1 %collective-permute-start = (bf16[2,1,48,768]{3,2,0,1:T(8,128)(2,1)S(1)}, bf16[2,1,48,768]{3,2,0,1:T(8,128)(2,1)S(1)}, u32[]{:S(2)}, u32[]{:S(2)}) collective-permute-start(bf16[2,1,48,768]{3,2,0,1:T(8,128)(2,1)S(1)} %get-tuple-element.116), channel_id=1, source_target_pairs={{0,16},{1,17},{2,18},{3,19},{4,20},{5,21},{6,22},{7,23},{8,24},{9,... | collective-permute-start | bytes 442376 | tf_op jit(solution)/shard_map/ppermute | solution.py:135
  7.5 5.2 %collective-permute-start.1 = (bf16[2,1,48,768]{3,2,1,0:T(8,128)(2,1)S(1)}, bf16[2,1,48,768]{3,2,1,0:T(8,128)(2,1)S(1)}, u32[]{:S(2)}, u32[]{:S(2)}) collective-permute-start(bf16[2,1,48,768]{3,2,1,0:T(8,128)(2,1)S(1)} %pad_maximum_fusion.2.refs_2_), channel_id=1, source_target_pairs={{0,2},{1,5},{2,0},{3,7},{4,6},{5,1},{6,4},{7,3},{8,10},{9,13},{10,... | collective-permute-start | bytes 442376 | tf_op jit(solution)/shard_map/ppermute | solution.py:135
  12.8 11.3 %collective-permute-start.4 = (bf16[2,2,48,768]{3,2,1,0:T(8,128)(2,1)S(1)}, bf16[2,2,48,768]{3,2,1,0:T(8,128)(2,1)S(1)}, u32[]{:S(2)}, u32[]{:S(2)}) collective-permute-start(bf16[2,2,48,768]{3,2,1,0:T(8,128)(2,1)S(1)} %get-tuple-element.44.refs_0_), channel_id=1, source_target_pairs={{0,8},{1,9},{2,10},{3,11},{4,12},{5,13},{6,14},{7,15},{8,0},{9,1},... | collective-permute-start | bytes 884744 | tf_op jit(solution)/shard_map/ppermute | solution.py:135
  14.5 12.0 %collective-permute-start.2 = (bf16[2,32,1536]{2,1,0:T(8,128)(2,1)S(1)}, bf16[2,32,1536]{2,1,0:T(8,128)(2,1)S(1)}, u32[]{:S(2)}, u32[]{:S(2)}) collective-permute-start(bf16[2,32,1536]{2,1,0:T(8,128)(2,1)S(1)} %get-tuple-element.111), channel_id=1, source_target_pairs={{0,1},{1,2},{2,3},{3,4},{4,5},{5,6},{6,7},{7,8},{8,9},{9,10},{10,1... | collective-permute-start | bytes 589832 | tf_op jit(solution)/shard_map/ppermute | solution.py:24
  15.8 7.1 %collective-permute-start.5 = (bf16[1,2,48,768]{3,2,1,0:T(8,128)(2,1)S(1)}, bf16[1,2,48,768]{3,2,1,0:T(8,128)(2,1)S(1)}, u32[]{:S(2)}, u32[]{:S(2)}) collective-permute-start(bf16[1,2,48,768]{3,2,1,0:T(8,128)(2,1)S(1)} %get-tuple-element.46.refs_2_), channel_id=1, source_target_pairs={{0,16},{1,17},{2,18},{3,19},{4,20},{5,21},{6,22},{7,23},{8,24},{9,... | collective-permute-start | bytes 442376 | tf_op jit(solution)/shard_map/ppermute | solution.py:135
  19.0 5.1 %collective-permute-start.6 = (bf16[1,2,48,768]{3,2,1,0:T(8,128)(2,1)S(1)}, bf16[1,2,48,768]{3,2,1,0:T(8,128)(2,1)S(1)}, u32[]{:S(2)}, u32[]{:S(2)}) collective-permute-start(bf16[1,2,48,768]{3,2,1,0:T(8,128)(2,1)S(1)} %get-tuple-element.47.refs_4_), channel_id=1, source_target_pairs={{0,4},{1,3},{2,6},{3,1},{4,0},{5,7},{6,2},{7,5},{8,12},{9,11},{10,... | collective-permute-start | bytes 442376 | tf_op jit(solution)/shard_map/ppermute | solution.py:135
  20.5 9.4 %collective-permute-start.3 = (bf16[2,32,1536]{2,1,0:T(8,128)(2,1)S(1)}, bf16[2,32,1536]{2,1,0:T(8,128)(2,1)S(1)}, u32[]{:S(2)}, u32[]{:S(2)}) collective-permute-start(bf16[2,32,1536]{2,1,0:T(8,128)(2,1)S(1)} %get-tuple-element.110), channel_id=1, source_target_pairs={{1,0},{2,1},{3,2},{4,3},{5,4},{6,5},{7,6},{8,7},{9,8},{10,9},{11,1... | collective-permute-start | bytes 589832 | tf_op jit(solution)/shard_map/ppermute | solution.py:27
  24.9 12.4 %collective-permute-start.7 = (bf16[2,4,48,768]{3,2,1,0:T(8,128)(2,1)S(1)}, bf16[2,4,48,768]{3,2,1,0:T(8,128)(2,1)S(1)}, u32[]{:S(2)}, u32[]{:S(2)}) collective-permute-start(bf16[2,4,48,768]{3,2,1,0:T(8,128)(2,1)S(1)} %get-tuple-element.50.refs_0_), channel_id=1, source_target_pairs={{0,2},{1,5},{2,0},{3,7},{4,6},{5,1},{6,4},{7,3},{8,10},{9,13},{10,... | collective-permute-start | bytes 1769480 | tf_op jit(solution)/shard_map/ppermute | solution.py:135
  26.5 10.9 %collective-permute-start.8 = (bf16[1,4,48,768]{3,2,1,0:T(8,128)(2,1)S(1)}, bf16[1,4,48,768]{3,2,1,0:T(8,128)(2,1)S(1)}, u32[]{:S(2)}, u32[]{:S(2)}) collective-permute-start(bf16[1,4,48,768]{3,2,1,0:T(8,128)(2,1)S(1)} %get-tuple-element.52.refs_2_), channel_id=1, source_target_pairs={{0,8},{1,9},{2,10},{3,11},{4,12},{5,13},{6,14},{7,15},{8,0},{9,1},... | collective-permute-start | bytes 884744 | tf_op jit(solution)/shard_map/ppermute | solution.py:135
  31.0 9.5 %copy-start.23 = (f32[1536]{0:T(1024)S(1)}, f32[1536]{0:T(1024)}, u32[]{:S(2)}) copy-start(f32[1536]{0:T(1024)} %param.10) | copy-start | bytes 18436
  37.4 19.2 %collective-permute-start.10 = (bf16[3,8,48,768]{3,2,1,0:T(8,128)(2,1)S(1)}, bf16[3,8,48,768]{3,2,1,0:T(8,128)(2,1)S(1)}, u32[]{:S(2)}, u32[]{:S(2)}) collective-permute-start(bf16[3,8,48,768]{3,2,1,0:T(8,128)(2,1)S(1)} %assemble.6.refs_0_), channel_id=1, source_target_pairs={{0,1},{1,0},{2,3},{3,2},{4,5},{5,4},{6,7},{7,6},{8,9},{9,8},{10,11... | collective-permute-start | bytes 5308424 | tf_op jit(solution)/shard_map/ppermute | solution.py:135
  37.7 22.6 %collective-permute-start.11 = (bf16[3,8,48,768]{3,2,1,0:T(8,128)(2,1)S(1)}, bf16[3,8,48,768]{3,2,1,0:T(8,128)(2,1)}, u32[]{:S(2)}, u32[]{:S(2)}) collective-permute-start(bf16[3,8,48,768]{3,2,1,0:T(8,128)(2,1)S(1)} %assemble.6.refs_0_), channel_id=1, source_target_pairs={{0,4},{1,3},{2,6},{3,1},{4,0},{5,7},{6,2},{7,5},{8,12},{9,11},{10,... | collective-permute-start | bytes 5308424 | tf_op jit(solution)/shard_map/ppermute | solution.py:135
  38.7 15.9 %collective-permute-start.9 = (bf16[1,4,48,768]{3,2,1,0:T(8,128)(2,1)}, bf16[1,4,48,768]{3,2,1,0:T(8,128)(2,1)}, u32[]{:S(2)}, u32[]{:S(2)}) collective-permute-start(bf16[1,4,48,768]{3,2,1,0:T(8,128)(2,1)} %get-tuple-element.56.refs_0_), channel_id=1, source_target_pairs={{0,16},{1,17},{2,18},{3,19},{4,20},{5,21},{6,22},{7,23},{8,24},{9,... | collective-permute-start | bytes 884744 | tf_op jit(solution)/shard_map/ppermute | solution.py:135
  46.2 20.5 %copy-start.10 = (bf16[2,2,1,8,48,256]{5,4,3,2,1,0:T(8,128)(2,1)}, bf16[2,2,1,8,48,256]{5,4,3,2,1,0:T(8,128)(2,1)S(1)}, u32[]{:S(2)}) copy-start(bf16[2,2,1,8,48,256]{5,4,3,2,1,0:T(8,128)(2,1)S(1)} %get-tuple-element.60) | copy-start | bytes 2359300
  46.2 35.6 %copy-start = (bf16[2,2,3,8,48,256]{5,4,3,2,1,0:T(8,128)(2,1)}, bf16[2,2,3,8,48,256]{5,4,3,2,1,0:T(8,128)(2,1)S(1)}, u32[]{:S(2)}) copy-start(bf16[2,2,3,8,48,256]{5,4,3,2,1,0:T(8,128)(2,1)S(1)} %get-tuple-element.55) | copy-start | bytes 7077892
  55.6 20.4 %copy-start.6 = (bf16[1,8,48,768]{3,2,1,0:T(8,128)(2,1)}, bf16[1,8,48,768]{3,2,1,0:T(8,128)(2,1)S(1)}, u32[]{:S(2)}) copy-start(bf16[1,8,48,768]{3,2,1,0:T(8,128)(2,1)S(1)} %assemble.7.refs_0_) | copy-start | bytes 1769476
  60.3 4.7 %collective-permute-start.12 = (bf16[3,8,48,768]{3,2,1,0:T(8,128)(2,1)}, bf16[3,8,48,768]{3,2,1,0:T(8,128)(2,1)S(1)}, u32[]{:S(2)}, u32[]{:S(2)}) collective-permute-start(bf16[3,8,48,768]{3,2,1,0:T(8,128)(2,1)} %collective-permute-done.11.refs_1_), channel_id=1, source_target_pairs={{0,1},{1,0},{2,3},{3,2},{4,5},{5,4},{6,7},{7,6},{8,9},{9,8},{10,11... | collective-permute-start | bytes 5308424 | tf_op jit(solution)/shard_map/ppermute | solution.py:135
  60.3 16.2 %collective-permute-start.13 = (bf16[1,8,48,768]{3,2,1,0:T(8,128)(2,1)S(1)}, bf16[1,8,48,768]{3,2,1,0:T(8,128)(2,1)S(1)}, u32[]{:S(2)}, u32[]{:S(2)}) collective-permute-start(bf16[1,8,48,768]{3,2,1,0:T(8,128)(2,1)S(1)} %assemble.7.refs_0_), channel_id=1, source_target_pairs={{0,1},{1,0},{2,3},{3,2},{4,5},{5,4},{6,7},{7,6},{8,9},{9,8},{10,11... | collective-permute-start | bytes 1769480 | tf_op jit(solution)/shard_map/ppermute | solution.py:135
  60.8 15.2 %collective-permute-start.14 = (bf16[1,8,48,768]{3,2,1,0:T(8,128)(2,1)S(1)}, bf16[1,8,48,768]{3,2,1,0:T(8,128)(2,1)S(1)}, u32[]{:S(2)}, u32[]{:S(2)}) collective-permute-start(bf16[1,8,48,768]{3,2,1,0:T(8,128)(2,1)S(1)} %assemble.7.refs_0_), channel_id=1, source_target_pairs={{0,8},{1,9},{2,10},{3,11},{4,12},{5,13},{6,14},{7,15},{8,0},{9,1},... | collective-permute-start | bytes 1769480 | tf_op jit(solution)/shard_map/ppermute | solution.py:135
  76.1 2.0 %collective-permute-start.15 = (bf16[1,8,48,768]{3,2,1,0:T(8,128)(2,1)S(1)}, bf16[1,8,48,768]{3,2,1,0:T(8,128)(2,1)S(1)}, u32[]{:S(2)}, u32[]{:S(2)}) collective-permute-start(bf16[1,8,48,768]{3,2,1,0:T(8,128)(2,1)S(1)} %collective-permute-done.14.refs_1_), channel_id=1, source_target_pairs={{0,1},{1,0},{2,3},{3,2},{4,5},{5,4},{6,7},{7,6},{8,9},{9,8},{10,11... | collective-permute-start | bytes 1769480 | tf_op jit(solution)/shard_map/ppermute | solution.py:135
  81.3 26.0 %collective-permute-start.17 = (bf16[3,8,48,768]{3,2,1,0:T(8,128)(2,1)}, bf16[3,8,48,768]{3,2,1,0:T(8,128)(2,1)}, u32[]{:S(2)}, u32[]{:S(2)}) collective-permute-start(bf16[3,8,48,768]{3,2,1,0:T(8,128)(2,1)} %convolution_convert_fusion.1), channel_id=1, source_target_pairs={{0,1},{1,0},{2,3},{3,2},{4,5},{5,4},{6,7},{7,6},{8,9},{9,8},{10,11... | collective-permute-start | bytes 5308424 | tf_op jit(solution)/shard_map/ppermute | solution.py:135
  81.4 14.3 %collective-permute-start.16 = (bf16[2,8,48,768]{3,2,1,0:T(8,128)(2,1)}, bf16[2,8,48,768]{3,2,1,0:T(8,128)(2,1)}, u32[]{:S(2)}, u32[]{:S(2)}) collective-permute-start(bf16[2,8,48,768]{3,2,1,0:T(8,128)(2,1)} %convolution_convert_fusion.2), channel_id=1, source_target_pairs={{0,1},{1,0},{2,3},{3,2},{4,5},{5,4},{6,7},{7,6},{8,9},{9,8},{10,11... | collective-permute-start | bytes 3538952 | tf_op jit(solution)/shard_map/ppermute | solution.py:135
  83.8 27.5 %collective-permute-start.21 = (bf16[3,8,48,768]{3,2,1,0:T(8,128)(2,1)}, bf16[3,8,48,768]{3,2,1,0:T(8,128)(2,1)}, u32[]{:S(2)}, u32[]{:S(2)}) collective-permute-start(bf16[3,8,48,768]{3,2,1,0:T(8,128)(2,1)} %convolution_convert_fusion), channel_id=1, source_target_pairs={{0,1},{1,0},{2,3},{3,2},{4,5},{5,4},{6,7},{7,6},{8,9},{9,8},{10,11... | collective-permute-start | bytes 5308424 | tf_op jit(solution)/shard_map/ppermute | solution.py:135
  85.8 7.9 %copy-start.21 = (bf16[2,128,768]{1,0,2:T(2,128)(2,1)S(1)}, bf16[2,128,768]{1,0,2:T(2,128)(2,1)}, u32[]{:S(2)}) copy-start(bf16[2,128,768]{1,0,2:T(2,128)(2,1)} %reshape.156) | copy-start | bytes 1179652
  85.8 10.0 %copy-start.11 = (bf16[2,2,1,8,48,256]{5,4,3,2,1,0:T(8,128)(2,1)S(1)}, bf16[2,2,1,8,48,256]{5,4,3,2,1,0:T(8,128)(2,1)}, u32[]{:S(2)}) copy-start(bf16[2,2,1,8,48,256]{5,4,3,2,1,0:T(8,128)(2,1)} %copy-done.10) | copy-start | bytes 2359300
  87.7 4.8 %collective-permute-start.20 = (bf16[2,32,768]{1,0,2:T(2,128)(2,1)S(1)}, bf16[2,32,768]{1,0,2:T(2,128)(2,1)S(1)}, u32[]{:S(2)}, u32[]{:S(2)}) collective-permute-start(bf16[2,32,768]{1,0,2:T(2,128)(2,1)S(1)} %get-tuple-element.113), channel_id=1, source_target_pairs={{1,0},{2,1},{3,2},{4,3},{5,4},{6,5},{7,6},{8,7},{9,8},{10,9},{11,1... | collective-permute-start | bytes 294920 | tf_op jit(solution)/shard_map/ppermute | solution.py:27
  89.0 18.4 %copy-start.1 = (bf16[2,2,3,8,48,256]{5,4,3,2,1,0:T(8,128)(2,1)S(1)}, bf16[2,2,3,8,48,256]{5,4,3,2,1,0:T(8,128)(2,1)}, u32[]{:S(2)}) copy-start(bf16[2,2,3,8,48,256]{5,4,3,2,1,0:T(8,128)(2,1)} %copy-done) | copy-start | bytes 7077892
  89.0 18.4 %copy-start.19 = (bf16[256,768]{0,1:T(8,128)(2,1)S(1)}, bf16[256,768]{0,1:T(8,128)(2,1)}, u32[]{:S(2)}) copy-start(bf16[256,768]{0,1:T(8,128)(2,1)} %copy-done.18) | copy-start | bytes 1179652
  89.0 4.6 %collective-permute-start.19 = (bf16[2,32,768]{1,0,2:T(2,128)(2,1)S(1)}, bf16[2,32,768]{1,0,2:T(2,128)(2,1)S(1)}, u32[]{:S(2)}, u32[]{:S(2)}) collective-permute-start(bf16[2,32,768]{1,0,2:T(2,128)(2,1)S(1)} %get-tuple-element.112), channel_id=1, source_target_pairs={{0,1},{1,2},{2,3},{3,4},{4,5},{5,6},{6,7},{7,8},{8,9},{9,10},{10,1... | collective-permute-start | bytes 294920 | tf_op jit(solution)/shard_map/ppermute | solution.py:24
  97.2 23.5 %collective-permute-start.18 = (bf16[1,8,48,768]{3,2,1,0:T(8,128)(2,1)S(1)}, bf16[1,8,48,768]{3,2,1,0:T(8,128)(2,1)S(1)}, u32[]{:S(2)}, u32[]{:S(2)}) collective-permute-start(bf16[1,8,48,768]{3,2,1,0:T(8,128)(2,1)S(1)} %add_convert_fusion.2), channel_id=1, source_target_pairs={{0,8},{1,9},{2,10},{3,11},{4,12},{5,13},{6,14},{7,15},{8,0},{9,1},... | collective-permute-start | bytes 1769480 | tf_op jit(solution)/shard_map/ppermute | solution.py:135
  109.5 23.0 %collective-permute-start.24 = (bf16[3,8,48,768]{3,2,1,0:T(8,128)(2,1)S(1)}, bf16[3,8,48,768]{3,2,1,0:T(8,128)(2,1)S(1)}, u32[]{:S(2)}, u32[]{:S(2)}) collective-permute-start(bf16[3,8,48,768]{3,2,1,0:T(8,128)(2,1)S(1)} %add_convert_fusion), channel_id=1, source_target_pairs={{0,4},{1,3},{2,6},{3,1},{4,0},{5,7},{6,2},{7,5},{8,12},{9,11},{10,... | collective-permute-start | bytes 5308424 | tf_op jit(solution)/shard_map/ppermute | solution.py:135
  122.3 7.9 %copy-start.7 = (bf16[1,8,48,768]{3,2,1,0:T(8,128)(2,1)S(1)}, bf16[1,8,48,768]{3,2,1,0:T(8,128)(2,1)}, u32[]{:S(2)}) copy-start(bf16[1,8,48,768]{3,2,1,0:T(8,128)(2,1)} %copy-done.6) | copy-start | bytes 1769476
  125.0 1.2 collective-permute-start.22
  126.2 3.9 %collective-permute-start.23 = (f32[2304]{0:T(1024)S(1)}, f32[2304]{0:T(1024)S(1)}, u32[]{:S(2)}, u32[]{:S(2)}) collective-permute-start(f32[2304]{0:T(1024)S(1)} %fusion.65), channel_id=1, source_target_pairs={{0,2},{1,3},{2,0},{3,1},{4,6},{5,7},{6,4},{7,5},{8,10},{9,11},{10,... | collective-permute-start | bytes 27656 | tf_op jit(solution)/shard_map/ppermute | solution.py:135
  133.6 19.3 %collective-permute-start.25 = (bf16[2,4,48,768]{3,2,1,0:T(8,128)(2,1)}, bf16[2,4,48,768]{3,2,1,0:T(8,128)(2,1)S(1)}, u32[]{:S(2)}, u32[]{:S(2)}) collective-permute-start(bf16[2,4,48,768]{3,2,1,0:T(8,128)(2,1)} %get-tuple-element.88), channel_id=1, source_target_pairs={{0,2},{1,5},{2,0},{3,7},{4,6},{5,1},{6,4},{7,3},{8,10},{9,13},{10,... | collective-permute-start | bytes 1769480 | tf_op jit(solution)/shard_map/ppermute | solution.py:135
  135.1 15.5 %collective-permute-start.27 = (bf16[1,4,48,768]{3,2,1,0:T(8,128)(2,1)}, bf16[1,4,48,768]{3,2,1,0:T(8,128)(2,1)S(1)}, u32[]{:S(2)}, u32[]{:S(2)}) collective-permute-start(bf16[1,4,48,768]{3,2,1,0:T(8,128)(2,1)} %get-tuple-element.98), channel_id=1, source_target_pairs={{0,16},{1,17},{2,18},{3,19},{4,20},{5,21},{6,22},{7,23},{8,24},{9,... | collective-permute-start | bytes 884744 | tf_op jit(solution)/shard_map/ppermute | solution.py:135
  138.0 14.9 %collective-permute-start.26 = (bf16[1,4,48,768]{3,2,1,0:T(8,128)(2,1)}, bf16[1,4,48,768]{3,2,1,0:T(8,128)(2,1)}, u32[]{:S(2)}, u32[]{:S(2)}) collective-permute-start(bf16[1,4,48,768]{3,2,1,0:T(8,128)(2,1)} %get-tuple-element.89), channel_id=1, source_target_pairs={{0,8},{1,9},{2,10},{3,11},{4,12},{5,13},{6,14},{7,15},{8,0},{9,1},... | collective-permute-start | bytes 884744 | tf_op jit(solution)/shard_map/ppermute | solution.py:135
  139.0 3.9 %collective-permute-start.28 = (f32[2304]{0:T(1024)S(1)}, f32[2304]{0:T(1024)S(1)}, u32[]{:S(2)}, u32[]{:S(2)}) collective-permute-start(f32[2304]{0:T(1024)S(1)} %add.193), channel_id=1, source_target_pairs={{0,4},{1,5},{2,6},{3,7},{4,0},{5,1},{6,2},{7,3},{8,12},{9,13},{10,... | collective-permute-start | bytes 27656 | tf_op jit(solution)/shard_map/ppermute | solution.py:135
  153.0 10.9 %collective-permute-start.29 = (bf16[2,2,48,768]{3,2,1,0:T(8,128)(2,1)S(1)}, bf16[2,2,48,768]{3,2,1,0:T(8,128)(2,1)S(1)}, u32[]{:S(2)}, u32[]{:S(2)}) collective-permute-start(bf16[2,2,48,768]{3,2,1,0:T(8,128)(2,1)S(1)} %get-tuple-element.96), channel_id=1, source_target_pairs={{0,8},{1,9},{2,10},{3,11},{4,12},{5,13},{6,14},{7,15},{8,0},{9,1},... | collective-permute-start | bytes 884744 | tf_op jit(solution)/shard_map/ppermute | solution.py:135
  154.2 13.0 %copy-start.9 = (bf16[2,128,1536]{2,1,0:T(8,128)(2,1)S(1)}, bf16[2,128,1536]{2,1,0:T(8,128)(2,1)}, u32[]{:S(2)}) copy-start(bf16[2,128,1536]{2,1,0:T(8,128)(2,1)} %param.7) | copy-start | bytes 2359300
  154.2 13.0 %copy-start.20 = (f32[2,128,1536]{2,1,0:T(8,128)S(1)}, f32[2,128,1536]{2,1,0:T(8,128)}, u32[]{:S(2)}) copy-start(f32[2,128,1536]{2,1,0:T(8,128)} %get-tuple-element.86) | copy-start | bytes 4718596
  154.2 9.8 %collective-permute-start.30 = (bf16[1,2,48,768]{3,2,1,0:T(8,128)(2,1)S(1)}, bf16[1,2,48,768]{3,2,1,0:T(8,128)(2,1)S(1)}, u32[]{:S(2)}, u32[]{:S(2)}) collective-permute-start(bf16[1,2,48,768]{3,2,1,0:T(8,128)(2,1)S(1)} %get-tuple-element.101), channel_id=1, source_target_pairs={{0,16},{1,17},{2,18},{3,19},{4,20},{5,21},{6,22},{7,23},{8,24},{9,... | collective-permute-start | bytes 442376 | tf_op jit(solution)/shard_map/ppermute | solution.py:135
  155.1 8.8 %collective-permute-start.31 = (bf16[1,2,48,768]{3,2,1,0:T(8,128)(2,1)S(1)}, bf16[1,2,48,768]{3,2,1,0:T(8,128)(2,1)S(1)}, u32[]{:S(2)}, u32[]{:S(2)}) collective-permute-start(bf16[1,2,48,768]{3,2,1,0:T(8,128)(2,1)S(1)} %get-tuple-element.99), channel_id=1, source_target_pairs={{0,4},{1,3},{2,6},{3,1},{4,0},{5,7},{6,2},{7,5},{8,12},{9,11},{10,... | collective-permute-start | bytes 442376 | tf_op jit(solution)/shard_map/ppermute | solution.py:135
  156.9 7.1 %collective-permute-start.32 = (f32[2304]{0:T(1024)S(1)}, f32[2304]{0:T(1024)S(1)}, u32[]{:S(2)}, u32[]{:S(2)}) collective-permute-start(f32[2304]{0:T(1024)S(1)} %add.199), channel_id=1, source_target_pairs={{0,8},{1,9},{2,10},{3,11},{4,12},{5,13},{6,14},{7,15},{8,0},{9,1},... | collective-permute-start | bytes 27656 | tf_op jit(solution)/shard_map/ppermute | solution.py:135
  164.0 9.2 %collective-permute-start.33 = (bf16[2,1,48,768]{3,2,1,0:T(8,128)(2,1)S(1)}, bf16[2,1,48,768]{3,2,1,0:T(8,128)(2,1)S(1)}, u32[]{:S(2)}, u32[]{:S(2)}) collective-permute-start(bf16[2,1,48,768]{3,2,1,0:T(8,128)(2,1)S(1)} %fusion.50), channel_id=1, source_target_pairs={{0,16},{1,17},{2,18},{3,19},{4,20},{5,21},{6,22},{7,23},{8,24},{9,... | collective-permute-start | bytes 442376 | tf_op jit(solution)/shard_map/ppermute | solution.py:135
  165.2 6.8 %collective-permute-start.35 = (f32[2304]{0:T(1024)S(1)}, f32[2304]{0:T(1024)S(1)}, u32[]{:S(2)}, u32[]{:S(2)}) collective-permute-start(f32[2304]{0:T(1024)S(1)} %add.206), channel_id=1, source_target_pairs={{0,16},{1,17},{2,18},{3,19},{4,20},{5,21},{6,22},{7,23},{8,24},{9,... | collective-permute-start | bytes 27656 | tf_op jit(solution)/shard_map/ppermute | solution.py:135
  168.5 5.1 %collective-permute-start.34 = (bf16[2,1,48,768]{3,2,1,0:T(8,128)(2,1)S(1)}, bf16[2,1,48,768]{3,2,1,0:T(8,128)(2,1)S(1)}, u32[]{:S(2)}, u32[]{:S(2)}) collective-permute-start(bf16[2,1,48,768]{3,2,1,0:T(8,128)(2,1)S(1)} %pad_maximum_fusion.3), channel_id=1, source_target_pairs={{0,2},{1,5},{2,0},{3,7},{4,6},{5,1},{6,4},{7,3},{8,10},{9,13},{10,... | collective-permute-start | bytes 442376 | tf_op jit(solution)/shard_map/ppermute | solution.py:135
  (13 other events, 27.5 us)

commit v4 on v3

--- a/solution.py
+++ b/solution.py
@@ -1,4 +1,3 @@
-import functools
 import math
 
 import jax
@@ -16,15 +15,20 @@
 eps = 1e-06
 
 
+def edges(block, axis, dim, width):
+    count = lax.axis_size(axis)
+    forward = [(i, i + 1) for i in range(count - 1)]
+    backward = [(target, source) for source, target in forward]
+    low = lax.ppermute(
+        lax.slice_in_dim(block, block.shape[dim] - width, None, axis=dim), axis, forward
+    )
+    high = lax.ppermute(lax.slice_in_dim(block, 0, width, axis=dim), axis, backward)
+    return low, high
+
+
 def padded(block, sides, width):
     for axis, dim in sides:
-        count = lax.axis_size(axis)
-        forward = [(i, i + 1) for i in range(count - 1)]
-        backward = [(target, source) for source, target in forward]
-        low = lax.ppermute(
-            lax.slice_in_dim(block, block.shape[dim] - width, None, axis=dim), axis, forward
-        )
-        high = lax.ppermute(lax.slice_in_dim(block, 0, width, axis=dim), axis, backward)
+        low, high = edges(block, axis, dim, width)
         block = jnp.concatenate([low, block, high], axis=dim)
     return block
 
@@ -123,7 +127,7 @@
 PAIR_ORDER = [(r2, r1, low, high) for r2 in BITS for r1 in BITS for low in BITS for high in BITS]
 LAST_ORDER = [(r2, r1, low, high) for r2 in BITS for low in BITS for high in BITS for r1 in BITS]
 TAP_ORDERS = [PAIR_ORDER, PAIR_ORDER, LAST_ORDER]
-PROJECT_ORDER = [(r2, r1, low, high) for low in BITS for high in BITS for r2 in BITS for r1 in BITS]
+PROJECT_ORDER = LAST_ORDER
 BLOCKS = 16
 HALF = 8
 
@@ -170,7 +174,7 @@
         ],
         in_specs=[VMEM] * len(inputs),
         out_specs=[VMEM] * len(outputs),
-        compiler_params=pltpu.CompilerParams(vmem_limit_bytes=24 << 20),
+        compiler_params=pltpu.CompilerParams(vmem_limit_bytes=8 << 20),
         name="assemble",
     )(*inputs)
 
@@ -242,49 +246,84 @@
             pltpu.VMEM(features_padded.shape, jnp.bfloat16),
             pltpu.VMEM((channels, tokens), jnp.bfloat16),
         ],
-        compiler_params=pltpu.CompilerParams(vmem_limit_bytes=32 << 20),
+        compiler_params=pltpu.CompilerParams(vmem_limit_bytes=16 << 20),
         name="prepare",
     )(device_index(), features_padded, cotangent, gain.reshape(1, channels))
 
 
-def back_kernel(order_of, index_ref, turned_ref, *refs):
-    parts, out_ref, placed = refs[:4], refs[4], refs[5]
-    device = index_ref[0]
-    matrices, inner, tokens = turned_ref.shape
-    rows = parts[0].shape[2]
+def place_products(device, parts, turned, orders, placed):
+    rows, inner = parts[0].shape[2:]
     for other in BITS:
         for which in BITS:
             part = parts[2 * other + which]
-            for matrix in range(matrices):
+            for matrix, right in enumerate(turned):
                 product = jnp.dot(
                     part[matrix].reshape(HALF * rows, inner),
-                    turned_ref[matrix],
+                    right,
                     preferred_element_type=jnp.float32,
                 )
                 for at in range(HALF):
-                    block = block_of(device, order_of[matrix][which * HALF + at], other)
+                    block = block_of(device, orders[matrix][which * HALF + at], other)
                     target = pl.ds(pl.multiple_of(block * rows, 16), rows)
                     rows_of = product[at * rows : (at + 1) * rows]
                     if matrix == 0:
                         placed[target, :] = rows_of
                     else:
                         placed[target, :] += rows_of
+
+
+def project_back_kernel(index_ref, hidden_ref, features_ref, *refs):
+    parts, out_ref, placed = refs[:4], refs[4], refs[5]
+    place_products(index_ref[0], parts, [hidden_ref[...].T], [PROJECT_ORDER], placed)
+    out_ref[...] = (features_ref[...].astype(jnp.float32) + placed[...].T).astype(jnp.bfloat16)
+
+
+def project_back(hidden, features, parts):
+    return pl.pallas_call(
+        project_back_kernel,
+        out_shape=jax.ShapeDtypeStruct(features.shape, features.dtype),
+        in_specs=[SMEM] + [VMEM] * 6,
+        out_specs=VMEM,
+        scratch_shapes=[pltpu.VMEM(features.shape[::-1], jnp.float32)],
+        compiler_params=pltpu.CompilerParams(vmem_limit_bytes=16 << 20),
+        name="project_back",
+    )(device_index(), hidden, features, *parts)
+
+
+def grad_active_kernel(index_ref, grad_ref, low_ref, high_ref, *refs):
+    parts, (out_ref, padded_ref, placed) = refs[:4], refs[4:]
+    batch, padded_bins, _ = padded_ref.shape
+    bins = padded_bins - 2 * DILATION_STEP
+    for b in range(batch):
+        padded_ref[b, :DILATION_STEP] = low_ref[b]
+        padded_ref[b, DILATION_STEP : DILATION_STEP + bins] = grad_ref[b * bins : (b + 1) * bins]
+        padded_ref[b, DILATION_STEP + bins :] = high_ref[b]
+    turned = []
+    for tap in range(KERNEL_TAPS):
+        shift = (KERNEL_TAPS - 1 - tap) * DILATION_STEP
+        turned.append(
+            jnp.concatenate([padded_ref[b, shift : shift + bins] for b in range(batch)], axis=0).T
+        )
+    place_products(index_ref[0], parts, turned, TAP_ORDERS, placed)
     out_ref[...] = placed[...].T
 
 
-def back(turned, parts, order_of):
-    rows = parts[0].shape[2]
-    tokens = turned.shape[2]
-    channels = 2 * BLOCKS * rows
+def grad_of_active(grad, low, high, parts):
+    tokens, inner = grad.shape
+    batch = low.shape[0]
+    channels = 2 * BLOCKS * parts[0].shape[2]
     return pl.pallas_call(
-        functools.partial(back_kernel, order_of),
+        grad_active_kernel,
         out_shape=jax.ShapeDtypeStruct((tokens, channels), jnp.float32),
-        in_specs=[SMEM] + [VMEM] * 5,
+        in_specs=[SMEM] + [VMEM] * 7,
         out_specs=VMEM,
-        scratch_shapes=[pltpu.VMEM((channels, tokens), jnp.float32)],
-        compiler_params=pltpu.CompilerParams(vmem_limit_bytes=40 << 20),
-        name="back",
-    )(device_index(), turned, *parts)
+        scratch_shapes=[
+            pltpu.VMEM((batch, tokens // batch + 2 * DILATION_STEP, inner), grad.dtype),
+            pltpu.VMEM((channels, tokens), jnp.float32),
+        ],
+        compiler_params=pltpu.CompilerParams(vmem_limit_bytes=24 << 20),
+        name="grad_active",
+    )(device_index(), grad, low, high, *parts)
 
 
 def rows_dot(left, right):
@@ -313,6 +352,8 @@
     pair = taps[:2]
     rest = jnp.concatenate([taps[2:], project_weight[None, None]])
     pair_in, rest_in = send(pair, Z_FAR), send(rest, FIRST)
+    low, high = edges(features, "seq", 1, DILATION_STEP)
+    pair_in = after(pair_in, low, high)
     pair, last, proj = assemble(
         (pair, pair_in, rest, rest_in),
         (
@@ -321,107 +362,112 @@
             (1, 2, ((2, 1, 1, 0, 0), (3, 1, 1, 0, 1))),
         ),
     )
-    pair_in, last_in, proj_in = send(pair, Z_NEAR), send(last, Z_FAR), send(proj, SECOND)
-    features_padded = padded(after(features, pair), (("seq", 1),), DILATION_STEP)
+    pair_in, last_in, proj_b = send(pair, Z_NEAR), send(last, Z_FAR), send(proj, SECOND)
     grow = lambda m, n, a: (m, 2 * n, ((a, 0, m, 0, 0), (a + 1, 0, m, 0, n)))
-    pair, last, proj = assemble(
+    pair_in = after(pair_in, proj_b)
+    pair, last = assemble((pair, pair_in, last, last_in), (grow(2, 2, 0), grow(1, 2, 2)))
+    pair_in, last_in, proj_in = send(pair, FIRST), send(last, Z_NEAR), send(proj, Z_FAR)
+    near, proj_a = assemble(
         (pair, pair_in, last, last_in, proj, proj_in),
-        (grow(2, 2, 0), grow(1, 2, 2), grow(1, 2, 4)),
-    )
-    pair_in, last_in, proj_in = send(pair, FIRST), send(last, Z_NEAR), send(proj, Z_FAR)
-    (near,) = assemble(
-        after((pair, pair_in, last, last_in), features_padded),
         (
-            (
-                3,
-                8,
-                ((0, 0, 2, 0, 0), (1, 0, 2, 0, 4), (2, 0, 1, 2, 0), (3, 0, 1, 2, 4)),
-            ),
+            (3, 8, ((0, 0, 2, 0, 0), (1, 0, 2, 0, 4), (2, 0, 1, 2, 0), (3, 0, 1, 2, 4))),
+            grow(1, 2, 4),
         ),
     )
     far, near_other = send(near, SECOND), send(near, CORE)
+    proj_in, proj_b_in = send(proj_a, Z_NEAR), send(proj_b, Z_FAR)
     flat_cotangent = cotangent.reshape(tokens, channels)
-    act, act_p = prepare(after(features_padded, near), flat_cotangent, outer_gain, rows)
-    (proj,) = assemble((proj, after(proj_in, act)), (grow(1, 4, 0),))
-    proj_far, proj_other = send(proj, Z_NEAR), send(proj, CORE)
-    conv_output = contract(act[0, 0], after(near, proj)) + contract(act[1, 0], near_other)
-    far = after(far, conv_output)
+    features_padded = jnp.concatenate([low, after(features, near), high], axis=1)
+    act, act_p = prepare(features_padded, flat_cotangent, outer_gain, rows)
+    proj_a, proj_b = assemble(
+        (proj_a, after(proj_in, act), proj_b, proj_b_in), (grow(1, 4, 0), grow(1, 2, 2))
+    )
+    proj_b_in, proj_a_other = send(proj_b, Z_NEAR), send(proj_a, CORE)
+    conv_output = contract(act[0, 0], after(near, proj_b)) + contract(act[1, 0], near_other)
+    grad_hidden = contract(act_p[0, 0], after(proj_a, conv_output)) + contract(
+        act_p[1, 0], proj_a_other
+    )
+    (proj_b,) = assemble((proj_b, after(proj_b_in, grad_hidden)), (grow(1, 4, 0),))
+    proj_b_other = send(proj_b, CORE)
+    far = after(far, proj_b)
     far_other = send(far, CORE)
     conv_output = conv_output + contract(act[0, 1], far) + contract(act[1, 1], far_other)
-    grad_hidden = contract(act_p[0, 0], after(proj, conv_output)) + contract(
-        act_p[1, 0], proj_other
+    grad_hidden = (
+        grad_hidden + contract(act_p[0, 1], proj_b) + contract(act_p[1, 1], proj_b_other)
     )
     hidden32, pull_inner = jax.vjp(act_norm, conv_output, inner_gain)
     hidden = as_bf16(hidden32)
     give_p = as_bf16(rows_dot(act_p[1].reshape(2, HALF, rows, tokens), hidden))
     recv_p = send(give_p, CORE)
-    proj_far = after(proj_far, give_p)
-    proj_far_other = send(proj_far, CORE)
-    grad_hidden = (
-        grad_hidden + contract(act_p[0, 1], proj_far) + contract(act_p[1, 1], proj_far_other)
-    )
-    grad_conv, grad_gain_inner = pull_inner(grad_hidden)
+    grad_conv, grad_gain_inner = pull_inner(after(grad_hidden, give_p))
     grad_conv = as_bf16(grad_conv)
-    grad_padded = padded(
-        grad_conv.reshape(batch, bin_count, inner), (("seq", 1),), DILATION_STEP
-    )
 
     give = as_bf16(rows_dot(act[1, 1], grad_conv))
     recv_far = send(give, CORE)
     give = as_bf16(rows_dot(act[1, 0], after(grad_conv, give)))
     recv_near = send(give, CORE)
-    message_p = as_bf16(rows_dot(act_p[0, 1], after(hidden, give)) + as_f32(recv_p[1:]))
-    far_p = send(message_p, Z_NEAR)
-    message = as_bf16(
-        rows_dot(act[0, 1], after(grad_conv, message_p)) + as_f32(recv_far)
-    )
+    low, high = edges(
+        after(grad_conv, give).reshape(batch, bin_count, inner), "seq", 1, DILATION_STEP
+    )
+    message = as_bf16(rows_dot(act[0, 1], after(grad_conv, give)) + as_f32(recv_far))
     recv = send(message, SECOND)
-    kept = rows_dot(act[0, 0], after(grad_conv, message)) + as_f32(recv_near)
-    kept_p = rows_dot(act_p[0, 0], after(hidden, message)) + as_f32(recv_p[:1])
-
-    grad_padded = after(grad_padded, kept, kept_p)
-    turned = jnp.stack(
-        [
-            grad_padded[:, shift : shift + bin_count].reshape(tokens, inner).T
-            for shift in (2 * DILATION_STEP, DILATION_STEP, 0)
-        ]
-    )
-    grad_active = back(turned, (near, far, near_other, far_other), TAP_ORDERS)
-    far_p = after(far_p, grad_active)
-    message_p = upper(kept_p, far_p)
-    kept_p, recv_p = lower(kept_p, far_p), send(message_p, Z_FAR)
-    unused, pull_outer = jax.vjp(act_norm, as_f32(after(features, message_p)), outer_gain)
+    grad_p = after(hidden, message)
+    split = lambda which: act_p[0, which].reshape(2, HALF // 2, rows, tokens)
+    parts_of = lambda array, which: array[which].reshape(2, HALF // 2, rows, inner)
+    message_b = as_bf16(
+        rows_dot(split(1)[1:], grad_p) + as_f32(parts_of(recv_p, 1)[1:])
+    )
+    recv_b = send(message_b, Z_NEAR)
+    message_a = as_bf16(
+        rows_dot(split(0)[1:], grad_p) + as_f32(parts_of(recv_p, 0)[1:])
+    )
+    grad_p = after(hidden, message_a, message_b)
+    kept_b = rows_dot(split(1)[:1], grad_p) + as_f32(parts_of(recv_p, 1)[:1])
+    kept_a = rows_dot(split(0)[:1], grad_p) + as_f32(parts_of(recv_p, 0)[:1])
+    kept = rows_dot(act[0, 0], after(grad_conv, kept_a, kept_b)) + as_f32(recv_near)
+
+    flat = features.reshape(tokens, channels)
+    grad_active = grad_of_active(
+        after(grad_conv, kept), low, high, (near, far, near_other, far_other)
+    )
+    recv_b = after(recv_b, grad_active)
+    message_b = upper(kept_b, recv_b)
+    kept_b, recv_b = lower(kept_b, recv_b), send(message_b, Z_FAR)
+    recv_a = send(after(message_a, message_b), Z_NEAR)
+    unused, pull_outer = jax.vjp(act_norm, as_f32(after(features, message_b)), outer_gain)
     grad_branch, grad_gain_outer = pull_outer(grad_active.reshape(features.shape))
     grad_features = as_bf16(as_f32(cotangent) + grad_branch)
     gains = jnp.concatenate([grad_gain_outer, grad_gain_inner]) * factor
     gains = gains + send(gains, CORE)
+    block_out = project_back(
+        after(hidden, gains), flat, (proj_a, proj_b, proj_a_other, proj_b_other)
+    ).reshape(features.shape)
+    gains = after(gains, block_out)
     gains = gains + send(gains, links(lambda i: i ^ 2))
-    projected = back(
-        after(hidden, gains).T[None],
-        (proj, proj_far, proj_other, proj_far_other),
-        [PROJECT_ORDER],
-    )
-    block_out = as_bf16(as_f32(features) + projected.reshape(features.shape))
-
-    recv = after(recv, gains, block_out)
+    recv_a, recv_b = after((recv_a, recv_b), gains)
+    message_a, kept_a = upper(kept_a, recv_a), lower(kept_a, recv_a)
+    kept_b = kept_b + as_f32(recv_b)
+
+    recv = after(recv, message_a, kept_b)
     pair, last = slice(0, 2), slice(2, 3)
     message, message_l = upper(kept, recv, pair), upper(kept, recv, last)
     kept, kept_l = lower(kept, recv, pair), lower(kept, recv, last)
-    recv, recv_l = send(message, FIRST), send(message_l, Z_NEAR)
+    recv, recv_l, recv_a = send(message, FIRST), send(message_l, Z_NEAR), send(message_a, Z_FAR)
     gains = after(gains, message, message_l)
     gains = gains + send(gains, links(lambda i: i ^ 4))
 
-    recv, recv_l, recv_p, _ = lax.optimization_barrier((recv, recv_l, recv_p, gains))
-    message, message_l, message_p = upper(kept, recv), upper(kept_l, recv_l), upper(kept_p, recv_p)
-    kept, kept_l, kept_p = lower(kept, recv), lower(kept_l, recv_l), lower(kept_p, recv_p)
+    recv, recv_l, recv_a, _ = lax.optimization_barrier((recv, recv_l, recv_a, gains))
+    message, message_l, message_p = upper(kept, recv), upper(kept_l, recv_l), as_bf16(kept_b)
+    kept, kept_l, kept_p = lower(kept, recv), lower(kept_l, recv_l), kept_a + as_f32(recv_a)
     recv, recv_l, recv_p = send(message, Z_NEAR), send(message_l, Z_FAR), send(message_p, SECOND)
     gains = after(gains, message, message_l, message_p)
     gains = gains + send(gains, Z_NEAR)
 
     recv, recv_l, recv_p, _ = lax.optimization_barrier((recv, recv_l, recv_p, gains))
     message = upper(kept, recv)
-    message_r = jnp.concatenate([upper(kept_l, recv_l), upper(kept_p, recv_p)])
-    kept, kept_l, kept_p = lower(kept, recv), lower(kept_l, recv_l), lower(kept_p, recv_p)
+    kept_p = kept_p + as_f32(recv_p)
+    message_r = jnp.concatenate([upper(kept_l, recv_l), as_bf16(kept_p[:, 1:])])
+    kept, kept_l, kept_p = lower(kept, recv), lower(kept_l, recv_l), kept_p[:, :1]
     recv, recv_r = send(message, Z_FAR), send(message_r, FIRST)
     gains = after(gains, message, message_r)
     gains = gains + send(gains, Z_FAR)

time: 176 us -> 154 us (0.88)
  matrix products: 19.7 us -> 9.93 us
  local copies, waits for them, and re-layouts: 14.9 us -> 5.27 us
  starting transfers between devices: 55.1 us -> 53.1 us
    dot_general x7 -> x9, matrix products: 12.5 us -> 3.98 us  [rows_dot(): jnp.einsum('mnrt,ti->mnri', left, right, preferred_element_type=jnp.float32)]
    unnamed x53 -> x22, local copies, waits for them, and re-layouts: 6.58 us -> 0.9 us
    slice x3, local copies, waits for them, and re-layouts: 3.07 us -> 1.08 us  [the longest x1 1.06 us: edges(): lax.slice_in_dim(block, block.shape[dim] - width, None, axis=dim)]
    reshape x1 -> x0, local copies, waits for them, and re-layouts: 1.86 us -> none  [body_torus(): grad_conv.reshape(batch, bin_count, inner)]
    ppermute x32 -> x36, starting transfers between devices: 47.7 us -> 46.7 us  [send(): return lax.ppermute(block, 'seq', pairs)]
    ppermute x32 -> x36, waiting for transfers between devices: 57.6 us -> 58.1 us  [send(): return lax.ppermute(block, 'seq', pairs)]
  transfers between devices with their start and end apart: 36 -> 40, of which waited for: 18 -> 17; matrix products, arithmetic and copies ran while one was open for 21% -> 14% of each run, Pallas kernels for 6% -> 6%
where the time goes in v4:
time: 154 us; the launch traced here: 153 us
  waiting for transfers between devices  58.1 us (38%)
  starting transfers between devices  53.1 us (34%)
  other arithmetic  15.9 us (10%)
  matrix products  9.93 us (6%)
  Pallas kernels  9.86 us (6%)
  local copies, waits for them, and re-layouts  5.27 us (3%)
    ppermute x36, waiting for transfers between devices, send(): return lax.ppermute(block, 'seq', pairs)  58.1 us
    ppermute x36, starting transfers between devices, send(): return lax.ppermute(block, 'seq', pairs)  46.7 us
    dot_general x8, matrix products, contract(): jnp.einsum('ct,ci->ti', left.reshape(-1, left.shape[-1]), right.reshape(-...  5.96 us
    pallas_call x1, Pallas kernels, grad_of_active(): pl.pallas_call(grad_active_kernel, out_shape=jax.ShapeDtypeStruct((tokens...  4.06 us
    dot_general x9, matrix products, rows_dot(): jnp.einsum('mnrt,ti->mnri', left, right, preferred_element_type=jnp.float32)  3.98 us
    ppermute x2, starting transfers between devices, edges(): lax.ppermute(lax.slice_in_dim(block, block.shape[dim] - width, None, axis...  3.57 us
    pallas_call x1, Pallas kernels, prepare(): pl.pallas_call(prepare_kernel, out_shape=[shape(KERNEL_TAPS), shape(1)],...  3.28 us
  transfers between devices with their start and end apart: 40, of which 17 were waited for; matrix products, arithmetic and copies ran while one was open for 14% of the time, Pallas kernels for 6%

profile of v4, /device:TPU:0, one launch (start us, length us, event | category | flops | bytes accessed | tf_op | source)
XLA Modules:
  0.0 153.3 jit_solution(13285003516970535126)
XLA Ops:
  0.6 1.1 fusion.105
  1.7 1.3 collective-permute-start.2
  3.9 6.5 %collective-permute-start.1 = (bf16[2,1,48,768]{3,2,0,1:T(8,128)(2,1)S(1)}, bf16[2,1,48,768]{3,2,0,1:T(8,128)(2,1)S(1)}, u32[]{:S(2)}, u32[]{:S(2)}) collective-permute-start(bf16[2,1,48,768]{3,2,0,1:T(8,128)(2,1)S(1)} %get-tuple-element.120), channel_id=1, source_target_pairs={{0,16},{1,17},{2,18},{3,19},{4,20},{5,21},{6,22},{7,23},{8,24},{9,... | collective-permute-start | bytes 442376 | tf_op jit(solution)/shard_map/ppermute | solution.py:139
  10.4 1.3 collective-permute-start
  14.1 4.3 %collective-permute-done.1 = bf16[2,1,48,768]{3,2,0,1:T(8,128)(2,1)S(1)} collective-permute-done((bf16[2,1,48,768]{3,2,0,1:T(8,128)(2,1)S(1)}, bf16[2,1,48,768]{3,2,0,1:T(8,128)(2,1)S(1)}, u32[]{:S(2)}, u32[]{:S(2)}) %collective-permute-start.1) | collective-permute-done | bytes 147488 | tf_op jit(solution)/shard_map/ppermute | solution.py:139
  19.2 2.5 %collective-permute-start.4 = (bf16[2,2,48,768]{3,2,1,0:T(8,128)(2,1)S(1)}, bf16[2,2,48,768]{3,2,1,0:T(8,128)(2,1)S(1)}, u32[]{:S(2)}, u32[]{:S(2)}) collective-permute-start(bf16[2,2,48,768]{3,2,1,0:T(8,128)(2,1)S(1)} %get-tuple-element.50.refs_0_), channel_id=1, source_target_pairs={{0,8},{1,9},{2,10},{3,11},{4,12},{5,13},{6,14},{7,15},{8,0},{9,1},... | collective-permute-start | bytes 884744 | tf_op jit(solution)/shard_map/ppermute | solution.py:139
  21.7 1.3 collective-permute-start.5
  23.1 1.9 %collective-permute-start.6 = (bf16[1,2,48,768]{3,2,1,0:T(8,128)(2,1)S(1)}, bf16[1,2,48,768]{3,2,1,0:T(8,128)(2,1)S(1)}, u32[]{:S(2)}, u32[]{:S(2)}) collective-permute-start(bf16[1,2,48,768]{3,2,1,0:T(8,128)(2,1)S(1)} %get-tuple-element.53.refs_2_), channel_id=1, source_target_pairs={{0,16},{1,17},{2,18},{3,19},{4,20},{5,21},{6,22},{7,23},{8,24},{9,... | collective-permute-start | bytes 442376 | tf_op jit(solution)/shard_map/ppermute | solution.py:139
  25.0 1.9 %collective-permute-done.5.refs_2_ = bf16[1,2,48,768]{3,2,1,0:T(8,128)(2,1)S(1)} collective-permute-done((bf16[1,2,48,768]{3,2,1,0:T(8,128)(2,1)S(1)}, bf16[1,2,48,768]{3,2,1,0:T(8,128)(2,1)S(1)}, u32[]{:S(2)}, u32[]{:S(2)}) %collective-permute-start.5) | collective-permute-done | bytes 147488 | tf_op jit(solution)/shard_map/ppermute | solution.py:139
  26.9 5.3 %collective-permute-done.4.refs_1_ = bf16[2,2,48,768]{3,2,1,0:T(8,128)(2,1)S(1)} collective-permute-done((bf16[2,2,48,768]{3,2,1,0:T(8,128)(2,1)S(1)}, bf16[2,2,48,768]{3,2,1,0:T(8,128)(2,1)S(1)}, u32[]{:S(2)}, u32[]{:S(2)}) %collective-permute-start.4) | collective-permute-done | bytes 294944 | tf_op jit(solution)/shard_map/ppermute | solution.py:139
  32.2 1.1 collective-permute-start.7
  33.8 1.4 collective-permute-start.9
  35.2 7.0 %collective-permute-done.9.refs_5_ = bf16[1,2,48,768]{3,2,1,0:T(8,128)(2,1)S(1)} collective-permute-done((bf16[1,2,48,768]{3,2,1,0:T(8,128)(2,1)S(1)}, bf16[1,2,48,768]{3,2,1,0:T(8,128)(2,1)S(1)}, u32[]{:S(2)}, u32[]{:S(2)}) %collective-permute-start.9) | collective-permute-done | bytes 147488 | tf_op jit(solution)/shard_map/ppermute | solution.py:139
  42.2 1.9 %collective-permute-done.8.refs_3_ = bf16[1,4,48,768]{3,2,1,0:T(8,128)(2,1)S(1)} collective-permute-done((bf16[1,4,48,768]{3,2,1,0:T(8,128)(2,1)S(1)}, bf16[1,4,48,768]{3,2,1,0:T(8,128)(2,1)S(1)}, u32[]{:S(2)}, u32[]{:S(2)}) %collective-permute-start.8) | collective-permute-done | bytes 294944 | tf_op jit(solution)/shard_map/ppermute | solution.py:139
  44.9 1.5 %collective-permute-start.11 = (bf16[1,2,48,768]{3,2,1,0:T(8,128)(2,1)S(1)}, bf16[1,2,48,768]{3,2,1,0:T(8,128)(2,1)S(1)}, u32[]{:S(2)}, u32[]{:S(2)}) collective-permute-start(bf16[1,2,48,768]{3,2,1,0:T(8,128)(2,1)S(1)} %collective-permute-done.5.refs_2_), channel_id=1, source_target_pairs={{0,16},{1,17},{2,18},{3,19},{4,20},{5,21},{6,22},{7,23},{8,24},{9,... | collective-permute-start | bytes 442376 | tf_op jit(solution)/shard_map/ppermute | solution.py:139
  46.5 1.4 collective-permute-start.13
  47.9 1.4 collective-permute-start.10
  49.3 1.1 pad_maximum_fusion.features_ref
  50.4 3.3 %prepare.1 = (bf16[2,2,3,8,48,256]{5,4,3,2,1,0:T(8,128)(2,1)S(1)}, bf16[2,2,1,8,48,256]{5,4,3,2,1,0:T(8,128)(2,1)S(1)}) custom-call(s32[1]{0:T(128)} %bitcast.index_ref, bf16[2,192,1536]{2,1,0:T(8,128)(2,1)S(1)} %pad_maximum_fusion.features_ref, bf16[256,1536]{1,0:T(8,128)(2,1)S(1)} %bitcast.173, f32[1,1536]{1,0:T(1,128)S(1)} %reshape.179.gain_ref), custom_call_target="tpu_custom_call" | custom-call | tf_op jit(solution)/shard_map/prepare/pallas_call | solution.py:240
  54.0 5.1 %collective-permute-done.10.refs_1_ = bf16[1,4,48,768]{3,2,1,0:T(8,128)(2,1)S(1)} collective-permute-done((bf16[1,4,48,768]{3,2,1,0:T(8,128)(2,1)}, bf16[1,4,48,768]{3,2,1,0:T(8,128)(2,1)S(1)}, u32[]{:S(2)}, u32[]{:S(2)}) %collective-permute-start.10) | collective-permute-done | bytes 294944 | tf_op jit(solution)/shard_map/ppermute | solution.py:139
  60.3 2.2 %convolution_add_fusion.5 = f32[256,768]{1,0:T(8,128)S(1)} fusion(f32[256,768]{1,0:T(8,128)S(1)} %fusion.107, bf16[1152,256]{1,0:T(8,128)(2,1)S(1)} %bitcast.180, bf16[1152,768]{1,0:T(8,128)(2,1)} %bitcast.11), kind=kOutput, calls=%fused_computation.33 | convolution fusion | flops 453181440 | bytes 3932160 | tf_op jit(solution)/shard_map/ct,ci->ti/dot_general | solution.py:334
  63.3 5.1 %collective-permute-done.14.refs_1_ = bf16[1,4,48,768]{3,2,1,0:T(8,128)(2,1)S(1)} collective-permute-done((bf16[1,4,48,768]{3,2,1,0:T(8,128)(2,1)S(1)}, bf16[1,4,48,768]{3,2,1,0:T(8,128)(2,1)S(1)}, u32[]{:S(2)}, u32[]{:S(2)}) %collective-permute-start.14) | collective-permute-done | bytes 294944 | tf_op jit(solution)/shard_map/ppermute | solution.py:139
  70.6 2.9 %collective-permute-done.17.refs_3_ = bf16[1,8,48,768]{3,2,1,0:T(8,128)(2,1)S(1)} collective-permute-done((bf16[1,8,48,768]{3,2,1,0:T(8,128)(2,1)S(1)}, bf16[1,8,48,768]{3,2,1,0:T(8,128)(2,1)S(1)}, u32[]{:S(2)}, u32[]{:S(2)}) %collective-permute-start.17) | collective-permute-done | bytes 589856 | tf_op jit(solution)/shard_map/ppermute | solution.py:139
  78.8 2.3 %collective-permute-start.22 = (bf16[2,32,768]{2,1,0:T(8,128)(2,1)S(1)}, bf16[2,32,768]{2,1,0:T(8,128)(2,1)S(1)}, u32[]{:S(2)}, u32[]{:S(2)}) collective-permute-start(bf16[2,32,768]{2,1,0:T(8,128)(2,1)S(1)} %get-tuple-element.117), channel_id=1, source_target_pairs={{0,1},{1,2},{2,3},{3,4},{4,5},{5,6},{6,7},{7,8},{8,9},{9,10},{10,1... | collective-permute-start | bytes 294920 | tf_op jit(solution)/shard_map/ppermute | solution.py:22
  81.1 1.5 collective-permute-start.23
  83.2 4.3 %collective-permute-start.25 = (bf16[3,8,48,768]{3,2,1,0:T(8,128)(2,1)S(1)}, bf16[3,8,48,768]{3,2,1,0:T(8,128)(2,1)S(1)}, u32[]{:S(2)}, u32[]{:S(2)}) collective-permute-start(bf16[3,8,48,768]{3,2,1,0:T(8,128)(2,1)S(1)} %add_convert_fusion), channel_id=1, source_target_pairs={{0,4},{1,3},{2,6},{3,1},{4,0},{5,7},{6,2},{7,5},{8,12},{9,11},{10,... | collective-permute-start | bytes 5308424 | tf_op jit(solution)/shard_map/ppermute | solution.py:139
  87.8 1.5 collective-permute-start.20
  90.7 4.1 %grad_active.1 = f32[256,1536]{1,0:T(8,128)S(1)} custom-call(s32[1]{0:T(128)} %bitcast.index_ref, bf16[256,768]{1,0:T(8,128)(2,1)S(1)} %fusion.23.grad_ref, bf16[2,32,768]{2,1,0:T(8,128)(2,1)S(1)} %collective-permute-done.22.low_ref, bf16[2,32,768]{2,1,0:T(8,128)(2,1)S(1)} %collective-permute-done.23.high_ref, ...), custom_call_target="tpu_custom_call" | custom-call | tf_op jit(solution)/shard_map/grad_active/pallas_call | solution.py:315
  94.8 1.4 collective-permute-done.20
  97.2 1.7 %fusion.15 = (f32[2,128]{1,0:T(2,128)S(1)}, f32[1536]{0:T(1024)S(1)}, f32[2,128,1536]{2,1,0:T(8,128)S(1)}) fusion(bf16[2,128,1536]{2,1,0:T(8,128)(2,1)S(1)} %copy-done, f32[1536]{0:T(1024)S(1)} %copy-done.9, f32[2,128]{1,0:T(2,128)S(1)} %fusion.95, f32[2,128,1536]{2,1,0:T(8,128)S(1)} %bitcast.171), kind=kLoop, calls=%fused_computation.26 | loop fusion | flops 10615040 | bytes 3946496 | tf_op jit(solution)/shard_map/transpose(jvp())/reduce_sum | solution.py:38
  99.0 2.7 %collective-permute-start.27 = (bf16[1,2,48,768]{3,2,1,0:T(8,128)(2,1)S(1)}, bf16[1,2,48,768]{3,2,1,0:T(8,128)(2,1)S(1)}, u32[]{:S(2)}, u32[]{:S(2)}) collective-permute-start(bf16[1,2,48,768]{3,2,1,0:T(8,128)(2,1)S(1)} %fusion.64), channel_id=1, source_target_pairs={{0,16},{1,17},{2,18},{3,19},{4,20},{5,21},{6,22},{7,23},{8,24},{9,... | collective-permute-start | bytes 442376 | tf_op jit(solution)/shard_map/ppermute | solution.py:139
  101.7 2.2 %project_back.1 = bf16[256,1536]{1,0:T(8,128)(2,1)} custom-call(s32[1]{0:T(128)} %bitcast.index_ref, bf16[256,768]{1,0:T(8,128)(2,1)S(1)} %multiply_convert_fusion.hidden_ref, bf16[256,1536]{1,0:T(8,128)(2,1)S(1)} %bitcast.166, bf16[1,8,48,768]{3,2,1,0:T(8,128)(2,1)S(1)} %get-tuple-element.65.refs_0_, bf16[1,8,48,768]{3,2,1,0:T(8,128)(2,1)S(1)} %assemble.9.refs_1_, ...), custom_call_target="tpu_custom_call" | custom-call | tf_op jit(solution)/shard_map/project_back/pallas_call | solution.py:282
  104.4 3.4 %collective-permute-done.28 = f32[2304]{0:T(1024)S(1)} collective-permute-done((f32[2304]{0:T(1024)S(1)}, f32[2304]{0:T(1024)S(1)}, u32[]{:S(2)}, u32[]{:S(2)}) %collective-permute-start.28) | collective-permute-done | bytes 9248 | tf_op jit(solution)/shard_map/ppermute | solution.py:139
  109.3 1.5 slice_add_fusion.1
  110.7 2.2 %collective-permute-start.29 = (bf16[2,4,48,768]{3,2,1,0:T(8,128)(2,1)}, bf16[2,4,48,768]{3,2,1,0:T(8,128)(2,1)}, u32[]{:S(2)}, u32[]{:S(2)}) collective-permute-start(bf16[2,4,48,768]{3,2,1,0:T(8,128)(2,1)} %get-tuple-element.99), channel_id=1, source_target_pairs={{0,2},{1,5},{2,0},{3,7},{4,6},{5,1},{6,4},{7,3},{8,10},{9,13},{10,... | collective-permute-start | bytes 1769480 | tf_op jit(solution)/shard_map/ppermute | solution.py:139
  114.0 3.2 %collective-permute-start.31 = (bf16[1,2,48,768]{3,2,1,0:T(8,128)(2,1)}, bf16[1,2,48,768]{3,2,1,0:T(8,128)(2,1)}, u32[]{:S(2)}, u32[]{:S(2)}) collective-permute-start(bf16[1,2,48,768]{3,2,1,0:T(8,128)(2,1)} %fusion.63), channel_id=1, source_target_pairs={{0,16},{1,17},{2,18},{3,19},{4,20},{5,21},{6,22},{7,23},{8,24},{9,... | collective-permute-start | bytes 442376 | tf_op jit(solution)/shard_map/ppermute | solution.py:139
  118.1 1.2 collective-permute-start.35
  119.2 1.7 %collective-permute-done.32 = f32[2304]{0:T(1024)S(1)} collective-permute-done((f32[2304]{0:T(1024)S(1)}, f32[2304]{0:T(1024)S(1)}, u32[]{:S(2)}, u32[]{:S(2)}) %collective-permute-start.32) | collective-permute-done | bytes 9248 | tf_op jit(solution)/shard_map/ppermute | solution.py:139
  120.9 3.0 %collective-permute-done.31 = bf16[1,2,48,768]{3,2,1,0:T(8,128)(2,1)} collective-permute-done((bf16[1,2,48,768]{3,2,1,0:T(8,128)(2,1)}, bf16[1,2,48,768]{3,2,1,0:T(8,128)(2,1)}, u32[]{:S(2)}, u32[]{:S(2)}) %collective-permute-start.31) | collective-permute-done | bytes 147488 | tf_op jit(solution)/shard_map/ppermute | solution.py:139
  123.9 1.8 %collective-permute-done.30 = bf16[1,4,48,768]{3,2,1,0:T(8,128)(2,1)} collective-permute-done((bf16[1,4,48,768]{3,2,1,0:T(8,128)(2,1)}, bf16[1,4,48,768]{3,2,1,0:T(8,128)(2,1)}, u32[]{:S(2)}, u32[]{:S(2)}) %collective-permute-start.30) | collective-permute-done | bytes 294944 | tf_op jit(solution)/shard_map/ppermute | solution.py:139
  125.7 1.6 %slice_add_fusion.5 = (f32[2,2,48,768]{3,2,1,0:T(8,128)S(1)}, bf16[2,2,48,768]{3,2,1,0:T(8,128)(2,1)S(1)}) fusion(f32[2,4,48,768]{3,2,1,0:T(8,128)} %get-tuple-element.98, bf16[2,4,48,768]{3,2,1,0:T(8,128)(2,1)} %collective-permute-done.29), kind=kLoop, calls=%fused_computation.58 | loop fusion | flops 737280 | bytes 2654208 | tf_op jit(solution)/shard_map/add | solution.py:190
  127.3 2.4 %collective-permute-start.33 = (bf16[2,2,48,768]{3,2,1,0:T(8,128)(2,1)S(1)}, bf16[2,2,48,768]{3,2,1,0:T(8,128)(2,1)S(1)}, u32[]{:S(2)}, u32[]{:S(2)}) collective-permute-start(bf16[2,2,48,768]{3,2,1,0:T(8,128)(2,1)S(1)} %get-tuple-element.107), channel_id=1, source_target_pairs={{0,8},{1,9},{2,10},{3,11},{4,12},{5,13},{6,14},{7,15},{8,0},{9,1},... | collective-permute-start | bytes 884744 | tf_op jit(solution)/shard_map/ppermute | solution.py:139
  129.7 1.0 fusion.60
  130.7 1.8 %collective-permute-start.34 = (bf16[1,2,48,768]{3,2,1,0:T(8,128)(2,1)S(1)}, bf16[1,2,48,768]{3,2,1,0:T(8,128)(2,1)S(1)}, u32[]{:S(2)}, u32[]{:S(2)}) collective-permute-start(bf16[1,2,48,768]{3,2,1,0:T(8,128)(2,1)S(1)} %get-tuple-element.108), channel_id=1, source_target_pairs={{0,16},{1,17},{2,18},{3,19},{4,20},{5,21},{6,22},{7,23},{8,24},{9,... | collective-permute-start | bytes 442376 | tf_op jit(solution)/shard_map/ppermute | solution.py:139
  132.6 7.4 %collective-permute-done.36 = f32[2304]{0:T(1024)S(1)} collective-permute-done((f32[2304]{0:T(1024)S(1)}, f32[2304]{0:T(1024)S(1)}, u32[]{:S(2)}, u32[]{:S(2)}) %collective-permute-start.36) | collective-permute-done | bytes 9248 | tf_op jit(solution)/shard_map/ppermute | solution.py:139
  141.0 2.5 %collective-permute-start.37 = (bf16[2,1,48,768]{3,2,1,0:T(8,128)(2,1)S(1)}, bf16[2,1,48,768]{3,2,1,0:T(8,128)(2,1)S(1)}, u32[]{:S(2)}, u32[]{:S(2)}) collective-permute-start(bf16[2,1,48,768]{3,2,1,0:T(8,128)(2,1)S(1)} %fusion.59), channel_id=1, source_target_pairs={{0,16},{1,17},{2,18},{3,19},{4,20},{5,21},{6,22},{7,23},{8,24},{9,... | collective-permute-start | bytes 442376 | tf_op jit(solution)/shard_map/ppermute | solution.py:139
  144.1 1.4 fusion.13
  145.8 4.8 %collective-permute-done.39 = f32[2304]{0:T(1024)S(1)} collective-permute-done((f32[2304]{0:T(1024)S(1)}, f32[2304]{0:T(1024)S(1)}, u32[]{:S(2)}, u32[]{:S(2)}) %collective-permute-start.39) | collective-permute-done | bytes 9248 | tf_op jit(solution)/shard_map/ppermute | solution.py:139
  (122 shorter events, 27.1 us)
Async XLA Ops:
  1.7 16.7 %collective-permute-start.2 = (bf16[2,32,1536]{2,1,0:T(8,128)(2,1)S(1)}, bf16[2,32,1536]{2,1,0:T(8,128)(2,1)S(1)}, u32[]{:S(2)}, u32[]{:S(2)}) collective-permute-start(bf16[2,32,1536]{2,1,0:T(8,128)(2,1)S(1)} %get-tuple-element.115), channel_id=1, source_target_pairs={{1,0},{2,1},{3,2},{4,3},{5,4},{6,5},{7,6},{8,7},{9,8},{10,9},{11,1... | collective-permute-start | bytes 589832 | tf_op jit(solution)/shard_map/ppermute | solution.py:25
  3.9 14.5 %collective-permute-start.1 = (bf16[2,1,48,768]{3,2,0,1:T(8,128)(2,1)S(1)}, bf16[2,1,48,768]{3,2,0,1:T(8,128)(2,1)S(1)}, u32[]{:S(2)}, u32[]{:S(2)}) collective-permute-start(bf16[2,1,48,768]{3,2,0,1:T(8,128)(2,1)S(1)} %get-tuple-element.120), channel_id=1, source_target_pairs={{0,16},{1,17},{2,18},{3,19},{4,20},{5,21},{6,22},{7,23},{8,24},{9,... | collective-permute-start | bytes 442376 | tf_op jit(solution)/shard_map/ppermute | solution.py:139
  10.4 8.0 %collective-permute-start = (bf16[2,32,1536]{2,1,0:T(8,128)(2,1)S(1)}, bf16[2,32,1536]{2,1,0:T(8,128)(2,1)S(1)}, u32[]{:S(2)}, u32[]{:S(2)}) collective-permute-start(bf16[2,32,1536]{2,1,0:T(8,128)(2,1)S(1)} %get-tuple-element.114), channel_id=1, source_target_pairs={{0,1},{1,2},{2,3},{3,4},{4,5},{5,6},{6,7},{7,8},{8,9},{9,10},{10,1... | collective-permute-start | bytes 589832 | tf_op jit(solution)/shard_map/ppermute | solution.py:22
  13.5 5.5 %collective-permute-start.3 = (bf16[2,1,48,768]{3,2,1,0:T(8,128)(2,1)S(1)}, bf16[2,1,48,768]{3,2,1,0:T(8,128)(2,1)S(1)}, u32[]{:S(2)}, u32[]{:S(2)}) collective-permute-start(bf16[2,1,48,768]{3,2,1,0:T(8,128)(2,1)S(1)} %pad_maximum_fusion.1.refs_2_), channel_id=1, source_target_pairs={{0,2},{1,5},{2,0},{3,7},{4,6},{5,1},{6,4},{7,3},{8,10},{9,13},{10,... | collective-permute-start | bytes 442376 | tf_op jit(solution)/shard_map/ppermute | solution.py:139
  19.2 25.7 %copy-start.9 = (f32[1536]{0:T(1024)S(1)}, f32[1536]{0:T(1024)}, u32[]{:S(2)}) copy-start(f32[1536]{0:T(1024)} %param.10) | copy-start | bytes 18436
  19.2 30.0 %copy-start = (bf16[2,128,1536]{2,1,0:T(8,128)(2,1)S(1)}, bf16[2,128,1536]{2,1,0:T(8,128)(2,1)}, u32[]{:S(2)}) copy-start(bf16[2,128,1536]{2,1,0:T(8,128)(2,1)} %param.6) | copy-start | bytes 2359300
  19.2 12.9 %collective-permute-start.4 = (bf16[2,2,48,768]{3,2,1,0:T(8,128)(2,1)S(1)}, bf16[2,2,48,768]{3,2,1,0:T(8,128)(2,1)S(1)}, u32[]{:S(2)}, u32[]{:S(2)}) collective-permute-start(bf16[2,2,48,768]{3,2,1,0:T(8,128)(2,1)S(1)} %get-tuple-element.50.refs_0_), channel_id=1, source_target_pairs={{0,8},{1,9},{2,10},{3,11},{4,12},{5,13},{6,14},{7,15},{8,0},{9,1},... | collective-permute-start | bytes 884744 | tf_op jit(solution)/shard_map/ppermute | solution.py:139
  21.7 5.1 %collective-permute-start.5 = (bf16[1,2,48,768]{3,2,1,0:T(8,128)(2,1)S(1)}, bf16[1,2,48,768]{3,2,1,0:T(8,128)(2,1)S(1)}, u32[]{:S(2)}, u32[]{:S(2)}) collective-permute-start(bf16[1,2,48,768]{3,2,1,0:T(8,128)(2,1)S(1)} %get-tuple-element.51.refs_4_), channel_id=1, source_target_pairs={{0,4},{1,3},{2,6},{3,1},{4,0},{5,7},{6,2},{7,5},{8,12},{9,11},{10,... | collective-permute-start | bytes 442376 | tf_op jit(solution)/shard_map/ppermute | solution.py:139
  23.1 9.1 %collective-permute-start.6 = (bf16[1,2,48,768]{3,2,1,0:T(8,128)(2,1)S(1)}, bf16[1,2,48,768]{3,2,1,0:T(8,128)(2,1)S(1)}, u32[]{:S(2)}, u32[]{:S(2)}) collective-permute-start(bf16[1,2,48,768]{3,2,1,0:T(8,128)(2,1)S(1)} %get-tuple-element.53.refs_2_), channel_id=1, source_target_pairs={{0,16},{1,17},{2,18},{3,19},{4,20},{5,21},{6,22},{7,23},{8,24},{9,... | collective-permute-start | bytes 442376 | tf_op jit(solution)/shard_map/ppermute | solution.py:139
  32.2 11.8 %collective-permute-start.7 = (bf16[2,4,48,768]{3,2,1,0:T(8,128)(2,1)S(1)}, bf16[2,4,48,768]{3,2,1,0:T(8,128)(2,1)S(1)}, u32[]{:S(2)}, u32[]{:S(2)}) collective-permute-start(bf16[2,4,48,768]{3,2,1,0:T(8,128)(2,1)S(1)} %get-tuple-element.54.refs_0_), channel_id=1, source_target_pairs={{0,2},{1,5},{2,0},{3,7},{4,6},{5,1},{6,4},{7,3},{8,10},{9,13},{10,... | collective-permute-start | bytes 1769480 | tf_op jit(solution)/shard_map/ppermute | solution.py:139
  33.3 10.8 %collective-permute-start.8 = (bf16[1,4,48,768]{3,2,1,0:T(8,128)(2,1)S(1)}, bf16[1,4,48,768]{3,2,1,0:T(8,128)(2,1)S(1)}, u32[]{:S(2)}, u32[]{:S(2)}) collective-permute-start(bf16[1,4,48,768]{3,2,1,0:T(8,128)(2,1)S(1)} %get-tuple-element.55.refs_2_), channel_id=1, source_target_pairs={{0,8},{1,9},{2,10},{3,11},{4,12},{5,13},{6,14},{7,15},{8,0},{9,1},... | collective-permute-start | bytes 884744 | tf_op jit(solution)/shard_map/ppermute | solution.py:139
  33.8 8.3 %collective-permute-start.9 = (bf16[1,2,48,768]{3,2,1,0:T(8,128)(2,1)S(1)}, bf16[1,2,48,768]{3,2,1,0:T(8,128)(2,1)S(1)}, u32[]{:S(2)}, u32[]{:S(2)}) collective-permute-start(bf16[1,2,48,768]{3,2,1,0:T(8,128)(2,1)S(1)} %get-tuple-element.51.refs_4_), channel_id=1, source_target_pairs={{0,16},{1,17},{2,18},{3,19},{4,20},{5,21},{6,22},{7,23},{8,24},{9,... | collective-permute-start | bytes 442376 | tf_op jit(solution)/shard_map/ppermute | solution.py:139
  44.9 5.5 %copy-start.1 = (bf16[2,128,1536]{2,1,0:T(8,128)(2,1)S(1)}, bf16[2,128,1536]{2,1,0:T(8,128)(2,1)}, u32[]{:S(2)}) copy-start(bf16[2,128,1536]{2,1,0:T(8,128)(2,1)} %param.7) | copy-start | bytes 2359300
  44.9 15.4 %collective-permute-start.12 = (bf16[3,8,48,768]{3,2,1,0:T(8,128)(2,1)S(1)}, bf16[3,8,48,768]{3,2,1,0:T(8,128)(2,1)}, u32[]{:S(2)}, u32[]{:S(2)}) collective-permute-start(bf16[3,8,48,768]{3,2,1,0:T(8,128)(2,1)S(1)} %get-tuple-element.62.refs_0_), channel_id=1, source_target_pairs={{0,1},{1,0},{2,3},{3,2},{4,5},{5,4},{6,7},{7,6},{8,9},{9,8},{10,11... | collective-permute-start | bytes 5308424 | tf_op jit(solution)/shard_map/ppermute | solution.py:139
  44.9 14.1 %collective-permute-start.11 = (bf16[1,2,48,768]{3,2,1,0:T(8,128)(2,1)S(1)}, bf16[1,2,48,768]{3,2,1,0:T(8,128)(2,1)S(1)}, u32[]{:S(2)}, u32[]{:S(2)}) collective-permute-start(bf16[1,2,48,768]{3,2,1,0:T(8,128)(2,1)S(1)} %collective-permute-done.5.refs_2_), channel_id=1, source_target_pairs={{0,16},{1,17},{2,18},{3,19},{4,20},{5,21},{6,22},{7,23},{8,24},{9,... | collective-permute-start | bytes 442376 | tf_op jit(solution)/shard_map/ppermute | solution.py:139
  46.5 22.5 %collective-permute-start.13 = (bf16[3,8,48,768]{3,2,1,0:T(8,128)(2,1)S(1)}, bf16[3,8,48,768]{3,2,1,0:T(8,128)(2,1)S(1)}, u32[]{:S(2)}, u32[]{:S(2)}) collective-permute-start(bf16[3,8,48,768]{3,2,1,0:T(8,128)(2,1)S(1)} %get-tuple-element.62.refs_0_), channel_id=1, source_target_pairs={{0,4},{1,3},{2,6},{3,1},{4,0},{5,7},{6,2},{7,5},{8,12},{9,11},{10,... | collective-permute-start | bytes 5308424 | tf_op jit(solution)/shard_map/ppermute | solution.py:139
  47.9 11.2 %collective-permute-start.10 = (bf16[1,4,48,768]{3,2,1,0:T(8,128)(2,1)}, bf16[1,4,48,768]{3,2,1,0:T(8,128)(2,1)S(1)}, u32[]{:S(2)}, u32[]{:S(2)}) collective-permute-start(bf16[1,4,48,768]{3,2,1,0:T(8,128)(2,1)} %copy-done.2), channel_id=1, source_target_pairs={{0,8},{1,9},{2,10},{3,11},{4,12},{5,13},{6,14},{7,15},{8,0},{9,1},... | collective-permute-start | bytes 884744 | tf_op jit(solution)/shard_map/ppermute | solution.py:139
  53.9 5.2 %copy-start.3 = (bf16[1,4,48,768]{3,2,1,0:T(8,128)(2,1)S(1)}, bf16[1,4,48,768]{3,2,1,0:T(8,128)(2,1)}, u32[]{:S(2)}) copy-start(bf16[1,4,48,768]{3,2,1,0:T(8,128)(2,1)} %copy-done.2) | copy-start | bytes 884740
  59.1 9.3 %collective-permute-start.14 = (bf16[1,4,48,768]{3,2,1,0:T(8,128)(2,1)S(1)}, bf16[1,4,48,768]{3,2,1,0:T(8,128)(2,1)S(1)}, u32[]{:S(2)}, u32[]{:S(2)}) collective-permute-start(bf16[1,4,48,768]{3,2,1,0:T(8,128)(2,1)S(1)} %get-tuple-element.61.refs_0_), channel_id=1, source_target_pairs={{0,8},{1,9},{2,10},{3,11},{4,12},{5,13},{6,14},{7,15},{8,0},{9,1},... | collective-permute-start | bytes 884744 | tf_op jit(solution)/shard_map/ppermute | solution.py:139
  59.2 3.6 %collective-permute-start.15 = (bf16[1,8,48,768]{3,2,1,0:T(8,128)(2,1)S(1)}, bf16[1,8,48,768]{3,2,1,0:T(8,128)(2,1)S(1)}, u32[]{:S(2)}, u32[]{:S(2)}) collective-permute-start(bf16[1,8,48,768]{3,2,1,0:T(8,128)(2,1)S(1)} %get-tuple-element.65.refs_0_), channel_id=1, source_target_pairs={{0,1},{1,0},{2,3},{3,2},{4,5},{5,4},{6,7},{7,6},{8,9},{9,8},{10,11... | collective-permute-start | bytes 1769480 | tf_op jit(solution)/shard_map/ppermute | solution.py:139
  69.0 4.9 %collective-permute-start.16 = (bf16[3,8,48,768]{3,2,1,0:T(8,128)(2,1)S(1)}, bf16[3,8,48,768]{3,2,1,0:T(8,128)(2,1)S(1)}, u32[]{:S(2)}, u32[]{:S(2)}) collective-permute-start(bf16[3,8,48,768]{3,2,1,0:T(8,128)(2,1)S(1)} %collective-permute-done.13.refs_1_), channel_id=1, source_target_pairs={{0,1},{1,0},{2,3},{3,2},{4,5},{5,4},{6,7},{7,6},{8,9},{9,8},{10,11... | collective-permute-start | bytes 5308424 | tf_op jit(solution)/shard_map/ppermute | solution.py:139
  69.1 4.4 %collective-permute-start.17 = (bf16[1,8,48,768]{3,2,1,0:T(8,128)(2,1)S(1)}, bf16[1,8,48,768]{3,2,1,0:T(8,128)(2,1)S(1)}, u32[]{:S(2)}, u32[]{:S(2)}) collective-permute-start(bf16[1,8,48,768]{3,2,1,0:T(8,128)(2,1)S(1)} %assemble.9.refs_1_), channel_id=1, source_target_pairs={{0,1},{1,0},{2,3},{3,2},{4,5},{5,4},{6,7},{7,6},{8,9},{9,8},{10,11... | collective-permute-start | bytes 1769480 | tf_op jit(solution)/shard_map/ppermute | solution.py:139
  73.9 0.8 copy-start.10
  77.3 5.2 %collective-permute-start.18 = (bf16[3,8,48,768]{3,2,1,0:T(8,128)(2,1)S(1)}, bf16[3,8,48,768]{3,2,1,0:T(8,128)(2,1)S(1)}, u32[]{:S(2)}, u32[]{:S(2)}) collective-permute-start(bf16[3,8,48,768]{3,2,1,0:T(8,128)(2,1)S(1)} %convolution_convert_fusion.1), channel_id=1, source_target_pairs={{0,1},{1,0},{2,3},{3,2},{4,5},{5,4},{6,7},{7,6},{8,9},{9,8},{10,11... | collective-permute-start | bytes 5308424 | tf_op jit(solution)/shard_map/ppermute | solution.py:139
  77.5 10.0 %collective-permute-start.19 = (bf16[2,8,48,768]{3,2,1,0:T(8,128)(2,1)S(1)}, bf16[2,8,48,768]{3,2,1,0:T(8,128)(2,1)S(1)}, u32[]{:S(2)}, u32[]{:S(2)}) collective-permute-start(bf16[2,8,48,768]{3,2,1,0:T(8,128)(2,1)S(1)} %convolution_convert_fusion.2), channel_id=1, source_target_pairs={{0,1},{1,0},{2,3},{3,2},{4,5},{5,4},{6,7},{7,6},{8,9},{9,8},{10,11... | collective-permute-start | bytes 3538952 | tf_op jit(solution)/shard_map/ppermute | solution.py:139
  78.5 11.5 %collective-permute-start.21 = (bf16[3,8,48,768]{3,2,1,0:T(8,128)(2,1)S(1)}, bf16[3,8,48,768]{3,2,1,0:T(8,128)(2,1)S(1)}, u32[]{:S(2)}, u32[]{:S(2)}) collective-permute-start(bf16[3,8,48,768]{3,2,1,0:T(8,128)(2,1)S(1)} %convolution_convert_fusion), channel_id=1, source_target_pairs={{0,1},{1,0},{2,3},{3,2},{4,5},{5,4},{6,7},{7,6},{8,9},{9,8},{10,11... | collective-permute-start | bytes 5308424 | tf_op jit(solution)/shard_map/ppermute | solution.py:139
  78.8 11.9 %collective-permute-start.22 = (bf16[2,32,768]{2,1,0:T(8,128)(2,1)S(1)}, bf16[2,32,768]{2,1,0:T(8,128)(2,1)S(1)}, u32[]{:S(2)}, u32[]{:S(2)}) collective-permute-start(bf16[2,32,768]{2,1,0:T(8,128)(2,1)S(1)} %get-tuple-element.117), channel_id=1, source_target_pairs={{0,1},{1,2},{2,3},{3,4},{4,5},{5,6},{6,7},{7,8},{8,9},{9,10},{10,1... | collective-permute-start | bytes 294920 | tf_op jit(solution)/shard_map/ppermute | solution.py:22
  81.1 9.6 %collective-permute-start.23 = (bf16[2,32,768]{2,1,0:T(8,128)(2,1)S(1)}, bf16[2,32,768]{2,1,0:T(8,128)(2,1)S(1)}, u32[]{:S(2)}, u32[]{:S(2)}) collective-permute-start(bf16[2,32,768]{2,1,0:T(8,128)(2,1)S(1)} %get-tuple-element.116), channel_id=1, source_target_pairs={{1,0},{2,1},{3,2},{4,3},{5,4},{6,5},{7,6},{8,7},{9,8},{10,9},{11,1... | collective-permute-start | bytes 294920 | tf_op jit(solution)/shard_map/ppermute | solution.py:25
  83.2 26.0 %collective-permute-start.25 = (bf16[3,8,48,768]{3,2,1,0:T(8,128)(2,1)S(1)}, bf16[3,8,48,768]{3,2,1,0:T(8,128)(2,1)S(1)}, u32[]{:S(2)}, u32[]{:S(2)}) collective-permute-start(bf16[3,8,48,768]{3,2,1,0:T(8,128)(2,1)S(1)} %add_convert_fusion), channel_id=1, source_target_pairs={{0,4},{1,3},{2,6},{3,1},{4,0},{5,7},{6,2},{7,5},{8,12},{9,11},{10,... | collective-permute-start | bytes 5308424 | tf_op jit(solution)/shard_map/ppermute | solution.py:139
  87.8 8.3 %collective-permute-start.20 = (bf16[1,4,48,768]{3,2,1,0:T(8,128)(2,1)S(1)}, bf16[1,4,48,768]{3,2,1,0:T(8,128)(2,1)S(1)}, u32[]{:S(2)}, u32[]{:S(2)}) collective-permute-start(bf16[1,4,48,768]{3,2,1,0:T(8,128)(2,1)S(1)} %fusion.56), channel_id=1, source_target_pairs={{0,8},{1,9},{2,10},{3,11},{4,12},{5,13},{6,14},{7,15},{8,0},{9,1},... | collective-permute-start | bytes 884744 | tf_op jit(solution)/shard_map/ppermute | solution.py:139
  90.0 17.8 %copy-start.4 = (f32[1,4,48,768]{3,2,1,0:T(8,128)}, f32[1,4,48,768]{3,2,1,0:T(8,128)S(1)}, u32[]{:S(2)}) copy-start(f32[1,4,48,768]{3,2,1,0:T(8,128)S(1)} %fusion.26) | copy-start | bytes 1769476
  96.2 11.7 %collective-permute-start.26 = (bf16[1,4,48,768]{3,2,1,0:T(8,128)(2,1)S(1)}, bf16[1,4,48,768]{3,2,1,0:T(8,128)(2,1)S(1)}, u32[]{:S(2)}, u32[]{:S(2)}) collective-permute-start(bf16[1,4,48,768]{3,2,1,0:T(8,128)(2,1)S(1)} %fusion.55), channel_id=1, source_target_pairs={{0,8},{1,9},{2,10},{3,11},{4,12},{5,13},{6,14},{7,15},{8,0},{9,1},... | collective-permute-start | bytes 884744 | tf_op jit(solution)/shard_map/ppermute | solution.py:139
  98.9 2.8 %collective-permute-start.24 = (f32[2304]{0:T(1024)S(1)}, f32[2304]{0:T(1024)S(1)}, u32[]{:S(2)}, u32[]{:S(2)}) collective-permute-start(f32[2304]{0:T(1024)S(1)} %maximum_multiply_fusion.1), channel_id=1, source_target_pairs={{0,1},{1,0},{2,3},{3,2},{4,5},{5,4},{6,7},{7,6},{8,9},{9,8},{10,11... | collective-permute-start | bytes 27656 | tf_op jit(solution)/shard_map/ppermute | solution.py:139
  99.0 8.8 %collective-permute-start.27 = (bf16[1,2,48,768]{3,2,1,0:T(8,128)(2,1)S(1)}, bf16[1,2,48,768]{3,2,1,0:T(8,128)(2,1)S(1)}, u32[]{:S(2)}, u32[]{:S(2)}) collective-permute-start(bf16[1,2,48,768]{3,2,1,0:T(8,128)(2,1)S(1)} %fusion.64), channel_id=1, source_target_pairs={{0,16},{1,17},{2,18},{3,19},{4,20},{5,21},{6,22},{7,23},{8,24},{9,... | collective-permute-start | bytes 442376 | tf_op jit(solution)/shard_map/ppermute | solution.py:139
  103.9 3.9 %collective-permute-start.28 = (f32[2304]{0:T(1024)S(1)}, f32[2304]{0:T(1024)S(1)}, u32[]{:S(2)}, u32[]{:S(2)}) collective-permute-start(f32[2304]{0:T(1024)S(1)} %fusion.96), channel_id=1, source_target_pairs={{0,2},{1,3},{2,0},{3,1},{4,6},{5,7},{6,4},{7,5},{8,10},{9,11},{10,... | collective-permute-start | bytes 27656 | tf_op jit(solution)/shard_map/ppermute | solution.py:139
  110.7 15.0 %collective-permute-start.29 = (bf16[2,4,48,768]{3,2,1,0:T(8,128)(2,1)}, bf16[2,4,48,768]{3,2,1,0:T(8,128)(2,1)}, u32[]{:S(2)}, u32[]{:S(2)}) collective-permute-start(bf16[2,4,48,768]{3,2,1,0:T(8,128)(2,1)} %get-tuple-element.99), channel_id=1, source_target_pairs={{0,2},{1,5},{2,0},{3,7},{4,6},{5,1},{6,4},{7,3},{8,10},{9,13},{10,... | collective-permute-start | bytes 1769480 | tf_op jit(solution)/shard_map/ppermute | solution.py:139
  113.9 11.8 %collective-permute-start.30 = (bf16[1,4,48,768]{3,2,1,0:T(8,128)(2,1)}, bf16[1,4,48,768]{3,2,1,0:T(8,128)(2,1)}, u32[]{:S(2)}, u32[]{:S(2)}) collective-permute-start(bf16[1,4,48,768]{3,2,1,0:T(8,128)(2,1)} %get-tuple-element.100), channel_id=1, source_target_pairs={{0,8},{1,9},{2,10},{3,11},{4,12},{5,13},{6,14},{7,15},{8,0},{9,1},... | collective-permute-start | bytes 884744 | tf_op jit(solution)/shard_map/ppermute | solution.py:139
  114.0 9.9 %collective-permute-start.31 = (bf16[1,2,48,768]{3,2,1,0:T(8,128)(2,1)}, bf16[1,2,48,768]{3,2,1,0:T(8,128)(2,1)}, u32[]{:S(2)}, u32[]{:S(2)}) collective-permute-start(bf16[1,2,48,768]{3,2,1,0:T(8,128)(2,1)} %fusion.63), channel_id=1, source_target_pairs={{0,16},{1,17},{2,18},{3,19},{4,20},{5,21},{6,22},{7,23},{8,24},{9,... | collective-permute-start | bytes 442376 | tf_op jit(solution)/shard_map/ppermute | solution.py:139
  117.2 3.7 %collective-permute-start.32 = (f32[2304]{0:T(1024)S(1)}, f32[2304]{0:T(1024)S(1)}, u32[]{:S(2)}, u32[]{:S(2)}) collective-permute-start(f32[2304]{0:T(1024)S(1)} %add.212), channel_id=1, source_target_pairs={{0,4},{1,5},{2,6},{3,7},{4,0},{5,1},{6,2},{7,3},{8,12},{9,13},{10,... | collective-permute-start | bytes 27656 | tf_op jit(solution)/shard_map/ppermute | solution.py:139
  118.1 11.6 %copy-start.6 = (f32[1,4,48,768]{3,2,1,0:T(8,128)S(1)}, f32[1,4,48,768]{3,2,1,0:T(8,128)}, u32[]{:S(2)}) copy-start(f32[1,4,48,768]{3,2,1,0:T(8,128)} %get-tuple-element.101) | copy-start | bytes 1769476
  118.1 21.9 %collective-permute-start.35 = (bf16[1,2,48,768]{3,2,1,0:T(8,128)(2,1)}, bf16[1,2,48,768]{3,2,1,0:T(8,128)(2,1)S(1)}, u32[]{:S(2)}, u32[]{:S(2)}) collective-permute-start(bf16[1,2,48,768]{3,2,1,0:T(8,128)(2,1)} %fusion.62), channel_id=1, source_target_pairs={{0,4},{1,3},{2,6},{3,1},{4,0},{5,7},{6,2},{7,5},{8,12},{9,11},{10,... | collective-permute-start | bytes 442376 | tf_op jit(solution)/shard_map/ppermute | solution.py:139
  125.7 14.3 %copy-start.5 = (f32[1,4,48,768]{3,2,1,0:T(8,128)S(1)}, f32[1,4,48,768]{3,2,1,0:T(8,128)}, u32[]{:S(2)}) copy-start(f32[1,4,48,768]{3,2,1,0:T(8,128)} %copy-done.4) | copy-start | bytes 1769476
  127.3 12.7 %collective-permute-start.33 = (bf16[2,2,48,768]{3,2,1,0:T(8,128)(2,1)S(1)}, bf16[2,2,48,768]{3,2,1,0:T(8,128)(2,1)S(1)}, u32[]{:S(2)}, u32[]{:S(2)}) collective-permute-start(bf16[2,2,48,768]{3,2,1,0:T(8,128)(2,1)S(1)} %get-tuple-element.107), channel_id=1, source_target_pairs={{0,8},{1,9},{2,10},{3,11},{4,12},{5,13},{6,14},{7,15},{8,0},{9,1},... | collective-permute-start | bytes 884744 | tf_op jit(solution)/shard_map/ppermute | solution.py:139
  130.7 9.2 %collective-permute-start.34 = (bf16[1,2,48,768]{3,2,1,0:T(8,128)(2,1)S(1)}, bf16[1,2,48,768]{3,2,1,0:T(8,128)(2,1)S(1)}, u32[]{:S(2)}, u32[]{:S(2)}) collective-permute-start(bf16[1,2,48,768]{3,2,1,0:T(8,128)(2,1)S(1)} %get-tuple-element.108), channel_id=1, source_target_pairs={{0,16},{1,17},{2,18},{3,19},{4,20},{5,21},{6,22},{7,23},{8,24},{9,... | collective-permute-start | bytes 442376 | tf_op jit(solution)/shard_map/ppermute | solution.py:139
  132.5 7.4 %collective-permute-start.36 = (f32[2304]{0:T(1024)S(1)}, f32[2304]{0:T(1024)S(1)}, u32[]{:S(2)}, u32[]{:S(2)}) collective-permute-start(f32[2304]{0:T(1024)S(1)} %add.219), channel_id=1, source_target_pairs={{0,8},{1,9},{2,10},{3,11},{4,12},{5,13},{6,14},{7,15},{8,0},{9,1},... | collective-permute-start | bytes 27656 | tf_op jit(solution)/shard_map/ppermute | solution.py:139
  141.0 10.7 %collective-permute-start.37 = (bf16[2,1,48,768]{3,2,1,0:T(8,128)(2,1)S(1)}, bf16[2,1,48,768]{3,2,1,0:T(8,128)(2,1)S(1)}, u32[]{:S(2)}, u32[]{:S(2)}) collective-permute-start(bf16[2,1,48,768]{3,2,1,0:T(8,128)(2,1)S(1)} %fusion.59), channel_id=1, source_target_pairs={{0,16},{1,17},{2,18},{3,19},{4,20},{5,21},{6,22},{7,23},{8,24},{9,... | collective-permute-start | bytes 442376 | tf_op jit(solution)/shard_map/ppermute | solution.py:139
  143.6 6.9 %collective-permute-start.39 = (f32[2304]{0:T(1024)S(1)}, f32[2304]{0:T(1024)S(1)}, u32[]{:S(2)}, u32[]{:S(2)}) collective-permute-start(f32[2304]{0:T(1024)S(1)} %add.224), channel_id=1, source_target_pairs={{0,16},{1,17},{2,18},{3,19},{4,20},{5,21},{6,22},{7,23},{8,24},{9,... | collective-permute-start | bytes 27656 | tf_op jit(solution)/shard_map/ppermute | solution.py:139
  145.5 6.3 %collective-permute-start.38 = (bf16[2,1,48,768]{3,2,1,0:T(8,128)(2,1)S(1)}, bf16[2,1,48,768]{3,2,1,0:T(8,128)(2,1)S(1)}, u32[]{:S(2)}, u32[]{:S(2)}) collective-permute-start(bf16[2,1,48,768]{3,2,1,0:T(8,128)(2,1)S(1)} %pad_maximum_fusion.2), channel_id=1, source_target_pairs={{0,2},{1,5},{2,0},{3,7},{4,6},{5,1},{6,4},{7,3},{8,10},{9,13},{10,... | collective-permute-start | bytes 442376 | tf_op jit(solution)/shard_map/ppermute | solution.py:139
  (3 other events, 2.1 us)

commit v5 on v4

--- a/solution.py
+++ b/solution.py
@@ -15,20 +15,15 @@
 eps = 1e-06
 
 
-def edges(block, axis, dim, width):
-    count = lax.axis_size(axis)
-    forward = [(i, i + 1) for i in range(count - 1)]
-    backward = [(target, source) for source, target in forward]
-    low = lax.ppermute(
-        lax.slice_in_dim(block, block.shape[dim] - width, None, axis=dim), axis, forward
-    )
-    high = lax.ppermute(lax.slice_in_dim(block, 0, width, axis=dim), axis, backward)
-    return low, high
-
-
 def padded(block, sides, width):
     for axis, dim in sides:
-        low, high = edges(block, axis, dim, width)
+        count = lax.axis_size(axis)
+        forward = [(i, i + 1) for i in range(count - 1)]
+        backward = [(target, source) for source, target in forward]
+        low = lax.ppermute(
+            lax.slice_in_dim(block, block.shape[dim] - width, None, axis=dim), axis, forward
+        )
+        high = lax.ppermute(lax.slice_in_dim(block, 0, width, axis=dim), axis, backward)
         block = jnp.concatenate([low, block, high], axis=dim)
     return block
 
@@ -131,6 +126,12 @@
 BLOCKS = 16
 HALF = 8
 
+OUTER = [
+    (i, j)
+    for odd in range(1, TORUS_DEVICES - 1, 2)
+    for i, j in ((odd, odd + 1), (odd + 1, odd))
+]
+
 VMEM = pl.BlockSpec(memory_space=pltpu.VMEM)
 SMEM = pl.BlockSpec(memory_space=pltpu.SMEM)
 
@@ -154,6 +155,39 @@
     dx = r1 + parity * (r2 - r1)
     dy = r2 + parity * (r1 - r2)
     return owner ^ (16 * high + 8 * low + 4 * dy + 2 * dx)
+
+
+def edge_swaps(block, parity):
+    width = DILATION_STEP
+    last = block.shape[1] - width
+    inside = lax.dynamic_slice_in_dim(block, (1 - parity) * last, width, axis=1)
+    outside = lax.dynamic_slice_in_dim(block, parity * last, width, axis=1)
+    return send(inside, CORE), send(outside, OUTER)
+
+
+def fold(inputs, outputs):
+    def kernel(*refs):
+        sources, targets = refs[: len(inputs)], refs[len(inputs) :]
+        for target, (dtype, _, _, pieces) in zip(targets, outputs):
+            for added, (m, m_count), (n, n_count), to_m, to_n in pieces:
+                total = None
+                for source in added:
+                    value = sources[source][m : m + m_count, n : n + n_count]
+                    value = value.astype(jnp.float32)
+                    total = value if total is None else total + value
+                target[to_m : to_m + m_count, to_n : to_n + n_count] = total.astype(dtype)
+
+    tail = inputs[0].shape[2:]
+    return pl.pallas_call(
+        kernel,
+        out_shape=[
+            jax.ShapeDtypeStruct((m, n) + tail, dtype) for dtype, m, n, pieces in outputs
+        ],
+        in_specs=[VMEM] * len(inputs),
+        out_specs=[VMEM] * len(outputs),
+        compiler_params=pltpu.CompilerParams(vmem_limit_bytes=12 << 20),
+        name="fold",
+    )(*inputs)
 
 
 def assemble(inputs, outputs):
@@ -179,42 +213,55 @@
     )(*inputs)
 
 
-def upper(kept, received, pick=slice(None)):
-    n = kept.shape[1] // 2
-    total = kept[pick, n:] + received[pick, n:].astype(jnp.float32)
-    return total.astype(jnp.bfloat16)
-
-
-def lower(kept, received, pick=slice(None)):
-    n = kept.shape[1] // 2
-    return kept[pick, :n] + received[pick, :n].astype(jnp.float32)
-
-
 GELU_SCALE = math.sqrt(2.0 / math.pi)
 GELU_CUBE = 0.044715
 
 
+def edge_places(device, bins):
+    parity = device & 1
+    beyond = bins + DILATION_STEP
+    core_at = pl.multiple_of((1 - parity) * beyond, DILATION_STEP)
+    outer_at = pl.multiple_of(parity * beyond, DILATION_STEP)
+    return core_at, outer_at
+
+
 def prepare_kernel(
-    index_ref, features_ref, cotangent_ref, gain_ref, taps_ref, project_ref, active, turned
+    index_ref,
+    features_ref,
+    core_ref,
+    outer_ref,
+    cotangent_ref,
+    gain_ref,
+    taps_ref,
+    project_ref,
+    active,
+    turned,
 ):
     device = index_ref[0]
-    batch, padded_bins, channels = features_ref.shape
-    bins = padded_bins - 2 * DILATION_STEP
+    batch, bins, channels = features_ref.shape
     rows = taps_ref.shape[4]
-    step = 32
+    width = DILATION_STEP
     gain = gain_ref[...]
+    core_at, outer_at = edge_places(device, bins)
+
+    def activate(x):
+        x = x.astype(jnp.float32)
+        inverse = lax.rsqrt(jnp.sum(x * x, axis=-1, keepdims=True) * (1.0 / channels) + eps)
+        v = x * inverse * gain
+        t = jnp.tanh(GELU_SCALE * (v + GELU_CUBE * (v * v * v)))
+        return (0.5 * v * (1.0 + t)).astype(jnp.bfloat16)
+
     for b in range(batch):
 
         def some_rows(i, carry):
-            at = pl.multiple_of(i * step, step)
-            x = features_ref[b, pl.ds(at, step), :].astype(jnp.float32)
-            inverse = lax.rsqrt(jnp.sum(x * x, axis=-1, keepdims=True) * (1.0 / channels) + eps)
-            v = x * inverse * gain
-            t = jnp.tanh(GELU_SCALE * (v + GELU_CUBE * (v * v * v)))
-            active[b, pl.ds(at, step), :] = (0.5 * v * (1.0 + t)).astype(jnp.bfloat16)
+            at = pl.multiple_of(i * width, width)
+            rows_of = activate(features_ref[b, pl.ds(at, width), :])
+            active[b, pl.ds(pl.multiple_of(at + width, width), width), :] = rows_of
             return carry
 
-        lax.fori_loop(0, padded_bins // step, some_rows, 0)
+        lax.fori_loop(0, bins // width, some_rows, 0)
+        active[b, pl.ds(core_at, width), :] = activate(core_ref[b])
+        active[b, pl.ds(outer_at, width), :] = activate(outer_ref[b])
 
     def blocks(order):
         for other in BITS:
@@ -234,21 +281,22 @@
         project_ref[other, at // HALF, 0, at % HALF] = block
 
 
-def prepare(features_padded, cotangent, gain, rows):
+def prepare(features, edges_of, cotangent, gain, rows):
     tokens, channels = cotangent.shape
+    batch, bins, _ = features.shape
     shape = lambda count: jax.ShapeDtypeStruct((2, 2, count, HALF, rows, tokens), cotangent.dtype)
     return pl.pallas_call(
         prepare_kernel,
         out_shape=[shape(KERNEL_TAPS), shape(1)],
-        in_specs=[SMEM, VMEM, VMEM, VMEM],
+        in_specs=[SMEM] + [VMEM] * 5,
         out_specs=[VMEM] * 2,
         scratch_shapes=[
-            pltpu.VMEM(features_padded.shape, jnp.bfloat16),
+            pltpu.VMEM((batch, bins + 2 * DILATION_STEP, channels), jnp.bfloat16),
             pltpu.VMEM((channels, tokens), jnp.bfloat16),
         ],
         compiler_params=pltpu.CompilerParams(vmem_limit_bytes=16 << 20),
         name="prepare",
-    )(device_index(), features_padded, cotangent, gain.reshape(1, channels))
+    )(device_index(), features, *edges_of, cotangent, gain.reshape(1, channels))
 
 
 def place_products(device, parts, turned, orders, placed):
@@ -290,14 +338,15 @@
     )(device_index(), hidden, features, *parts)
 
 
-def grad_active_kernel(index_ref, grad_ref, low_ref, high_ref, *refs):
+def grad_active_kernel(index_ref, grad_ref, core_ref, outer_ref, *refs):
     parts, (out_ref, padded_ref, placed) = refs[:4], refs[4:]
     batch, padded_bins, _ = padded_ref.shape
     bins = padded_bins - 2 * DILATION_STEP
+    core_at, outer_at = edge_places(index_ref[0], bins)
     for b in range(batch):
-        padded_ref[b, :DILATION_STEP] = low_ref[b]
         padded_ref[b, DILATION_STEP : DILATION_STEP + bins] = grad_ref[b * bins : (b + 1) * bins]
-        padded_ref[b, DILATION_STEP + bins :] = high_ref[b]
+        padded_ref[b, pl.ds(core_at, DILATION_STEP), :] = core_ref[b]
+        padded_ref[b, pl.ds(outer_at, DILATION_STEP), :] = outer_ref[b]
     turned = []
     for tap in range(KERNEL_TAPS):
         shift = (KERNEL_TAPS - 1 - tap) * DILATION_STEP
@@ -308,9 +357,9 @@
     out_ref[...] = placed[...].T
 
 
-def grad_of_active(grad, low, high, parts):
+def grad_of_active(grad, edges_of, parts):
     tokens, inner = grad.shape
-    batch = low.shape[0]
+    batch = edges_of[0].shape[0]
     channels = 2 * BLOCKS * parts[0].shape[2]
     return pl.pallas_call(
         grad_active_kernel,
@@ -323,7 +372,7 @@
         ],
         compiler_params=pltpu.CompilerParams(vmem_limit_bytes=24 << 20),
         name="grad_active",
-    )(device_index(), grad, low, high, *parts)
+    )(device_index(), grad, *edges_of, *parts)
 
 
 def rows_dot(left, right):
@@ -352,8 +401,6 @@
     pair = taps[:2]
     rest = jnp.concatenate([taps[2:], project_weight[None, None]])
     pair_in, rest_in = send(pair, Z_FAR), send(rest, FIRST)
-    low, high = edges(features, "seq", 1, DILATION_STEP)
-    pair_in = after(pair_in, low, high)
     pair, last, proj = assemble(
         (pair, pair_in, rest, rest_in),
         (
@@ -363,8 +410,10 @@
         ),
     )
     pair_in, last_in, proj_b = send(pair, Z_NEAR), send(last, Z_FAR), send(proj, SECOND)
+    parity = lax.axis_index("seq") & 1
+    feature_edges = edge_swaps(after(features, pair), parity)
     grow = lambda m, n, a: (m, 2 * n, ((a, 0, m, 0, 0), (a + 1, 0, m, 0, n)))
-    pair_in = after(pair_in, proj_b)
+    pair_in = after(pair_in, proj_b, *feature_edges)
     pair, last = assemble((pair, pair_in, last, last_in), (grow(2, 2, 0), grow(1, 2, 2)))
     pair_in, last_in, proj_in = send(pair, FIRST), send(last, Z_NEAR), send(proj, Z_FAR)
     near, proj_a = assemble(
@@ -377,8 +426,9 @@
     far, near_other = send(near, SECOND), send(near, CORE)
     proj_in, proj_b_in = send(proj_a, Z_NEAR), send(proj_b, Z_FAR)
     flat_cotangent = cotangent.reshape(tokens, channels)
-    features_padded = jnp.concatenate([low, after(features, near), high], axis=1)
-    act, act_p = prepare(features_padded, flat_cotangent, outer_gain, rows)
+    act, act_p = prepare(
+        after(features, near), feature_edges, flat_cotangent, outer_gain, rows
+    )
     proj_a, proj_b = assemble(
         (proj_a, after(proj_in, act), proj_b, proj_b_in), (grow(1, 4, 0), grow(1, 2, 2))
     )
@@ -406,9 +456,7 @@
     recv_far = send(give, CORE)
     give = as_bf16(rows_dot(act[1, 0], after(grad_conv, give)))
     recv_near = send(give, CORE)
-    low, high = edges(
-        after(grad_conv, give).reshape(batch, bin_count, inner), "seq", 1, DILATION_STEP
-    )
+    grad_edges = edge_swaps(after(grad_conv, give).reshape(batch, bin_count, inner), parity)
     message = as_bf16(rows_dot(act[0, 1], after(grad_conv, give)) + as_f32(recv_far))
     recv = send(message, SECOND)
     grad_p = after(hidden, message)
@@ -428,55 +476,82 @@
 
     flat = features.reshape(tokens, channels)
     grad_active = grad_of_active(
-        after(grad_conv, kept), low, high, (near, far, near_other, far_other)
-    )
+        after(grad_conv, kept), grad_edges, (near, far, near_other, far_other)
+    )
+    f32, bf16 = jnp.float32, jnp.bfloat16
     recv_b = after(recv_b, grad_active)
-    message_b = upper(kept_b, recv_b)
-    kept_b, recv_b = lower(kept_b, recv_b), send(message_b, Z_FAR)
+    message_b, kept_b = fold(
+        (kept_b, recv_b),
+        (
+            (bf16, 1, 2, (((0, 1), (0, 1), (2, 2), 0, 0),)),
+            (f32, 1, 2, (((0, 1), (0, 1), (0, 2), 0, 0),)),
+        ),
+    )
+    recv_b = send(message_b, Z_FAR)
     recv_a = send(after(message_a, message_b), Z_NEAR)
     unused, pull_outer = jax.vjp(act_norm, as_f32(after(features, message_b)), outer_gain)
     grad_branch, grad_gain_outer = pull_outer(grad_active.reshape(features.shape))
     grad_features = as_bf16(as_f32(cotangent) + grad_branch)
     gains = jnp.concatenate([grad_gain_outer, grad_gain_inner]) * factor
     gains = gains + send(gains, CORE)
+
+    recv_a = after(recv_a, gains)
+    message, message_l, message_a, message_p, kept, kept_l, kept_a, kept_b = fold(
+        (kept, recv, kept_a, recv_a, kept_b, recv_b),
+        (
+            (bf16, 2, 4, (((0, 1), (0, 2), (4, 4), 0, 0),)),
+            (bf16, 1, 4, (((0, 1), (2, 1), (4, 4), 0, 0),)),
+            (bf16, 1, 2, (((2, 3), (0, 1), (2, 2), 0, 0),)),
+            (bf16, 1, 2, (((4, 5), (0, 1), (0, 2), 0, 0),)),
+            (f32, 2, 4, (((0, 1), (0, 2), (0, 4), 0, 0),)),
+            (f32, 1, 4, (((0, 1), (2, 1), (0, 4), 0, 0),)),
+            (f32, 1, 2, (((2, 3), (0, 1), (0, 2), 0, 0),)),
+            (f32, 1, 2, (((4, 5), (0, 1), (0, 2), 0, 0),)),
+        ),
+    )
+    recv, recv_l, recv_a = send(message, FIRST), send(message_l, Z_NEAR), send(message_a, Z_FAR)
+    gains = after(gains, message)
+    gains = gains + send(gains, links(lambda i: i ^ 2))
     block_out = project_back(
-        after(hidden, gains), flat, (proj_a, proj_b, proj_a_other, proj_b_other)
+        after(hidden, message), flat, (proj_a, proj_b, proj_a_other, proj_b_other)
     ).reshape(features.shape)
     gains = after(gains, block_out)
-    gains = gains + send(gains, links(lambda i: i ^ 2))
-    recv_a, recv_b = after((recv_a, recv_b), gains)
-    message_a, kept_a = upper(kept_a, recv_a), lower(kept_a, recv_a)
-    kept_b = kept_b + as_f32(recv_b)
-
-    recv = after(recv, message_a, kept_b)
-    pair, last = slice(0, 2), slice(2, 3)
-    message, message_l = upper(kept, recv, pair), upper(kept, recv, last)
-    kept, kept_l = lower(kept, recv, pair), lower(kept, recv, last)
-    recv, recv_l, recv_a = send(message, FIRST), send(message_l, Z_NEAR), send(message_a, Z_FAR)
-    gains = after(gains, message, message_l)
+
+    recv = after(recv, gains)
+    message, message_l, kept, kept_l, kept_p = fold(
+        (kept, recv, kept_l, recv_l, kept_a, recv_a),
+        (
+            (bf16, 2, 2, (((0, 1), (0, 2), (2, 2), 0, 0),)),
+            (bf16, 1, 2, (((2, 3), (0, 1), (2, 2), 0, 0),)),
+            (f32, 2, 2, (((0, 1), (0, 2), (0, 2), 0, 0),)),
+            (f32, 1, 2, (((2, 3), (0, 1), (0, 2), 0, 0),)),
+            (f32, 1, 2, (((4, 5), (0, 1), (0, 2), 0, 0),)),
+        ),
+    )
+    message_p = after(message_p, message)
+    recv, recv_l, recv_p = send(message, Z_NEAR), send(message_l, Z_FAR), send(message_p, SECOND)
+    gains = after(gains, message)
     gains = gains + send(gains, links(lambda i: i ^ 4))
 
-    recv, recv_l, recv_a, _ = lax.optimization_barrier((recv, recv_l, recv_a, gains))
-    message, message_l, message_p = upper(kept, recv), upper(kept_l, recv_l), as_bf16(kept_b)
-    kept, kept_l, kept_p = lower(kept, recv), lower(kept_l, recv_l), kept_a + as_f32(recv_a)
-    recv, recv_l, recv_p = send(message, Z_NEAR), send(message_l, Z_FAR), send(message_p, SECOND)
-    gains = after(gains, message, message_l, message_p)
+    recv = after(recv, gains)
+    message, message_r, kept, kept_r = fold(
+        (kept, recv, kept_l, recv_l, kept_p, recv_p),
+        (
+            (bf16, 2, 1, (((0, 1), (0, 2), (1, 1), 0, 0),)),
+            (bf16, 2, 1, (((2, 3), (0, 1), (1, 1), 0, 0), ((4, 5), (0, 1), (1, 1), 1, 0))),
+            (f32, 2, 1, (((0, 1), (0, 2), (0, 1), 0, 0),)),
+            (f32, 2, 1, (((2, 3), (0, 1), (0, 1), 0, 0), ((4, 5), (0, 1), (0, 1), 1, 0))),
+        ),
+    )
+    recv, recv_r = send(message, Z_FAR), send(message_r, FIRST)
+    gains = after(gains, message)
     gains = gains + send(gains, Z_NEAR)
-
-    recv, recv_l, recv_p, _ = lax.optimization_barrier((recv, recv_l, recv_p, gains))
-    message = upper(kept, recv)
-    kept_p = kept_p + as_f32(recv_p)
-    message_r = jnp.concatenate([upper(kept_l, recv_l), as_bf16(kept_p[:, 1:])])
-    kept, kept_l, kept_p = lower(kept, recv), lower(kept_l, recv_l), kept_p[:, :1]
-    recv, recv_r = send(message, Z_FAR), send(message_r, FIRST)
-    gains = after(gains, message, message_r)
     gains = gains + send(gains, Z_FAR)
 
-    grad_project = (kept_p[0, 0] + as_f32(recv_r[1, 0])) * factor
     sums = kept + as_f32(recv)
-    grad_dilated = (
-        jnp.stack([sums[0, 0], sums[1, 0], kept_l[0, 0] + as_f32(recv_r[0, 0])], axis=1) * factor
-    )
+    sums_r = kept_r + as_f32(recv_r)
+    grad_project = sums_r[1, 0] * factor
+    grad_dilated = jnp.stack([sums[0, 0], sums[1, 0], sums_r[0, 0]], axis=1) * factor
 
     device = lax.axis_index("seq")
     grad_outer_gain = lax.dynamic_slice(gains, (device * rows,), (rows,))

time: 154 us -> 146 us (0.948)
  other arithmetic: 15.9 us -> 8.25 us
  waiting for transfers between devices: 58.1 us -> 65.7 us
  starting transfers between devices: 53.1 us -> 48.6 us
  local copies, waits for them, and re-layouts: 5.27 us -> 3.37 us
    ppermute x36 -> x40, waiting for transfers between devices: 58.1 us -> 65.7 us  [send(): return lax.ppermute(block, 'seq', pairs)]
    ppermute x4 -> x0, starting transfers between devices: 6.33 us -> none  [the longest x2 3.57 us: edges(): lax.ppermute(lax.slice_in_dim(block, block.shape[dim] - width, None, axis...]
    add x4 -> x1, other arithmetic: 4.73 us -> 0.03 us  [body_torus(): sums_r = kept_r + as_f32(recv_r)]
    convert_element_type x6 -> x0, other arithmetic: 2.81 us -> none  [upper(): return total.astype(jnp.bfloat16)]
    pallas_call x0 -> x4, Pallas kernels: none -> 2.1 us  [fold(): pl.pallas_call(kernel, out_shape=[jax.ShapeDtypeStruct((m, n) + tail, dty...]
    ppermute x36 -> x40, starting transfers between devices: 46.7 us -> 48.6 us  [send(): return lax.ppermute(block, 'seq', pairs)]
  transfers between devices with their start and end apart: 40 -> 40, of which waited for: 17 -> 20; matrix products, arithmetic and copies ran while one was open for 14% -> 10% of each run, Pallas kernels for 6% -> 5%
where the time goes in v5:
time: 146 us
  waiting for transfers between devices  65.7 us (45%)
  starting transfers between devices  48.6 us (33%)
  Pallas kernels  10.3 us (7%)
  matrix products  8.43 us (6%)
  other arithmetic  8.25 us (6%)
  local copies, waits for them, and re-layouts  3.37 us (2%)
    ppermute x40, waiting for transfers between devices, send(): return lax.ppermute(block, 'seq', pairs)  65.7 us
    ppermute x40, starting transfers between devices, send(): return lax.ppermute(block, 'seq', pairs)  48.6 us
    dot_general x8, matrix products, contract(): jnp.einsum('ct,ci->ti', left.reshape(-1, left.shape[-1]), right.reshape(-...  4.48 us
    dot_general x9, matrix products, rows_dot(): jnp.einsum('mnrt,ti->mnri', left, right, preferred_element_type=jnp.float32)  3.94 us
    reduce_sum x2, other arithmetic, act_norm(): values * lax.rsqrt(meansq + eps) * gain  3.55 us
    pallas_call x1, Pallas kernels, prepare(): pl.pallas_call(prepare_kernel, out_shape=[shape(KERNEL_TAPS), shape(1)],...  2.95 us
  transfers between devices with their start and end apart: 40, of which 20 were waited for; matrix products, arithmetic and copies ran while one was open for 10% of the time, Pallas kernels for 5%

profile of v5, /device:TPU:0, one launch (start us, length us, event | category | flops | bytes accessed | tf_op | source)
XLA Modules:
  0.0 145.6 jit_solution(7694147883394211549)
XLA Ops:
  0.6 1.0 slice_bitcast_fusion.8
  1.6 4.1 %collective-permute-start = (bf16[2,1,48,768]{3,2,0,1:T(8,128)(2,1)S(1)}, bf16[2,1,48,768]{3,2,0,1:T(8,128)(2,1)S(1)}, u32[]{:S(2)}, u32[]{:S(2)}) collective-permute-start(bf16[2,1,48,768]{3,2,0,1:T(8,128)(2,1)S(1)} %get-tuple-element.140), channel_id=1, source_target_pairs={{0,16},{1,17},{2,18},{3,19},{4,20},{5,21},{6,22},{7,23},{8,24},{9,... | collective-permute-start | bytes 442376 | tf_op jit(solution)/shard_map/ppermute | solution.py:140
  6.6 0.9 pad_maximum_fusion.refs_2_
  7.5 1.6 %collective-permute-start.1 = (bf16[2,1,48,768]{3,2,1,0:T(8,128)(2,1)S(1)}, bf16[2,1,48,768]{3,2,1,0:T(8,128)(2,1)S(1)}, u32[]{:S(2)}, u32[]{:S(2)}) collective-permute-start(bf16[2,1,48,768]{3,2,1,0:T(8,128)(2,1)S(1)} %pad_maximum_fusion.refs_2_), channel_id=1, source_target_pairs={{0,2},{1,5},{2,0},{3,7},{4,6},{5,1},{6,4},{7,3},{8,10},{9,13},{10,... | collective-permute-start | bytes 442376 | tf_op jit(solution)/shard_map/ppermute | solution.py:140
  9.1 3.7 %collective-permute-done = bf16[2,1,48,768]{3,2,0,1:T(8,128)(2,1)S(1)} collective-permute-done((bf16[2,1,48,768]{3,2,0,1:T(8,128)(2,1)S(1)}, bf16[2,1,48,768]{3,2,0,1:T(8,128)(2,1)S(1)}, u32[]{:S(2)}, u32[]{:S(2)}) %collective-permute-start) | collective-permute-done | bytes 147488 | tf_op jit(solution)/shard_map/ppermute | solution.py:140
  12.8 1.6 %collective-permute-start.2 = (bf16[2,2,48,768]{3,2,1,0:T(8,128)(2,1)S(1)}, bf16[2,2,48,768]{3,2,1,0:T(8,128)(2,1)S(1)}, u32[]{:S(2)}, u32[]{:S(2)}) collective-permute-start(bf16[2,2,48,768]{3,2,1,0:T(8,128)(2,1)S(1)} %get-tuple-element.62.refs_0_), channel_id=1, source_target_pairs={{0,8},{1,9},{2,10},{3,11},{4,12},{5,13},{6,14},{7,15},{8,0},{9,1},... | collective-permute-start | bytes 884744 | tf_op jit(solution)/shard_map/ppermute | solution.py:140
  15.4 4.2 %collective-permute-start.3 = (bf16[1,2,48,768]{3,2,1,0:T(8,128)(2,1)S(1)}, bf16[1,2,48,768]{3,2,1,0:T(8,128)(2,1)S(1)}, u32[]{:S(2)}, u32[]{:S(2)}) collective-permute-start(bf16[1,2,48,768]{3,2,1,0:T(8,128)(2,1)S(1)} %get-tuple-element.63.refs_4_), channel_id=1, source_target_pairs={{0,4},{1,3},{2,6},{3,1},{4,0},{5,7},{6,2},{7,5},{8,12},{9,11},{10,... | collective-permute-start | bytes 442376 | tf_op jit(solution)/shard_map/ppermute | solution.py:140
  19.6 2.5 %collective-permute-start.6 = (bf16[1,2,48,768]{3,2,1,0:T(8,128)(2,1)S(1)}, bf16[1,2,48,768]{3,2,1,0:T(8,128)(2,1)S(1)}, u32[]{:S(2)}, u32[]{:S(2)}) collective-permute-start(bf16[1,2,48,768]{3,2,1,0:T(8,128)(2,1)S(1)} %get-tuple-element.66.refs_2_), channel_id=1, source_target_pairs={{0,16},{1,17},{2,18},{3,19},{4,20},{5,21},{6,22},{7,23},{8,24},{9,... | collective-permute-start | bytes 442376 | tf_op jit(solution)/shard_map/ppermute | solution.py:140
  22.1 1.6 %collective-permute-done.3.refs_2_ = bf16[1,2,48,768]{3,2,1,0:T(8,128)(2,1)S(1)} collective-permute-done((bf16[1,2,48,768]{3,2,1,0:T(8,128)(2,1)S(1)}, bf16[1,2,48,768]{3,2,1,0:T(8,128)(2,1)S(1)}, u32[]{:S(2)}, u32[]{:S(2)}) %collective-permute-start.3) | collective-permute-done | bytes 147488 | tf_op jit(solution)/shard_map/ppermute | solution.py:140
  23.8 6.6 %collective-permute-done.6.refs_3_ = bf16[1,2,48,768]{3,2,1,0:T(8,128)(2,1)S(1)} collective-permute-done((bf16[1,2,48,768]{3,2,1,0:T(8,128)(2,1)S(1)}, bf16[1,2,48,768]{3,2,1,0:T(8,128)(2,1)S(1)}, u32[]{:S(2)}, u32[]{:S(2)}) %collective-permute-start.6) | collective-permute-done | bytes 147488 | tf_op jit(solution)/shard_map/ppermute | solution.py:140
  30.6 2.0 %collective-permute-start.9 = (bf16[1,2,48,768]{3,2,1,0:T(8,128)(2,1)S(1)}, bf16[1,2,48,768]{3,2,1,0:T(8,128)(2,1)S(1)}, u32[]{:S(2)}, u32[]{:S(2)}) collective-permute-start(bf16[1,2,48,768]{3,2,1,0:T(8,128)(2,1)S(1)} %get-tuple-element.63.refs_4_), channel_id=1, source_target_pairs={{0,16},{1,17},{2,18},{3,19},{4,20},{5,21},{6,22},{7,23},{8,24},{9,... | collective-permute-start | bytes 442376 | tf_op jit(solution)/shard_map/ppermute | solution.py:140
  32.6 6.9 %collective-permute-done.9.refs_5_ = bf16[1,2,48,768]{3,2,1,0:T(8,128)(2,1)S(1)} collective-permute-done((bf16[1,2,48,768]{3,2,1,0:T(8,128)(2,1)S(1)}, bf16[1,2,48,768]{3,2,1,0:T(8,128)(2,1)S(1)}, u32[]{:S(2)}, u32[]{:S(2)}) %collective-permute-start.9) | collective-permute-done | bytes 147488 | tf_op jit(solution)/shard_map/ppermute | solution.py:140
  39.5 2.2 %collective-permute-done.8.refs_3_ = bf16[1,4,48,768]{3,2,1,0:T(8,128)(2,1)S(1)} collective-permute-done((bf16[1,4,48,768]{3,2,1,0:T(8,128)(2,1)S(1)}, bf16[1,4,48,768]{3,2,1,0:T(8,128)(2,1)S(1)}, u32[]{:S(2)}, u32[]{:S(2)}) %collective-permute-start.8) | collective-permute-done | bytes 294944 | tf_op jit(solution)/shard_map/ppermute | solution.py:140
  42.1 1.7 %collective-permute-start.11 = (bf16[1,2,48,768]{3,2,1,0:T(8,128)(2,1)S(1)}, bf16[1,2,48,768]{3,2,1,0:T(8,128)(2,1)S(1)}, u32[]{:S(2)}, u32[]{:S(2)}) collective-permute-start(bf16[1,2,48,768]{3,2,1,0:T(8,128)(2,1)S(1)} %collective-permute-done.3.refs_2_), channel_id=1, source_target_pairs={{0,16},{1,17},{2,18},{3,19},{4,20},{5,21},{6,22},{7,23},{8,24},{9,... | collective-permute-start | bytes 442376 | tf_op jit(solution)/shard_map/ppermute | solution.py:140
  43.8 1.1 collective-permute-start.13
  44.9 2.9 %prepare.1 = (bf16[2,2,3,8,48,256]{5,4,3,2,1,0:T(8,128)(2,1)S(1)}, bf16[2,2,1,8,48,256]{5,4,3,2,1,0:T(8,128)(2,1)S(1)}) custom-call(s32[1]{0:T(128)} %bitcast.index_ref, bf16[2,128,1536]{2,1,0:T(8,128)(2,1)S(1)} %copy-done, bf16[2,32,1536]{2,1,0:T(8,128)(2,1)S(1)} %collective-permute-done.4.core_ref, ...), custom_call_target="tpu_custom_call" | custom-call | tf_op jit(solution)/shard_map/prepare/pallas_call | solution.py:288
  47.9 6.6 %collective-permute-done.10.refs_1_ = bf16[1,4,48,768]{3,2,1,0:T(8,128)(2,1)S(1)} collective-permute-done((bf16[1,4,48,768]{3,2,1,0:T(8,128)(2,1)S(1)}, bf16[1,4,48,768]{3,2,1,0:T(8,128)(2,1)S(1)}, u32[]{:S(2)}, u32[]{:S(2)}) %collective-permute-start.10) | collective-permute-done | bytes 294944 | tf_op jit(solution)/shard_map/ppermute | solution.py:140
  54.9 1.2 collective-permute-start.14
  58.9 5.5 %collective-permute-done.14.refs_1_ = bf16[1,4,48,768]{3,2,1,0:T(8,128)(2,1)S(1)} collective-permute-done((bf16[1,4,48,768]{3,2,1,0:T(8,128)(2,1)S(1)}, bf16[1,4,48,768]{3,2,1,0:T(8,128)(2,1)S(1)}, u32[]{:S(2)}, u32[]{:S(2)}) %collective-permute-start.14) | collective-permute-done | bytes 294944 | tf_op jit(solution)/shard_map/ppermute | solution.py:140
  64.4 2.0 %collective-permute-done.13.refs_1_ = bf16[3,8,48,768]{3,2,1,0:T(8,128)(2,1)S(1)} collective-permute-done((bf16[3,8,48,768]{3,2,1,0:T(8,128)(2,1)S(1)}, bf16[3,8,48,768]{3,2,1,0:T(8,128)(2,1)S(1)}, u32[]{:S(2)}, u32[]{:S(2)}) %collective-permute-start.13) | collective-permute-done | bytes 1769504 | tf_op jit(solution)/shard_map/ppermute | solution.py:140
  68.0 2.9 %collective-permute-done.17.refs_3_ = bf16[1,8,48,768]{3,2,1,0:T(8,128)(2,1)S(1)} collective-permute-done((bf16[1,8,48,768]{3,2,1,0:T(8,128)(2,1)S(1)}, bf16[1,8,48,768]{3,2,1,0:T(8,128)(2,1)S(1)}, u32[]{:S(2)}, u32[]{:S(2)}) %collective-permute-start.17) | collective-permute-done | bytes 589856 | tf_op jit(solution)/shard_map/ppermute | solution.py:140
  77.4 1.0 collective-permute-done.18
  79.1 4.6 %collective-permute-start.21 = (bf16[3,8,48,768]{3,2,1,0:T(8,128)(2,1)S(1)}, bf16[3,8,48,768]{3,2,1,0:T(8,128)(2,1)S(1)}, u32[]{:S(2)}, u32[]{:S(2)}) collective-permute-start(bf16[3,8,48,768]{3,2,1,0:T(8,128)(2,1)S(1)} %add_convert_fusion), channel_id=1, source_target_pairs={{0,4},{1,3},{2,6},{3,1},{4,0},{5,7},{6,2},{7,5},{8,12},{9,11},{10,... | collective-permute-start | bytes 5308424 | tf_op jit(solution)/shard_map/ppermute | solution.py:140
  85.6 2.7 %grad_active.1 = f32[256,1536]{1,0:T(8,128)S(1)} custom-call(s32[1]{0:T(128)} %bitcast.index_ref, bf16[256,768]{1,0:T(8,128)(2,1)S(1)} %fusion.28.grad_ref, bf16[2,32,768]{2,1,0:T(8,128)(2,1)S(1)} %collective-permute-done.23.core_ref, bf16[2,32,768]{2,1,0:T(8,128)(2,1)S(1)} %collective-permute-done.24.outer_ref, ...), custom_call_target="tpu_custom_call" | custom-call | tf_op jit(solution)/shard_map/grad_active/pallas_call | solution.py:364
  88.3 3.7 %collective-permute-done.22.refs_1_ = bf16[1,4,48,768]{3,2,1,0:T(8,128)(2,1)S(1)} collective-permute-done((bf16[1,4,48,768]{3,2,1,0:T(8,128)(2,1)S(1)}, bf16[1,4,48,768]{3,2,1,0:T(8,128)(2,1)S(1)}, u32[]{:S(2)}, u32[]{:S(2)}) %collective-permute-start.22) | collective-permute-done | bytes 294944 | tf_op jit(solution)/shard_map/ppermute | solution.py:140
  92.0 1.1 collective-permute-start.25
  93.3 2.7 %fusion.15 = (f32[2,128]{1,0:T(2,128)S(1)}, f32[1536]{0:T(1024)S(1)}, f32[2,128,1536]{2,1,0:T(8,128)}) fusion(bf16[2,128,1536]{2,1,0:T(8,128)(2,1)S(1)} %copy-done, f32[1536]{0:T(1024)S(1)} %copy-done.3, f32[2,128]{1,0:T(2,128)S(1)} %fusion.54, f32[2,128,1536]{2,1,0:T(8,128)S(1)} %bitcast.152), kind=kLoop, calls=%fused_computation.26 | loop fusion | flops 10615040 | bytes 3946496 | tf_op jit(solution)/shard_map/transpose(jvp())/reduce_sum | solution.py:33
  96.0 1.8 %collective-permute-start.27 = (bf16[1,2,48,768]{3,2,1,0:T(8,128)(2,1)S(1)}, bf16[1,2,48,768]{3,2,1,0:T(8,128)(2,1)S(1)}, u32[]{:S(2)}, u32[]{:S(2)}) collective-permute-start(bf16[1,2,48,768]{3,2,1,0:T(8,128)(2,1)S(1)} %get-tuple-element.89), channel_id=1, source_target_pairs={{0,16},{1,17},{2,18},{3,19},{4,20},{5,21},{6,22},{7,23},{8,24},{9,... | collective-permute-start | bytes 442376 | tf_op jit(solution)/shard_map/ppermute | solution.py:140
  97.8 1.4 collective-permute-done.25.refs_3_
  99.2 7.1 %collective-permute-done.27.refs_5_ = bf16[1,2,48,768]{3,2,1,0:T(8,128)(2,1)S(1)} collective-permute-done((bf16[1,2,48,768]{3,2,1,0:T(8,128)(2,1)S(1)}, bf16[1,2,48,768]{3,2,1,0:T(8,128)(2,1)S(1)}, u32[]{:S(2)}, u32[]{:S(2)}) %collective-permute-start.27) | collective-permute-done | bytes 147488 | tf_op jit(solution)/shard_map/ppermute | solution.py:140
  106.3 1.0 fold.5
  107.4 1.0 collective-permute-start.28
  108.4 2.7 %collective-permute-start.31 = (bf16[1,2,48,768]{3,2,1,0:T(8,128)(2,1)S(1)}, bf16[1,2,48,768]{3,2,1,0:T(8,128)(2,1)S(1)}, u32[]{:S(2)}, u32[]{:S(2)}) collective-permute-start(bf16[1,2,48,768]{3,2,1,0:T(8,128)(2,1)S(1)} %get-tuple-element.103), channel_id=1, source_target_pairs={{0,16},{1,17},{2,18},{3,19},{4,20},{5,21},{6,22},{7,23},{8,24},{9,... | collective-permute-start | bytes 442376 | tf_op jit(solution)/shard_map/ppermute | solution.py:140
  111.6 2.2 %project_back.1 = bf16[256,1536]{1,0:T(8,128)(2,1)} custom-call(s32[1]{0:T(128)} %bitcast.index_ref, bf16[256,768]{1,0:T(8,128)(2,1)S(1)} %multiply_convert_fusion.hidden_ref, bf16[256,1536]{1,0:T(8,128)(2,1)S(1)} %bitcast.146, bf16[1,8,48,768]{3,2,1,0:T(8,128)(2,1)S(1)} %get-tuple-element.78.refs_0_, bf16[1,8,48,768]{3,2,1,0:T(8,128)(2,1)S(1)} %assemble.9.refs_1_, ...), custom_call_target="tpu_custom_call" | custom-call | tf_op jit(solution)/shard_map/project_back/pallas_call | solution.py:330
  113.8 3.7 %collective-permute-done.29 = f32[2304]{0:T(1024)S(1)} collective-permute-done((f32[2304]{0:T(1024)S(1)}, f32[2304]{0:T(1024)S(1)}, u32[]{:S(2)}, u32[]{:S(2)}) %collective-permute-start.29) | collective-permute-done | bytes 9248 | tf_op jit(solution)/shard_map/ppermute | solution.py:140
  117.5 1.6 %collective-permute-done.30.refs_3_ = bf16[1,4,48,768]{3,2,1,0:T(8,128)(2,1)S(1)} collective-permute-done((bf16[1,4,48,768]{3,2,1,0:T(8,128)(2,1)S(1)}, bf16[1,4,48,768]{3,2,1,0:T(8,128)(2,1)S(1)}, u32[]{:S(2)}, u32[]{:S(2)}) %collective-permute-start.30) | collective-permute-done | bytes 294944 | tf_op jit(solution)/shard_map/ppermute | solution.py:140
  119.1 0.9 fold.6
  120.0 1.7 %collective-permute-start.32 = (bf16[2,2,48,768]{3,2,1,0:T(8,128)(2,1)}, bf16[2,2,48,768]{3,2,1,0:T(8,128)(2,1)S(1)}, u32[]{:S(2)}, u32[]{:S(2)}) collective-permute-start(bf16[2,2,48,768]{3,2,1,0:T(8,128)(2,1)} %get-tuple-element.105), channel_id=1, source_target_pairs={{0,8},{1,9},{2,10},{3,11},{4,12},{5,13},{6,14},{7,15},{8,0},{9,1},... | collective-permute-start | bytes 884744 | tf_op jit(solution)/shard_map/ppermute | solution.py:140
  122.2 1.7 %collective-permute-start.34 = (bf16[1,2,48,768]{3,2,1,0:T(8,128)(2,1)}, bf16[1,2,48,768]{3,2,1,0:T(8,128)(2,1)S(1)}, u32[]{:S(2)}, u32[]{:S(2)}) collective-permute-start(bf16[1,2,48,768]{3,2,1,0:T(8,128)(2,1)} %get-tuple-element.109), channel_id=1, source_target_pairs={{0,16},{1,17},{2,18},{3,19},{4,20},{5,21},{6,22},{7,23},{8,24},{9,... | collective-permute-start | bytes 442376 | tf_op jit(solution)/shard_map/ppermute | solution.py:140
  124.0 1.5 %collective-permute-start.33 = (f32[2304]{0:T(1024)S(1)}, f32[2304]{0:T(1024)S(1)}, u32[]{:S(2)}, u32[]{:S(2)}) collective-permute-start(f32[2304]{0:T(1024)S(1)} %add.148), channel_id=1, source_target_pairs={{0,4},{1,5},{2,6},{3,7},{4,0},{5,1},{6,2},{7,3},{8,12},{9,13},{10,... | collective-permute-start | bytes 27656 | tf_op jit(solution)/shard_map/ppermute | solution.py:140
  125.4 2.2 %collective-permute-done.33 = f32[2304]{0:T(1024)S(1)} collective-permute-done((f32[2304]{0:T(1024)S(1)}, f32[2304]{0:T(1024)S(1)}, u32[]{:S(2)}, u32[]{:S(2)}) %collective-permute-start.33) | collective-permute-done | bytes 9248 | tf_op jit(solution)/shard_map/ppermute | solution.py:140
  127.7 3.3 %collective-permute-done.32.refs_1_ = bf16[2,2,48,768]{3,2,1,0:T(8,128)(2,1)S(1)} collective-permute-done((bf16[2,2,48,768]{3,2,1,0:T(8,128)(2,1)}, bf16[2,2,48,768]{3,2,1,0:T(8,128)(2,1)S(1)}, u32[]{:S(2)}, u32[]{:S(2)}) %collective-permute-start.32) | collective-permute-done | bytes 294944 | tf_op jit(solution)/shard_map/ppermute | solution.py:140
  131.1 2.1 %collective-permute-start.38 = (f32[2304]{0:T(1024)S(1)}, f32[2304]{0:T(1024)S(1)}, u32[]{:S(2)}, u32[]{:S(2)}) collective-permute-start(f32[2304]{0:T(1024)S(1)} %add.149), channel_id=1, source_target_pairs={{0,8},{1,9},{2,10},{3,11},{4,12},{5,13},{6,14},{7,15},{8,0},{9,1},... | collective-permute-start | bytes 27656 | tf_op jit(solution)/shard_map/ppermute | solution.py:140
  133.2 1.8 %collective-permute-start.36 = (bf16[2,1,48,768]{3,2,1,0:T(8,128)(2,1)S(1)}, bf16[2,1,48,768]{3,2,1,0:T(8,128)(2,1)S(1)}, u32[]{:S(2)}, u32[]{:S(2)}) collective-permute-start(bf16[2,1,48,768]{3,2,1,0:T(8,128)(2,1)S(1)} %get-tuple-element.114), channel_id=1, source_target_pairs={{0,16},{1,17},{2,18},{3,19},{4,20},{5,21},{6,22},{7,23},{8,24},{9,... | collective-permute-start | bytes 442376 | tf_op jit(solution)/shard_map/ppermute | solution.py:140
  134.9 2.6 %collective-permute-start.39 = (f32[2304]{0:T(1024)S(1)}, f32[2304]{0:T(1024)S(1)}, u32[]{:S(2)}, u32[]{:S(2)}) collective-permute-start(f32[2304]{0:T(1024)S(1)} %add.152), channel_id=1, source_target_pairs={{0,16},{1,17},{2,18},{3,19},{4,20},{5,21},{6,22},{7,23},{8,24},{9,... | collective-permute-start | bytes 27656 | tf_op jit(solution)/shard_map/ppermute | solution.py:140
  137.6 1.4 fusion.13
  139.7 1.4 collective-permute-done.39
  142.4 1.7 %collective-permute-done.37 = bf16[2,1,48,768]{3,2,1,0:T(8,128)(2,1)S(1)} collective-permute-done((bf16[2,1,48,768]{3,2,1,0:T(8,128)(2,1)S(1)}, bf16[2,1,48,768]{3,2,1,0:T(8,128)(2,1)S(1)}, u32[]{:S(2)}, u32[]{:S(2)}) %collective-permute-start.37) | collective-permute-done | bytes 147488 | tf_op jit(solution)/shard_map/ppermute | solution.py:140
  (102 shorter events, 21.0 us)
Async XLA Ops:
  0.6 13.8 %copy-start = (bf16[2,128,1536]{2,1,0:T(8,128)(2,1)S(1)}, bf16[2,128,1536]{2,1,0:T(8,128)(2,1)}, u32[]{:S(2)}) copy-start(bf16[2,128,1536]{2,1,0:T(8,128)(2,1)} %features_ref) | copy-start | bytes 2359300
  1.6 11.1 %collective-permute-start = (bf16[2,1,48,768]{3,2,0,1:T(8,128)(2,1)S(1)}, bf16[2,1,48,768]{3,2,0,1:T(8,128)(2,1)S(1)}, u32[]{:S(2)}, u32[]{:S(2)}) collective-permute-start(bf16[2,1,48,768]{3,2,0,1:T(8,128)(2,1)S(1)} %get-tuple-element.140), channel_id=1, source_target_pairs={{0,16},{1,17},{2,18},{3,19},{4,20},{5,21},{6,22},{7,23},{8,24},{9,... | collective-permute-start | bytes 442376 | tf_op jit(solution)/shard_map/ppermute | solution.py:140
  7.5 5.2 %collective-permute-start.1 = (bf16[2,1,48,768]{3,2,1,0:T(8,128)(2,1)S(1)}, bf16[2,1,48,768]{3,2,1,0:T(8,128)(2,1)S(1)}, u32[]{:S(2)}, u32[]{:S(2)}) collective-permute-start(bf16[2,1,48,768]{3,2,1,0:T(8,128)(2,1)S(1)} %pad_maximum_fusion.refs_2_), channel_id=1, source_target_pairs={{0,2},{1,5},{2,0},{3,7},{4,6},{5,1},{6,4},{7,3},{8,10},{9,13},{10,... | collective-permute-start | bytes 442376 | tf_op jit(solution)/shard_map/ppermute | solution.py:140
  12.8 11.0 %collective-permute-start.2 = (bf16[2,2,48,768]{3,2,1,0:T(8,128)(2,1)S(1)}, bf16[2,2,48,768]{3,2,1,0:T(8,128)(2,1)S(1)}, u32[]{:S(2)}, u32[]{:S(2)}) collective-permute-start(bf16[2,2,48,768]{3,2,1,0:T(8,128)(2,1)S(1)} %get-tuple-element.62.refs_0_), channel_id=1, source_target_pairs={{0,8},{1,9},{2,10},{3,11},{4,12},{5,13},{6,14},{7,15},{8,0},{9,1},... | collective-permute-start | bytes 884744 | tf_op jit(solution)/shard_map/ppermute | solution.py:140
  14.5 30.5 %copy-start.3 = (f32[1536]{0:T(1024)S(1)}, f32[1536]{0:T(1024)}, u32[]{:S(2)}) copy-start(f32[1536]{0:T(1024)} %param.10) | copy-start | bytes 18436
  14.5 30.5 %copy-start.1 = (bf16[2,128,1536]{2,1,0:T(8,128)(2,1)S(1)}, bf16[2,128,1536]{2,1,0:T(8,128)(2,1)}, u32[]{:S(2)}) copy-start(bf16[2,128,1536]{2,1,0:T(8,128)(2,1)} %param.7) | copy-start | bytes 2359300
  14.5 9.3 %collective-permute-start.4 = (bf16[2,32,1536]{2,1,0:T(8,128)(2,1)S(1)}, bf16[2,32,1536]{2,1,0:T(8,128)(2,1)S(1)}, u32[]{:S(2)}, u32[]{:S(2)}) collective-permute-start(bf16[2,32,1536]{2,1,0:T(8,128)(2,1)S(1)} %get-tuple-element.133), channel_id=1, source_target_pairs={{0,1},{1,0},{2,3},{3,2},{4,5},{5,4},{6,7},{7,6},{8,9},{9,8},{10,11... | collective-permute-start | bytes 589832 | tf_op jit(solution)/shard_map/ppermute | solution.py:140
  14.6 9.2 %collective-permute-start.5 = (bf16[2,32,1536]{2,1,0:T(8,128)(2,1)S(1)}, bf16[2,32,1536]{2,1,0:T(8,128)(2,1)S(1)}, u32[]{:S(2)}, u32[]{:S(2)}) collective-permute-start(bf16[2,32,1536]{2,1,0:T(8,128)(2,1)S(1)} %get-tuple-element.132), channel_id=1, source_target_pairs={{1,2},{2,1},{3,4},{4,3},{5,6},{6,5},{7,8},{8,7},{9,10},{10,9},{11,... | collective-permute-start | bytes 589832 | tf_op jit(solution)/shard_map/ppermute | solution.py:140
  15.4 8.4 %collective-permute-start.3 = (bf16[1,2,48,768]{3,2,1,0:T(8,128)(2,1)S(1)}, bf16[1,2,48,768]{3,2,1,0:T(8,128)(2,1)S(1)}, u32[]{:S(2)}, u32[]{:S(2)}) collective-permute-start(bf16[1,2,48,768]{3,2,1,0:T(8,128)(2,1)S(1)} %get-tuple-element.63.refs_4_), channel_id=1, source_target_pairs={{0,4},{1,3},{2,6},{3,1},{4,0},{5,7},{6,2},{7,5},{8,12},{9,11},{10,... | collective-permute-start | bytes 442376 | tf_op jit(solution)/shard_map/ppermute | solution.py:140
  19.6 10.8 %collective-permute-start.6 = (bf16[1,2,48,768]{3,2,1,0:T(8,128)(2,1)S(1)}, bf16[1,2,48,768]{3,2,1,0:T(8,128)(2,1)S(1)}, u32[]{:S(2)}, u32[]{:S(2)}) collective-permute-start(bf16[1,2,48,768]{3,2,1,0:T(8,128)(2,1)S(1)} %get-tuple-element.66.refs_2_), channel_id=1, source_target_pairs={{0,16},{1,17},{2,18},{3,19},{4,20},{5,21},{6,22},{7,23},{8,24},{9,... | collective-permute-start | bytes 442376 | tf_op jit(solution)/shard_map/ppermute | solution.py:140
  30.5 11.2 %collective-permute-start.7 = (bf16[2,4,48,768]{3,2,1,0:T(8,128)(2,1)S(1)}, bf16[2,4,48,768]{3,2,1,0:T(8,128)(2,1)S(1)}, u32[]{:S(2)}, u32[]{:S(2)}) collective-permute-start(bf16[2,4,48,768]{3,2,1,0:T(8,128)(2,1)S(1)} %get-tuple-element.67.refs_0_), channel_id=1, source_target_pairs={{0,2},{1,5},{2,0},{3,7},{4,6},{5,1},{6,4},{7,3},{8,10},{9,13},{10,... | collective-permute-start | bytes 1769480 | tf_op jit(solution)/shard_map/ppermute | solution.py:140
  30.6 11.1 %collective-permute-start.8 = (bf16[1,4,48,768]{3,2,1,0:T(8,128)(2,1)S(1)}, bf16[1,4,48,768]{3,2,1,0:T(8,128)(2,1)S(1)}, u32[]{:S(2)}, u32[]{:S(2)}) collective-permute-start(bf16[1,4,48,768]{3,2,1,0:T(8,128)(2,1)S(1)} %get-tuple-element.68.refs_2_), channel_id=1, source_target_pairs={{0,8},{1,9},{2,10},{3,11},{4,12},{5,13},{6,14},{7,15},{8,0},{9,1},... | collective-permute-start | bytes 884744 | tf_op jit(solution)/shard_map/ppermute | solution.py:140
  30.6 8.9 %collective-permute-start.9 = (bf16[1,2,48,768]{3,2,1,0:T(8,128)(2,1)S(1)}, bf16[1,2,48,768]{3,2,1,0:T(8,128)(2,1)S(1)}, u32[]{:S(2)}, u32[]{:S(2)}) collective-permute-start(bf16[1,2,48,768]{3,2,1,0:T(8,128)(2,1)S(1)} %get-tuple-element.63.refs_4_), channel_id=1, source_target_pairs={{0,16},{1,17},{2,18},{3,19},{4,20},{5,21},{6,22},{7,23},{8,24},{9,... | collective-permute-start | bytes 442376 | tf_op jit(solution)/shard_map/ppermute | solution.py:140
  41.8 15.2 %collective-permute-start.12 = (bf16[3,8,48,768]{3,2,1,0:T(8,128)(2,1)S(1)}, bf16[3,8,48,768]{3,2,1,0:T(8,128)(2,1)S(1)}, u32[]{:S(2)}, u32[]{:S(2)}) collective-permute-start(bf16[3,8,48,768]{3,2,1,0:T(8,128)(2,1)S(1)} %get-tuple-element.75.refs_0_), channel_id=1, source_target_pairs={{0,1},{1,0},{2,3},{3,2},{4,5},{5,4},{6,7},{7,6},{8,9},{9,8},{10,11... | collective-permute-start | bytes 5308424 | tf_op jit(solution)/shard_map/ppermute | solution.py:140
  41.9 12.6 %collective-permute-start.10 = (bf16[1,4,48,768]{3,2,1,0:T(8,128)(2,1)S(1)}, bf16[1,4,48,768]{3,2,1,0:T(8,128)(2,1)S(1)}, u32[]{:S(2)}, u32[]{:S(2)}) collective-permute-start(bf16[1,4,48,768]{3,2,1,0:T(8,128)(2,1)S(1)} %get-tuple-element.72.refs_0_), channel_id=1, source_target_pairs={{0,8},{1,9},{2,10},{3,11},{4,12},{5,13},{6,14},{7,15},{8,0},{9,1},... | collective-permute-start | bytes 884744 | tf_op jit(solution)/shard_map/ppermute | solution.py:140
  42.1 12.4 %collective-permute-start.11 = (bf16[1,2,48,768]{3,2,1,0:T(8,128)(2,1)S(1)}, bf16[1,2,48,768]{3,2,1,0:T(8,128)(2,1)S(1)}, u32[]{:S(2)}, u32[]{:S(2)}) collective-permute-start(bf16[1,2,48,768]{3,2,1,0:T(8,128)(2,1)S(1)} %collective-permute-done.3.refs_2_), channel_id=1, source_target_pairs={{0,16},{1,17},{2,18},{3,19},{4,20},{5,21},{6,22},{7,23},{8,24},{9,... | collective-permute-start | bytes 442376 | tf_op jit(solution)/shard_map/ppermute | solution.py:140
  43.8 22.5 %collective-permute-start.13 = (bf16[3,8,48,768]{3,2,1,0:T(8,128)(2,1)S(1)}, bf16[3,8,48,768]{3,2,1,0:T(8,128)(2,1)S(1)}, u32[]{:S(2)}, u32[]{:S(2)}) collective-permute-start(bf16[3,8,48,768]{3,2,1,0:T(8,128)(2,1)S(1)} %get-tuple-element.75.refs_0_), channel_id=1, source_target_pairs={{0,4},{1,3},{2,6},{3,1},{4,0},{5,7},{6,2},{7,5},{8,12},{9,11},{10,... | collective-permute-start | bytes 5308424 | tf_op jit(solution)/shard_map/ppermute | solution.py:140
  54.6 2.1 %collective-permute-start.15 = (bf16[1,8,48,768]{3,2,1,0:T(8,128)(2,1)S(1)}, bf16[1,8,48,768]{3,2,1,0:T(8,128)(2,1)S(1)}, u32[]{:S(2)}, u32[]{:S(2)}) collective-permute-start(bf16[1,8,48,768]{3,2,1,0:T(8,128)(2,1)S(1)} %get-tuple-element.78.refs_0_), channel_id=1, source_target_pairs={{0,1},{1,0},{2,3},{3,2},{4,5},{5,4},{6,7},{7,6},{8,9},{9,8},{10,11... | collective-permute-start | bytes 1769480 | tf_op jit(solution)/shard_map/ppermute | solution.py:140
  54.9 9.5 %collective-permute-start.14 = (bf16[1,4,48,768]{3,2,1,0:T(8,128)(2,1)S(1)}, bf16[1,4,48,768]{3,2,1,0:T(8,128)(2,1)S(1)}, u32[]{:S(2)}, u32[]{:S(2)}) collective-permute-start(bf16[1,4,48,768]{3,2,1,0:T(8,128)(2,1)S(1)} %get-tuple-element.74.refs_0_), channel_id=1, source_target_pairs={{0,8},{1,9},{2,10},{3,11},{4,12},{5,13},{6,14},{7,15},{8,0},{9,1},... | collective-permute-start | bytes 884744 | tf_op jit(solution)/shard_map/ppermute | solution.py:140
  66.4 4.9 %collective-permute-start.16 = (bf16[3,8,48,768]{3,2,1,0:T(8,128)(2,1)S(1)}, bf16[3,8,48,768]{3,2,1,0:T(8,128)(2,1)S(1)}, u32[]{:S(2)}, u32[]{:S(2)}) collective-permute-start(bf16[3,8,48,768]{3,2,1,0:T(8,128)(2,1)S(1)} %collective-permute-done.13.refs_1_), channel_id=1, source_target_pairs={{0,1},{1,0},{2,3},{3,2},{4,5},{5,4},{6,7},{7,6},{8,9},{9,8},{10,11... | collective-permute-start | bytes 5308424 | tf_op jit(solution)/shard_map/ppermute | solution.py:140
  66.5 4.4 %collective-permute-start.17 = (bf16[1,8,48,768]{3,2,1,0:T(8,128)(2,1)S(1)}, bf16[1,8,48,768]{3,2,1,0:T(8,128)(2,1)S(1)}, u32[]{:S(2)}, u32[]{:S(2)}) collective-permute-start(bf16[1,8,48,768]{3,2,1,0:T(8,128)(2,1)S(1)} %assemble.9.refs_1_), channel_id=1, source_target_pairs={{0,1},{1,0},{2,3},{3,2},{4,5},{5,4},{6,7},{7,6},{8,9},{9,8},{10,11... | collective-permute-start | bytes 1769480 | tf_op jit(solution)/shard_map/ppermute | solution.py:140
  71.3 0.8 copy-start.4
  74.7 3.8 %collective-permute-start.18 = (bf16[3,8,48,768]{3,2,1,0:T(8,128)(2,1)S(1)}, bf16[3,8,48,768]{3,2,1,0:T(8,128)(2,1)S(1)}, u32[]{:S(2)}, u32[]{:S(2)}) collective-permute-start(bf16[3,8,48,768]{3,2,1,0:T(8,128)(2,1)S(1)} %convolution_convert_fusion.1), channel_id=1, source_target_pairs={{0,1},{1,0},{2,3},{3,2},{4,5},{5,4},{6,7},{7,6},{8,9},{9,8},{10,11... | collective-permute-start | bytes 5308424 | tf_op jit(solution)/shard_map/ppermute | solution.py:140
  75.0 8.8 %collective-permute-start.19 = (bf16[2,8,48,768]{3,2,1,0:T(8,128)(2,1)S(1)}, bf16[2,8,48,768]{3,2,1,0:T(8,128)(2,1)S(1)}, u32[]{:S(2)}, u32[]{:S(2)}) collective-permute-start(bf16[2,8,48,768]{3,2,1,0:T(8,128)(2,1)S(1)} %convolution_convert_fusion.2), channel_id=1, source_target_pairs={{0,1},{1,0},{2,3},{3,2},{4,5},{5,4},{6,7},{7,6},{8,9},{9,8},{10,11... | collective-permute-start | bytes 3538952 | tf_op jit(solution)/shard_map/ppermute | solution.py:140
  75.9 9.0 %collective-permute-start.20 = (bf16[3,8,48,768]{3,2,1,0:T(8,128)(2,1)S(1)}, bf16[3,8,48,768]{3,2,1,0:T(8,128)(2,1)S(1)}, u32[]{:S(2)}, u32[]{:S(2)}) collective-permute-start(bf16[3,8,48,768]{3,2,1,0:T(8,128)(2,1)S(1)} %convolution_convert_fusion), channel_id=1, source_target_pairs={{0,1},{1,0},{2,3},{3,2},{4,5},{5,4},{6,7},{7,6},{8,9},{9,8},{10,11... | collective-permute-start | bytes 5308424 | tf_op jit(solution)/shard_map/ppermute | solution.py:140
  76.2 9.4 %collective-permute-start.23 = (bf16[2,32,768]{2,1,0:T(8,128)(2,1)S(1)}, bf16[2,32,768]{2,1,0:T(8,128)(2,1)S(1)}, u32[]{:S(2)}, u32[]{:S(2)}) collective-permute-start(bf16[2,32,768]{2,1,0:T(8,128)(2,1)S(1)} %get-tuple-element.135), channel_id=1, source_target_pairs={{0,1},{1,0},{2,3},{3,2},{4,5},{5,4},{6,7},{7,6},{8,9},{9,8},{10,11... | collective-permute-start | bytes 294920 | tf_op jit(solution)/shard_map/ppermute | solution.py:140
  76.6 9.0 %collective-permute-start.24 = (bf16[2,32,768]{2,1,0:T(8,128)(2,1)S(1)}, bf16[2,32,768]{2,1,0:T(8,128)(2,1)S(1)}, u32[]{:S(2)}, u32[]{:S(2)}) collective-permute-start(bf16[2,32,768]{2,1,0:T(8,128)(2,1)S(1)} %get-tuple-element.134), channel_id=1, source_target_pairs={{1,2},{2,1},{3,4},{4,3},{5,6},{6,5},{7,8},{8,7},{9,10},{10,9},{11,... | collective-permute-start | bytes 294920 | tf_op jit(solution)/shard_map/ppermute | solution.py:140
  79.1 27.2 %collective-permute-start.21 = (bf16[3,8,48,768]{3,2,1,0:T(8,128)(2,1)S(1)}, bf16[3,8,48,768]{3,2,1,0:T(8,128)(2,1)S(1)}, u32[]{:S(2)}, u32[]{:S(2)}) collective-permute-start(bf16[3,8,48,768]{3,2,1,0:T(8,128)(2,1)S(1)} %add_convert_fusion), channel_id=1, source_target_pairs={{0,4},{1,3},{2,6},{3,1},{4,0},{5,7},{6,2},{7,5},{8,12},{9,11},{10,... | collective-permute-start | bytes 5308424 | tf_op jit(solution)/shard_map/ppermute | solution.py:140
  84.0 7.9 %collective-permute-start.22 = (bf16[1,4,48,768]{3,2,1,0:T(8,128)(2,1)S(1)}, bf16[1,4,48,768]{3,2,1,0:T(8,128)(2,1)S(1)}, u32[]{:S(2)}, u32[]{:S(2)}) collective-permute-start(bf16[1,4,48,768]{3,2,1,0:T(8,128)(2,1)S(1)} %fusion.20), channel_id=1, source_target_pairs={{0,8},{1,9},{2,10},{3,11},{4,12},{5,13},{6,14},{7,15},{8,0},{9,1},... | collective-permute-start | bytes 884744 | tf_op jit(solution)/shard_map/ppermute | solution.py:140
  92.0 7.3 %collective-permute-start.25 = (bf16[1,4,48,768]{3,2,1,0:T(8,128)(2,1)S(1)}, bf16[1,4,48,768]{3,2,1,0:T(8,128)(2,1)S(1)}, u32[]{:S(2)}, u32[]{:S(2)}) collective-permute-start(bf16[1,4,48,768]{3,2,1,0:T(8,128)(2,1)S(1)} %fusion.21), channel_id=1, source_target_pairs={{0,8},{1,9},{2,10},{3,11},{4,12},{5,13},{6,14},{7,15},{8,0},{9,1},... | collective-permute-start | bytes 884744 | tf_op jit(solution)/shard_map/ppermute | solution.py:140
  96.0 1.8 %collective-permute-start.26 = (f32[2304]{0:T(1024)S(1)}, f32[2304]{0:T(1024)S(1)}, u32[]{:S(2)}, u32[]{:S(2)}) collective-permute-start(f32[2304]{0:T(1024)S(1)} %maximum_multiply_fusion.1), channel_id=1, source_target_pairs={{0,1},{1,0},{2,3},{3,2},{4,5},{5,4},{6,7},{7,6},{8,9},{9,8},{10,11... | collective-permute-start | bytes 27656 | tf_op jit(solution)/shard_map/ppermute | solution.py:140
  96.0 10.3 %collective-permute-start.27 = (bf16[1,2,48,768]{3,2,1,0:T(8,128)(2,1)S(1)}, bf16[1,2,48,768]{3,2,1,0:T(8,128)(2,1)S(1)}, u32[]{:S(2)}, u32[]{:S(2)}) collective-permute-start(bf16[1,2,48,768]{3,2,1,0:T(8,128)(2,1)S(1)} %get-tuple-element.89), channel_id=1, source_target_pairs={{0,16},{1,17},{2,18},{3,19},{4,20},{5,21},{6,22},{7,23},{8,24},{9,... | collective-permute-start | bytes 442376 | tf_op jit(solution)/shard_map/ppermute | solution.py:140
  107.4 10.2 %collective-permute-start.28 = (bf16[2,4,48,768]{3,2,1,0:T(8,128)(2,1)S(1)}, bf16[2,4,48,768]{3,2,1,0:T(8,128)(2,1)S(1)}, u32[]{:S(2)}, u32[]{:S(2)}) collective-permute-start(bf16[2,4,48,768]{3,2,1,0:T(8,128)(2,1)S(1)} %get-tuple-element.94), channel_id=1, source_target_pairs={{0,2},{1,5},{2,0},{3,7},{4,6},{5,1},{6,4},{7,3},{8,10},{9,13},{10,... | collective-permute-start | bytes 1769480 | tf_op jit(solution)/shard_map/ppermute | solution.py:140
  108.4 10.7 %collective-permute-start.30 = (bf16[1,4,48,768]{3,2,1,0:T(8,128)(2,1)S(1)}, bf16[1,4,48,768]{3,2,1,0:T(8,128)(2,1)S(1)}, u32[]{:S(2)}, u32[]{:S(2)}) collective-permute-start(bf16[1,4,48,768]{3,2,1,0:T(8,128)(2,1)S(1)} %get-tuple-element.101), channel_id=1, source_target_pairs={{0,8},{1,9},{2,10},{3,11},{4,12},{5,13},{6,14},{7,15},{8,0},{9,1},... | collective-permute-start | bytes 884744 | tf_op jit(solution)/shard_map/ppermute | solution.py:140
  108.4 9.1 %collective-permute-start.31 = (bf16[1,2,48,768]{3,2,1,0:T(8,128)(2,1)S(1)}, bf16[1,2,48,768]{3,2,1,0:T(8,128)(2,1)S(1)}, u32[]{:S(2)}, u32[]{:S(2)}) collective-permute-start(bf16[1,2,48,768]{3,2,1,0:T(8,128)(2,1)S(1)} %get-tuple-element.103), channel_id=1, source_target_pairs={{0,16},{1,17},{2,18},{3,19},{4,20},{5,21},{6,22},{7,23},{8,24},{9,... | collective-permute-start | bytes 442376 | tf_op jit(solution)/shard_map/ppermute | solution.py:140
  111.1 6.4 %collective-permute-start.29 = (f32[2304]{0:T(1024)S(1)}, f32[2304]{0:T(1024)S(1)}, u32[]{:S(2)}, u32[]{:S(2)}) collective-permute-start(f32[2304]{0:T(1024)S(1)} %fusion.55), channel_id=1, source_target_pairs={{0,2},{1,3},{2,0},{3,1},{4,6},{5,7},{6,4},{7,5},{8,10},{9,11},{10,... | collective-permute-start | bytes 27656 | tf_op jit(solution)/shard_map/ppermute | solution.py:140
  120.0 10.9 %collective-permute-start.32 = (bf16[2,2,48,768]{3,2,1,0:T(8,128)(2,1)}, bf16[2,2,48,768]{3,2,1,0:T(8,128)(2,1)S(1)}, u32[]{:S(2)}, u32[]{:S(2)}) collective-permute-start(bf16[2,2,48,768]{3,2,1,0:T(8,128)(2,1)} %get-tuple-element.105), channel_id=1, source_target_pairs={{0,8},{1,9},{2,10},{3,11},{4,12},{5,13},{6,14},{7,15},{8,0},{9,1},... | collective-permute-start | bytes 884744 | tf_op jit(solution)/shard_map/ppermute | solution.py:140
  121.7 9.3 %collective-permute-start.35 = (bf16[1,2,48,768]{3,2,1,0:T(8,128)(2,1)S(1)}, bf16[1,2,48,768]{3,2,1,0:T(8,128)(2,1)S(1)}, u32[]{:S(2)}, u32[]{:S(2)}) collective-permute-start(bf16[1,2,48,768]{3,2,1,0:T(8,128)(2,1)S(1)} %get-tuple-element.112), channel_id=1, source_target_pairs={{0,4},{1,3},{2,6},{3,1},{4,0},{5,7},{6,2},{7,5},{8,12},{9,11},{10,... | collective-permute-start | bytes 442376 | tf_op jit(solution)/shard_map/ppermute | solution.py:140
  122.2 8.7 %collective-permute-start.34 = (bf16[1,2,48,768]{3,2,1,0:T(8,128)(2,1)}, bf16[1,2,48,768]{3,2,1,0:T(8,128)(2,1)S(1)}, u32[]{:S(2)}, u32[]{:S(2)}) collective-permute-start(bf16[1,2,48,768]{3,2,1,0:T(8,128)(2,1)} %get-tuple-element.109), channel_id=1, source_target_pairs={{0,16},{1,17},{2,18},{3,19},{4,20},{5,21},{6,22},{7,23},{8,24},{9,... | collective-permute-start | bytes 442376 | tf_op jit(solution)/shard_map/ppermute | solution.py:140
  124.0 3.7 %collective-permute-start.33 = (f32[2304]{0:T(1024)S(1)}, f32[2304]{0:T(1024)S(1)}, u32[]{:S(2)}, u32[]{:S(2)}) collective-permute-start(f32[2304]{0:T(1024)S(1)} %add.148), channel_id=1, source_target_pairs={{0,4},{1,5},{2,6},{3,7},{4,0},{5,1},{6,2},{7,3},{8,12},{9,13},{10,... | collective-permute-start | bytes 27656 | tf_op jit(solution)/shard_map/ppermute | solution.py:140
  125.4 12.1 %copy-start.2 = (f32[2,128,1536]{2,1,0:T(8,128)S(1)}, f32[2,128,1536]{2,1,0:T(8,128)}, u32[]{:S(2)}) copy-start(f32[2,128,1536]{2,1,0:T(8,128)} %get-tuple-element.122) | copy-start | bytes 4718596
  131.1 3.9 %collective-permute-start.38 = (f32[2304]{0:T(1024)S(1)}, f32[2304]{0:T(1024)S(1)}, u32[]{:S(2)}, u32[]{:S(2)}) collective-permute-start(f32[2304]{0:T(1024)S(1)} %add.149), channel_id=1, source_target_pairs={{0,8},{1,9},{2,10},{3,11},{4,12},{5,13},{6,14},{7,15},{8,0},{9,1},... | collective-permute-start | bytes 27656 | tf_op jit(solution)/shard_map/ppermute | solution.py:140
  133.2 9.1 %collective-permute-start.36 = (bf16[2,1,48,768]{3,2,1,0:T(8,128)(2,1)S(1)}, bf16[2,1,48,768]{3,2,1,0:T(8,128)(2,1)S(1)}, u32[]{:S(2)}, u32[]{:S(2)}) collective-permute-start(bf16[2,1,48,768]{3,2,1,0:T(8,128)(2,1)S(1)} %get-tuple-element.114), channel_id=1, source_target_pairs={{0,16},{1,17},{2,18},{3,19},{4,20},{5,21},{6,22},{7,23},{8,24},{9,... | collective-permute-start | bytes 442376 | tf_op jit(solution)/shard_map/ppermute | solution.py:140
  134.9 6.2 %collective-permute-start.39 = (f32[2304]{0:T(1024)S(1)}, f32[2304]{0:T(1024)S(1)}, u32[]{:S(2)}, u32[]{:S(2)}) collective-permute-start(f32[2304]{0:T(1024)S(1)} %add.152), channel_id=1, source_target_pairs={{0,16},{1,17},{2,18},{3,19},{4,20},{5,21},{6,22},{7,23},{8,24},{9,... | collective-permute-start | bytes 27656 | tf_op jit(solution)/shard_map/ppermute | solution.py:140
  139.0 5.1 %collective-permute-start.37 = (bf16[2,1,48,768]{3,2,1,0:T(8,128)(2,1)S(1)}, bf16[2,1,48,768]{3,2,1,0:T(8,128)(2,1)S(1)}, u32[]{:S(2)}, u32[]{:S(2)}) collective-permute-start(bf16[2,1,48,768]{3,2,1,0:T(8,128)(2,1)S(1)} %get-tuple-element.116), channel_id=1, source_target_pairs={{0,2},{1,5},{2,0},{3,7},{4,6},{5,1},{6,4},{7,3},{8,10},{9,13},{10,... | collective-permute-start | bytes 442376 | tf_op jit(solution)/shard_map/ppermute | solution.py:140

commit v6 on v5

--- a/solution.py
+++ b/solution.py
@@ -228,17 +228,14 @@
 def prepare_kernel(
     index_ref,
     features_ref,
-    core_ref,
-    outer_ref,
     cotangent_ref,
     gain_ref,
-    taps_ref,
-    project_ref,
-    active,
-    turned,
+    *refs,
 ):
     device = index_ref[0]
     batch, bins, channels = features_ref.shape
+    core_refs, outer_refs = refs[:batch], refs[batch : 2 * batch]
+    taps_ref, project_ref, active, turned = refs[2 * batch :]
     rows = taps_ref.shape[4]
     width = DILATION_STEP
     gain = gain_ref[...]
@@ -260,8 +257,8 @@
             return carry
 
         lax.fori_loop(0, bins // width, some_rows, 0)
-        active[b, pl.ds(core_at, width), :] = activate(core_ref[b])
-        active[b, pl.ds(outer_at, width), :] = activate(outer_ref[b])
+        active[b, pl.ds(core_at, width), :] = activate(core_refs[b][0])
+        active[b, pl.ds(outer_at, width), :] = activate(outer_refs[b][0])
 
     def blocks(order):
         for other in BITS:
@@ -288,7 +285,7 @@
     return pl.pallas_call(
         prepare_kernel,
         out_shape=[shape(KERNEL_TAPS), shape(1)],
-        in_specs=[SMEM] + [VMEM] * 5,
+        in_specs=[SMEM] + [VMEM] * (3 + 2 * batch),
         out_specs=[VMEM] * 2,
         scratch_shapes=[
             pltpu.VMEM((batch, bins + 2 * DILATION_STEP, channels), jnp.bfloat16),
@@ -296,7 +293,7 @@
         ],
         compiler_params=pltpu.CompilerParams(vmem_limit_bytes=16 << 20),
         name="prepare",
-    )(device_index(), features, *edges_of, cotangent, gain.reshape(1, channels))
+    )(device_index(), features, cotangent, gain.reshape(1, channels), *edges_of)
 
 
 def place_products(device, parts, turned, orders, placed):
@@ -411,17 +408,18 @@
     )
     pair_in, last_in, proj_b = send(pair, Z_NEAR), send(last, Z_FAR), send(proj, SECOND)
     parity = lax.axis_index("seq") & 1
-    feature_edges = edge_swaps(after(features, pair), parity)
+    feature_edges = list(
+        zip(*(edge_swaps(after(features, pair)[b : b + 1], parity) for b in range(batch)))
+    )
+    feature_edges = [array for side in feature_edges for array in side]
     grow = lambda m, n, a: (m, 2 * n, ((a, 0, m, 0, 0), (a + 1, 0, m, 0, n)))
     pair_in = after(pair_in, proj_b, *feature_edges)
     pair, last = assemble((pair, pair_in, last, last_in), (grow(2, 2, 0), grow(1, 2, 2)))
     pair_in, last_in, proj_in = send(pair, FIRST), send(last, Z_NEAR), send(proj, Z_FAR)
-    near, proj_a = assemble(
-        (pair, pair_in, last, last_in, proj, proj_in),
-        (
-            (3, 8, ((0, 0, 2, 0, 0), (1, 0, 2, 0, 4), (2, 0, 1, 2, 0), (3, 0, 1, 2, 4))),
-            grow(1, 2, 4),
-        ),
+    (proj_a,) = assemble((proj, proj_in), (grow(1, 2, 0),))
+    (near,) = assemble(
+        after((pair, pair_in, last, last_in), proj_a),
+        ((3, 8, ((0, 0, 2, 0, 0), (1, 0, 2, 0, 4), (2, 0, 1, 2, 0), (3, 0, 1, 2, 4))),),
     )
     far, near_other = send(near, SECOND), send(near, CORE)
     proj_in, proj_b_in = send(proj_a, Z_NEAR), send(proj_b, Z_FAR)
@@ -429,17 +427,16 @@
     act, act_p = prepare(
         after(features, near), feature_edges, flat_cotangent, outer_gain, rows
     )
-    proj_a, proj_b = assemble(
-        (proj_a, after(proj_in, act), proj_b, proj_b_in), (grow(1, 4, 0), grow(1, 2, 2))
-    )
-    proj_b_in, proj_a_other = send(proj_b, Z_NEAR), send(proj_a, CORE)
-    conv_output = contract(act[0, 0], after(near, proj_b)) + contract(act[1, 0], near_other)
-    grad_hidden = contract(act_p[0, 0], after(proj_a, conv_output)) + contract(
-        act_p[1, 0], proj_a_other
-    )
+    (proj_b,) = assemble((proj_b, after(proj_b_in, act)), (grow(1, 2, 0),))
+    proj_b_in = send(proj_b, Z_NEAR)
+    conv_output = contract(act[0, 0], after(near, proj_b))
+    (proj_a,) = assemble((proj_a, after(proj_in, conv_output)), (grow(1, 4, 0),))
+    proj_a_other = send(proj_a, CORE)
+    grad_hidden = contract(act_p[0, 0], proj_a) + contract(act_p[1, 0], proj_a_other)
     (proj_b,) = assemble((proj_b, after(proj_b_in, grad_hidden)), (grow(1, 4, 0),))
     proj_b_other = send(proj_b, CORE)
-    far = after(far, proj_b)
+    far = after(far, conv_output, proj_b)
+    conv_output = conv_output + contract(act[1, 0], after(near_other, far))
     far_other = send(far, CORE)
     conv_output = conv_output + contract(act[0, 1], far) + contract(act[1, 1], far_other)
     grad_hidden = (
@@ -447,15 +444,17 @@
     )
     hidden32, pull_inner = jax.vjp(act_norm, conv_output, inner_gain)
     hidden = as_bf16(hidden32)
-    give_p = as_bf16(rows_dot(act_p[1].reshape(2, HALF, rows, tokens), hidden))
-    recv_p = send(give_p, CORE)
-    grad_conv, grad_gain_inner = pull_inner(after(grad_hidden, give_p))
+    grad_conv, grad_gain_inner = pull_inner(grad_hidden)
     grad_conv = as_bf16(grad_conv)
 
     give = as_bf16(rows_dot(act[1, 1], grad_conv))
     recv_far = send(give, CORE)
     give = as_bf16(rows_dot(act[1, 0], after(grad_conv, give)))
     recv_near = send(give, CORE)
+    give = as_bf16(
+        rows_dot(act_p[1].reshape(2, HALF, rows, tokens), after(hidden, give))
+    )
+    recv_p = send(give, CORE)
     grad_edges = edge_swaps(after(grad_conv, give).reshape(batch, bin_count, inner), parity)
     message = as_bf16(rows_dot(act[0, 1], after(grad_conv, give)) + as_f32(recv_far))
     recv = send(message, SECOND)
@@ -479,7 +478,11 @@
         after(grad_conv, kept), grad_edges, (near, far, near_other, far_other)
     )
     f32, bf16 = jnp.float32, jnp.bfloat16
-    recv_b = after(recv_b, grad_active)
+    unused, pull_outer = jax.vjp(act_norm, as_f32(after(features, grad_active)), outer_gain)
+    grad_branch, grad_gain_outer = pull_outer(grad_active.reshape(features.shape))
+    grad_features = as_bf16(as_f32(cotangent) + grad_branch)
+    gains = jnp.concatenate([grad_gain_outer, grad_gain_inner]) * factor
+    recv_b = after(recv_b, grad_features, gains)
     message_b, kept_b = fold(
         (kept_b, recv_b),
         (
@@ -489,10 +492,7 @@
     )
     recv_b = send(message_b, Z_FAR)
     recv_a = send(after(message_a, message_b), Z_NEAR)
-    unused, pull_outer = jax.vjp(act_norm, as_f32(after(features, message_b)), outer_gain)
-    grad_branch, grad_gain_outer = pull_outer(grad_active.reshape(features.shape))
-    grad_features = as_bf16(as_f32(cotangent) + grad_branch)
-    gains = jnp.concatenate([grad_gain_outer, grad_gain_inner]) * factor
+    gains = after(gains, message_b)
     gains = gains + send(gains, CORE)
 
     recv_a = after(recv_a, gains)
@@ -516,6 +516,7 @@
         after(hidden, message), flat, (proj_a, proj_b, proj_a_other, proj_b_other)
     ).reshape(features.shape)
     gains = after(gains, block_out)
+    gains = gains + send(gains, links(lambda i: i ^ 4))
 
     recv = after(recv, gains)
     message, message_l, kept, kept_l, kept_p = fold(
@@ -531,7 +532,7 @@
     message_p = after(message_p, message)
     recv, recv_l, recv_p = send(message, Z_NEAR), send(message_l, Z_FAR), send(message_p, SECOND)
     gains = after(gains, message)
-    gains = gains + send(gains, links(lambda i: i ^ 4))
+    gains = gains + send(gains, Z_NEAR)
 
     recv = after(recv, gains)
     message, message_r, kept, kept_r = fold(
@@ -545,7 +546,6 @@
     )
     recv, recv_r = send(message, Z_FAR), send(message_r, FIRST)
     gains = after(gains, message)
-    gains = gains + send(gains, Z_NEAR)
     gains = gains + send(gains, Z_FAR)
 
     sums = kept + as_f32(recv)

time: 146 us -> 141 us (0.966)
  waiting for transfers between devices: 65.7 us -> 58 us
  starting transfers between devices: 48.6 us -> 53.3 us
  other arithmetic: 8.25 us -> 6.47 us
    ppermute x40 -> x42, waiting for transfers between devices: 65.7 us -> 58 us  [send(): return lax.ppermute(block, 'seq', pairs)]
    ppermute x40 -> x42, starting transfers between devices: 48.6 us -> 53.3 us  [send(): return lax.ppermute(block, 'seq', pairs)]
    reduce_sum x2 -> x1, other arithmetic: 3.55 us -> 1.81 us  [act_norm(): values * lax.rsqrt(meansq + eps) * gain]
  transfers between devices with their start and end apart: 40 -> 42, of which waited for: 20 -> 18; matrix products, arithmetic and copies ran while one was open for 10% -> 10% of each run, Pallas kernels for 5% -> 6%
where the time goes in v6:
time: 141 us
  waiting for transfers between devices  58 us (41%)
  starting transfers between devices  53.3 us (38%)
  Pallas kernels  9.57 us (7%)
  matrix products  9.14 us (6%)
  other arithmetic  6.47 us (5%)
  local copies, waits for them, and re-layouts  3.52 us (2%)
    ppermute x42, waiting for transfers between devices, send(): return lax.ppermute(block, 'seq', pairs)  58 us
    ppermute x42, starting transfers between devices, send(): return lax.ppermute(block, 'seq', pairs)  53.3 us
    dot_general x8, matrix products, contract(): jnp.einsum('ct,ci->ti', left.reshape(-1, left.shape[-1]), right.reshape(-...  5.2 us
    dot_general x9, matrix products, rows_dot(): jnp.einsum('mnrt,ti->mnri', left, right, preferred_element_type=jnp.float32)  3.94 us
    pallas_call x1, Pallas kernels, prepare(): pl.pallas_call(prepare_kernel, out_shape=[shape(KERNEL_TAPS), shape(1)],...  2.95 us
  transfers between devices with their start and end apart: 42, of which 18 were waited for; matrix products, arithmetic and copies ran while one was open for 10% of the time, Pallas kernels for 6%

profile of v6, /device:TPU:0, one launch (start us, length us, event | category | flops | bytes accessed | tf_op | source)
XLA Modules:
  0.0 141.1 jit_solution(12838071529983130026)
XLA Ops:
  0.6 1.0 slice_bitcast_fusion.8
  1.6 4.1 %collective-permute-start = (bf16[2,1,48,768]{3,2,0,1:T(8,128)(2,1)S(1)}, bf16[2,1,48,768]{3,2,0,1:T(8,128)(2,1)S(1)}, u32[]{:S(2)}, u32[]{:S(2)}) collective-permute-start(bf16[2,1,48,768]{3,2,0,1:T(8,128)(2,1)S(1)} %get-tuple-element.149), channel_id=1, source_target_pairs={{0,16},{1,17},{2,18},{3,19},{4,20},{5,21},{6,22},{7,23},{8,24},{9,... | collective-permute-start | bytes 442376 | tf_op jit(solution)/shard_map/ppermute | solution.py:140
  5.8 0.9 slice_bitcast_fusion.9
  6.6 0.9 pad_maximum_fusion.refs_2_
  7.5 1.6 %collective-permute-start.1 = (bf16[2,1,48,768]{3,2,1,0:T(8,128)(2,1)S(1)}, bf16[2,1,48,768]{3,2,1,0:T(8,128)(2,1)S(1)}, u32[]{:S(2)}, u32[]{:S(2)}) collective-permute-start(bf16[2,1,48,768]{3,2,1,0:T(8,128)(2,1)S(1)} %pad_maximum_fusion.refs_2_), channel_id=1, source_target_pairs={{0,2},{1,5},{2,0},{3,7},{4,6},{5,1},{6,4},{7,3},{8,10},{9,13},{10,... | collective-permute-start | bytes 442376 | tf_op jit(solution)/shard_map/ppermute | solution.py:140
  9.1 3.7 %collective-permute-done = bf16[2,1,48,768]{3,2,0,1:T(8,128)(2,1)S(1)} collective-permute-done((bf16[2,1,48,768]{3,2,0,1:T(8,128)(2,1)S(1)}, bf16[2,1,48,768]{3,2,0,1:T(8,128)(2,1)S(1)}, u32[]{:S(2)}, u32[]{:S(2)}) %collective-permute-start) | collective-permute-done | bytes 147488 | tf_op jit(solution)/shard_map/ppermute | solution.py:140
  12.8 1.6 %collective-permute-start.2 = (bf16[2,2,48,768]{3,2,1,0:T(8,128)(2,1)S(1)}, bf16[2,2,48,768]{3,2,1,0:T(8,128)(2,1)S(1)}, u32[]{:S(2)}, u32[]{:S(2)}) collective-permute-start(bf16[2,2,48,768]{3,2,1,0:T(8,128)(2,1)S(1)} %get-tuple-element.64.refs_0_), channel_id=1, source_target_pairs={{0,8},{1,9},{2,10},{3,11},{4,12},{5,13},{6,14},{7,15},{8,0},{9,1},... | collective-permute-start | bytes 884744 | tf_op jit(solution)/shard_map/ppermute | solution.py:140
  15.2 1.5 %collective-permute-start.3 = (bf16[1,2,48,768]{3,2,1,0:T(8,128)(2,1)S(1)}, bf16[1,2,48,768]{3,2,1,0:T(8,128)(2,1)S(1)}, u32[]{:S(2)}, u32[]{:S(2)}) collective-permute-start(bf16[1,2,48,768]{3,2,1,0:T(8,128)(2,1)S(1)} %get-tuple-element.65.refs_0_), channel_id=1, source_target_pairs={{0,4},{1,3},{2,6},{3,1},{4,0},{5,7},{6,2},{7,5},{8,12},{9,11},{10,... | collective-permute-start | bytes 442376 | tf_op jit(solution)/shard_map/ppermute | solution.py:140
  16.7 2.5 %collective-permute-start.8 = (bf16[1,2,48,768]{3,2,1,0:T(8,128)(2,1)S(1)}, bf16[1,2,48,768]{3,2,1,0:T(8,128)(2,1)S(1)}, u32[]{:S(2)}, u32[]{:S(2)}) collective-permute-start(bf16[1,2,48,768]{3,2,1,0:T(8,128)(2,1)S(1)} %get-tuple-element.68.refs_2_), channel_id=1, source_target_pairs={{0,16},{1,17},{2,18},{3,19},{4,20},{5,21},{6,22},{7,23},{8,24},{9,... | collective-permute-start | bytes 442376 | tf_op jit(solution)/shard_map/ppermute | solution.py:140
  20.6 3.6 %collective-permute-done.2.refs_1_ = bf16[2,2,48,768]{3,2,1,0:T(8,128)(2,1)S(1)} collective-permute-done((bf16[2,2,48,768]{3,2,1,0:T(8,128)(2,1)S(1)}, bf16[2,2,48,768]{3,2,1,0:T(8,128)(2,1)S(1)}, u32[]{:S(2)}, u32[]{:S(2)}) %collective-permute-start.2) | collective-permute-done | bytes 294944 | tf_op jit(solution)/shard_map/ppermute | solution.py:140
  24.3 4.6 %collective-permute-start.9 = (bf16[2,4,48,768]{3,2,1,0:T(8,128)(2,1)S(1)}, bf16[2,4,48,768]{3,2,1,0:T(8,128)(2,1)S(1)}, u32[]{:S(2)}, u32[]{:S(2)}) collective-permute-start(bf16[2,4,48,768]{3,2,1,0:T(8,128)(2,1)S(1)} %get-tuple-element.71.refs_0_), channel_id=1, source_target_pairs={{0,2},{1,5},{2,0},{3,7},{4,6},{5,1},{6,4},{7,3},{8,10},{9,13},{10,... | collective-permute-start | bytes 1769480 | tf_op jit(solution)/shard_map/ppermute | solution.py:140
  28.9 2.3 %collective-permute-start.10 = (bf16[1,4,48,768]{3,2,1,0:T(8,128)(2,1)S(1)}, bf16[1,4,48,768]{3,2,1,0:T(8,128)(2,1)S(1)}, u32[]{:S(2)}, u32[]{:S(2)}) collective-permute-start(bf16[1,4,48,768]{3,2,1,0:T(8,128)(2,1)S(1)} %get-tuple-element.73.refs_2_), channel_id=1, source_target_pairs={{0,8},{1,9},{2,10},{3,11},{4,12},{5,13},{6,14},{7,15},{8,0},{9,1},... | collective-permute-start | bytes 884744 | tf_op jit(solution)/shard_map/ppermute | solution.py:140
  31.2 2.2 %collective-permute-start.11 = (bf16[1,2,48,768]{3,2,1,0:T(8,128)(2,1)S(1)}, bf16[1,2,48,768]{3,2,1,0:T(8,128)(2,1)S(1)}, u32[]{:S(2)}, u32[]{:S(2)}) collective-permute-start(bf16[1,2,48,768]{3,2,1,0:T(8,128)(2,1)S(1)} %get-tuple-element.65.refs_0_), channel_id=1, source_target_pairs={{0,16},{1,17},{2,18},{3,19},{4,20},{5,21},{6,22},{7,23},{8,24},{9,... | collective-permute-start | bytes 442376 | tf_op jit(solution)/shard_map/ppermute | solution.py:140
  34.1 6.5 %collective-permute-done.11.refs_1_ = bf16[1,2,48,768]{3,2,1,0:T(8,128)(2,1)S(1)} collective-permute-done((bf16[1,2,48,768]{3,2,1,0:T(8,128)(2,1)S(1)}, bf16[1,2,48,768]{3,2,1,0:T(8,128)(2,1)S(1)}, u32[]{:S(2)}, u32[]{:S(2)}) %collective-permute-start.11) | collective-permute-done | bytes 147488 | tf_op jit(solution)/shard_map/ppermute | solution.py:140
  40.6 3.3 %collective-permute-done.10.refs_3_ = bf16[1,4,48,768]{3,2,1,0:T(8,128)(2,1)S(1)} collective-permute-done((bf16[1,4,48,768]{3,2,1,0:T(8,128)(2,1)S(1)}, bf16[1,4,48,768]{3,2,1,0:T(8,128)(2,1)S(1)}, u32[]{:S(2)}, u32[]{:S(2)}) %collective-permute-start.10) | collective-permute-done | bytes 294944 | tf_op jit(solution)/shard_map/ppermute | solution.py:140
  44.0 1.2 collective-permute-start.14
  45.3 3.0 %prepare.1 = (bf16[2,2,3,8,48,256]{5,4,3,2,1,0:T(8,128)(2,1)S(1)}, bf16[2,2,1,8,48,256]{5,4,3,2,1,0:T(8,128)(2,1)S(1)}) custom-call(s32[1]{0:T(128)} %bitcast.index_ref, bf16[2,128,1536]{2,1,0:T(8,128)(2,1)S(1)} %copy-done, bf16[256,1536]{1,0:T(8,128)(2,1)S(1)} %bitcast.154, f32[1,1536]{1,0:T(1,128)S(1)} %reshape.155.gain_ref, ...), custom_call_target="tpu_custom_call" | custom-call | tf_op jit(solution)/shard_map/prepare/pallas_call | solution.py:285
  49.3 5.4 %collective-permute-done.16.refs_1_ = bf16[1,4,48,768]{3,2,1,0:T(8,128)(2,1)S(1)} collective-permute-done((bf16[1,4,48,768]{3,2,1,0:T(8,128)(2,1)S(1)}, bf16[1,4,48,768]{3,2,1,0:T(8,128)(2,1)S(1)}, u32[]{:S(2)}, u32[]{:S(2)}) %collective-permute-start.16) | collective-permute-done | bytes 294944 | tf_op jit(solution)/shard_map/ppermute | solution.py:140
  55.4 1.4 %collective-permute-done.17.refs_2_ = bf16[1,8,48,768]{3,2,1,0:T(8,128)(2,1)S(1)} collective-permute-done((bf16[1,8,48,768]{3,2,1,0:T(8,128)(2,1)S(1)}, bf16[1,8,48,768]{3,2,1,0:T(8,128)(2,1)S(1)}, u32[]{:S(2)}, u32[]{:S(2)}) %collective-permute-start.17) | collective-permute-done | bytes 589856 | tf_op jit(solution)/shard_map/ppermute | solution.py:140
  57.6 6.6 %collective-permute-done.15.refs_1_ = bf16[1,4,48,768]{3,2,1,0:T(8,128)(2,1)S(1)} collective-permute-done((bf16[1,4,48,768]{3,2,1,0:T(8,128)(2,1)S(1)}, bf16[1,4,48,768]{3,2,1,0:T(8,128)(2,1)S(1)}, u32[]{:S(2)}, u32[]{:S(2)}) %collective-permute-start.15) | collective-permute-done | bytes 294944 | tf_op jit(solution)/shard_map/ppermute | solution.py:140
  64.2 2.4 %collective-permute-done.14.refs_1_ = bf16[3,8,48,768]{3,2,1,0:T(8,128)(2,1)S(1)} collective-permute-done((bf16[3,8,48,768]{3,2,1,0:T(8,128)(2,1)S(1)}, bf16[3,8,48,768]{3,2,1,0:T(8,128)(2,1)S(1)}, u32[]{:S(2)}, u32[]{:S(2)}) %collective-permute-start.14) | collective-permute-done | bytes 1769504 | tf_op jit(solution)/shard_map/ppermute | solution.py:140
  67.1 4.0 %collective-permute-done.19.refs_3_ = bf16[1,8,48,768]{3,2,1,0:T(8,128)(2,1)S(1)} collective-permute-done((bf16[1,8,48,768]{3,2,1,0:T(8,128)(2,1)S(1)}, bf16[1,8,48,768]{3,2,1,0:T(8,128)(2,1)S(1)}, u32[]{:S(2)}, u32[]{:S(2)}) %collective-permute-start.19) | collective-permute-done | bytes 589856 | tf_op jit(solution)/shard_map/ppermute | solution.py:140
  73.8 1.1 multiply_reduce_fusion
  78.4 0.8 collective-permute-start.26
  80.5 3.9 %collective-permute-start.23 = (bf16[3,8,48,768]{3,2,1,0:T(8,128)(2,1)S(1)}, bf16[3,8,48,768]{3,2,1,0:T(8,128)(2,1)S(1)}, u32[]{:S(2)}, u32[]{:S(2)}) collective-permute-start(bf16[3,8,48,768]{3,2,1,0:T(8,128)(2,1)S(1)} %add_convert_fusion), channel_id=1, source_target_pairs={{0,4},{1,3},{2,6},{3,1},{4,0},{5,7},{6,2},{7,5},{8,12},{9,11},{10,... | collective-permute-start | bytes 5308424 | tf_op jit(solution)/shard_map/ppermute | solution.py:140
  86.8 2.7 %grad_active.1 = f32[256,1536]{1,0:T(8,128)S(1)} custom-call(s32[1]{0:T(128)} %bitcast.index_ref, bf16[256,768]{1,0:T(8,128)(2,1)S(1)} %get-tuple-element.90.grad_ref, bf16[2,32,768]{2,1,0:T(8,128)(2,1)S(1)} %collective-permute-done.25.core_ref, bf16[2,32,768]{2,1,0:T(8,128)(2,1)S(1)} %collective-permute-done.26.outer_ref, ...), custom_call_target="tpu_custom_call" | custom-call | tf_op jit(solution)/shard_map/grad_active/pallas_call | solution.py:361
  89.7 1.8 %fusion.8 = (f32[1536]{0:T(1024)S(1)}, f32[2,128]{1,0:T(2,128)S(1)}, f32[2,128,1536]{2,1,0:T(8,128)S(1)}) fusion(bf16[2,128,1536]{2,1,0:T(8,128)(2,1)S(1)} %copy-done, f32[2,128]{1,0:T(2,128)S(1)} %fusion.55, f32[1536]{0:T(1024)S(1)} %copy-done.2, f32[2,128,1536]{2,1,0:T(8,128)S(1)} %bitcast.152), kind=kLoop, calls=%fused_computation.19 | loop fusion | flops 10615040 | bytes 3946496 | tf_op jit(solution)/shard_map/transpose(jvp())/reduce_sum | solution.py:33
  91.6 1.4 fusion.13
  93.0 1.4 %collective-permute-start.27 = (bf16[1,4,48,768]{3,2,1,0:T(8,128)(2,1)S(1)}, bf16[1,4,48,768]{3,2,1,0:T(8,128)(2,1)S(1)}, u32[]{:S(2)}, u32[]{:S(2)}) collective-permute-start(bf16[1,4,48,768]{3,2,1,0:T(8,128)(2,1)S(1)} %fusion.22), channel_id=1, source_target_pairs={{0,8},{1,9},{2,10},{3,11},{4,12},{5,13},{6,14},{7,15},{8,0},{9,1},... | collective-permute-start | bytes 884744 | tf_op jit(solution)/shard_map/ppermute | solution.py:140
  94.5 1.4 collective-permute-start.29
  95.9 1.2 collective-permute-done.28
  97.1 7.1 %collective-permute-done.27.refs_3_ = bf16[1,4,48,768]{3,2,1,0:T(8,128)(2,1)S(1)} collective-permute-done((bf16[1,4,48,768]{3,2,1,0:T(8,128)(2,1)S(1)}, bf16[1,4,48,768]{3,2,1,0:T(8,128)(2,1)S(1)}, u32[]{:S(2)}, u32[]{:S(2)}) %collective-permute-start.27) | collective-permute-done | bytes 294944 | tf_op jit(solution)/shard_map/ppermute | solution.py:140
  104.9 1.1 fold.5
  106.0 1.9 %collective-permute-start.30 = (bf16[2,4,48,768]{3,2,1,0:T(8,128)(2,1)S(1)}, bf16[2,4,48,768]{3,2,1,0:T(8,128)(2,1)S(1)}, u32[]{:S(2)}, u32[]{:S(2)}) collective-permute-start(bf16[2,4,48,768]{3,2,1,0:T(8,128)(2,1)S(1)} %get-tuple-element.98), channel_id=1, source_target_pairs={{0,2},{1,5},{2,0},{3,7},{4,6},{5,1},{6,4},{7,3},{8,10},{9,13},{10,... | collective-permute-start | bytes 1769480 | tf_op jit(solution)/shard_map/ppermute | solution.py:140
  107.9 1.2 collective-permute-start.33
  109.8 1.1 collective-permute-start.31
  110.9 2.2 %project_back.1 = bf16[256,1536]{1,0:T(8,128)(2,1)} custom-call(s32[1]{0:T(128)} %bitcast.index_ref, bf16[256,768]{1,0:T(8,128)(2,1)S(1)} %get-tuple-element.99.hidden_ref, bf16[256,1536]{1,0:T(8,128)(2,1)S(1)} %bitcast.146, bf16[1,8,48,768]{3,2,1,0:T(8,128)(2,1)S(1)} %assemble.12.refs_0_, bf16[1,8,48,768]{3,2,1,0:T(8,128)(2,1)S(1)} %assemble.13.refs_1_, ...), custom_call_target="tpu_custom_call" | custom-call | tf_op jit(solution)/shard_map/project_back/pallas_call | solution.py:327
  113.1 3.1 %collective-permute-done.31 = f32[2304]{0:T(1024)S(1)} collective-permute-done((f32[2304]{0:T(1024)S(1)}, f32[2304]{0:T(1024)S(1)}, u32[]{:S(2)}, u32[]{:S(2)}) %collective-permute-start.31) | collective-permute-done | bytes 9248 | tf_op jit(solution)/shard_map/ppermute | solution.py:140
  116.1 2.0 %collective-permute-start.32 = (f32[2304]{0:T(1024)S(1)}, f32[2304]{0:T(1024)S(1)}, u32[]{:S(2)}, u32[]{:S(2)}) collective-permute-start(f32[2304]{0:T(1024)S(1)} %add.150), channel_id=1, source_target_pairs={{0,4},{1,5},{2,6},{3,7},{4,0},{5,1},{6,2},{7,3},{8,12},{9,13},{10,... | collective-permute-start | bytes 27656 | tf_op jit(solution)/shard_map/ppermute | solution.py:140
  118.2 1.7 %collective-permute-done.32 = f32[2304]{0:T(1024)S(1)} collective-permute-done((f32[2304]{0:T(1024)S(1)}, f32[2304]{0:T(1024)S(1)}, u32[]{:S(2)}, u32[]{:S(2)}) %collective-permute-start.32) | collective-permute-done | bytes 9248 | tf_op jit(solution)/shard_map/ppermute | solution.py:140
  120.0 2.4 %collective-permute-start.35 = (bf16[2,2,48,768]{3,2,1,0:T(8,128)(2,1)S(1)}, bf16[2,2,48,768]{3,2,1,0:T(8,128)(2,1)S(1)}, u32[]{:S(2)}, u32[]{:S(2)}) collective-permute-start(bf16[2,2,48,768]{3,2,1,0:T(8,128)(2,1)S(1)} %get-tuple-element.109), channel_id=1, source_target_pairs={{0,8},{1,9},{2,10},{3,11},{4,12},{5,13},{6,14},{7,15},{8,0},{9,1},... | collective-permute-start | bytes 884744 | tf_op jit(solution)/shard_map/ppermute | solution.py:140
  122.8 1.4 collective-permute-start.37
  124.1 1.4 collective-permute-start.36
  125.5 4.9 %collective-permute-done.36 = f32[2304]{0:T(1024)S(1)} collective-permute-done((f32[2304]{0:T(1024)S(1)}, f32[2304]{0:T(1024)S(1)}, u32[]{:S(2)}, u32[]{:S(2)}) %collective-permute-start.36) | collective-permute-done | bytes 9248 | tf_op jit(solution)/shard_map/ppermute | solution.py:140
  130.5 2.0 %collective-permute-start.39 = (bf16[2,1,48,768]{3,2,1,0:T(8,128)(2,1)S(1)}, bf16[2,1,48,768]{3,2,1,0:T(8,128)(2,1)S(1)}, u32[]{:S(2)}, u32[]{:S(2)}) collective-permute-start(bf16[2,1,48,768]{3,2,1,0:T(8,128)(2,1)S(1)} %get-tuple-element.118), channel_id=1, source_target_pairs={{0,16},{1,17},{2,18},{3,19},{4,20},{5,21},{6,22},{7,23},{8,24},{9,... | collective-permute-start | bytes 442376 | tf_op jit(solution)/shard_map/ppermute | solution.py:140
  132.5 1.0 collective-permute-start.41
  133.5 3.0 %collective-permute-start.40 = (bf16[2,1,48,768]{3,2,1,0:T(8,128)(2,1)S(1)}, bf16[2,1,48,768]{3,2,1,0:T(8,128)(2,1)S(1)}, u32[]{:S(2)}, u32[]{:S(2)}) collective-permute-start(bf16[2,1,48,768]{3,2,1,0:T(8,128)(2,1)S(1)} %get-tuple-element.120), channel_id=1, source_target_pairs={{0,2},{1,5},{2,0},{3,7},{4,6},{5,1},{6,4},{7,3},{8,10},{9,13},{10,... | collective-permute-start | bytes 442376 | tf_op jit(solution)/shard_map/ppermute | solution.py:140
  138.4 1.2 collective-permute-done.40
  (106 shorter events, 21.6 us)
Async XLA Ops:
  0.6 13.8 %copy-start = (bf16[2,128,1536]{2,1,0:T(8,128)(2,1)S(1)}, bf16[2,128,1536]{2,1,0:T(8,128)(2,1)}, u32[]{:S(2)}) copy-start(bf16[2,128,1536]{2,1,0:T(8,128)(2,1)} %features_ref) | copy-start | bytes 2359300
  1.6 11.1 %collective-permute-start = (bf16[2,1,48,768]{3,2,0,1:T(8,128)(2,1)S(1)}, bf16[2,1,48,768]{3,2,0,1:T(8,128)(2,1)S(1)}, u32[]{:S(2)}, u32[]{:S(2)}) collective-permute-start(bf16[2,1,48,768]{3,2,0,1:T(8,128)(2,1)S(1)} %get-tuple-element.149), channel_id=1, source_target_pairs={{0,16},{1,17},{2,18},{3,19},{4,20},{5,21},{6,22},{7,23},{8,24},{9,... | collective-permute-start | bytes 442376 | tf_op jit(solution)/shard_map/ppermute | solution.py:140
  7.5 5.2 %collective-permute-start.1 = (bf16[2,1,48,768]{3,2,1,0:T(8,128)(2,1)S(1)}, bf16[2,1,48,768]{3,2,1,0:T(8,128)(2,1)S(1)}, u32[]{:S(2)}, u32[]{:S(2)}) collective-permute-start(bf16[2,1,48,768]{3,2,1,0:T(8,128)(2,1)S(1)} %pad_maximum_fusion.refs_2_), channel_id=1, source_target_pairs={{0,2},{1,5},{2,0},{3,7},{4,6},{5,1},{6,4},{7,3},{8,10},{9,13},{10,... | collective-permute-start | bytes 442376 | tf_op jit(solution)/shard_map/ppermute | solution.py:140
  12.8 11.4 %collective-permute-start.2 = (bf16[2,2,48,768]{3,2,1,0:T(8,128)(2,1)S(1)}, bf16[2,2,48,768]{3,2,1,0:T(8,128)(2,1)S(1)}, u32[]{:S(2)}, u32[]{:S(2)}) collective-permute-start(bf16[2,2,48,768]{3,2,1,0:T(8,128)(2,1)S(1)} %get-tuple-element.64.refs_0_), channel_id=1, source_target_pairs={{0,8},{1,9},{2,10},{3,11},{4,12},{5,13},{6,14},{7,15},{8,0},{9,1},... | collective-permute-start | bytes 884744 | tf_op jit(solution)/shard_map/ppermute | solution.py:140
  14.5 4.7 %collective-permute-start.4 = (bf16[1,32,1536]{2,1,0:T(8,128)(2,1)S(1)}, bf16[1,32,1536]{2,1,0:T(8,128)(2,1)S(1)}, u32[]{:S(2)}, u32[]{:S(2)}) collective-permute-start(bf16[1,32,1536]{2,1,0:T(8,128)(2,1)S(1)} %get-tuple-element.144), channel_id=1, source_target_pairs={{0,1},{1,0},{2,3},{3,2},{4,5},{5,4},{6,7},{7,6},{8,9},{9,8},{10,11... | collective-permute-start | bytes 294920 | tf_op jit(solution)/shard_map/ppermute | solution.py:140
  14.6 5.3 %collective-permute-start.5 = (bf16[1,32,1536]{2,1,0:T(8,128)(2,1)S(1)}, bf16[1,32,1536]{2,1,0:T(8,128)(2,1)S(1)}, u32[]{:S(2)}, u32[]{:S(2)}) collective-permute-start(bf16[1,32,1536]{2,1,0:T(8,128)(2,1)S(1)} %get-tuple-element.142), channel_id=1, source_target_pairs={{0,1},{1,0},{2,3},{3,2},{4,5},{5,4},{6,7},{7,6},{8,9},{9,8},{10,11... | collective-permute-start | bytes 294920 | tf_op jit(solution)/shard_map/ppermute | solution.py:140
  15.2 5.4 %collective-permute-start.3 = (bf16[1,2,48,768]{3,2,1,0:T(8,128)(2,1)S(1)}, bf16[1,2,48,768]{3,2,1,0:T(8,128)(2,1)S(1)}, u32[]{:S(2)}, u32[]{:S(2)}) collective-permute-start(bf16[1,2,48,768]{3,2,1,0:T(8,128)(2,1)S(1)} %get-tuple-element.65.refs_0_), channel_id=1, source_target_pairs={{0,4},{1,3},{2,6},{3,1},{4,0},{5,7},{6,2},{7,5},{8,12},{9,11},{10,... | collective-permute-start | bytes 442376 | tf_op jit(solution)/shard_map/ppermute | solution.py:140
  16.7 7.5 %collective-permute-start.8 = (bf16[1,2,48,768]{3,2,1,0:T(8,128)(2,1)S(1)}, bf16[1,2,48,768]{3,2,1,0:T(8,128)(2,1)S(1)}, u32[]{:S(2)}, u32[]{:S(2)}) collective-permute-start(bf16[1,2,48,768]{3,2,1,0:T(8,128)(2,1)S(1)} %get-tuple-element.68.refs_2_), channel_id=1, source_target_pairs={{0,16},{1,17},{2,18},{3,19},{4,20},{5,21},{6,22},{7,23},{8,24},{9,... | collective-permute-start | bytes 442376 | tf_op jit(solution)/shard_map/ppermute | solution.py:140
  19.2 1.4 collective-permute-start.6
  19.9 0.7 collective-permute-start.7
  24.3 19.6 %collective-permute-start.9 = (bf16[2,4,48,768]{3,2,1,0:T(8,128)(2,1)S(1)}, bf16[2,4,48,768]{3,2,1,0:T(8,128)(2,1)S(1)}, u32[]{:S(2)}, u32[]{:S(2)}) collective-permute-start(bf16[2,4,48,768]{3,2,1,0:T(8,128)(2,1)S(1)} %get-tuple-element.71.refs_0_), channel_id=1, source_target_pairs={{0,2},{1,5},{2,0},{3,7},{4,6},{5,1},{6,4},{7,3},{8,10},{9,13},{10,... | collective-permute-start | bytes 1769480 | tf_op jit(solution)/shard_map/ppermute | solution.py:140
  28.9 15.0 %collective-permute-start.10 = (bf16[1,4,48,768]{3,2,1,0:T(8,128)(2,1)S(1)}, bf16[1,4,48,768]{3,2,1,0:T(8,128)(2,1)S(1)}, u32[]{:S(2)}, u32[]{:S(2)}) collective-permute-start(bf16[1,4,48,768]{3,2,1,0:T(8,128)(2,1)S(1)} %get-tuple-element.73.refs_2_), channel_id=1, source_target_pairs={{0,8},{1,9},{2,10},{3,11},{4,12},{5,13},{6,14},{7,15},{8,0},{9,1},... | collective-permute-start | bytes 884744 | tf_op jit(solution)/shard_map/ppermute | solution.py:140
  31.2 9.4 %collective-permute-start.11 = (bf16[1,2,48,768]{3,2,1,0:T(8,128)(2,1)S(1)}, bf16[1,2,48,768]{3,2,1,0:T(8,128)(2,1)S(1)}, u32[]{:S(2)}, u32[]{:S(2)}) collective-permute-start(bf16[1,2,48,768]{3,2,1,0:T(8,128)(2,1)S(1)} %get-tuple-element.65.refs_0_), channel_id=1, source_target_pairs={{0,16},{1,17},{2,18},{3,19},{4,20},{5,21},{6,22},{7,23},{8,24},{9,... | collective-permute-start | bytes 442376 | tf_op jit(solution)/shard_map/ppermute | solution.py:140
  33.4 14.9 %collective-permute-start.12 = (bf16[1,2,48,768]{3,2,1,0:T(8,128)(2,1)S(1)}, bf16[1,2,48,768]{3,2,1,0:T(8,128)(2,1)S(1)}, u32[]{:S(2)}, u32[]{:S(2)}) collective-permute-start(bf16[1,2,48,768]{3,2,1,0:T(8,128)(2,1)S(1)} %collective-permute-done.3.refs_0_), channel_id=1, source_target_pairs={{0,16},{1,17},{2,18},{3,19},{4,20},{5,21},{6,22},{7,23},{8,24},{9,... | collective-permute-start | bytes 442376 | tf_op jit(solution)/shard_map/ppermute | solution.py:140
  40.6 4.6 %copy-start.2 = (f32[1536]{0:T(1024)S(1)}, f32[1536]{0:T(1024)}, u32[]{:S(2)}) copy-start(f32[1536]{0:T(1024)} %param.10) | copy-start | bytes 18436
  40.6 4.7 %copy-start.1 = (bf16[2,128,1536]{2,1,0:T(8,128)(2,1)S(1)}, bf16[2,128,1536]{2,1,0:T(8,128)(2,1)}, u32[]{:S(2)}) copy-start(bf16[2,128,1536]{2,1,0:T(8,128)(2,1)} %param.7) | copy-start | bytes 2359300
  44.0 22.6 %collective-permute-start.14 = (bf16[3,8,48,768]{3,2,1,0:T(8,128)(2,1)S(1)}, bf16[3,8,48,768]{3,2,1,0:T(8,128)(2,1)S(1)}, u32[]{:S(2)}, u32[]{:S(2)}) collective-permute-start(bf16[3,8,48,768]{3,2,1,0:T(8,128)(2,1)S(1)} %assemble.10.refs_0_), channel_id=1, source_target_pairs={{0,4},{1,3},{2,6},{3,1},{4,0},{5,7},{6,2},{7,5},{8,12},{9,11},{10,... | collective-permute-start | bytes 5308424 | tf_op jit(solution)/shard_map/ppermute | solution.py:140
  45.2 9.4 %collective-permute-start.16 = (bf16[1,4,48,768]{3,2,1,0:T(8,128)(2,1)S(1)}, bf16[1,4,48,768]{3,2,1,0:T(8,128)(2,1)S(1)}, u32[]{:S(2)}, u32[]{:S(2)}) collective-permute-start(bf16[1,4,48,768]{3,2,1,0:T(8,128)(2,1)S(1)} %assemble.9.refs_0_), channel_id=1, source_target_pairs={{0,8},{1,9},{2,10},{3,11},{4,12},{5,13},{6,14},{7,15},{8,0},{9,1},... | collective-permute-start | bytes 884744 | tf_op jit(solution)/shard_map/ppermute | solution.py:140
  54.7 2.1 %collective-permute-start.17 = (bf16[1,8,48,768]{3,2,1,0:T(8,128)(2,1)S(1)}, bf16[1,8,48,768]{3,2,1,0:T(8,128)(2,1)S(1)}, u32[]{:S(2)}, u32[]{:S(2)}) collective-permute-start(bf16[1,8,48,768]{3,2,1,0:T(8,128)(2,1)S(1)} %assemble.12.refs_0_), channel_id=1, source_target_pairs={{0,1},{1,0},{2,3},{3,2},{4,5},{5,4},{6,7},{7,6},{8,9},{9,8},{10,11... | collective-permute-start | bytes 1769480 | tf_op jit(solution)/shard_map/ppermute | solution.py:140
  54.8 9.4 %collective-permute-start.15 = (bf16[1,4,48,768]{3,2,1,0:T(8,128)(2,1)S(1)}, bf16[1,4,48,768]{3,2,1,0:T(8,128)(2,1)S(1)}, u32[]{:S(2)}, u32[]{:S(2)}) collective-permute-start(bf16[1,4,48,768]{3,2,1,0:T(8,128)(2,1)S(1)} %assemble.11.refs_0_), channel_id=1, source_target_pairs={{0,8},{1,9},{2,10},{3,11},{4,12},{5,13},{6,14},{7,15},{8,0},{9,1},... | collective-permute-start | bytes 884744 | tf_op jit(solution)/shard_map/ppermute | solution.py:140
  55.1 16.4 %collective-permute-start.13 = (bf16[3,8,48,768]{3,2,1,0:T(8,128)(2,1)S(1)}, bf16[3,8,48,768]{3,2,1,0:T(8,128)(2,1)S(1)}, u32[]{:S(2)}, u32[]{:S(2)}) collective-permute-start(bf16[3,8,48,768]{3,2,1,0:T(8,128)(2,1)S(1)} %assemble.10.refs_0_), channel_id=1, source_target_pairs={{0,1},{1,0},{2,3},{3,2},{4,5},{5,4},{6,7},{7,6},{8,9},{9,8},{10,11... | collective-permute-start | bytes 5308424 | tf_op jit(solution)/shard_map/ppermute | solution.py:140
  66.6 6.4 %collective-permute-start.18 = (bf16[3,8,48,768]{3,2,1,0:T(8,128)(2,1)S(1)}, bf16[3,8,48,768]{3,2,1,0:T(8,128)(2,1)S(1)}, u32[]{:S(2)}, u32[]{:S(2)}) collective-permute-start(bf16[3,8,48,768]{3,2,1,0:T(8,128)(2,1)S(1)} %collective-permute-done.14.refs_1_), channel_id=1, source_target_pairs={{0,1},{1,0},{2,3},{3,2},{4,5},{5,4},{6,7},{7,6},{8,9},{9,8},{10,11... | collective-permute-start | bytes 5308424 | tf_op jit(solution)/shard_map/ppermute | solution.py:140
  66.6 4.5 %collective-permute-start.19 = (bf16[1,8,48,768]{3,2,1,0:T(8,128)(2,1)S(1)}, bf16[1,8,48,768]{3,2,1,0:T(8,128)(2,1)S(1)}, u32[]{:S(2)}, u32[]{:S(2)}) collective-permute-start(bf16[1,8,48,768]{3,2,1,0:T(8,128)(2,1)S(1)} %assemble.13.refs_1_), channel_id=1, source_target_pairs={{0,1},{1,0},{2,3},{3,2},{4,5},{5,4},{6,7},{7,6},{8,9},{9,8},{10,11... | collective-permute-start | bytes 1769480 | tf_op jit(solution)/shard_map/ppermute | solution.py:140
  73.0 0.8 copy-start.3
  76.1 3.8 %collective-permute-start.20 = (bf16[3,8,48,768]{3,2,1,0:T(8,128)(2,1)S(1)}, bf16[3,8,48,768]{3,2,1,0:T(8,128)(2,1)S(1)}, u32[]{:S(2)}, u32[]{:S(2)}) collective-permute-start(bf16[3,8,48,768]{3,2,1,0:T(8,128)(2,1)S(1)} %convolution_convert_fusion.1), channel_id=1, source_target_pairs={{0,1},{1,0},{2,3},{3,2},{4,5},{5,4},{6,7},{7,6},{8,9},{9,8},{10,11... | collective-permute-start | bytes 5308424 | tf_op jit(solution)/shard_map/ppermute | solution.py:140
  77.4 7.0 %collective-permute-start.21 = (bf16[2,8,48,768]{3,2,1,0:T(8,128)(2,1)S(1)}, bf16[2,8,48,768]{3,2,1,0:T(8,128)(2,1)S(1)}, u32[]{:S(2)}, u32[]{:S(2)}) collective-permute-start(bf16[2,8,48,768]{3,2,1,0:T(8,128)(2,1)S(1)} %convolution_convert_fusion.2), channel_id=1, source_target_pairs={{0,1},{1,0},{2,3},{3,2},{4,5},{5,4},{6,7},{7,6},{8,9},{9,8},{10,11... | collective-permute-start | bytes 3538952 | tf_op jit(solution)/shard_map/ppermute | solution.py:140
  77.8 8.3 %collective-permute-start.22 = (bf16[3,8,48,768]{3,2,1,0:T(8,128)(2,1)S(1)}, bf16[3,8,48,768]{3,2,1,0:T(8,128)(2,1)S(1)}, u32[]{:S(2)}, u32[]{:S(2)}) collective-permute-start(bf16[3,8,48,768]{3,2,1,0:T(8,128)(2,1)S(1)} %convolution_convert_fusion), channel_id=1, source_target_pairs={{0,1},{1,0},{2,3},{3,2},{4,5},{5,4},{6,7},{7,6},{8,9},{9,8},{10,11... | collective-permute-start | bytes 5308424 | tf_op jit(solution)/shard_map/ppermute | solution.py:140
  78.0 8.8 %collective-permute-start.25 = (bf16[2,32,768]{2,1,0:T(8,128)(2,1)S(1)}, bf16[2,32,768]{2,1,0:T(8,128)(2,1)S(1)}, u32[]{:S(2)}, u32[]{:S(2)}) collective-permute-start(bf16[2,32,768]{2,1,0:T(8,128)(2,1)S(1)} %get-tuple-element.140), channel_id=1, source_target_pairs={{0,1},{1,0},{2,3},{3,2},{4,5},{5,4},{6,7},{7,6},{8,9},{9,8},{10,11... | collective-permute-start | bytes 294920 | tf_op jit(solution)/shard_map/ppermute | solution.py:140
  78.4 8.4 %collective-permute-start.26 = (bf16[2,32,768]{2,1,0:T(8,128)(2,1)S(1)}, bf16[2,32,768]{2,1,0:T(8,128)(2,1)S(1)}, u32[]{:S(2)}, u32[]{:S(2)}) collective-permute-start(bf16[2,32,768]{2,1,0:T(8,128)(2,1)S(1)} %get-tuple-element.139), channel_id=1, source_target_pairs={{1,2},{2,1},{3,4},{4,3},{5,6},{6,5},{7,8},{8,7},{9,10},{10,9},{11,... | collective-permute-start | bytes 294920 | tf_op jit(solution)/shard_map/ppermute | solution.py:140
  80.5 24.4 %collective-permute-start.23 = (bf16[3,8,48,768]{3,2,1,0:T(8,128)(2,1)S(1)}, bf16[3,8,48,768]{3,2,1,0:T(8,128)(2,1)S(1)}, u32[]{:S(2)}, u32[]{:S(2)}) collective-permute-start(bf16[3,8,48,768]{3,2,1,0:T(8,128)(2,1)S(1)} %add_convert_fusion), channel_id=1, source_target_pairs={{0,4},{1,3},{2,6},{3,1},{4,0},{5,7},{6,2},{7,5},{8,12},{9,11},{10,... | collective-permute-start | bytes 5308424 | tf_op jit(solution)/shard_map/ppermute | solution.py:140
  84.7 8.3 %collective-permute-start.24 = (bf16[1,4,48,768]{3,2,1,0:T(8,128)(2,1)S(1)}, bf16[1,4,48,768]{3,2,1,0:T(8,128)(2,1)S(1)}, u32[]{:S(2)}, u32[]{:S(2)}) collective-permute-start(bf16[1,4,48,768]{3,2,1,0:T(8,128)(2,1)S(1)} %fusion.21), channel_id=1, source_target_pairs={{0,8},{1,9},{2,10},{3,11},{4,12},{5,13},{6,14},{7,15},{8,0},{9,1},... | collective-permute-start | bytes 884744 | tf_op jit(solution)/shard_map/ppermute | solution.py:140
  93.0 11.1 %collective-permute-start.27 = (bf16[1,4,48,768]{3,2,1,0:T(8,128)(2,1)S(1)}, bf16[1,4,48,768]{3,2,1,0:T(8,128)(2,1)S(1)}, u32[]{:S(2)}, u32[]{:S(2)}) collective-permute-start(bf16[1,4,48,768]{3,2,1,0:T(8,128)(2,1)S(1)} %fusion.22), channel_id=1, source_target_pairs={{0,8},{1,9},{2,10},{3,11},{4,12},{5,13},{6,14},{7,15},{8,0},{9,1},... | collective-permute-start | bytes 884744 | tf_op jit(solution)/shard_map/ppermute | solution.py:140
  94.5 9.6 %collective-permute-start.29 = (bf16[1,2,48,768]{3,2,1,0:T(8,128)(2,1)S(1)}, bf16[1,2,48,768]{3,2,1,0:T(8,128)(2,1)S(1)}, u32[]{:S(2)}, u32[]{:S(2)}) collective-permute-start(bf16[1,2,48,768]{3,2,1,0:T(8,128)(2,1)S(1)} %get-tuple-element.93), channel_id=1, source_target_pairs={{0,16},{1,17},{2,18},{3,19},{4,20},{5,21},{6,22},{7,23},{8,24},{9,... | collective-permute-start | bytes 442376 | tf_op jit(solution)/shard_map/ppermute | solution.py:140
  95.9 1.2 collective-permute-start.28
  106.0 13.9 %collective-permute-start.30 = (bf16[2,4,48,768]{3,2,1,0:T(8,128)(2,1)S(1)}, bf16[2,4,48,768]{3,2,1,0:T(8,128)(2,1)S(1)}, u32[]{:S(2)}, u32[]{:S(2)}) collective-permute-start(bf16[2,4,48,768]{3,2,1,0:T(8,128)(2,1)S(1)} %get-tuple-element.98), channel_id=1, source_target_pairs={{0,2},{1,5},{2,0},{3,7},{4,6},{5,1},{6,4},{7,3},{8,10},{9,13},{10,... | collective-permute-start | bytes 1769480 | tf_op jit(solution)/shard_map/ppermute | solution.py:140
  107.9 12.0 %collective-permute-start.33 = (bf16[1,4,48,768]{3,2,1,0:T(8,128)(2,1)S(1)}, bf16[1,4,48,768]{3,2,1,0:T(8,128)(2,1)S(1)}, u32[]{:S(2)}, u32[]{:S(2)}) collective-permute-start(bf16[1,4,48,768]{3,2,1,0:T(8,128)(2,1)S(1)} %get-tuple-element.105), channel_id=1, source_target_pairs={{0,8},{1,9},{2,10},{3,11},{4,12},{5,13},{6,14},{7,15},{8,0},{9,1},... | collective-permute-start | bytes 884744 | tf_op jit(solution)/shard_map/ppermute | solution.py:140
  109.1 10.8 %collective-permute-start.34 = (bf16[1,2,48,768]{3,2,1,0:T(8,128)(2,1)S(1)}, bf16[1,2,48,768]{3,2,1,0:T(8,128)(2,1)S(1)}, u32[]{:S(2)}, u32[]{:S(2)}) collective-permute-start(bf16[1,2,48,768]{3,2,1,0:T(8,128)(2,1)S(1)} %get-tuple-element.107), channel_id=1, source_target_pairs={{0,16},{1,17},{2,18},{3,19},{4,20},{5,21},{6,22},{7,23},{8,24},{9,... | collective-permute-start | bytes 442376 | tf_op jit(solution)/shard_map/ppermute | solution.py:140
  109.8 6.4 %collective-permute-start.31 = (f32[2304]{0:T(1024)S(1)}, f32[2304]{0:T(1024)S(1)}, u32[]{:S(2)}, u32[]{:S(2)}) collective-permute-start(f32[2304]{0:T(1024)S(1)} %add.149), channel_id=1, source_target_pairs={{0,2},{1,3},{2,0},{3,1},{4,6},{5,7},{6,4},{7,5},{8,10},{9,11},{10,... | collective-permute-start | bytes 27656 | tf_op jit(solution)/shard_map/ppermute | solution.py:140
  116.1 3.7 %collective-permute-start.32 = (f32[2304]{0:T(1024)S(1)}, f32[2304]{0:T(1024)S(1)}, u32[]{:S(2)}, u32[]{:S(2)}) collective-permute-start(f32[2304]{0:T(1024)S(1)} %add.150), channel_id=1, source_target_pairs={{0,4},{1,5},{2,6},{3,7},{4,0},{5,1},{6,2},{7,3},{8,12},{9,13},{10,... | collective-permute-start | bytes 27656 | tf_op jit(solution)/shard_map/ppermute | solution.py:140
  120.0 10.4 %collective-permute-start.35 = (bf16[2,2,48,768]{3,2,1,0:T(8,128)(2,1)S(1)}, bf16[2,2,48,768]{3,2,1,0:T(8,128)(2,1)S(1)}, u32[]{:S(2)}, u32[]{:S(2)}) collective-permute-start(bf16[2,2,48,768]{3,2,1,0:T(8,128)(2,1)S(1)} %get-tuple-element.109), channel_id=1, source_target_pairs={{0,8},{1,9},{2,10},{3,11},{4,12},{5,13},{6,14},{7,15},{8,0},{9,1},... | collective-permute-start | bytes 884744 | tf_op jit(solution)/shard_map/ppermute | solution.py:140
  122.4 8.0 %collective-permute-start.38 = (bf16[1,2,48,768]{3,2,1,0:T(8,128)(2,1)S(1)}, bf16[1,2,48,768]{3,2,1,0:T(8,128)(2,1)S(1)}, u32[]{:S(2)}, u32[]{:S(2)}) collective-permute-start(bf16[1,2,48,768]{3,2,1,0:T(8,128)(2,1)S(1)} %get-tuple-element.116), channel_id=1, source_target_pairs={{0,4},{1,3},{2,6},{3,1},{4,0},{5,7},{6,2},{7,5},{8,12},{9,11},{10,... | collective-permute-start | bytes 442376 | tf_op jit(solution)/shard_map/ppermute | solution.py:140
  122.8 7.7 %collective-permute-start.37 = (bf16[1,2,48,768]{3,2,1,0:T(8,128)(2,1)S(1)}, bf16[1,2,48,768]{3,2,1,0:T(8,128)(2,1)S(1)}, u32[]{:S(2)}, u32[]{:S(2)}) collective-permute-start(bf16[1,2,48,768]{3,2,1,0:T(8,128)(2,1)S(1)} %get-tuple-element.113), channel_id=1, source_target_pairs={{0,16},{1,17},{2,18},{3,19},{4,20},{5,21},{6,22},{7,23},{8,24},{9,... | collective-permute-start | bytes 442376 | tf_op jit(solution)/shard_map/ppermute | solution.py:140
  124.1 6.3 %collective-permute-start.36 = (f32[2304]{0:T(1024)S(1)}, f32[2304]{0:T(1024)S(1)}, u32[]{:S(2)}, u32[]{:S(2)}) collective-permute-start(f32[2304]{0:T(1024)S(1)} %add.151), channel_id=1, source_target_pairs={{0,8},{1,9},{2,10},{3,11},{4,12},{5,13},{6,14},{7,15},{8,0},{9,1},... | collective-permute-start | bytes 27656 | tf_op jit(solution)/shard_map/ppermute | solution.py:140
  130.5 7.8 %collective-permute-start.39 = (bf16[2,1,48,768]{3,2,1,0:T(8,128)(2,1)S(1)}, bf16[2,1,48,768]{3,2,1,0:T(8,128)(2,1)S(1)}, u32[]{:S(2)}, u32[]{:S(2)}) collective-permute-start(bf16[2,1,48,768]{3,2,1,0:T(8,128)(2,1)S(1)} %get-tuple-element.118), channel_id=1, source_target_pairs={{0,16},{1,17},{2,18},{3,19},{4,20},{5,21},{6,22},{7,23},{8,24},{9,... | collective-permute-start | bytes 442376 | tf_op jit(solution)/shard_map/ppermute | solution.py:140
  132.5 4.6 %collective-permute-start.41 = (f32[2304]{0:T(1024)S(1)}, f32[2304]{0:T(1024)S(1)}, u32[]{:S(2)}, u32[]{:S(2)}) collective-permute-start(f32[2304]{0:T(1024)S(1)} %add.152), channel_id=1, source_target_pairs={{0,16},{1,17},{2,18},{3,19},{4,20},{5,21},{6,22},{7,23},{8,24},{9,... | collective-permute-start | bytes 27656 | tf_op jit(solution)/shard_map/ppermute | solution.py:140
  133.5 6.1 %collective-permute-start.40 = (bf16[2,1,48,768]{3,2,1,0:T(8,128)(2,1)S(1)}, bf16[2,1,48,768]{3,2,1,0:T(8,128)(2,1)S(1)}, u32[]{:S(2)}, u32[]{:S(2)}) collective-permute-start(bf16[2,1,48,768]{3,2,1,0:T(8,128)(2,1)S(1)} %get-tuple-element.120), channel_id=1, source_target_pairs={{0,2},{1,5},{2,0},{3,7},{4,6},{5,1},{6,4},{7,3},{8,10},{9,13},{10,... | collective-permute-start | bytes 442376 | tf_op jit(solution)/shard_map/ppermute | solution.py:140

commit v7 on v6

--- a/solution.py
+++ b/solution.py
@@ -432,16 +432,19 @@
     conv_output = contract(act[0, 0], after(near, proj_b))
     (proj_a,) = assemble((proj_a, after(proj_in, conv_output)), (grow(1, 4, 0),))
     proj_a_other = send(proj_a, CORE)
-    grad_hidden = contract(act_p[0, 0], proj_a) + contract(act_p[1, 0], proj_a_other)
-    (proj_b,) = assemble((proj_b, after(proj_b_in, grad_hidden)), (grow(1, 4, 0),))
+    (proj_b,) = assemble((proj_b, after(proj_b_in, proj_a)), (grow(1, 4, 0),))
     proj_b_other = send(proj_b, CORE)
-    far = after(far, conv_output, proj_b)
+    far = after(far, proj_b_other, proj_a_other)
+    far_other = send(far, CORE)
     conv_output = conv_output + contract(act[1, 0], after(near_other, far))
-    far_other = send(far, CORE)
+    proj_a_late, proj_b_late = after((proj_a, proj_b), far)
+    grad_hidden = (
+        contract(act_p[0, 0], proj_a_late)
+        + contract(act_p[1, 0], proj_a_other)
+        + contract(act_p[0, 1], proj_b_late)
+        + contract(act_p[1, 1], proj_b_other)
+    )
     conv_output = conv_output + contract(act[0, 1], far) + contract(act[1, 1], far_other)
-    grad_hidden = (
-        grad_hidden + contract(act_p[0, 1], proj_b) + contract(act_p[1, 1], proj_b_other)
-    )
     hidden32, pull_inner = jax.vjp(act_norm, conv_output, inner_gain)
     hidden = as_bf16(hidden32)
     grad_conv, grad_gain_inner = pull_inner(grad_hidden)
@@ -494,6 +497,7 @@
     recv_a = send(after(message_a, message_b), Z_NEAR)
     gains = after(gains, message_b)
     gains = gains + send(gains, CORE)
+    gains = gains + send(gains, links(lambda i: i ^ 2))
 
     recv_a = after(recv_a, gains)
     message, message_l, message_a, message_p, kept, kept_l, kept_a, kept_b = fold(
@@ -511,12 +515,11 @@
     )
     recv, recv_l, recv_a = send(message, FIRST), send(message_l, Z_NEAR), send(message_a, Z_FAR)
     gains = after(gains, message)
-    gains = gains + send(gains, links(lambda i: i ^ 2))
+    gains = gains + send(gains, links(lambda i: i ^ 4))
     block_out = project_back(
         after(hidden, message), flat, (proj_a, proj_b, proj_a_other, proj_b_other)
     ).reshape(features.shape)
     gains = after(gains, block_out)
-    gains = gains + send(gains, links(lambda i: i ^ 4))
 
     recv = after(recv, gains)
     message, message_l, kept, kept_l, kept_p = fold(

time: 141 us -> 137 us (0.972)
  starting transfers between devices: 53.3 us -> 48.9 us
    ppermute x42, starting transfers between devices: 53.3 us -> 48.9 us  [send(): return lax.ppermute(block, 'seq', pairs)]
  transfers between devices with their start and end apart: 42 -> 42, of which waited for: 18 -> 20; matrix products, arithmetic and copies ran while one was open for 10% -> 10% of each run, Pallas kernels for 6% -> 6%
where the time goes in v7:
time: 137 us
  waiting for transfers between devices  58.1 us (42%)
  starting transfers between devices  48.9 us (36%)
  Pallas kernels  9.55 us (7%)
  matrix products  9.09 us (7%)
  other arithmetic  6.47 us (5%)
  local copies, waits for them, and re-layouts  3.48 us (3%)
    ppermute x42, waiting for transfers between devices, send(): return lax.ppermute(block, 'seq', pairs)  58.1 us
    ppermute x42, starting transfers between devices, send(): return lax.ppermute(block, 'seq', pairs)  48.9 us
    dot_general x8, matrix products, contract(): jnp.einsum('ct,ci->ti', left.reshape(-1, left.shape[-1]), right.reshape(-...  5.16 us
    dot_general x9, matrix products, rows_dot(): jnp.einsum('mnrt,ti->mnri', left, right, preferred_element_type=jnp.float32)  3.94 us
    pallas_call x1, Pallas kernels, prepare(): pl.pallas_call(prepare_kernel, out_shape=[shape(KERNEL_TAPS), shape(1)],...  2.95 us
  transfers between devices with their start and end apart: 42, of which 20 were waited for; matrix products, arithmetic and copies ran while one was open for 10% of the time, Pallas kernels for 6%

profile of v7, /device:TPU:0, one launch (start us, length us, event | category | flops | bytes accessed | tf_op | source)
XLA Modules:
  0.0 136.7 jit_solution(9447337151433868517)
XLA Ops:
  0.6 1.0 slice_bitcast_fusion.8
  1.6 4.1 %collective-permute-start = (bf16[2,1,48,768]{3,2,0,1:T(8,128)(2,1)S(1)}, bf16[2,1,48,768]{3,2,0,1:T(8,128)(2,1)S(1)}, u32[]{:S(2)}, u32[]{:S(2)}) collective-permute-start(bf16[2,1,48,768]{3,2,0,1:T(8,128)(2,1)S(1)} %get-tuple-element.153), channel_id=1, source_target_pairs={{0,16},{1,17},{2,18},{3,19},{4,20},{5,21},{6,22},{7,23},{8,24},{9,... | collective-permute-start | bytes 442376 | tf_op jit(solution)/shard_map/ppermute | solution.py:140
  6.6 0.9 pad_maximum_fusion.refs_2_
  7.5 1.6 %collective-permute-start.1 = (bf16[2,1,48,768]{3,2,1,0:T(8,128)(2,1)S(1)}, bf16[2,1,48,768]{3,2,1,0:T(8,128)(2,1)S(1)}, u32[]{:S(2)}, u32[]{:S(2)}) collective-permute-start(bf16[2,1,48,768]{3,2,1,0:T(8,128)(2,1)S(1)} %pad_maximum_fusion.refs_2_), channel_id=1, source_target_pairs={{0,2},{1,5},{2,0},{3,7},{4,6},{5,1},{6,4},{7,3},{8,10},{9,13},{10,... | collective-permute-start | bytes 442376 | tf_op jit(solution)/shard_map/ppermute | solution.py:140
  9.1 3.7 %collective-permute-done = bf16[2,1,48,768]{3,2,0,1:T(8,128)(2,1)S(1)} collective-permute-done((bf16[2,1,48,768]{3,2,0,1:T(8,128)(2,1)S(1)}, bf16[2,1,48,768]{3,2,0,1:T(8,128)(2,1)S(1)}, u32[]{:S(2)}, u32[]{:S(2)}) %collective-permute-start) | collective-permute-done | bytes 147488 | tf_op jit(solution)/shard_map/ppermute | solution.py:140
  12.8 1.6 %collective-permute-start.2 = (bf16[2,2,48,768]{3,2,1,0:T(8,128)(2,1)S(1)}, bf16[2,2,48,768]{3,2,1,0:T(8,128)(2,1)S(1)}, u32[]{:S(2)}, u32[]{:S(2)}) collective-permute-start(bf16[2,2,48,768]{3,2,1,0:T(8,128)(2,1)S(1)} %get-tuple-element.66.refs_0_), channel_id=1, source_target_pairs={{0,8},{1,9},{2,10},{3,11},{4,12},{5,13},{6,14},{7,15},{8,0},{9,1},... | collective-permute-start | bytes 884744 | tf_op jit(solution)/shard_map/ppermute | solution.py:140
  15.2 1.5 %collective-permute-start.3 = (bf16[1,2,48,768]{3,2,1,0:T(8,128)(2,1)S(1)}, bf16[1,2,48,768]{3,2,1,0:T(8,128)(2,1)S(1)}, u32[]{:S(2)}, u32[]{:S(2)}) collective-permute-start(bf16[1,2,48,768]{3,2,1,0:T(8,128)(2,1)S(1)} %get-tuple-element.67.refs_0_), channel_id=1, source_target_pairs={{0,4},{1,3},{2,6},{3,1},{4,0},{5,7},{6,2},{7,5},{8,12},{9,11},{10,... | collective-permute-start | bytes 442376 | tf_op jit(solution)/shard_map/ppermute | solution.py:140
  16.7 2.5 %collective-permute-start.8 = (bf16[1,2,48,768]{3,2,1,0:T(8,128)(2,1)S(1)}, bf16[1,2,48,768]{3,2,1,0:T(8,128)(2,1)S(1)}, u32[]{:S(2)}, u32[]{:S(2)}) collective-permute-start(bf16[1,2,48,768]{3,2,1,0:T(8,128)(2,1)S(1)} %get-tuple-element.70.refs_2_), channel_id=1, source_target_pairs={{0,16},{1,17},{2,18},{3,19},{4,20},{5,21},{6,22},{7,23},{8,24},{9,... | collective-permute-start | bytes 442376 | tf_op jit(solution)/shard_map/ppermute | solution.py:140
  20.6 3.6 %collective-permute-done.2.refs_1_ = bf16[2,2,48,768]{3,2,1,0:T(8,128)(2,1)S(1)} collective-permute-done((bf16[2,2,48,768]{3,2,1,0:T(8,128)(2,1)S(1)}, bf16[2,2,48,768]{3,2,1,0:T(8,128)(2,1)S(1)}, u32[]{:S(2)}, u32[]{:S(2)}) %collective-permute-start.2) | collective-permute-done | bytes 294944 | tf_op jit(solution)/shard_map/ppermute | solution.py:140
  24.3 4.6 %collective-permute-start.9 = (bf16[2,4,48,768]{3,2,1,0:T(8,128)(2,1)S(1)}, bf16[2,4,48,768]{3,2,1,0:T(8,128)(2,1)S(1)}, u32[]{:S(2)}, u32[]{:S(2)}) collective-permute-start(bf16[2,4,48,768]{3,2,1,0:T(8,128)(2,1)S(1)} %get-tuple-element.73.refs_0_), channel_id=1, source_target_pairs={{0,2},{1,5},{2,0},{3,7},{4,6},{5,1},{6,4},{7,3},{8,10},{9,13},{10,... | collective-permute-start | bytes 1769480 | tf_op jit(solution)/shard_map/ppermute | solution.py:140
  28.9 2.3 %collective-permute-start.10 = (bf16[1,4,48,768]{3,2,1,0:T(8,128)(2,1)S(1)}, bf16[1,4,48,768]{3,2,1,0:T(8,128)(2,1)S(1)}, u32[]{:S(2)}, u32[]{:S(2)}) collective-permute-start(bf16[1,4,48,768]{3,2,1,0:T(8,128)(2,1)S(1)} %get-tuple-element.75.refs_2_), channel_id=1, source_target_pairs={{0,8},{1,9},{2,10},{3,11},{4,12},{5,13},{6,14},{7,15},{8,0},{9,1},... | collective-permute-start | bytes 884744 | tf_op jit(solution)/shard_map/ppermute | solution.py:140
  31.2 2.2 %collective-permute-start.11 = (bf16[1,2,48,768]{3,2,1,0:T(8,128)(2,1)S(1)}, bf16[1,2,48,768]{3,2,1,0:T(8,128)(2,1)S(1)}, u32[]{:S(2)}, u32[]{:S(2)}) collective-permute-start(bf16[1,2,48,768]{3,2,1,0:T(8,128)(2,1)S(1)} %get-tuple-element.67.refs_0_), channel_id=1, source_target_pairs={{0,16},{1,17},{2,18},{3,19},{4,20},{5,21},{6,22},{7,23},{8,24},{9,... | collective-permute-start | bytes 442376 | tf_op jit(solution)/shard_map/ppermute | solution.py:140
  33.4 5.6 %collective-permute-done.11.refs_1_ = bf16[1,2,48,768]{3,2,1,0:T(8,128)(2,1)S(1)} collective-permute-done((bf16[1,2,48,768]{3,2,1,0:T(8,128)(2,1)S(1)}, bf16[1,2,48,768]{3,2,1,0:T(8,128)(2,1)S(1)}, u32[]{:S(2)}, u32[]{:S(2)}) %collective-permute-start.11) | collective-permute-done | bytes 147488 | tf_op jit(solution)/shard_map/ppermute | solution.py:140
  39.0 2.1 %collective-permute-done.10.refs_3_ = bf16[1,4,48,768]{3,2,1,0:T(8,128)(2,1)S(1)} collective-permute-done((bf16[1,4,48,768]{3,2,1,0:T(8,128)(2,1)S(1)}, bf16[1,4,48,768]{3,2,1,0:T(8,128)(2,1)S(1)}, u32[]{:S(2)}, u32[]{:S(2)}) %collective-permute-start.10) | collective-permute-done | bytes 294944 | tf_op jit(solution)/shard_map/ppermute | solution.py:140
  41.3 1.6 %collective-permute-start.14 = (bf16[3,8,48,768]{3,2,1,0:T(8,128)(2,1)S(1)}, bf16[3,8,48,768]{3,2,1,0:T(8,128)(2,1)S(1)}, u32[]{:S(2)}, u32[]{:S(2)}) collective-permute-start(bf16[3,8,48,768]{3,2,1,0:T(8,128)(2,1)S(1)} %assemble.10.refs_0_), channel_id=1, source_target_pairs={{0,4},{1,3},{2,6},{3,1},{4,0},{5,7},{6,2},{7,5},{8,12},{9,11},{10,... | collective-permute-start | bytes 5308424 | tf_op jit(solution)/shard_map/ppermute | solution.py:140
  42.9 1.3 collective-permute-start.12
  44.3 3.0 %prepare.1 = (bf16[2,2,3,8,48,256]{5,4,3,2,1,0:T(8,128)(2,1)S(1)}, bf16[2,2,1,8,48,256]{5,4,3,2,1,0:T(8,128)(2,1)S(1)}) custom-call(s32[1]{0:T(128)} %bitcast.index_ref, bf16[2,128,1536]{2,1,0:T(8,128)(2,1)S(1)} %copy-done, bf16[256,1536]{1,0:T(8,128)(2,1)S(1)} %bitcast.155, f32[1,1536]{1,0:T(1,128)S(1)} %reshape.155.gain_ref, ...), custom_call_target="tpu_custom_call" | custom-call | tf_op jit(solution)/shard_map/prepare/pallas_call | solution.py:285
  47.2 5.4 %collective-permute-done.12.refs_1_ = bf16[1,2,48,768]{3,2,1,0:T(8,128)(2,1)S(1)} collective-permute-done((bf16[1,2,48,768]{3,2,1,0:T(8,128)(2,1)S(1)}, bf16[1,2,48,768]{3,2,1,0:T(8,128)(2,1)S(1)}, u32[]{:S(2)}, u32[]{:S(2)}) %collective-permute-start.12) | collective-permute-done | bytes 147488 | tf_op jit(solution)/shard_map/ppermute | solution.py:140
  53.6 3.5 %collective-permute-done.16.refs_1_ = bf16[1,4,48,768]{3,2,1,0:T(8,128)(2,1)S(1)} collective-permute-done((bf16[1,4,48,768]{3,2,1,0:T(8,128)(2,1)S(1)}, bf16[1,4,48,768]{3,2,1,0:T(8,128)(2,1)S(1)}, u32[]{:S(2)}, u32[]{:S(2)}) %collective-permute-start.16) | collective-permute-done | bytes 294944 | tf_op jit(solution)/shard_map/ppermute | solution.py:140
  57.3 5.8 %collective-permute-done.15.refs_1_ = bf16[1,4,48,768]{3,2,1,0:T(8,128)(2,1)S(1)} collective-permute-done((bf16[1,4,48,768]{3,2,1,0:T(8,128)(2,1)S(1)}, bf16[1,4,48,768]{3,2,1,0:T(8,128)(2,1)S(1)}, u32[]{:S(2)}, u32[]{:S(2)}) %collective-permute-start.15) | collective-permute-done | bytes 294944 | tf_op jit(solution)/shard_map/ppermute | solution.py:140
  63.2 2.0 %collective-permute-done.17.refs_3_ = bf16[1,8,48,768]{3,2,1,0:T(8,128)(2,1)S(1)} collective-permute-done((bf16[1,8,48,768]{3,2,1,0:T(8,128)(2,1)S(1)}, bf16[1,8,48,768]{3,2,1,0:T(8,128)(2,1)S(1)}, u32[]{:S(2)}, u32[]{:S(2)}) %collective-permute-start.17) | collective-permute-done | bytes 589856 | tf_op jit(solution)/shard_map/ppermute | solution.py:140
  69.7 1.1 multiply_reduce_fusion
  76.3 3.4 %collective-permute-start.23 = (bf16[3,8,48,768]{3,2,1,0:T(8,128)(2,1)S(1)}, bf16[3,8,48,768]{3,2,1,0:T(8,128)(2,1)S(1)}, u32[]{:S(2)}, u32[]{:S(2)}) collective-permute-start(bf16[3,8,48,768]{3,2,1,0:T(8,128)(2,1)S(1)} %add_convert_fusion), channel_id=1, source_target_pairs={{0,4},{1,3},{2,6},{3,1},{4,0},{5,7},{6,2},{7,5},{8,12},{9,11},{10,... | collective-permute-start | bytes 5308424 | tf_op jit(solution)/shard_map/ppermute | solution.py:140
  79.9 1.0 collective-permute-start.24
  82.4 2.7 %grad_active.1 = f32[256,1536]{1,0:T(8,128)S(1)} custom-call(s32[1]{0:T(128)} %bitcast.index_ref, bf16[256,768]{1,0:T(8,128)(2,1)S(1)} %get-tuple-element.94.grad_ref, bf16[2,32,768]{2,1,0:T(8,128)(2,1)S(1)} %collective-permute-done.25.core_ref, bf16[2,32,768]{2,1,0:T(8,128)(2,1)S(1)} %collective-permute-done.26.outer_ref, ...), custom_call_target="tpu_custom_call" | custom-call | tf_op jit(solution)/shard_map/grad_active/pallas_call | solution.py:361
  85.3 1.8 %fusion.8 = (f32[1536]{0:T(1024)S(1)}, f32[2,128]{1,0:T(2,128)S(1)}, f32[2,128,1536]{2,1,0:T(8,128)S(1)}) fusion(bf16[2,128,1536]{2,1,0:T(8,128)(2,1)S(1)} %copy-done, f32[2,128]{1,0:T(2,128)S(1)} %fusion.54, f32[1536]{0:T(1024)S(1)} %copy-done.2, f32[2,128,1536]{2,1,0:T(8,128)S(1)} %bitcast.152), kind=kLoop, calls=%fused_computation.19 | loop fusion | flops 10615040 | bytes 3946496 | tf_op jit(solution)/shard_map/transpose(jvp())/reduce_sum | solution.py:33
  87.1 1.4 %fusion.13 = bf16[2,128,1536]{2,1,0:T(8,128)(2,1)} fusion(bf16[2,128,1536]{2,1,0:T(8,128)(2,1)S(1)} %copy-done, bf16[2,128,1536]{2,1,0:T(8,128)(2,1)S(1)} %copy-done.1, f32[2,128,1536]{2,1,0:T(8,128)S(1)} %get-tuple-element.130, f32[2,128]{1,0:T(2,128)S(1)} %multiply_multiply_fusion.5, f32[1536]{0:T(1024)S(1)} %copy-done.2, f32[2,128]{1,0:T(2,128)S(1)} %fusion.54), kind=kLoop, calls=%fused_computation.24 | loop fusion | flops 3538944 | bytes 3940352 | tf_op jit(solution)/shard_map/convert_element_type | solution.py:394
  88.6 1.2 collective-permute-start.27
  89.8 1.9 %collective-permute-start.30 = (bf16[1,2,48,768]{3,2,1,0:T(8,128)(2,1)S(1)}, bf16[1,2,48,768]{3,2,1,0:T(8,128)(2,1)S(1)}, u32[]{:S(2)}, u32[]{:S(2)}) collective-permute-start(bf16[1,2,48,768]{3,2,1,0:T(8,128)(2,1)S(1)} %get-tuple-element.97), channel_id=1, source_target_pairs={{0,16},{1,17},{2,18},{3,19},{4,20},{5,21},{6,22},{7,23},{8,24},{9,... | collective-permute-start | bytes 442376 | tf_op jit(solution)/shard_map/ppermute | solution.py:140
  91.7 1.2 collective-permute-done.28
  92.8 3.9 %collective-permute-done.29 = f32[2304]{0:T(1024)S(1)} collective-permute-done((f32[2304]{0:T(1024)S(1)}, f32[2304]{0:T(1024)S(1)}, u32[]{:S(2)}, u32[]{:S(2)}) %collective-permute-start.29) | collective-permute-done | bytes 9248 | tf_op jit(solution)/shard_map/ppermute | solution.py:140
  96.7 2.7 %collective-permute-done.27.refs_3_ = bf16[1,4,48,768]{3,2,1,0:T(8,128)(2,1)S(1)} collective-permute-done((bf16[1,4,48,768]{3,2,1,0:T(8,128)(2,1)S(1)}, bf16[1,4,48,768]{3,2,1,0:T(8,128)(2,1)S(1)}, u32[]{:S(2)}, u32[]{:S(2)}) %collective-permute-start.27) | collective-permute-done | bytes 294944 | tf_op jit(solution)/shard_map/ppermute | solution.py:140
  100.2 1.1 fold.5
  101.3 1.9 %collective-permute-start.31 = (bf16[2,4,48,768]{3,2,1,0:T(8,128)(2,1)S(1)}, bf16[2,4,48,768]{3,2,1,0:T(8,128)(2,1)S(1)}, u32[]{:S(2)}, u32[]{:S(2)}) collective-permute-start(bf16[2,4,48,768]{3,2,1,0:T(8,128)(2,1)S(1)} %get-tuple-element.102), channel_id=1, source_target_pairs={{0,2},{1,5},{2,0},{3,7},{4,6},{5,1},{6,4},{7,3},{8,10},{9,13},{10,... | collective-permute-start | bytes 1769480 | tf_op jit(solution)/shard_map/ppermute | solution.py:140
  103.2 1.7 %collective-permute-start.33 = (bf16[1,4,48,768]{3,2,1,0:T(8,128)(2,1)S(1)}, bf16[1,4,48,768]{3,2,1,0:T(8,128)(2,1)S(1)}, u32[]{:S(2)}, u32[]{:S(2)}) collective-permute-start(bf16[1,4,48,768]{3,2,1,0:T(8,128)(2,1)S(1)} %get-tuple-element.109), channel_id=1, source_target_pairs={{0,8},{1,9},{2,10},{3,11},{4,12},{5,13},{6,14},{7,15},{8,0},{9,1},... | collective-permute-start | bytes 884744 | tf_op jit(solution)/shard_map/ppermute | solution.py:140
  105.5 2.2 %project_back.1 = bf16[256,1536]{1,0:T(8,128)(2,1)} custom-call(s32[1]{0:T(128)} %bitcast.index_ref, bf16[256,768]{1,0:T(8,128)(2,1)S(1)} %get-tuple-element.103.hidden_ref, bf16[256,1536]{1,0:T(8,128)(2,1)S(1)} %bitcast.146, bf16[1,8,48,768]{3,2,1,0:T(8,128)(2,1)S(1)} %assemble.12.refs_0_, bf16[1,8,48,768]{3,2,1,0:T(8,128)(2,1)S(1)} %assemble.13.refs_1_, ...), custom_call_target="tpu_custom_call" | custom-call | tf_op jit(solution)/shard_map/project_back/pallas_call | solution.py:327
  107.7 1.1 collective-permute-done.32
  108.8 2.3 %collective-permute-done.31.refs_1_ = bf16[2,4,48,768]{3,2,1,0:T(8,128)(2,1)S(1)} collective-permute-done((bf16[2,4,48,768]{3,2,1,0:T(8,128)(2,1)S(1)}, bf16[2,4,48,768]{3,2,1,0:T(8,128)(2,1)S(1)}, u32[]{:S(2)}, u32[]{:S(2)}) %collective-permute-start.31) | collective-permute-done | bytes 589856 | tf_op jit(solution)/shard_map/ppermute | solution.py:140
  111.1 1.2 collective-permute-done.34.refs_5_
  112.4 2.2 %collective-permute-done.33.refs_3_ = bf16[1,4,48,768]{3,2,1,0:T(8,128)(2,1)S(1)} collective-permute-done((bf16[1,4,48,768]{3,2,1,0:T(8,128)(2,1)S(1)}, bf16[1,4,48,768]{3,2,1,0:T(8,128)(2,1)S(1)}, u32[]{:S(2)}, u32[]{:S(2)}) %collective-permute-start.33) | collective-permute-done | bytes 294944 | tf_op jit(solution)/shard_map/ppermute | solution.py:140
  114.7 1.1 collective-permute-start.35
  115.9 1.7 %collective-permute-start.38 = (bf16[1,2,48,768]{3,2,1,0:T(8,128)(2,1)S(1)}, bf16[1,2,48,768]{3,2,1,0:T(8,128)(2,1)S(1)}, u32[]{:S(2)}, u32[]{:S(2)}) collective-permute-start(bf16[1,2,48,768]{3,2,1,0:T(8,128)(2,1)S(1)} %get-tuple-element.120), channel_id=1, source_target_pairs={{0,4},{1,3},{2,6},{3,1},{4,0},{5,7},{6,2},{7,5},{8,12},{9,11},{10,... | collective-permute-start | bytes 442376 | tf_op jit(solution)/shard_map/ppermute | solution.py:140
  117.9 1.7 %collective-permute-start.36 = (f32[2304]{0:T(1024)S(1)}, f32[2304]{0:T(1024)S(1)}, u32[]{:S(2)}, u32[]{:S(2)}) collective-permute-start(f32[2304]{0:T(1024)S(1)} %add.151), channel_id=1, source_target_pairs={{0,8},{1,9},{2,10},{3,11},{4,12},{5,13},{6,14},{7,15},{8,0},{9,1},... | collective-permute-start | bytes 27656 | tf_op jit(solution)/shard_map/ppermute | solution.py:140
  119.6 6.6 %collective-permute-done.36 = f32[2304]{0:T(1024)S(1)} collective-permute-done((f32[2304]{0:T(1024)S(1)}, f32[2304]{0:T(1024)S(1)}, u32[]{:S(2)}, u32[]{:S(2)}) %collective-permute-start.36) | collective-permute-done | bytes 9248 | tf_op jit(solution)/shard_map/ppermute | solution.py:140
  126.3 1.2 collective-permute-start.39
  127.5 1.8 %collective-permute-start.41 = (f32[2304]{0:T(1024)S(1)}, f32[2304]{0:T(1024)S(1)}, u32[]{:S(2)}, u32[]{:S(2)}) collective-permute-start(f32[2304]{0:T(1024)S(1)} %add.152), channel_id=1, source_target_pairs={{0,16},{1,17},{2,18},{3,19},{4,20},{5,21},{6,22},{7,23},{8,24},{9,... | collective-permute-start | bytes 27656 | tf_op jit(solution)/shard_map/ppermute | solution.py:140
  129.3 1.7 %collective-permute-start.40 = (bf16[2,1,48,768]{3,2,1,0:T(8,128)(2,1)S(1)}, bf16[2,1,48,768]{3,2,1,0:T(8,128)(2,1)S(1)}, u32[]{:S(2)}, u32[]{:S(2)}) collective-permute-start(bf16[2,1,48,768]{3,2,1,0:T(8,128)(2,1)S(1)} %get-tuple-element.124), channel_id=1, source_target_pairs={{0,2},{1,5},{2,0},{3,7},{4,6},{5,1},{6,4},{7,3},{8,10},{9,13},{10,... | collective-permute-start | bytes 442376 | tf_op jit(solution)/shard_map/ppermute | solution.py:140
  131.0 3.0 %collective-permute-done.41 = f32[2304]{0:T(1024)S(1)} collective-permute-done((f32[2304]{0:T(1024)S(1)}, f32[2304]{0:T(1024)S(1)}, u32[]{:S(2)}, u32[]{:S(2)}) %collective-permute-start.41) | collective-permute-done | bytes 9248 | tf_op jit(solution)/shard_map/ppermute | solution.py:140
  (106 shorter events, 21.2 us)
Async XLA Ops:
  0.6 13.8 %copy-start = (bf16[2,128,1536]{2,1,0:T(8,128)(2,1)S(1)}, bf16[2,128,1536]{2,1,0:T(8,128)(2,1)}, u32[]{:S(2)}) copy-start(bf16[2,128,1536]{2,1,0:T(8,128)(2,1)} %features_ref) | copy-start | bytes 2359300
  1.6 11.1 %collective-permute-start = (bf16[2,1,48,768]{3,2,0,1:T(8,128)(2,1)S(1)}, bf16[2,1,48,768]{3,2,0,1:T(8,128)(2,1)S(1)}, u32[]{:S(2)}, u32[]{:S(2)}) collective-permute-start(bf16[2,1,48,768]{3,2,0,1:T(8,128)(2,1)S(1)} %get-tuple-element.153), channel_id=1, source_target_pairs={{0,16},{1,17},{2,18},{3,19},{4,20},{5,21},{6,22},{7,23},{8,24},{9,... | collective-permute-start | bytes 442376 | tf_op jit(solution)/shard_map/ppermute | solution.py:140
  7.5 5.2 %collective-permute-start.1 = (bf16[2,1,48,768]{3,2,1,0:T(8,128)(2,1)S(1)}, bf16[2,1,48,768]{3,2,1,0:T(8,128)(2,1)S(1)}, u32[]{:S(2)}, u32[]{:S(2)}) collective-permute-start(bf16[2,1,48,768]{3,2,1,0:T(8,128)(2,1)S(1)} %pad_maximum_fusion.refs_2_), channel_id=1, source_target_pairs={{0,2},{1,5},{2,0},{3,7},{4,6},{5,1},{6,4},{7,3},{8,10},{9,13},{10,... | collective-permute-start | bytes 442376 | tf_op jit(solution)/shard_map/ppermute | solution.py:140
  12.8 11.4 %collective-permute-start.2 = (bf16[2,2,48,768]{3,2,1,0:T(8,128)(2,1)S(1)}, bf16[2,2,48,768]{3,2,1,0:T(8,128)(2,1)S(1)}, u32[]{:S(2)}, u32[]{:S(2)}) collective-permute-start(bf16[2,2,48,768]{3,2,1,0:T(8,128)(2,1)S(1)} %get-tuple-element.66.refs_0_), channel_id=1, source_target_pairs={{0,8},{1,9},{2,10},{3,11},{4,12},{5,13},{6,14},{7,15},{8,0},{9,1},... | collective-permute-start | bytes 884744 | tf_op jit(solution)/shard_map/ppermute | solution.py:140
  14.5 4.7 %collective-permute-start.4 = (bf16[1,32,1536]{2,1,0:T(8,128)(2,1)S(1)}, bf16[1,32,1536]{2,1,0:T(8,128)(2,1)S(1)}, u32[]{:S(2)}, u32[]{:S(2)}) collective-permute-start(bf16[1,32,1536]{2,1,0:T(8,128)(2,1)S(1)} %get-tuple-element.148), channel_id=1, source_target_pairs={{0,1},{1,0},{2,3},{3,2},{4,5},{5,4},{6,7},{7,6},{8,9},{9,8},{10,11... | collective-permute-start | bytes 294920 | tf_op jit(solution)/shard_map/ppermute | solution.py:140
  14.6 5.3 %collective-permute-start.5 = (bf16[1,32,1536]{2,1,0:T(8,128)(2,1)S(1)}, bf16[1,32,1536]{2,1,0:T(8,128)(2,1)S(1)}, u32[]{:S(2)}, u32[]{:S(2)}) collective-permute-start(bf16[1,32,1536]{2,1,0:T(8,128)(2,1)S(1)} %get-tuple-element.146), channel_id=1, source_target_pairs={{0,1},{1,0},{2,3},{3,2},{4,5},{5,4},{6,7},{7,6},{8,9},{9,8},{10,11... | collective-permute-start | bytes 294920 | tf_op jit(solution)/shard_map/ppermute | solution.py:140
  15.2 5.4 %collective-permute-start.3 = (bf16[1,2,48,768]{3,2,1,0:T(8,128)(2,1)S(1)}, bf16[1,2,48,768]{3,2,1,0:T(8,128)(2,1)S(1)}, u32[]{:S(2)}, u32[]{:S(2)}) collective-permute-start(bf16[1,2,48,768]{3,2,1,0:T(8,128)(2,1)S(1)} %get-tuple-element.67.refs_0_), channel_id=1, source_target_pairs={{0,4},{1,3},{2,6},{3,1},{4,0},{5,7},{6,2},{7,5},{8,12},{9,11},{10,... | collective-permute-start | bytes 442376 | tf_op jit(solution)/shard_map/ppermute | solution.py:140
  16.7 7.5 %collective-permute-start.8 = (bf16[1,2,48,768]{3,2,1,0:T(8,128)(2,1)S(1)}, bf16[1,2,48,768]{3,2,1,0:T(8,128)(2,1)S(1)}, u32[]{:S(2)}, u32[]{:S(2)}) collective-permute-start(bf16[1,2,48,768]{3,2,1,0:T(8,128)(2,1)S(1)} %get-tuple-element.70.refs_2_), channel_id=1, source_target_pairs={{0,16},{1,17},{2,18},{3,19},{4,20},{5,21},{6,22},{7,23},{8,24},{9,... | collective-permute-start | bytes 442376 | tf_op jit(solution)/shard_map/ppermute | solution.py:140
  19.2 1.4 collective-permute-start.6
  19.9 0.7 collective-permute-start.7
  24.3 16.9 %collective-permute-start.9 = (bf16[2,4,48,768]{3,2,1,0:T(8,128)(2,1)S(1)}, bf16[2,4,48,768]{3,2,1,0:T(8,128)(2,1)S(1)}, u32[]{:S(2)}, u32[]{:S(2)}) collective-permute-start(bf16[2,4,48,768]{3,2,1,0:T(8,128)(2,1)S(1)} %get-tuple-element.73.refs_0_), channel_id=1, source_target_pairs={{0,2},{1,5},{2,0},{3,7},{4,6},{5,1},{6,4},{7,3},{8,10},{9,13},{10,... | collective-permute-start | bytes 1769480 | tf_op jit(solution)/shard_map/ppermute | solution.py:140
  28.9 12.2 %collective-permute-start.10 = (bf16[1,4,48,768]{3,2,1,0:T(8,128)(2,1)S(1)}, bf16[1,4,48,768]{3,2,1,0:T(8,128)(2,1)S(1)}, u32[]{:S(2)}, u32[]{:S(2)}) collective-permute-start(bf16[1,4,48,768]{3,2,1,0:T(8,128)(2,1)S(1)} %get-tuple-element.75.refs_2_), channel_id=1, source_target_pairs={{0,8},{1,9},{2,10},{3,11},{4,12},{5,13},{6,14},{7,15},{8,0},{9,1},... | collective-permute-start | bytes 884744 | tf_op jit(solution)/shard_map/ppermute | solution.py:140
  31.2 7.8 %collective-permute-start.11 = (bf16[1,2,48,768]{3,2,1,0:T(8,128)(2,1)S(1)}, bf16[1,2,48,768]{3,2,1,0:T(8,128)(2,1)S(1)}, u32[]{:S(2)}, u32[]{:S(2)}) collective-permute-start(bf16[1,2,48,768]{3,2,1,0:T(8,128)(2,1)S(1)} %get-tuple-element.67.refs_0_), channel_id=1, source_target_pairs={{0,16},{1,17},{2,18},{3,19},{4,20},{5,21},{6,22},{7,23},{8,24},{9,... | collective-permute-start | bytes 442376 | tf_op jit(solution)/shard_map/ppermute | solution.py:140
  39.0 5.2 %copy-start.2 = (f32[1536]{0:T(1024)S(1)}, f32[1536]{0:T(1024)}, u32[]{:S(2)}) copy-start(f32[1536]{0:T(1024)} %param.10) | copy-start | bytes 18436
  39.0 5.3 %copy-start.1 = (bf16[2,128,1536]{2,1,0:T(8,128)(2,1)S(1)}, bf16[2,128,1536]{2,1,0:T(8,128)(2,1)}, u32[]{:S(2)}) copy-start(bf16[2,128,1536]{2,1,0:T(8,128)(2,1)} %param.7) | copy-start | bytes 2359300
  41.3 23.9 %collective-permute-start.14 = (bf16[3,8,48,768]{3,2,1,0:T(8,128)(2,1)S(1)}, bf16[3,8,48,768]{3,2,1,0:T(8,128)(2,1)S(1)}, u32[]{:S(2)}, u32[]{:S(2)}) collective-permute-start(bf16[3,8,48,768]{3,2,1,0:T(8,128)(2,1)S(1)} %assemble.10.refs_0_), channel_id=1, source_target_pairs={{0,4},{1,3},{2,6},{3,1},{4,0},{5,7},{6,2},{7,5},{8,12},{9,11},{10,... | collective-permute-start | bytes 5308424 | tf_op jit(solution)/shard_map/ppermute | solution.py:140
  42.9 9.7 %collective-permute-start.12 = (bf16[1,2,48,768]{3,2,1,0:T(8,128)(2,1)S(1)}, bf16[1,2,48,768]{3,2,1,0:T(8,128)(2,1)S(1)}, u32[]{:S(2)}, u32[]{:S(2)}) collective-permute-start(bf16[1,2,48,768]{3,2,1,0:T(8,128)(2,1)S(1)} %collective-permute-done.3.refs_0_), channel_id=1, source_target_pairs={{0,16},{1,17},{2,18},{3,19},{4,20},{5,21},{6,22},{7,23},{8,24},{9,... | collective-permute-start | bytes 442376 | tf_op jit(solution)/shard_map/ppermute | solution.py:140
  44.1 21.7 %collective-permute-start.13 = (bf16[3,8,48,768]{3,2,1,0:T(8,128)(2,1)S(1)}, bf16[3,8,48,768]{3,2,1,0:T(8,128)(2,1)S(1)}, u32[]{:S(2)}, u32[]{:S(2)}) collective-permute-start(bf16[3,8,48,768]{3,2,1,0:T(8,128)(2,1)S(1)} %assemble.10.refs_0_), channel_id=1, source_target_pairs={{0,1},{1,0},{2,3},{3,2},{4,5},{5,4},{6,7},{7,6},{8,9},{9,8},{10,11... | collective-permute-start | bytes 5308424 | tf_op jit(solution)/shard_map/ppermute | solution.py:140
  44.2 13.0 %collective-permute-start.16 = (bf16[1,4,48,768]{3,2,1,0:T(8,128)(2,1)S(1)}, bf16[1,4,48,768]{3,2,1,0:T(8,128)(2,1)S(1)}, u32[]{:S(2)}, u32[]{:S(2)}) collective-permute-start(bf16[1,4,48,768]{3,2,1,0:T(8,128)(2,1)S(1)} %assemble.9.refs_0_), channel_id=1, source_target_pairs={{0,8},{1,9},{2,10},{3,11},{4,12},{5,13},{6,14},{7,15},{8,0},{9,1},... | collective-permute-start | bytes 884744 | tf_op jit(solution)/shard_map/ppermute | solution.py:140
  52.6 10.5 %collective-permute-start.15 = (bf16[1,4,48,768]{3,2,1,0:T(8,128)(2,1)S(1)}, bf16[1,4,48,768]{3,2,1,0:T(8,128)(2,1)S(1)}, u32[]{:S(2)}, u32[]{:S(2)}) collective-permute-start(bf16[1,4,48,768]{3,2,1,0:T(8,128)(2,1)S(1)} %assemble.11.refs_0_), channel_id=1, source_target_pairs={{0,8},{1,9},{2,10},{3,11},{4,12},{5,13},{6,14},{7,15},{8,0},{9,1},... | collective-permute-start | bytes 884744 | tf_op jit(solution)/shard_map/ppermute | solution.py:140
  57.2 6.0 %collective-permute-start.18 = (bf16[1,8,48,768]{3,2,1,0:T(8,128)(2,1)S(1)}, bf16[1,8,48,768]{3,2,1,0:T(8,128)(2,1)S(1)}, u32[]{:S(2)}, u32[]{:S(2)}) collective-permute-start(bf16[1,8,48,768]{3,2,1,0:T(8,128)(2,1)S(1)} %assemble.12.refs_0_), channel_id=1, source_target_pairs={{0,1},{1,0},{2,3},{3,2},{4,5},{5,4},{6,7},{7,6},{8,9},{9,8},{10,11... | collective-permute-start | bytes 1769480 | tf_op jit(solution)/shard_map/ppermute | solution.py:140
  63.1 2.1 %collective-permute-start.17 = (bf16[1,8,48,768]{3,2,1,0:T(8,128)(2,1)S(1)}, bf16[1,8,48,768]{3,2,1,0:T(8,128)(2,1)S(1)}, u32[]{:S(2)}, u32[]{:S(2)}) collective-permute-start(bf16[1,8,48,768]{3,2,1,0:T(8,128)(2,1)S(1)} %assemble.13.refs_1_), channel_id=1, source_target_pairs={{0,1},{1,0},{2,3},{3,2},{4,5},{5,4},{6,7},{7,6},{8,9},{9,8},{10,11... | collective-permute-start | bytes 1769480 | tf_op jit(solution)/shard_map/ppermute | solution.py:140
  65.2 3.7 %collective-permute-start.19 = (bf16[3,8,48,768]{3,2,1,0:T(8,128)(2,1)S(1)}, bf16[3,8,48,768]{3,2,1,0:T(8,128)(2,1)S(1)}, u32[]{:S(2)}, u32[]{:S(2)}) collective-permute-start(bf16[3,8,48,768]{3,2,1,0:T(8,128)(2,1)S(1)} %collective-permute-done.14.refs_1_), channel_id=1, source_target_pairs={{0,1},{1,0},{2,3},{3,2},{4,5},{5,4},{6,7},{7,6},{8,9},{9,8},{10,11... | collective-permute-start | bytes 5308424 | tf_op jit(solution)/shard_map/ppermute | solution.py:140
  68.9 0.8 copy-start.3
  71.9 3.8 %collective-permute-start.20 = (bf16[3,8,48,768]{3,2,1,0:T(8,128)(2,1)S(1)}, bf16[3,8,48,768]{3,2,1,0:T(8,128)(2,1)S(1)}, u32[]{:S(2)}, u32[]{:S(2)}) collective-permute-start(bf16[3,8,48,768]{3,2,1,0:T(8,128)(2,1)S(1)} %convolution_convert_fusion.1), channel_id=1, source_target_pairs={{0,1},{1,0},{2,3},{3,2},{4,5},{5,4},{6,7},{7,6},{8,9},{9,8},{10,11... | collective-permute-start | bytes 5308424 | tf_op jit(solution)/shard_map/ppermute | solution.py:140
  73.3 6.4 %collective-permute-start.21 = (bf16[2,8,48,768]{3,2,1,0:T(8,128)(2,1)S(1)}, bf16[2,8,48,768]{3,2,1,0:T(8,128)(2,1)S(1)}, u32[]{:S(2)}, u32[]{:S(2)}) collective-permute-start(bf16[2,8,48,768]{3,2,1,0:T(8,128)(2,1)S(1)} %convolution_convert_fusion.2), channel_id=1, source_target_pairs={{0,1},{1,0},{2,3},{3,2},{4,5},{5,4},{6,7},{7,6},{8,9},{9,8},{10,11... | collective-permute-start | bytes 3538952 | tf_op jit(solution)/shard_map/ppermute | solution.py:140
  73.7 8.0 %collective-permute-start.22 = (bf16[3,8,48,768]{3,2,1,0:T(8,128)(2,1)S(1)}, bf16[3,8,48,768]{3,2,1,0:T(8,128)(2,1)S(1)}, u32[]{:S(2)}, u32[]{:S(2)}) collective-permute-start(bf16[3,8,48,768]{3,2,1,0:T(8,128)(2,1)S(1)} %convolution_convert_fusion), channel_id=1, source_target_pairs={{0,1},{1,0},{2,3},{3,2},{4,5},{5,4},{6,7},{7,6},{8,9},{9,8},{10,11... | collective-permute-start | bytes 5308424 | tf_op jit(solution)/shard_map/ppermute | solution.py:140
  73.8 8.5 %collective-permute-start.25 = (bf16[2,32,768]{2,1,0:T(8,128)(2,1)S(1)}, bf16[2,32,768]{2,1,0:T(8,128)(2,1)S(1)}, u32[]{:S(2)}, u32[]{:S(2)}) collective-permute-start(bf16[2,32,768]{2,1,0:T(8,128)(2,1)S(1)} %get-tuple-element.144), channel_id=1, source_target_pairs={{0,1},{1,0},{2,3},{3,2},{4,5},{5,4},{6,7},{7,6},{8,9},{9,8},{10,11... | collective-permute-start | bytes 294920 | tf_op jit(solution)/shard_map/ppermute | solution.py:140
  74.3 8.1 %collective-permute-start.26 = (bf16[2,32,768]{2,1,0:T(8,128)(2,1)S(1)}, bf16[2,32,768]{2,1,0:T(8,128)(2,1)S(1)}, u32[]{:S(2)}, u32[]{:S(2)}) collective-permute-start(bf16[2,32,768]{2,1,0:T(8,128)(2,1)S(1)} %get-tuple-element.143), channel_id=1, source_target_pairs={{1,2},{2,1},{3,4},{4,3},{5,6},{6,5},{7,8},{8,7},{9,10},{10,9},{11,... | collective-permute-start | bytes 294920 | tf_op jit(solution)/shard_map/ppermute | solution.py:140
  76.3 23.9 %collective-permute-start.23 = (bf16[3,8,48,768]{3,2,1,0:T(8,128)(2,1)S(1)}, bf16[3,8,48,768]{3,2,1,0:T(8,128)(2,1)S(1)}, u32[]{:S(2)}, u32[]{:S(2)}) collective-permute-start(bf16[3,8,48,768]{3,2,1,0:T(8,128)(2,1)S(1)} %add_convert_fusion), channel_id=1, source_target_pairs={{0,4},{1,3},{2,6},{3,1},{4,0},{5,7},{6,2},{7,5},{8,12},{9,11},{10,... | collective-permute-start | bytes 5308424 | tf_op jit(solution)/shard_map/ppermute | solution.py:140
  79.9 8.6 %collective-permute-start.24 = (bf16[1,4,48,768]{3,2,1,0:T(8,128)(2,1)S(1)}, bf16[1,4,48,768]{3,2,1,0:T(8,128)(2,1)S(1)}, u32[]{:S(2)}, u32[]{:S(2)}) collective-permute-start(bf16[1,4,48,768]{3,2,1,0:T(8,128)(2,1)S(1)} %fusion.20), channel_id=1, source_target_pairs={{0,8},{1,9},{2,10},{3,11},{4,12},{5,13},{6,14},{7,15},{8,0},{9,1},... | collective-permute-start | bytes 884744 | tf_op jit(solution)/shard_map/ppermute | solution.py:140
  88.6 10.8 %collective-permute-start.27 = (bf16[1,4,48,768]{3,2,1,0:T(8,128)(2,1)S(1)}, bf16[1,4,48,768]{3,2,1,0:T(8,128)(2,1)S(1)}, u32[]{:S(2)}, u32[]{:S(2)}) collective-permute-start(bf16[1,4,48,768]{3,2,1,0:T(8,128)(2,1)S(1)} %fusion.21), channel_id=1, source_target_pairs={{0,8},{1,9},{2,10},{3,11},{4,12},{5,13},{6,14},{7,15},{8,0},{9,1},... | collective-permute-start | bytes 884744 | tf_op jit(solution)/shard_map/ppermute | solution.py:140
  89.8 9.6 %collective-permute-start.30 = (bf16[1,2,48,768]{3,2,1,0:T(8,128)(2,1)S(1)}, bf16[1,2,48,768]{3,2,1,0:T(8,128)(2,1)S(1)}, u32[]{:S(2)}, u32[]{:S(2)}) collective-permute-start(bf16[1,2,48,768]{3,2,1,0:T(8,128)(2,1)S(1)} %get-tuple-element.97), channel_id=1, source_target_pairs={{0,16},{1,17},{2,18},{3,19},{4,20},{5,21},{6,22},{7,23},{8,24},{9,... | collective-permute-start | bytes 442376 | tf_op jit(solution)/shard_map/ppermute | solution.py:140
  91.7 1.2 collective-permute-start.28
  92.8 3.9 %collective-permute-start.29 = (f32[2304]{0:T(1024)S(1)}, f32[2304]{0:T(1024)S(1)}, u32[]{:S(2)}, u32[]{:S(2)}) collective-permute-start(f32[2304]{0:T(1024)S(1)} %add.149), channel_id=1, source_target_pairs={{0,2},{1,3},{2,0},{3,1},{4,6},{5,7},{6,4},{7,5},{8,10},{9,11},{10,... | collective-permute-start | bytes 27656 | tf_op jit(solution)/shard_map/ppermute | solution.py:140
  101.3 9.9 %collective-permute-start.31 = (bf16[2,4,48,768]{3,2,1,0:T(8,128)(2,1)S(1)}, bf16[2,4,48,768]{3,2,1,0:T(8,128)(2,1)S(1)}, u32[]{:S(2)}, u32[]{:S(2)}) collective-permute-start(bf16[2,4,48,768]{3,2,1,0:T(8,128)(2,1)S(1)} %get-tuple-element.102), channel_id=1, source_target_pairs={{0,2},{1,5},{2,0},{3,7},{4,6},{5,1},{6,4},{7,3},{8,10},{9,13},{10,... | collective-permute-start | bytes 1769480 | tf_op jit(solution)/shard_map/ppermute | solution.py:140
  103.2 11.4 %collective-permute-start.33 = (bf16[1,4,48,768]{3,2,1,0:T(8,128)(2,1)S(1)}, bf16[1,4,48,768]{3,2,1,0:T(8,128)(2,1)S(1)}, u32[]{:S(2)}, u32[]{:S(2)}) collective-permute-start(bf16[1,4,48,768]{3,2,1,0:T(8,128)(2,1)S(1)} %get-tuple-element.109), channel_id=1, source_target_pairs={{0,8},{1,9},{2,10},{3,11},{4,12},{5,13},{6,14},{7,15},{8,0},{9,1},... | collective-permute-start | bytes 884744 | tf_op jit(solution)/shard_map/ppermute | solution.py:140
  104.9 7.5 %collective-permute-start.34 = (bf16[1,2,48,768]{3,2,1,0:T(8,128)(2,1)S(1)}, bf16[1,2,48,768]{3,2,1,0:T(8,128)(2,1)S(1)}, u32[]{:S(2)}, u32[]{:S(2)}) collective-permute-start(bf16[1,2,48,768]{3,2,1,0:T(8,128)(2,1)S(1)} %get-tuple-element.111), channel_id=1, source_target_pairs={{0,16},{1,17},{2,18},{3,19},{4,20},{5,21},{6,22},{7,23},{8,24},{9,... | collective-permute-start | bytes 442376 | tf_op jit(solution)/shard_map/ppermute | solution.py:140
  104.9 3.9 %collective-permute-start.32 = (f32[2304]{0:T(1024)S(1)}, f32[2304]{0:T(1024)S(1)}, u32[]{:S(2)}, u32[]{:S(2)}) collective-permute-start(f32[2304]{0:T(1024)S(1)} %add.150), channel_id=1, source_target_pairs={{0,4},{1,5},{2,6},{3,7},{4,0},{5,1},{6,2},{7,3},{8,12},{9,13},{10,... | collective-permute-start | bytes 27656 | tf_op jit(solution)/shard_map/ppermute | solution.py:140
  114.7 11.5 %collective-permute-start.35 = (bf16[2,2,48,768]{3,2,1,0:T(8,128)(2,1)S(1)}, bf16[2,2,48,768]{3,2,1,0:T(8,128)(2,1)S(1)}, u32[]{:S(2)}, u32[]{:S(2)}) collective-permute-start(bf16[2,2,48,768]{3,2,1,0:T(8,128)(2,1)S(1)} %get-tuple-element.113), channel_id=1, source_target_pairs={{0,8},{1,9},{2,10},{3,11},{4,12},{5,13},{6,14},{7,15},{8,0},{9,1},... | collective-permute-start | bytes 884744 | tf_op jit(solution)/shard_map/ppermute | solution.py:140
  115.9 10.3 %collective-permute-start.38 = (bf16[1,2,48,768]{3,2,1,0:T(8,128)(2,1)S(1)}, bf16[1,2,48,768]{3,2,1,0:T(8,128)(2,1)S(1)}, u32[]{:S(2)}, u32[]{:S(2)}) collective-permute-start(bf16[1,2,48,768]{3,2,1,0:T(8,128)(2,1)S(1)} %get-tuple-element.120), channel_id=1, source_target_pairs={{0,4},{1,3},{2,6},{3,1},{4,0},{5,7},{6,2},{7,5},{8,12},{9,11},{10,... | collective-permute-start | bytes 442376 | tf_op jit(solution)/shard_map/ppermute | solution.py:140
  117.6 8.6 %collective-permute-start.37 = (bf16[1,2,48,768]{3,2,1,0:T(8,128)(2,1)S(1)}, bf16[1,2,48,768]{3,2,1,0:T(8,128)(2,1)S(1)}, u32[]{:S(2)}, u32[]{:S(2)}) collective-permute-start(bf16[1,2,48,768]{3,2,1,0:T(8,128)(2,1)S(1)} %get-tuple-element.117), channel_id=1, source_target_pairs={{0,16},{1,17},{2,18},{3,19},{4,20},{5,21},{6,22},{7,23},{8,24},{9,... | collective-permute-start | bytes 442376 | tf_op jit(solution)/shard_map/ppermute | solution.py:140
  117.9 8.3 %collective-permute-start.36 = (f32[2304]{0:T(1024)S(1)}, f32[2304]{0:T(1024)S(1)}, u32[]{:S(2)}, u32[]{:S(2)}) collective-permute-start(f32[2304]{0:T(1024)S(1)} %add.151), channel_id=1, source_target_pairs={{0,8},{1,9},{2,10},{3,11},{4,12},{5,13},{6,14},{7,15},{8,0},{9,1},... | collective-permute-start | bytes 27656 | tf_op jit(solution)/shard_map/ppermute | solution.py:140
  126.3 8.8 %collective-permute-start.39 = (bf16[2,1,48,768]{3,2,1,0:T(8,128)(2,1)S(1)}, bf16[2,1,48,768]{3,2,1,0:T(8,128)(2,1)S(1)}, u32[]{:S(2)}, u32[]{:S(2)}) collective-permute-start(bf16[2,1,48,768]{3,2,1,0:T(8,128)(2,1)S(1)} %get-tuple-element.122), channel_id=1, source_target_pairs={{0,16},{1,17},{2,18},{3,19},{4,20},{5,21},{6,22},{7,23},{8,24},{9,... | collective-permute-start | bytes 442376 | tf_op jit(solution)/shard_map/ppermute | solution.py:140
  127.5 6.5 %collective-permute-start.41 = (f32[2304]{0:T(1024)S(1)}, f32[2304]{0:T(1024)S(1)}, u32[]{:S(2)}, u32[]{:S(2)}) collective-permute-start(f32[2304]{0:T(1024)S(1)} %add.152), channel_id=1, source_target_pairs={{0,16},{1,17},{2,18},{3,19},{4,20},{5,21},{6,22},{7,23},{8,24},{9,... | collective-permute-start | bytes 27656 | tf_op jit(solution)/shard_map/ppermute | solution.py:140
  129.3 5.9 %collective-permute-start.40 = (bf16[2,1,48,768]{3,2,1,0:T(8,128)(2,1)S(1)}, bf16[2,1,48,768]{3,2,1,0:T(8,128)(2,1)S(1)}, u32[]{:S(2)}, u32[]{:S(2)}) collective-permute-start(bf16[2,1,48,768]{3,2,1,0:T(8,128)(2,1)S(1)} %get-tuple-element.124), channel_id=1, source_target_pairs={{0,2},{1,5},{2,0},{3,7},{4,6},{5,1},{6,4},{7,3},{8,10},{9,13},{10,... | collective-permute-start | bytes 442376 | tf_op jit(solution)/shard_map/ppermute | solution.py:140

commit v8 on v7

--- a/solution.py
+++ b/solution.py
@@ -497,7 +497,7 @@
     recv_a = send(after(message_a, message_b), Z_NEAR)
     gains = after(gains, message_b)
     gains = gains + send(gains, CORE)
-    gains = gains + send(gains, links(lambda i: i ^ 2))
+    gains = gains + send(gains, Z_NEAR)
 
     recv_a = after(recv_a, gains)
     message, message_l, message_a, message_p, kept, kept_l, kept_a, kept_b = fold(
@@ -515,7 +515,7 @@
     )
     recv, recv_l, recv_a = send(message, FIRST), send(message_l, Z_NEAR), send(message_a, Z_FAR)
     gains = after(gains, message)
-    gains = gains + send(gains, links(lambda i: i ^ 4))
+    gains = gains + send(gains, Z_FAR)
     block_out = project_back(
         after(hidden, message), flat, (proj_a, proj_b, proj_a_other, proj_b_other)
     ).reshape(features.shape)
@@ -535,7 +535,8 @@
     message_p = after(message_p, message)
     recv, recv_l, recv_p = send(message, Z_NEAR), send(message_l, Z_FAR), send(message_p, SECOND)
     gains = after(gains, message)
-    gains = gains + send(gains, Z_NEAR)
+    gains = gains + send(gains, links(lambda i: i ^ 2))
+    gains = gains + send(gains, links(lambda i: i ^ 4))
 
     recv = after(recv, gains)
     message, message_r, kept, kept_r = fold(
@@ -548,8 +549,6 @@
         ),
     )
     recv, recv_r = send(message, Z_FAR), send(message_r, FIRST)
-    gains = after(gains, message)
-    gains = gains + send(gains, Z_FAR)
 
     sums = kept + as_f32(recv)
     sums_r = kept_r + as_f32(recv_r)

time: 137 us -> 136 us (level)
  waiting for transfers between devices: 58.1 us -> 54.4 us
  starting transfers between devices: 48.9 us -> 51.8 us
    ppermute x42, waiting for transfers between devices: 58.1 us -> 54.4 us  [send(): return lax.ppermute(block, 'seq', pairs)]
    ppermute x42, starting transfers between devices: 48.9 us -> 51.8 us  [send(): return lax.ppermute(block, 'seq', pairs)]
where the time goes in v8:
time: 136 us
  waiting for transfers between devices  54.4 us (40%)
  starting transfers between devices  51.8 us (38%)
  Pallas kernels  9.55 us (7%)
  matrix products  9.09 us (7%)
  other arithmetic  6.47 us (5%)
  local copies, waits for them, and re-layouts  3.47 us (3%)
    ppermute x42, waiting for transfers between devices, send(): return lax.ppermute(block, 'seq', pairs)  54.4 us
    ppermute x42, starting transfers between devices, send(): return lax.ppermute(block, 'seq', pairs)  51.8 us
    dot_general x8, matrix products, contract(): jnp.einsum('ct,ci->ti', left.reshape(-1, left.shape[-1]), right.reshape(-...  5.16 us
    dot_general x9, matrix products, rows_dot(): jnp.einsum('mnrt,ti->mnri', left, right, preferred_element_type=jnp.float32)  3.94 us
    pallas_call x1, Pallas kernels, prepare(): pl.pallas_call(prepare_kernel, out_shape=[shape(KERNEL_TAPS), shape(1)],...  2.95 us
  transfers between devices with their start and end apart: 42, of which 20 were waited for; matrix products, arithmetic and copies ran while one was open for 10% of the time, Pallas kernels for 6%

profile of v8, /device:TPU:0, one launch (start us, length us, event | category | flops | bytes accessed | tf_op | source)
XLA Modules:
  0.0 135.9 jit_solution(9410715787328663428)
XLA Ops:
  0.6 1.0 slice_bitcast_fusion.8
  1.6 4.1 %collective-permute-start = (bf16[2,1,48,768]{3,2,0,1:T(8,128)(2,1)S(1)}, bf16[2,1,48,768]{3,2,0,1:T(8,128)(2,1)S(1)}, u32[]{:S(2)}, u32[]{:S(2)}) collective-permute-start(bf16[2,1,48,768]{3,2,0,1:T(8,128)(2,1)S(1)} %get-tuple-element.151), channel_id=1, source_target_pairs={{0,16},{1,17},{2,18},{3,19},{4,20},{5,21},{6,22},{7,23},{8,24},{9,... | collective-permute-start | bytes 442376 | tf_op jit(solution)/shard_map/ppermute | solution.py:140
  5.8 0.9 slice_bitcast_fusion.9
  6.6 0.9 pad_maximum_fusion.refs_2_
  7.5 1.6 %collective-permute-start.1 = (bf16[2,1,48,768]{3,2,1,0:T(8,128)(2,1)S(1)}, bf16[2,1,48,768]{3,2,1,0:T(8,128)(2,1)S(1)}, u32[]{:S(2)}, u32[]{:S(2)}) collective-permute-start(bf16[2,1,48,768]{3,2,1,0:T(8,128)(2,1)S(1)} %pad_maximum_fusion.refs_2_), channel_id=1, source_target_pairs={{0,2},{1,5},{2,0},{3,7},{4,6},{5,1},{6,4},{7,3},{8,10},{9,13},{10,... | collective-permute-start | bytes 442376 | tf_op jit(solution)/shard_map/ppermute | solution.py:140
  9.1 3.7 %collective-permute-done = bf16[2,1,48,768]{3,2,0,1:T(8,128)(2,1)S(1)} collective-permute-done((bf16[2,1,48,768]{3,2,0,1:T(8,128)(2,1)S(1)}, bf16[2,1,48,768]{3,2,0,1:T(8,128)(2,1)S(1)}, u32[]{:S(2)}, u32[]{:S(2)}) %collective-permute-start) | collective-permute-done | bytes 147488 | tf_op jit(solution)/shard_map/ppermute | solution.py:140
  12.8 1.6 %collective-permute-start.2 = (bf16[2,2,48,768]{3,2,1,0:T(8,128)(2,1)S(1)}, bf16[2,2,48,768]{3,2,1,0:T(8,128)(2,1)S(1)}, u32[]{:S(2)}, u32[]{:S(2)}) collective-permute-start(bf16[2,2,48,768]{3,2,1,0:T(8,128)(2,1)S(1)} %get-tuple-element.65.refs_0_), channel_id=1, source_target_pairs={{0,8},{1,9},{2,10},{3,11},{4,12},{5,13},{6,14},{7,15},{8,0},{9,1},... | collective-permute-start | bytes 884744 | tf_op jit(solution)/shard_map/ppermute | solution.py:140
  15.2 1.5 %collective-permute-start.3 = (bf16[1,2,48,768]{3,2,1,0:T(8,128)(2,1)S(1)}, bf16[1,2,48,768]{3,2,1,0:T(8,128)(2,1)S(1)}, u32[]{:S(2)}, u32[]{:S(2)}) collective-permute-start(bf16[1,2,48,768]{3,2,1,0:T(8,128)(2,1)S(1)} %get-tuple-element.66.refs_0_), channel_id=1, source_target_pairs={{0,4},{1,3},{2,6},{3,1},{4,0},{5,7},{6,2},{7,5},{8,12},{9,11},{10,... | collective-permute-start | bytes 442376 | tf_op jit(solution)/shard_map/ppermute | solution.py:140
  16.7 2.5 %collective-permute-start.8 = (bf16[1,2,48,768]{3,2,1,0:T(8,128)(2,1)S(1)}, bf16[1,2,48,768]{3,2,1,0:T(8,128)(2,1)S(1)}, u32[]{:S(2)}, u32[]{:S(2)}) collective-permute-start(bf16[1,2,48,768]{3,2,1,0:T(8,128)(2,1)S(1)} %get-tuple-element.69.refs_2_), channel_id=1, source_target_pairs={{0,16},{1,17},{2,18},{3,19},{4,20},{5,21},{6,22},{7,23},{8,24},{9,... | collective-permute-start | bytes 442376 | tf_op jit(solution)/shard_map/ppermute | solution.py:140
  20.6 3.6 %collective-permute-done.2.refs_1_ = bf16[2,2,48,768]{3,2,1,0:T(8,128)(2,1)S(1)} collective-permute-done((bf16[2,2,48,768]{3,2,1,0:T(8,128)(2,1)S(1)}, bf16[2,2,48,768]{3,2,1,0:T(8,128)(2,1)S(1)}, u32[]{:S(2)}, u32[]{:S(2)}) %collective-permute-start.2) | collective-permute-done | bytes 294944 | tf_op jit(solution)/shard_map/ppermute | solution.py:140
  24.3 4.6 %collective-permute-start.9 = (bf16[2,4,48,768]{3,2,1,0:T(8,128)(2,1)S(1)}, bf16[2,4,48,768]{3,2,1,0:T(8,128)(2,1)S(1)}, u32[]{:S(2)}, u32[]{:S(2)}) collective-permute-start(bf16[2,4,48,768]{3,2,1,0:T(8,128)(2,1)S(1)} %get-tuple-element.72.refs_0_), channel_id=1, source_target_pairs={{0,2},{1,5},{2,0},{3,7},{4,6},{5,1},{6,4},{7,3},{8,10},{9,13},{10,... | collective-permute-start | bytes 1769480 | tf_op jit(solution)/shard_map/ppermute | solution.py:140
  28.9 2.3 %collective-permute-start.10 = (bf16[1,4,48,768]{3,2,1,0:T(8,128)(2,1)S(1)}, bf16[1,4,48,768]{3,2,1,0:T(8,128)(2,1)S(1)}, u32[]{:S(2)}, u32[]{:S(2)}) collective-permute-start(bf16[1,4,48,768]{3,2,1,0:T(8,128)(2,1)S(1)} %get-tuple-element.74.refs_2_), channel_id=1, source_target_pairs={{0,8},{1,9},{2,10},{3,11},{4,12},{5,13},{6,14},{7,15},{8,0},{9,1},... | collective-permute-start | bytes 884744 | tf_op jit(solution)/shard_map/ppermute | solution.py:140
  31.2 2.2 %collective-permute-start.11 = (bf16[1,2,48,768]{3,2,1,0:T(8,128)(2,1)S(1)}, bf16[1,2,48,768]{3,2,1,0:T(8,128)(2,1)S(1)}, u32[]{:S(2)}, u32[]{:S(2)}) collective-permute-start(bf16[1,2,48,768]{3,2,1,0:T(8,128)(2,1)S(1)} %get-tuple-element.66.refs_0_), channel_id=1, source_target_pairs={{0,16},{1,17},{2,18},{3,19},{4,20},{5,21},{6,22},{7,23},{8,24},{9,... | collective-permute-start | bytes 442376 | tf_op jit(solution)/shard_map/ppermute | solution.py:140
  33.4 5.6 %collective-permute-done.11.refs_1_ = bf16[1,2,48,768]{3,2,1,0:T(8,128)(2,1)S(1)} collective-permute-done((bf16[1,2,48,768]{3,2,1,0:T(8,128)(2,1)S(1)}, bf16[1,2,48,768]{3,2,1,0:T(8,128)(2,1)S(1)}, u32[]{:S(2)}, u32[]{:S(2)}) %collective-permute-start.11) | collective-permute-done | bytes 147488 | tf_op jit(solution)/shard_map/ppermute | solution.py:140
  39.0 2.1 %collective-permute-done.10.refs_3_ = bf16[1,4,48,768]{3,2,1,0:T(8,128)(2,1)S(1)} collective-permute-done((bf16[1,4,48,768]{3,2,1,0:T(8,128)(2,1)S(1)}, bf16[1,4,48,768]{3,2,1,0:T(8,128)(2,1)S(1)}, u32[]{:S(2)}, u32[]{:S(2)}) %collective-permute-start.10) | collective-permute-done | bytes 294944 | tf_op jit(solution)/shard_map/ppermute | solution.py:140
  41.3 1.6 %collective-permute-start.14 = (bf16[3,8,48,768]{3,2,1,0:T(8,128)(2,1)S(1)}, bf16[3,8,48,768]{3,2,1,0:T(8,128)(2,1)S(1)}, u32[]{:S(2)}, u32[]{:S(2)}) collective-permute-start(bf16[3,8,48,768]{3,2,1,0:T(8,128)(2,1)S(1)} %assemble.10.refs_0_), channel_id=1, source_target_pairs={{0,4},{1,3},{2,6},{3,1},{4,0},{5,7},{6,2},{7,5},{8,12},{9,11},{10,... | collective-permute-start | bytes 5308424 | tf_op jit(solution)/shard_map/ppermute | solution.py:140
  42.9 1.3 collective-permute-start.12
  44.3 3.0 %prepare.1 = (bf16[2,2,3,8,48,256]{5,4,3,2,1,0:T(8,128)(2,1)S(1)}, bf16[2,2,1,8,48,256]{5,4,3,2,1,0:T(8,128)(2,1)S(1)}) custom-call(s32[1]{0:T(128)} %bitcast.index_ref, bf16[2,128,1536]{2,1,0:T(8,128)(2,1)S(1)} %copy-done, bf16[256,1536]{1,0:T(8,128)(2,1)S(1)} %bitcast.155, f32[1,1536]{1,0:T(1,128)S(1)} %reshape.155.gain_ref, ...), custom_call_target="tpu_custom_call" | custom-call | tf_op jit(solution)/shard_map/prepare/pallas_call | solution.py:285
  47.2 5.4 %collective-permute-done.12.refs_1_ = bf16[1,2,48,768]{3,2,1,0:T(8,128)(2,1)S(1)} collective-permute-done((bf16[1,2,48,768]{3,2,1,0:T(8,128)(2,1)S(1)}, bf16[1,2,48,768]{3,2,1,0:T(8,128)(2,1)S(1)}, u32[]{:S(2)}, u32[]{:S(2)}) %collective-permute-start.12) | collective-permute-done | bytes 147488 | tf_op jit(solution)/shard_map/ppermute | solution.py:140
  53.6 3.5 %collective-permute-done.16.refs_1_ = bf16[1,4,48,768]{3,2,1,0:T(8,128)(2,1)S(1)} collective-permute-done((bf16[1,4,48,768]{3,2,1,0:T(8,128)(2,1)S(1)}, bf16[1,4,48,768]{3,2,1,0:T(8,128)(2,1)S(1)}, u32[]{:S(2)}, u32[]{:S(2)}) %collective-permute-start.16) | collective-permute-done | bytes 294944 | tf_op jit(solution)/shard_map/ppermute | solution.py:140
  57.3 5.8 %collective-permute-done.15.refs_1_ = bf16[1,4,48,768]{3,2,1,0:T(8,128)(2,1)S(1)} collective-permute-done((bf16[1,4,48,768]{3,2,1,0:T(8,128)(2,1)S(1)}, bf16[1,4,48,768]{3,2,1,0:T(8,128)(2,1)S(1)}, u32[]{:S(2)}, u32[]{:S(2)}) %collective-permute-start.15) | collective-permute-done | bytes 294944 | tf_op jit(solution)/shard_map/ppermute | solution.py:140
  63.2 2.0 %collective-permute-done.17.refs_3_ = bf16[1,8,48,768]{3,2,1,0:T(8,128)(2,1)S(1)} collective-permute-done((bf16[1,8,48,768]{3,2,1,0:T(8,128)(2,1)S(1)}, bf16[1,8,48,768]{3,2,1,0:T(8,128)(2,1)S(1)}, u32[]{:S(2)}, u32[]{:S(2)}) %collective-permute-start.17) | collective-permute-done | bytes 589856 | tf_op jit(solution)/shard_map/ppermute | solution.py:140
  68.0 0.9 collective-permute-done.19.refs_3_
  69.7 1.1 multiply_reduce_fusion
  76.3 3.4 %collective-permute-start.23 = (bf16[3,8,48,768]{3,2,1,0:T(8,128)(2,1)S(1)}, bf16[3,8,48,768]{3,2,1,0:T(8,128)(2,1)S(1)}, u32[]{:S(2)}, u32[]{:S(2)}) collective-permute-start(bf16[3,8,48,768]{3,2,1,0:T(8,128)(2,1)S(1)} %add_convert_fusion), channel_id=1, source_target_pairs={{0,4},{1,3},{2,6},{3,1},{4,0},{5,7},{6,2},{7,5},{8,12},{9,11},{10,... | collective-permute-start | bytes 5308424 | tf_op jit(solution)/shard_map/ppermute | solution.py:140
  79.9 1.0 collective-permute-start.24
  82.4 2.7 %grad_active.1 = f32[256,1536]{1,0:T(8,128)S(1)} custom-call(s32[1]{0:T(128)} %bitcast.index_ref, bf16[256,768]{1,0:T(8,128)(2,1)S(1)} %get-tuple-element.93.grad_ref, bf16[2,32,768]{2,1,0:T(8,128)(2,1)S(1)} %collective-permute-done.25.core_ref, bf16[2,32,768]{2,1,0:T(8,128)(2,1)S(1)} %collective-permute-done.26.outer_ref, ...), custom_call_target="tpu_custom_call" | custom-call | tf_op jit(solution)/shard_map/grad_active/pallas_call | solution.py:361
  85.3 1.8 %fusion.8 = (f32[1536]{0:T(1024)S(1)}, f32[2,128]{1,0:T(2,128)S(1)}, f32[2,128,1536]{2,1,0:T(8,128)S(1)}) fusion(bf16[2,128,1536]{2,1,0:T(8,128)(2,1)S(1)} %copy-done, f32[2,128]{1,0:T(2,128)S(1)} %fusion.54, f32[1536]{0:T(1024)S(1)} %copy-done.2, f32[2,128,1536]{2,1,0:T(8,128)S(1)} %bitcast.152), kind=kLoop, calls=%fused_computation.19 | loop fusion | flops 10615040 | bytes 3946496 | tf_op jit(solution)/shard_map/transpose(jvp())/reduce_sum | solution.py:33
  87.1 1.4 %fusion.13 = bf16[2,128,1536]{2,1,0:T(8,128)(2,1)} fusion(bf16[2,128,1536]{2,1,0:T(8,128)(2,1)S(1)} %copy-done, bf16[2,128,1536]{2,1,0:T(8,128)(2,1)S(1)} %copy-done.1, f32[2,128,1536]{2,1,0:T(8,128)S(1)} %get-tuple-element.128, f32[2,128]{1,0:T(2,128)S(1)} %multiply_multiply_fusion.5, f32[1536]{0:T(1024)S(1)} %copy-done.2, f32[2,128]{1,0:T(2,128)S(1)} %fusion.54), kind=kLoop, calls=%fused_computation.24 | loop fusion | flops 3538944 | bytes 3940352 | tf_op jit(solution)/shard_map/convert_element_type | solution.py:394
  88.6 1.2 collective-permute-start.27
  89.8 1.9 %collective-permute-start.30 = (bf16[1,2,48,768]{3,2,1,0:T(8,128)(2,1)S(1)}, bf16[1,2,48,768]{3,2,1,0:T(8,128)(2,1)S(1)}, u32[]{:S(2)}, u32[]{:S(2)}) collective-permute-start(bf16[1,2,48,768]{3,2,1,0:T(8,128)(2,1)S(1)} %get-tuple-element.96), channel_id=1, source_target_pairs={{0,16},{1,17},{2,18},{3,19},{4,20},{5,21},{6,22},{7,23},{8,24},{9,... | collective-permute-start | bytes 442376 | tf_op jit(solution)/shard_map/ppermute | solution.py:140
  91.7 1.2 collective-permute-done.28
  93.1 6.6 %collective-permute-done.29 = f32[2304]{0:T(1024)S(1)} collective-permute-done((f32[2304]{0:T(1024)S(1)}, f32[2304]{0:T(1024)S(1)}, u32[]{:S(2)}, u32[]{:S(2)}) %collective-permute-start.29) | collective-permute-done | bytes 9248 | tf_op jit(solution)/shard_map/ppermute | solution.py:140
  100.2 1.1 fold.5
  101.3 2.1 %collective-permute-start.31 = (bf16[2,4,48,768]{3,2,1,0:T(8,128)(2,1)S(1)}, bf16[2,4,48,768]{3,2,1,0:T(8,128)(2,1)S(1)}, u32[]{:S(2)}, u32[]{:S(2)}) collective-permute-start(bf16[2,4,48,768]{3,2,1,0:T(8,128)(2,1)S(1)} %get-tuple-element.101), channel_id=1, source_target_pairs={{0,2},{1,5},{2,0},{3,7},{4,6},{5,1},{6,4},{7,3},{8,10},{9,13},{10,... | collective-permute-start | bytes 1769480 | tf_op jit(solution)/shard_map/ppermute | solution.py:140
  103.4 1.5 %collective-permute-start.33 = (bf16[1,4,48,768]{3,2,1,0:T(8,128)(2,1)S(1)}, bf16[1,4,48,768]{3,2,1,0:T(8,128)(2,1)S(1)}, u32[]{:S(2)}, u32[]{:S(2)}) collective-permute-start(bf16[1,4,48,768]{3,2,1,0:T(8,128)(2,1)S(1)} %get-tuple-element.108), channel_id=1, source_target_pairs={{0,8},{1,9},{2,10},{3,11},{4,12},{5,13},{6,14},{7,15},{8,0},{9,1},... | collective-permute-start | bytes 884744 | tf_op jit(solution)/shard_map/ppermute | solution.py:140
  105.1 2.6 %collective-permute-start.32 = (f32[2304]{0:T(1024)S(1)}, f32[2304]{0:T(1024)S(1)}, u32[]{:S(2)}, u32[]{:S(2)}) collective-permute-start(f32[2304]{0:T(1024)S(1)} %add.150), channel_id=1, source_target_pairs={{0,16},{1,17},{2,18},{3,19},{4,20},{5,21},{6,22},{7,23},{8,24},{9,... | collective-permute-start | bytes 27656 | tf_op jit(solution)/shard_map/ppermute | solution.py:140
  107.8 2.2 %project_back.1 = bf16[256,1536]{1,0:T(8,128)(2,1)} custom-call(s32[1]{0:T(128)} %bitcast.index_ref, bf16[256,768]{1,0:T(8,128)(2,1)S(1)} %get-tuple-element.102.hidden_ref, bf16[256,1536]{1,0:T(8,128)(2,1)S(1)} %bitcast.146, bf16[1,8,48,768]{3,2,1,0:T(8,128)(2,1)S(1)} %assemble.12.refs_0_, bf16[1,8,48,768]{3,2,1,0:T(8,128)(2,1)S(1)} %assemble.13.refs_1_, ...), custom_call_target="tpu_custom_call" | custom-call | tf_op jit(solution)/shard_map/project_back/pallas_call | solution.py:327
  110.0 2.5 %collective-permute-done.32 = f32[2304]{0:T(1024)S(1)} collective-permute-done((f32[2304]{0:T(1024)S(1)}, f32[2304]{0:T(1024)S(1)}, u32[]{:S(2)}, u32[]{:S(2)}) %collective-permute-start.32) | collective-permute-done | bytes 9248 | tf_op jit(solution)/shard_map/ppermute | solution.py:140
  112.5 2.0 %collective-permute-done.33.refs_3_ = bf16[1,4,48,768]{3,2,1,0:T(8,128)(2,1)S(1)} collective-permute-done((bf16[1,4,48,768]{3,2,1,0:T(8,128)(2,1)S(1)}, bf16[1,4,48,768]{3,2,1,0:T(8,128)(2,1)S(1)}, u32[]{:S(2)}, u32[]{:S(2)}) %collective-permute-start.33) | collective-permute-done | bytes 294944 | tf_op jit(solution)/shard_map/ppermute | solution.py:140
  114.7 1.6 %collective-permute-start.35 = (bf16[2,2,48,768]{3,2,1,0:T(8,128)(2,1)S(1)}, bf16[2,2,48,768]{3,2,1,0:T(8,128)(2,1)S(1)}, u32[]{:S(2)}, u32[]{:S(2)}) collective-permute-start(bf16[2,2,48,768]{3,2,1,0:T(8,128)(2,1)S(1)} %get-tuple-element.112), channel_id=1, source_target_pairs={{0,8},{1,9},{2,10},{3,11},{4,12},{5,13},{6,14},{7,15},{8,0},{9,1},... | collective-permute-start | bytes 884744 | tf_op jit(solution)/shard_map/ppermute | solution.py:140
  116.2 1.3 collective-permute-start.39
  117.8 2.5 %collective-permute-start.36 = (f32[2304]{0:T(1024)S(1)}, f32[2304]{0:T(1024)S(1)}, u32[]{:S(2)}, u32[]{:S(2)}) collective-permute-start(f32[2304]{0:T(1024)S(1)} %add.151), channel_id=1, source_target_pairs={{0,2},{1,3},{2,0},{3,1},{4,6},{5,7},{6,4},{7,5},{8,10},{9,11},{10,... | collective-permute-start | bytes 27656 | tf_op jit(solution)/shard_map/ppermute | solution.py:140
  120.3 1.7 %collective-permute-done.36 = f32[2304]{0:T(1024)S(1)} collective-permute-done((f32[2304]{0:T(1024)S(1)}, f32[2304]{0:T(1024)S(1)}, u32[]{:S(2)}, u32[]{:S(2)}) %collective-permute-start.36) | collective-permute-done | bytes 9248 | tf_op jit(solution)/shard_map/ppermute | solution.py:140
  122.3 3.4 %collective-permute-done.37 = f32[2304]{0:T(1024)S(1)} collective-permute-done((f32[2304]{0:T(1024)S(1)}, f32[2304]{0:T(1024)S(1)}, u32[]{:S(2)}, u32[]{:S(2)}) %collective-permute-start.37) | collective-permute-done | bytes 9248 | tf_op jit(solution)/shard_map/ppermute | solution.py:140
  126.1 2.0 %collective-permute-start.40 = (bf16[2,1,48,768]{3,2,1,0:T(8,128)(2,1)S(1)}, bf16[2,1,48,768]{3,2,1,0:T(8,128)(2,1)S(1)}, u32[]{:S(2)}, u32[]{:S(2)}) collective-permute-start(bf16[2,1,48,768]{3,2,1,0:T(8,128)(2,1)S(1)} %get-tuple-element.121), channel_id=1, source_target_pairs={{0,16},{1,17},{2,18},{3,19},{4,20},{5,21},{6,22},{7,23},{8,24},{9,... | collective-permute-start | bytes 442376 | tf_op jit(solution)/shard_map/ppermute | solution.py:140
  129.3 2.0 %collective-permute-start.41 = (bf16[2,1,48,768]{3,2,1,0:T(8,128)(2,1)S(1)}, bf16[2,1,48,768]{3,2,1,0:T(8,128)(2,1)S(1)}, u32[]{:S(2)}, u32[]{:S(2)}) collective-permute-start(bf16[2,1,48,768]{3,2,1,0:T(8,128)(2,1)S(1)} %get-tuple-element.123), channel_id=1, source_target_pairs={{0,2},{1,5},{2,0},{3,7},{4,6},{5,1},{6,4},{7,3},{8,10},{9,13},{10,... | collective-permute-start | bytes 442376 | tf_op jit(solution)/shard_map/ppermute | solution.py:140
  131.3 2.5 %collective-permute-done.40 = bf16[2,1,48,768]{3,2,1,0:T(8,128)(2,1)S(1)} collective-permute-done((bf16[2,1,48,768]{3,2,1,0:T(8,128)(2,1)S(1)}, bf16[2,1,48,768]{3,2,1,0:T(8,128)(2,1)S(1)}, u32[]{:S(2)}, u32[]{:S(2)}) %collective-permute-start.40) | collective-permute-done | bytes 147488 | tf_op jit(solution)/shard_map/ppermute | solution.py:140
  (106 shorter events, 20.2 us)
Async XLA Ops:
  0.6 13.8 %copy-start = (bf16[2,128,1536]{2,1,0:T(8,128)(2,1)S(1)}, bf16[2,128,1536]{2,1,0:T(8,128)(2,1)}, u32[]{:S(2)}) copy-start(bf16[2,128,1536]{2,1,0:T(8,128)(2,1)} %features_ref) | copy-start | bytes 2359300
  1.6 11.1 %collective-permute-start = (bf16[2,1,48,768]{3,2,0,1:T(8,128)(2,1)S(1)}, bf16[2,1,48,768]{3,2,0,1:T(8,128)(2,1)S(1)}, u32[]{:S(2)}, u32[]{:S(2)}) collective-permute-start(bf16[2,1,48,768]{3,2,0,1:T(8,128)(2,1)S(1)} %get-tuple-element.151), channel_id=1, source_target_pairs={{0,16},{1,17},{2,18},{3,19},{4,20},{5,21},{6,22},{7,23},{8,24},{9,... | collective-permute-start | bytes 442376 | tf_op jit(solution)/shard_map/ppermute | solution.py:140
  7.5 5.2 %collective-permute-start.1 = (bf16[2,1,48,768]{3,2,1,0:T(8,128)(2,1)S(1)}, bf16[2,1,48,768]{3,2,1,0:T(8,128)(2,1)S(1)}, u32[]{:S(2)}, u32[]{:S(2)}) collective-permute-start(bf16[2,1,48,768]{3,2,1,0:T(8,128)(2,1)S(1)} %pad_maximum_fusion.refs_2_), channel_id=1, source_target_pairs={{0,2},{1,5},{2,0},{3,7},{4,6},{5,1},{6,4},{7,3},{8,10},{9,13},{10,... | collective-permute-start | bytes 442376 | tf_op jit(solution)/shard_map/ppermute | solution.py:140
  12.8 11.4 %collective-permute-start.2 = (bf16[2,2,48,768]{3,2,1,0:T(8,128)(2,1)S(1)}, bf16[2,2,48,768]{3,2,1,0:T(8,128)(2,1)S(1)}, u32[]{:S(2)}, u32[]{:S(2)}) collective-permute-start(bf16[2,2,48,768]{3,2,1,0:T(8,128)(2,1)S(1)} %get-tuple-element.65.refs_0_), channel_id=1, source_target_pairs={{0,8},{1,9},{2,10},{3,11},{4,12},{5,13},{6,14},{7,15},{8,0},{9,1},... | collective-permute-start | bytes 884744 | tf_op jit(solution)/shard_map/ppermute | solution.py:140
  14.5 4.7 %collective-permute-start.4 = (bf16[1,32,1536]{2,1,0:T(8,128)(2,1)S(1)}, bf16[1,32,1536]{2,1,0:T(8,128)(2,1)S(1)}, u32[]{:S(2)}, u32[]{:S(2)}) collective-permute-start(bf16[1,32,1536]{2,1,0:T(8,128)(2,1)S(1)} %get-tuple-element.146), channel_id=1, source_target_pairs={{0,1},{1,0},{2,3},{3,2},{4,5},{5,4},{6,7},{7,6},{8,9},{9,8},{10,11... | collective-permute-start | bytes 294920 | tf_op jit(solution)/shard_map/ppermute | solution.py:140
  14.6 5.3 %collective-permute-start.5 = (bf16[1,32,1536]{2,1,0:T(8,128)(2,1)S(1)}, bf16[1,32,1536]{2,1,0:T(8,128)(2,1)S(1)}, u32[]{:S(2)}, u32[]{:S(2)}) collective-permute-start(bf16[1,32,1536]{2,1,0:T(8,128)(2,1)S(1)} %get-tuple-element.144), channel_id=1, source_target_pairs={{0,1},{1,0},{2,3},{3,2},{4,5},{5,4},{6,7},{7,6},{8,9},{9,8},{10,11... | collective-permute-start | bytes 294920 | tf_op jit(solution)/shard_map/ppermute | solution.py:140
  15.2 5.4 %collective-permute-start.3 = (bf16[1,2,48,768]{3,2,1,0:T(8,128)(2,1)S(1)}, bf16[1,2,48,768]{3,2,1,0:T(8,128)(2,1)S(1)}, u32[]{:S(2)}, u32[]{:S(2)}) collective-permute-start(bf16[1,2,48,768]{3,2,1,0:T(8,128)(2,1)S(1)} %get-tuple-element.66.refs_0_), channel_id=1, source_target_pairs={{0,4},{1,3},{2,6},{3,1},{4,0},{5,7},{6,2},{7,5},{8,12},{9,11},{10,... | collective-permute-start | bytes 442376 | tf_op jit(solution)/shard_map/ppermute | solution.py:140
  16.7 7.5 %collective-permute-start.8 = (bf16[1,2,48,768]{3,2,1,0:T(8,128)(2,1)S(1)}, bf16[1,2,48,768]{3,2,1,0:T(8,128)(2,1)S(1)}, u32[]{:S(2)}, u32[]{:S(2)}) collective-permute-start(bf16[1,2,48,768]{3,2,1,0:T(8,128)(2,1)S(1)} %get-tuple-element.69.refs_2_), channel_id=1, source_target_pairs={{0,16},{1,17},{2,18},{3,19},{4,20},{5,21},{6,22},{7,23},{8,24},{9,... | collective-permute-start | bytes 442376 | tf_op jit(solution)/shard_map/ppermute | solution.py:140
  19.2 1.4 collective-permute-start.6
  19.9 0.7 collective-permute-start.7
  24.3 16.9 %collective-permute-start.9 = (bf16[2,4,48,768]{3,2,1,0:T(8,128)(2,1)S(1)}, bf16[2,4,48,768]{3,2,1,0:T(8,128)(2,1)S(1)}, u32[]{:S(2)}, u32[]{:S(2)}) collective-permute-start(bf16[2,4,48,768]{3,2,1,0:T(8,128)(2,1)S(1)} %get-tuple-element.72.refs_0_), channel_id=1, source_target_pairs={{0,2},{1,5},{2,0},{3,7},{4,6},{5,1},{6,4},{7,3},{8,10},{9,13},{10,... | collective-permute-start | bytes 1769480 | tf_op jit(solution)/shard_map/ppermute | solution.py:140
  28.9 12.2 %collective-permute-start.10 = (bf16[1,4,48,768]{3,2,1,0:T(8,128)(2,1)S(1)}, bf16[1,4,48,768]{3,2,1,0:T(8,128)(2,1)S(1)}, u32[]{:S(2)}, u32[]{:S(2)}) collective-permute-start(bf16[1,4,48,768]{3,2,1,0:T(8,128)(2,1)S(1)} %get-tuple-element.74.refs_2_), channel_id=1, source_target_pairs={{0,8},{1,9},{2,10},{3,11},{4,12},{5,13},{6,14},{7,15},{8,0},{9,1},... | collective-permute-start | bytes 884744 | tf_op jit(solution)/shard_map/ppermute | solution.py:140
  31.2 7.8 %collective-permute-start.11 = (bf16[1,2,48,768]{3,2,1,0:T(8,128)(2,1)S(1)}, bf16[1,2,48,768]{3,2,1,0:T(8,128)(2,1)S(1)}, u32[]{:S(2)}, u32[]{:S(2)}) collective-permute-start(bf16[1,2,48,768]{3,2,1,0:T(8,128)(2,1)S(1)} %get-tuple-element.66.refs_0_), channel_id=1, source_target_pairs={{0,16},{1,17},{2,18},{3,19},{4,20},{5,21},{6,22},{7,23},{8,24},{9,... | collective-permute-start | bytes 442376 | tf_op jit(solution)/shard_map/ppermute | solution.py:140
  39.0 5.2 %copy-start.2 = (f32[1536]{0:T(1024)S(1)}, f32[1536]{0:T(1024)}, u32[]{:S(2)}) copy-start(f32[1536]{0:T(1024)} %param.10) | copy-start | bytes 18436
  39.0 5.3 %copy-start.1 = (bf16[2,128,1536]{2,1,0:T(8,128)(2,1)S(1)}, bf16[2,128,1536]{2,1,0:T(8,128)(2,1)}, u32[]{:S(2)}) copy-start(bf16[2,128,1536]{2,1,0:T(8,128)(2,1)} %param.7) | copy-start | bytes 2359300
  41.3 23.9 %collective-permute-start.14 = (bf16[3,8,48,768]{3,2,1,0:T(8,128)(2,1)S(1)}, bf16[3,8,48,768]{3,2,1,0:T(8,128)(2,1)S(1)}, u32[]{:S(2)}, u32[]{:S(2)}) collective-permute-start(bf16[3,8,48,768]{3,2,1,0:T(8,128)(2,1)S(1)} %assemble.10.refs_0_), channel_id=1, source_target_pairs={{0,4},{1,3},{2,6},{3,1},{4,0},{5,7},{6,2},{7,5},{8,12},{9,11},{10,... | collective-permute-start | bytes 5308424 | tf_op jit(solution)/shard_map/ppermute | solution.py:140
  42.9 9.7 %collective-permute-start.12 = (bf16[1,2,48,768]{3,2,1,0:T(8,128)(2,1)S(1)}, bf16[1,2,48,768]{3,2,1,0:T(8,128)(2,1)S(1)}, u32[]{:S(2)}, u32[]{:S(2)}) collective-permute-start(bf16[1,2,48,768]{3,2,1,0:T(8,128)(2,1)S(1)} %collective-permute-done.3.refs_0_), channel_id=1, source_target_pairs={{0,16},{1,17},{2,18},{3,19},{4,20},{5,21},{6,22},{7,23},{8,24},{9,... | collective-permute-start | bytes 442376 | tf_op jit(solution)/shard_map/ppermute | solution.py:140
  44.1 21.7 %collective-permute-start.13 = (bf16[3,8,48,768]{3,2,1,0:T(8,128)(2,1)S(1)}, bf16[3,8,48,768]{3,2,1,0:T(8,128)(2,1)S(1)}, u32[]{:S(2)}, u32[]{:S(2)}) collective-permute-start(bf16[3,8,48,768]{3,2,1,0:T(8,128)(2,1)S(1)} %assemble.10.refs_0_), channel_id=1, source_target_pairs={{0,1},{1,0},{2,3},{3,2},{4,5},{5,4},{6,7},{7,6},{8,9},{9,8},{10,11... | collective-permute-start | bytes 5308424 | tf_op jit(solution)/shard_map/ppermute | solution.py:140
  44.2 13.0 %collective-permute-start.16 = (bf16[1,4,48,768]{3,2,1,0:T(8,128)(2,1)S(1)}, bf16[1,4,48,768]{3,2,1,0:T(8,128)(2,1)S(1)}, u32[]{:S(2)}, u32[]{:S(2)}) collective-permute-start(bf16[1,4,48,768]{3,2,1,0:T(8,128)(2,1)S(1)} %assemble.9.refs_0_), channel_id=1, source_target_pairs={{0,8},{1,9},{2,10},{3,11},{4,12},{5,13},{6,14},{7,15},{8,0},{9,1},... | collective-permute-start | bytes 884744 | tf_op jit(solution)/shard_map/ppermute | solution.py:140
  52.6 10.5 %collective-permute-start.15 = (bf16[1,4,48,768]{3,2,1,0:T(8,128)(2,1)S(1)}, bf16[1,4,48,768]{3,2,1,0:T(8,128)(2,1)S(1)}, u32[]{:S(2)}, u32[]{:S(2)}) collective-permute-start(bf16[1,4,48,768]{3,2,1,0:T(8,128)(2,1)S(1)} %assemble.11.refs_0_), channel_id=1, source_target_pairs={{0,8},{1,9},{2,10},{3,11},{4,12},{5,13},{6,14},{7,15},{8,0},{9,1},... | collective-permute-start | bytes 884744 | tf_op jit(solution)/shard_map/ppermute | solution.py:140
  57.2 6.0 %collective-permute-start.18 = (bf16[1,8,48,768]{3,2,1,0:T(8,128)(2,1)S(1)}, bf16[1,8,48,768]{3,2,1,0:T(8,128)(2,1)S(1)}, u32[]{:S(2)}, u32[]{:S(2)}) collective-permute-start(bf16[1,8,48,768]{3,2,1,0:T(8,128)(2,1)S(1)} %assemble.12.refs_0_), channel_id=1, source_target_pairs={{0,1},{1,0},{2,3},{3,2},{4,5},{5,4},{6,7},{7,6},{8,9},{9,8},{10,11... | collective-permute-start | bytes 1769480 | tf_op jit(solution)/shard_map/ppermute | solution.py:140
  63.1 2.1 %collective-permute-start.17 = (bf16[1,8,48,768]{3,2,1,0:T(8,128)(2,1)S(1)}, bf16[1,8,48,768]{3,2,1,0:T(8,128)(2,1)S(1)}, u32[]{:S(2)}, u32[]{:S(2)}) collective-permute-start(bf16[1,8,48,768]{3,2,1,0:T(8,128)(2,1)S(1)} %assemble.13.refs_1_), channel_id=1, source_target_pairs={{0,1},{1,0},{2,3},{3,2},{4,5},{5,4},{6,7},{7,6},{8,9},{9,8},{10,11... | collective-permute-start | bytes 1769480 | tf_op jit(solution)/shard_map/ppermute | solution.py:140
  65.2 3.7 %collective-permute-start.19 = (bf16[3,8,48,768]{3,2,1,0:T(8,128)(2,1)S(1)}, bf16[3,8,48,768]{3,2,1,0:T(8,128)(2,1)S(1)}, u32[]{:S(2)}, u32[]{:S(2)}) collective-permute-start(bf16[3,8,48,768]{3,2,1,0:T(8,128)(2,1)S(1)} %collective-permute-done.14.refs_1_), channel_id=1, source_target_pairs={{0,1},{1,0},{2,3},{3,2},{4,5},{5,4},{6,7},{7,6},{8,9},{9,8},{10,11... | collective-permute-start | bytes 5308424 | tf_op jit(solution)/shard_map/ppermute | solution.py:140
  68.9 0.8 copy-start.3
  71.9 3.8 %collective-permute-start.20 = (bf16[3,8,48,768]{3,2,1,0:T(8,128)(2,1)S(1)}, bf16[3,8,48,768]{3,2,1,0:T(8,128)(2,1)S(1)}, u32[]{:S(2)}, u32[]{:S(2)}) collective-permute-start(bf16[3,8,48,768]{3,2,1,0:T(8,128)(2,1)S(1)} %convolution_convert_fusion.1), channel_id=1, source_target_pairs={{0,1},{1,0},{2,3},{3,2},{4,5},{5,4},{6,7},{7,6},{8,9},{9,8},{10,11... | collective-permute-start | bytes 5308424 | tf_op jit(solution)/shard_map/ppermute | solution.py:140
  73.3 6.4 %collective-permute-start.21 = (bf16[2,8,48,768]{3,2,1,0:T(8,128)(2,1)S(1)}, bf16[2,8,48,768]{3,2,1,0:T(8,128)(2,1)S(1)}, u32[]{:S(2)}, u32[]{:S(2)}) collective-permute-start(bf16[2,8,48,768]{3,2,1,0:T(8,128)(2,1)S(1)} %convolution_convert_fusion.2), channel_id=1, source_target_pairs={{0,1},{1,0},{2,3},{3,2},{4,5},{5,4},{6,7},{7,6},{8,9},{9,8},{10,11... | collective-permute-start | bytes 3538952 | tf_op jit(solution)/shard_map/ppermute | solution.py:140
  73.7 8.0 %collective-permute-start.22 = (bf16[3,8,48,768]{3,2,1,0:T(8,128)(2,1)S(1)}, bf16[3,8,48,768]{3,2,1,0:T(8,128)(2,1)S(1)}, u32[]{:S(2)}, u32[]{:S(2)}) collective-permute-start(bf16[3,8,48,768]{3,2,1,0:T(8,128)(2,1)S(1)} %convolution_convert_fusion), channel_id=1, source_target_pairs={{0,1},{1,0},{2,3},{3,2},{4,5},{5,4},{6,7},{7,6},{8,9},{9,8},{10,11... | collective-permute-start | bytes 5308424 | tf_op jit(solution)/shard_map/ppermute | solution.py:140
  73.8 8.5 %collective-permute-start.25 = (bf16[2,32,768]{2,1,0:T(8,128)(2,1)S(1)}, bf16[2,32,768]{2,1,0:T(8,128)(2,1)S(1)}, u32[]{:S(2)}, u32[]{:S(2)}) collective-permute-start(bf16[2,32,768]{2,1,0:T(8,128)(2,1)S(1)} %get-tuple-element.142), channel_id=1, source_target_pairs={{0,1},{1,0},{2,3},{3,2},{4,5},{5,4},{6,7},{7,6},{8,9},{9,8},{10,11... | collective-permute-start | bytes 294920 | tf_op jit(solution)/shard_map/ppermute | solution.py:140
  74.3 8.1 %collective-permute-start.26 = (bf16[2,32,768]{2,1,0:T(8,128)(2,1)S(1)}, bf16[2,32,768]{2,1,0:T(8,128)(2,1)S(1)}, u32[]{:S(2)}, u32[]{:S(2)}) collective-permute-start(bf16[2,32,768]{2,1,0:T(8,128)(2,1)S(1)} %get-tuple-element.141), channel_id=1, source_target_pairs={{1,2},{2,1},{3,4},{4,3},{5,6},{6,5},{7,8},{8,7},{9,10},{10,9},{11,... | collective-permute-start | bytes 294920 | tf_op jit(solution)/shard_map/ppermute | solution.py:140
  76.3 23.9 %collective-permute-start.23 = (bf16[3,8,48,768]{3,2,1,0:T(8,128)(2,1)S(1)}, bf16[3,8,48,768]{3,2,1,0:T(8,128)(2,1)S(1)}, u32[]{:S(2)}, u32[]{:S(2)}) collective-permute-start(bf16[3,8,48,768]{3,2,1,0:T(8,128)(2,1)S(1)} %add_convert_fusion), channel_id=1, source_target_pairs={{0,4},{1,3},{2,6},{3,1},{4,0},{5,7},{6,2},{7,5},{8,12},{9,11},{10,... | collective-permute-start | bytes 5308424 | tf_op jit(solution)/shard_map/ppermute | solution.py:140
  79.9 8.6 %collective-permute-start.24 = (bf16[1,4,48,768]{3,2,1,0:T(8,128)(2,1)S(1)}, bf16[1,4,48,768]{3,2,1,0:T(8,128)(2,1)S(1)}, u32[]{:S(2)}, u32[]{:S(2)}) collective-permute-start(bf16[1,4,48,768]{3,2,1,0:T(8,128)(2,1)S(1)} %fusion.20), channel_id=1, source_target_pairs={{0,8},{1,9},{2,10},{3,11},{4,12},{5,13},{6,14},{7,15},{8,0},{9,1},... | collective-permute-start | bytes 884744 | tf_op jit(solution)/shard_map/ppermute | solution.py:140
  88.6 11.1 %collective-permute-start.27 = (bf16[1,4,48,768]{3,2,1,0:T(8,128)(2,1)S(1)}, bf16[1,4,48,768]{3,2,1,0:T(8,128)(2,1)S(1)}, u32[]{:S(2)}, u32[]{:S(2)}) collective-permute-start(bf16[1,4,48,768]{3,2,1,0:T(8,128)(2,1)S(1)} %fusion.21), channel_id=1, source_target_pairs={{0,8},{1,9},{2,10},{3,11},{4,12},{5,13},{6,14},{7,15},{8,0},{9,1},... | collective-permute-start | bytes 884744 | tf_op jit(solution)/shard_map/ppermute | solution.py:140
  89.8 9.9 %collective-permute-start.30 = (bf16[1,2,48,768]{3,2,1,0:T(8,128)(2,1)S(1)}, bf16[1,2,48,768]{3,2,1,0:T(8,128)(2,1)S(1)}, u32[]{:S(2)}, u32[]{:S(2)}) collective-permute-start(bf16[1,2,48,768]{3,2,1,0:T(8,128)(2,1)S(1)} %get-tuple-element.96), channel_id=1, source_target_pairs={{0,16},{1,17},{2,18},{3,19},{4,20},{5,21},{6,22},{7,23},{8,24},{9,... | collective-permute-start | bytes 442376 | tf_op jit(solution)/shard_map/ppermute | solution.py:140
  91.7 1.2 collective-permute-start.28
  92.8 6.8 %collective-permute-start.29 = (f32[2304]{0:T(1024)S(1)}, f32[2304]{0:T(1024)S(1)}, u32[]{:S(2)}, u32[]{:S(2)}) collective-permute-start(f32[2304]{0:T(1024)S(1)} %add.149), channel_id=1, source_target_pairs={{0,8},{1,9},{2,10},{3,11},{4,12},{5,13},{6,14},{7,15},{8,0},{9,1},... | collective-permute-start | bytes 27656 | tf_op jit(solution)/shard_map/ppermute | solution.py:140
  101.3 11.3 %collective-permute-start.31 = (bf16[2,4,48,768]{3,2,1,0:T(8,128)(2,1)S(1)}, bf16[2,4,48,768]{3,2,1,0:T(8,128)(2,1)S(1)}, u32[]{:S(2)}, u32[]{:S(2)}) collective-permute-start(bf16[2,4,48,768]{3,2,1,0:T(8,128)(2,1)S(1)} %get-tuple-element.101), channel_id=1, source_target_pairs={{0,2},{1,5},{2,0},{3,7},{4,6},{5,1},{6,4},{7,3},{8,10},{9,13},{10,... | collective-permute-start | bytes 1769480 | tf_op jit(solution)/shard_map/ppermute | solution.py:140
  103.4 11.1 %collective-permute-start.33 = (bf16[1,4,48,768]{3,2,1,0:T(8,128)(2,1)S(1)}, bf16[1,4,48,768]{3,2,1,0:T(8,128)(2,1)S(1)}, u32[]{:S(2)}, u32[]{:S(2)}) collective-permute-start(bf16[1,4,48,768]{3,2,1,0:T(8,128)(2,1)S(1)} %get-tuple-element.108), channel_id=1, source_target_pairs={{0,8},{1,9},{2,10},{3,11},{4,12},{5,13},{6,14},{7,15},{8,0},{9,1},... | collective-permute-start | bytes 884744 | tf_op jit(solution)/shard_map/ppermute | solution.py:140
  104.9 7.7 %collective-permute-start.34 = (bf16[1,2,48,768]{3,2,1,0:T(8,128)(2,1)S(1)}, bf16[1,2,48,768]{3,2,1,0:T(8,128)(2,1)S(1)}, u32[]{:S(2)}, u32[]{:S(2)}) collective-permute-start(bf16[1,2,48,768]{3,2,1,0:T(8,128)(2,1)S(1)} %get-tuple-element.110), channel_id=1, source_target_pairs={{0,16},{1,17},{2,18},{3,19},{4,20},{5,21},{6,22},{7,23},{8,24},{9,... | collective-permute-start | bytes 442376 | tf_op jit(solution)/shard_map/ppermute | solution.py:140
  105.1 7.4 %collective-permute-start.32 = (f32[2304]{0:T(1024)S(1)}, f32[2304]{0:T(1024)S(1)}, u32[]{:S(2)}, u32[]{:S(2)}) collective-permute-start(f32[2304]{0:T(1024)S(1)} %add.150), channel_id=1, source_target_pairs={{0,16},{1,17},{2,18},{3,19},{4,20},{5,21},{6,22},{7,23},{8,24},{9,... | collective-permute-start | bytes 27656 | tf_op jit(solution)/shard_map/ppermute | solution.py:140
  114.7 11.0 %collective-permute-start.35 = (bf16[2,2,48,768]{3,2,1,0:T(8,128)(2,1)S(1)}, bf16[2,2,48,768]{3,2,1,0:T(8,128)(2,1)S(1)}, u32[]{:S(2)}, u32[]{:S(2)}) collective-permute-start(bf16[2,2,48,768]{3,2,1,0:T(8,128)(2,1)S(1)} %get-tuple-element.112), channel_id=1, source_target_pairs={{0,8},{1,9},{2,10},{3,11},{4,12},{5,13},{6,14},{7,15},{8,0},{9,1},... | collective-permute-start | bytes 884744 | tf_op jit(solution)/shard_map/ppermute | solution.py:140
  116.2 9.4 %collective-permute-start.39 = (bf16[1,2,48,768]{3,2,1,0:T(8,128)(2,1)S(1)}, bf16[1,2,48,768]{3,2,1,0:T(8,128)(2,1)S(1)}, u32[]{:S(2)}, u32[]{:S(2)}) collective-permute-start(bf16[1,2,48,768]{3,2,1,0:T(8,128)(2,1)S(1)} %get-tuple-element.119), channel_id=1, source_target_pairs={{0,4},{1,3},{2,6},{3,1},{4,0},{5,7},{6,2},{7,5},{8,12},{9,11},{10,... | collective-permute-start | bytes 442376 | tf_op jit(solution)/shard_map/ppermute | solution.py:140
  117.6 8.4 %collective-permute-start.38 = (bf16[1,2,48,768]{3,2,1,0:T(8,128)(2,1)S(1)}, bf16[1,2,48,768]{3,2,1,0:T(8,128)(2,1)S(1)}, u32[]{:S(2)}, u32[]{:S(2)}) collective-permute-start(bf16[1,2,48,768]{3,2,1,0:T(8,128)(2,1)S(1)} %get-tuple-element.116), channel_id=1, source_target_pairs={{0,16},{1,17},{2,18},{3,19},{4,20},{5,21},{6,22},{7,23},{8,24},{9,... | collective-permute-start | bytes 442376 | tf_op jit(solution)/shard_map/ppermute | solution.py:140
  117.8 4.1 %collective-permute-start.36 = (f32[2304]{0:T(1024)S(1)}, f32[2304]{0:T(1024)S(1)}, u32[]{:S(2)}, u32[]{:S(2)}) collective-permute-start(f32[2304]{0:T(1024)S(1)} %add.151), channel_id=1, source_target_pairs={{0,2},{1,3},{2,0},{3,1},{4,6},{5,7},{6,4},{7,5},{8,10},{9,11},{10,... | collective-permute-start | bytes 27656 | tf_op jit(solution)/shard_map/ppermute | solution.py:140
  122.0 3.7 %collective-permute-start.37 = (f32[2304]{0:T(1024)S(1)}, f32[2304]{0:T(1024)S(1)}, u32[]{:S(2)}, u32[]{:S(2)}) collective-permute-start(f32[2304]{0:T(1024)S(1)} %add.152), channel_id=1, source_target_pairs={{0,4},{1,5},{2,6},{3,7},{4,0},{5,1},{6,2},{7,3},{8,12},{9,13},{10,... | collective-permute-start | bytes 27656 | tf_op jit(solution)/shard_map/ppermute | solution.py:140
  126.1 7.7 %collective-permute-start.40 = (bf16[2,1,48,768]{3,2,1,0:T(8,128)(2,1)S(1)}, bf16[2,1,48,768]{3,2,1,0:T(8,128)(2,1)S(1)}, u32[]{:S(2)}, u32[]{:S(2)}) collective-permute-start(bf16[2,1,48,768]{3,2,1,0:T(8,128)(2,1)S(1)} %get-tuple-element.121), channel_id=1, source_target_pairs={{0,16},{1,17},{2,18},{3,19},{4,20},{5,21},{6,22},{7,23},{8,24},{9,... | collective-permute-start | bytes 442376 | tf_op jit(solution)/shard_map/ppermute | solution.py:140
  129.3 5.1 %collective-permute-start.41 = (bf16[2,1,48,768]{3,2,1,0:T(8,128)(2,1)S(1)}, bf16[2,1,48,768]{3,2,1,0:T(8,128)(2,1)S(1)}, u32[]{:S(2)}, u32[]{:S(2)}) collective-permute-start(bf16[2,1,48,768]{3,2,1,0:T(8,128)(2,1)S(1)} %get-tuple-element.123), channel_id=1, source_target_pairs={{0,2},{1,5},{2,0},{3,7},{4,6},{5,1},{6,4},{7,3},{8,10},{9,13},{10,... | collective-permute-start | bytes 442376 | tf_op jit(solution)/shard_map/ppermute | solution.py:140

commit v9 on v8

--- a/solution.py
+++ b/solution.py
@@ -484,7 +484,10 @@
     unused, pull_outer = jax.vjp(act_norm, as_f32(after(features, grad_active)), outer_gain)
     grad_branch, grad_gain_outer = pull_outer(grad_active.reshape(features.shape))
     grad_features = as_bf16(as_f32(cotangent) + grad_branch)
-    gains = jnp.concatenate([grad_gain_outer, grad_gain_inner]) * factor
+    part = inner // TORUS_DEVICES
+    gains = factor * jnp.concatenate(
+        [grad_gain_outer.reshape(-1, rows), grad_gain_inner.reshape(-1, part)], axis=1
+    )
     recv_b = after(recv_b, grad_features, gains)
     message_b, kept_b = fold(
         (kept_b, recv_b),
@@ -556,9 +559,8 @@
     grad_dilated = jnp.stack([sums[0, 0], sums[1, 0], sums_r[0, 0]], axis=1) * factor
 
     device = lax.axis_index("seq")
-    grad_outer_gain = lax.dynamic_slice(gains, (device * rows,), (rows,))
-    part = inner // TORUS_DEVICES
-    grad_inner_gain = lax.dynamic_slice(gains, (channels + device * part,), (part,))
+    mine = lax.dynamic_index_in_dim(gains, device, axis=0, keepdims=False)
+    grad_outer_gain, grad_inner_gain = mine[:rows], mine[rows:]
     return (block_out, grad_features, grad_dilated, grad_project, grad_outer_gain, grad_inner_gain)
 
 

time: 136 us -> 164 us (1.21)
  matrix products: 9.09 us -> 26.2 us
  local copies, waits for them, and re-layouts: 3.47 us -> 9.62 us
  Pallas kernels: 9.55 us -> 12.1 us
    dot_general x9, matrix products: 3.94 us -> 21 us  [rows_dot(): jnp.einsum('mnrt,ti->mnri', left, right, preferred_element_type=jnp.float32)]
    unnamed x8 -> x60, local copies, waits for them, and re-layouts: 0.02 us -> 4.85 us
    pallas_call x4, Pallas kernels: 1.39 us -> 3.94 us  [fold(): pl.pallas_call(kernel, out_shape=[jax.ShapeDtypeStruct((m, n) + tail, dty...]
  transfers between devices with their start and end apart: 42 -> 42, of which waited for: 20 -> 16; matrix products, arithmetic and copies ran while one was open for 10% -> 19% of each run, Pallas kernels for 6% -> 5%
where the time goes in v9:
time: 164 us; the launch traced here: 163 us
  waiting for transfers between devices  55.5 us (34%)
  starting transfers between devices  52.2 us (32%)
  matrix products  26.2 us (16%)
  Pallas kernels  12.1 us (7%)
  local copies, waits for them, and re-layouts  9.62 us (6%)
  other arithmetic  6.49 us (4%)
    ppermute x42, waiting for transfers between devices, send(): return lax.ppermute(block, 'seq', pairs)  55.5 us
    ppermute x42, starting transfers between devices, send(): return lax.ppermute(block, 'seq', pairs)  52.2 us
    dot_general x9, matrix products, rows_dot(): jnp.einsum('mnrt,ti->mnri', left, right, preferred_element_type=jnp.float32)  21 us
    dot_general x8, matrix products, contract(): jnp.einsum('ct,ci->ti', left.reshape(-1, left.shape[-1]), right.reshape(-...  5.14 us
    unnamed x60, local copies, waits for them, and re-layouts  4.85 us
    pallas_call x4, Pallas kernels, fold(): pl.pallas_call(kernel, out_shape=[jax.ShapeDtypeStruct((m, n) + tail, dty...  3.94 us
  transfers between devices with their start and end apart: 42, of which 16 were waited for; matrix products, arithmetic and copies ran while one was open for 19% of the time, Pallas kernels for 5%

profile of v9, /device:TPU:0, one launch (start us, length us, event | category | flops | bytes accessed | tf_op | source)
XLA Modules:
  0.0 163.2 jit_solution(7790697603213500255)
XLA Ops:
  1.6 4.1 %collective-permute-start = (bf16[2,1,48,768]{3,2,0,1:T(8,128)(2,1)S(1)}, bf16[2,1,48,768]{3,2,0,1:T(8,128)(2,1)S(1)}, u32[]{:S(2)}, u32[]{:S(2)}) collective-permute-start(bf16[2,1,48,768]{3,2,0,1:T(8,128)(2,1)S(1)} %get-tuple-element.151), channel_id=1, source_target_pairs={{0,16},{1,17},{2,18},{3,19},{4,20},{5,21},{6,22},{7,23},{8,24},{9,... | collective-permute-start | bytes 442376 | tf_op jit(solution)/shard_map/ppermute | solution.py:140
  7.5 1.6 collective-permute-start.1
  9.1 3.7 %collective-permute-done = bf16[2,1,48,768]{3,2,0,1:T(8,128)(2,1)S(1)} collective-permute-done((bf16[2,1,48,768]{3,2,0,1:T(8,128)(2,1)S(1)}, bf16[2,1,48,768]{3,2,0,1:T(8,128)(2,1)S(1)}, u32[]{:S(2)}, u32[]{:S(2)}) %collective-permute-start) | collective-permute-done | bytes 147488 | tf_op jit(solution)/shard_map/ppermute | solution.py:140
  12.8 1.6 collective-permute-start.2
  15.2 1.5 collective-permute-start.3
  16.7 2.5 %collective-permute-start.8 = (bf16[1,2,48,768]{3,2,1,0:T(8,128)(2,1)S(1)}, bf16[1,2,48,768]{3,2,1,0:T(8,128)(2,1)S(1)}, u32[]{:S(2)}, u32[]{:S(2)}) collective-permute-start(bf16[1,2,48,768]{3,2,1,0:T(8,128)(2,1)S(1)} %get-tuple-element.69.refs_2_), channel_id=1, source_target_pairs={{0,16},{1,17},{2,18},{3,19},{4,20},{5,21},{6,22},{7,23},{8,24},{9,... | collective-permute-start | bytes 442376 | tf_op jit(solution)/shard_map/ppermute | solution.py:140
  20.6 3.6 %collective-permute-done.2.refs_1_ = bf16[2,2,48,768]{3,2,1,0:T(8,128)(2,1)S(1)} collective-permute-done((bf16[2,2,48,768]{3,2,1,0:T(8,128)(2,1)S(1)}, bf16[2,2,48,768]{3,2,1,0:T(8,128)(2,1)S(1)}, u32[]{:S(2)}, u32[]{:S(2)}) %collective-permute-start.2) | collective-permute-done | bytes 294944 | tf_op jit(solution)/shard_map/ppermute | solution.py:140
  24.3 4.6 %collective-permute-start.9 = (bf16[2,4,48,768]{3,2,1,0:T(8,128)(2,1)S(1)}, bf16[2,4,48,768]{3,2,1,0:T(8,128)(2,1)S(1)}, u32[]{:S(2)}, u32[]{:S(2)}) collective-permute-start(bf16[2,4,48,768]{3,2,1,0:T(8,128)(2,1)S(1)} %get-tuple-element.72.refs_0_), channel_id=1, source_target_pairs={{0,2},{1,5},{2,0},{3,7},{4,6},{5,1},{6,4},{7,3},{8,10},{9,13},{10,... | collective-permute-start | bytes 1769480 | tf_op jit(solution)/shard_map/ppermute | solution.py:140
  28.9 2.3 %collective-permute-start.10 = (bf16[1,4,48,768]{3,2,1,0:T(8,128)(2,1)S(1)}, bf16[1,4,48,768]{3,2,1,0:T(8,128)(2,1)S(1)}, u32[]{:S(2)}, u32[]{:S(2)}) collective-permute-start(bf16[1,4,48,768]{3,2,1,0:T(8,128)(2,1)S(1)} %get-tuple-element.74.refs_2_), channel_id=1, source_target_pairs={{0,8},{1,9},{2,10},{3,11},{4,12},{5,13},{6,14},{7,15},{8,0},{9,1},... | collective-permute-start | bytes 884744 | tf_op jit(solution)/shard_map/ppermute | solution.py:140
  31.2 2.2 %collective-permute-start.11 = (bf16[1,2,48,768]{3,2,1,0:T(8,128)(2,1)S(1)}, bf16[1,2,48,768]{3,2,1,0:T(8,128)(2,1)S(1)}, u32[]{:S(2)}, u32[]{:S(2)}) collective-permute-start(bf16[1,2,48,768]{3,2,1,0:T(8,128)(2,1)S(1)} %get-tuple-element.66.refs_0_), channel_id=1, source_target_pairs={{0,16},{1,17},{2,18},{3,19},{4,20},{5,21},{6,22},{7,23},{8,24},{9,... | collective-permute-start | bytes 442376 | tf_op jit(solution)/shard_map/ppermute | solution.py:140
  33.4 5.6 %collective-permute-done.11.refs_1_ = bf16[1,2,48,768]{3,2,1,0:T(8,128)(2,1)S(1)} collective-permute-done((bf16[1,2,48,768]{3,2,1,0:T(8,128)(2,1)S(1)}, bf16[1,2,48,768]{3,2,1,0:T(8,128)(2,1)S(1)}, u32[]{:S(2)}, u32[]{:S(2)}) %collective-permute-start.11) | collective-permute-done | bytes 147488 | tf_op jit(solution)/shard_map/ppermute | solution.py:140
  39.0 2.2 %collective-permute-done.10.refs_3_ = bf16[1,4,48,768]{3,2,1,0:T(8,128)(2,1)S(1)} collective-permute-done((bf16[1,4,48,768]{3,2,1,0:T(8,128)(2,1)S(1)}, bf16[1,4,48,768]{3,2,1,0:T(8,128)(2,1)S(1)}, u32[]{:S(2)}, u32[]{:S(2)}) %collective-permute-start.10) | collective-permute-done | bytes 294944 | tf_op jit(solution)/shard_map/ppermute | solution.py:140
  41.3 1.6 collective-permute-start.14
  42.9 1.3 collective-permute-start.12
  44.3 3.0 %prepare.1 = (bf16[2,2,3,8,48,256]{5,4,3,2,1,0:T(8,128)(2,1)S(1)}, bf16[2,2,1,8,48,256]{5,4,3,2,1,0:T(8,128)(2,1)S(1)}) custom-call(s32[1]{0:T(128)} %bitcast.index_ref, bf16[2,128,1536]{2,1,0:T(8,128)(2,1)S(1)} %copy-done, bf16[256,1536]{1,0:T(8,128)(2,1)S(1)} %bitcast.159, f32[1,1536]{1,0:T(1,128)S(1)} %reshape.165.gain_ref, ...), custom_call_target="tpu_custom_call" | custom-call | tf_op jit(solution)/shard_map/prepare/pallas_call | solution.py:285
  47.2 5.3 %collective-permute-done.12.refs_1_ = bf16[1,2,48,768]{3,2,1,0:T(8,128)(2,1)S(1)} collective-permute-done((bf16[1,2,48,768]{3,2,1,0:T(8,128)(2,1)S(1)}, bf16[1,2,48,768]{3,2,1,0:T(8,128)(2,1)S(1)}, u32[]{:S(2)}, u32[]{:S(2)}) %collective-permute-start.12) | collective-permute-done | bytes 147488 | tf_op jit(solution)/shard_map/ppermute | solution.py:140
  53.6 3.6 %collective-permute-done.16.refs_1_ = bf16[1,4,48,768]{3,2,1,0:T(8,128)(2,1)S(1)} collective-permute-done((bf16[1,4,48,768]{3,2,1,0:T(8,128)(2,1)S(1)}, bf16[1,4,48,768]{3,2,1,0:T(8,128)(2,1)S(1)}, u32[]{:S(2)}, u32[]{:S(2)}) %collective-permute-start.16) | collective-permute-done | bytes 294944 | tf_op jit(solution)/shard_map/ppermute | solution.py:140
  57.3 5.8 %collective-permute-done.15.refs_1_ = bf16[1,4,48,768]{3,2,1,0:T(8,128)(2,1)S(1)} collective-permute-done((bf16[1,4,48,768]{3,2,1,0:T(8,128)(2,1)S(1)}, bf16[1,4,48,768]{3,2,1,0:T(8,128)(2,1)S(1)}, u32[]{:S(2)}, u32[]{:S(2)}) %collective-permute-start.15) | collective-permute-done | bytes 294944 | tf_op jit(solution)/shard_map/ppermute | solution.py:140
  63.2 2.0 %collective-permute-done.17.refs_3_ = bf16[1,8,48,768]{3,2,1,0:T(8,128)(2,1)S(1)} collective-permute-done((bf16[1,8,48,768]{3,2,1,0:T(8,128)(2,1)S(1)}, bf16[1,8,48,768]{3,2,1,0:T(8,128)(2,1)S(1)}, u32[]{:S(2)}, u32[]{:S(2)}) %collective-permute-start.17) | collective-permute-done | bytes 589856 | tf_op jit(solution)/shard_map/ppermute | solution.py:140
  71.9 1.9 %convolution_convert_fusion.1 = bf16[3,8,48,768]{3,2,1,0:T(8,128)(2,1)} fusion(bf16[256,768]{1,0:T(8,128)(2,1)S(1)} %get-tuple-element.93.grad_ref, bf16[2,2,3,8,48,256]{5,4,3,2,1,0:T(8,128)(2,1)S(1)} %get-tuple-element.77), kind=kOutput, calls=%fused_computation.14 | convolution fusion | flops 453869568 | bytes 2752512 | tf_op jit(solution)/shard_map/mnrt,ti->mnri/dot_general | solution.py:376
  74.0 1.8 %convolution_convert_fusion = bf16[3,8,48,768]{3,2,1,0:T(8,128)(2,1)} fusion(bf16[256,768]{1,0:T(8,128)(2,1)S(1)} %get-tuple-element.93.grad_ref, bf16[2,2,3,8,48,256]{5,4,3,2,1,0:T(8,128)(2,1)S(1)} %get-tuple-element.77), kind=kOutput, calls=%fused_computation.13 | convolution fusion | flops 453869568 | bytes 2752512 | tf_op jit(solution)/shard_map/mnrt,ti->mnri/dot_general | solution.py:376
  75.8 1.5 convolution_convert_fusion.2
  80.4 3.7 %add_convert_fusion = bf16[3,8,48,768]{3,2,1,0:T(8,128)(2,1)} fusion(bf16[3,8,48,768]{3,2,1,0:T(8,128)(2,1)} %collective-permute-done.20, bf16[256,768]{1,0:T(8,128)(2,1)S(1)} %get-tuple-element.93.grad_ref, bf16[2,2,3,8,48,256]{5,4,3,2,1,0:T(8,128)(2,1)} %copy-done.1), kind=kOutput, calls=%fused_computation.1 | convolution fusion | flops 455639040 | bytes 4521984 | tf_op jit(solution)/shard_map/mnrt,ti->mnri/dot_general | solution.py:376
  84.1 3.8 %collective-permute-start.23 = (bf16[3,8,48,768]{3,2,1,0:T(8,128)(2,1)}, bf16[3,8,48,768]{3,2,1,0:T(8,128)(2,1)}, u32[]{:S(2)}, u32[]{:S(2)}) collective-permute-start(bf16[3,8,48,768]{3,2,1,0:T(8,128)(2,1)} %add_convert_fusion), channel_id=1, source_target_pairs={{0,4},{1,3},{2,6},{3,1},{4,0},{5,7},{6,2},{7,5},{8,12},{9,11},{10,... | collective-permute-start | bytes 5308424 | tf_op jit(solution)/shard_map/ppermute | solution.py:140
  87.9 1.9 %fusion.20 = bf16[1,4,48,768]{3,2,1,0:T(8,128)(2,1)} fusion(bf16[256,768]{1,0:T(8,128)(2,1)S(1)} %get-tuple-element.102.hidden_ref, bf16[2,8,48,768]{3,2,1,0:T(8,128)(2,1)} %collective-permute-done.21, bf16[2,2,1,8,48,256]{5,4,3,2,1,0:T(8,128)(2,1)S(1)} %copy-done.17), kind=kOutput, calls=%fused_computation.43 | convolution fusion | flops 75939840 | bytes 1081344 | tf_op jit(solution)/shard_map/mnrt,ti->mnri/dot_general | solution.py:376
  90.7 1.9 %fusion.21 = bf16[1,4,48,768]{3,2,1,0:T(8,128)(2,1)} fusion(bf16[256,768]{1,0:T(8,128)(2,1)S(1)} %get-tuple-element.102.hidden_ref, bf16[2,8,48,768]{3,2,1,0:T(8,128)(2,1)} %collective-permute-done.21, bf16[2,2,1,8,48,256]{5,4,3,2,1,0:T(8,128)(2,1)S(1)} %copy-done.17), kind=kOutput, calls=%fused_computation.44 | convolution fusion | flops 75939840 | bytes 1081344 | tf_op jit(solution)/shard_map/mnrt,ti->mnri/dot_general | solution.py:376
  92.7 2.2 %fusion.17.refs_0_ = f32[1,4,48,768]{3,2,1,0:T(8,128)} fusion(bf16[256,768]{1,0:T(8,128)(2,1)S(1)} %get-tuple-element.102.hidden_ref, bf16[2,8,48,768]{3,2,1,0:T(8,128)(2,1)} %collective-permute-done.21, bf16[2,2,1,8,48,256]{5,4,3,2,1,0:T(8,128)(2,1)S(1)} %copy-done.17), kind=kOutput, calls=%fused_computation.39 | convolution fusion | flops 75792384 | bytes 1376256 | tf_op jit(solution)/shard_map/mnrt,ti->mnri/dot_general | solution.py:376
  94.9 2.0 %fusion.16.refs_2_ = f32[1,4,48,768]{3,2,1,0:T(8,128)} fusion(bf16[256,768]{1,0:T(8,128)(2,1)S(1)} %get-tuple-element.102.hidden_ref, bf16[2,8,48,768]{3,2,1,0:T(8,128)(2,1)} %collective-permute-done.21, bf16[2,2,1,8,48,256]{5,4,3,2,1,0:T(8,128)(2,1)S(1)} %copy-done.17), kind=kOutput, calls=%fused_computation.38 | convolution fusion | flops 75792384 | bytes 1376256 | tf_op jit(solution)/shard_map/mnrt,ti->mnri/dot_general | solution.py:376
  96.9 4.0 %convert_add_fusion.refs_0_ = f32[3,8,48,768]{3,2,1,0:T(8,128)} fusion(bf16[3,8,48,768]{3,2,1,0:T(8,128)(2,1)} %collective-permute-done.22, bf16[256,768]{1,0:T(8,128)(2,1)S(1)} %get-tuple-element.93.grad_ref, bf16[2,2,3,8,48,256]{5,4,3,2,1,0:T(8,128)(2,1)S(1)} %copy-done.2), kind=kOutput, calls=%fused_computation | convolution fusion | flops 454754304 | bytes 6291456 | tf_op jit(solution)/shard_map/mnrt,ti->mnri/dot_general | solution.py:376
  101.0 2.6 %grad_active.1 = f32[256,1536]{1,0:T(8,128)S(1)} custom-call(s32[1]{0:T(128)} %bitcast.index_ref, bf16[256,768]{1,0:T(8,128)(2,1)S(1)} %get-tuple-element.93.grad_ref, bf16[2,32,768]{2,1,0:T(8,128)(2,1)S(1)} %collective-permute-done.25.core_ref, bf16[2,32,768]{2,1,0:T(8,128)(2,1)S(1)} %collective-permute-done.26.outer_ref, ...), custom_call_target="tpu_custom_call" | custom-call | tf_op jit(solution)/shard_map/grad_active/pallas_call | solution.py:361
  103.9 1.8 %fusion.8 = (f32[1536]{0:T(1024)S(1)}, f32[2,128]{1,0:T(2,128)S(1)}, f32[2,128,1536]{2,1,0:T(8,128)S(1)}) fusion(bf16[2,128,1536]{2,1,0:T(8,128)(2,1)S(1)} %copy-done, f32[2,128]{1,0:T(2,128)S(1)} %fusion.54, f32[1536]{0:T(1024)S(1)} %copy-done.27, f32[2,128,1536]{2,1,0:T(8,128)S(1)} %bitcast.156), kind=kLoop, calls=%fused_computation.19 | loop fusion | flops 10615040 | bytes 3946496 | tf_op jit(solution)/shard_map/transpose(jvp())/reduce_sum | solution.py:33
  105.7 1.4 fusion.13
  110.5 1.9 %collective-permute-start.30 = (bf16[1,2,48,768]{3,2,1,0:T(8,128)(2,1)S(1)}, bf16[1,2,48,768]{3,2,1,0:T(8,128)(2,1)S(1)}, u32[]{:S(2)}, u32[]{:S(2)}) collective-permute-start(bf16[1,2,48,768]{3,2,1,0:T(8,128)(2,1)S(1)} %get-tuple-element.96), channel_id=1, source_target_pairs={{0,16},{1,17},{2,18},{3,19},{4,20},{5,21},{6,22},{7,23},{8,24},{9,... | collective-permute-start | bytes 442376 | tf_op jit(solution)/shard_map/ppermute | solution.py:140
  113.6 6.8 %collective-permute-done.29 = f32[32,72]{1,0:T(8,128)S(1)} collective-permute-done((f32[32,72]{1,0:T(8,128)S(1)}, f32[32,72]{1,0:T(8,128)S(1)}, u32[]{:S(2)}, u32[]{:S(2)}) %collective-permute-start.29) | collective-permute-done | bytes 9248 | tf_op jit(solution)/shard_map/ppermute | solution.py:140
  120.5 2.0 %copy-done.3 = f32[3,8,48,768]{3,2,1,0:T(8,128)S(1)} copy-done((f32[3,8,48,768]{3,2,1,0:T(8,128)S(1)}, f32[3,8,48,768]{3,2,1,0:T(8,128)}, u32[]{:S(2)}) %copy-start.3) | copy-done | bytes 3538968
  122.5 2.7 %fold.5 = (bf16[2,4,48,768]{3,2,1,0:T(8,128)(2,1)S(1)}, bf16[1,4,48,768]{3,2,1,0:T(8,128)(2,1)S(1)}, bf16[1,2,48,768]{3,2,1,0:T(8,128)(2,1)S(1)}, bf16[1,2,48,76...) custom-call(f32[3,8,48,768]{3,2,1,0:T(8,128)S(1)} %copy-done.3, ...), custom_call_target="tpu_custom_call" | custom-call | tf_op jit(solution)/shard_map/fold/pallas_call | solution.py:181
  127.1 1.6 collective-permute-start.33
  129.5 2.2 %collective-permute-start.32 = (f32[32,72]{1,0:T(8,128)S(1)}, f32[32,72]{1,0:T(8,128)S(1)}, u32[]{:S(2)}, u32[]{:S(2)}) collective-permute-start(f32[32,72]{1,0:T(8,128)S(1)} %add.146), channel_id=1, source_target_pairs={{0,16},{1,17},{2,18},{3,19},{4,20},{5,21},{6,22},{7,23},{8,24},{9,... | collective-permute-start | bytes 27656 | tf_op jit(solution)/shard_map/ppermute | solution.py:140
  131.6 2.2 %project_back.1 = bf16[256,1536]{1,0:T(8,128)(2,1)} custom-call(s32[1]{0:T(128)} %bitcast.index_ref, bf16[256,768]{1,0:T(8,128)(2,1)S(1)} %get-tuple-element.102.hidden_ref, bf16[256,1536]{1,0:T(8,128)(2,1)S(1)} %bitcast.150, bf16[1,8,48,768]{3,2,1,0:T(8,128)(2,1)S(1)} %copy-done.11, bf16[1,8,48,768]{3,2,1,0:T(8,128)(2,1)S(1)} %copy-done.13, ...), custom_call_target="tpu_custom_call" | custom-call | tf_op jit(solution)/shard_map/project_back/pallas_call | solution.py:327
  133.8 2.2 %collective-permute-done.32 = f32[32,72]{1,0:T(8,128)S(1)} collective-permute-done((f32[32,72]{1,0:T(8,128)S(1)}, f32[32,72]{1,0:T(8,128)S(1)}, u32[]{:S(2)}, u32[]{:S(2)}) %collective-permute-start.32) | collective-permute-done | bytes 9248 | tf_op jit(solution)/shard_map/ppermute | solution.py:140
  137.0 2.9 %collective-permute-start.36 = (f32[32,72]{1,0:T(8,128)S(1)}, f32[32,72]{1,0:T(8,128)S(1)}, u32[]{:S(2)}, u32[]{:S(2)}) collective-permute-start(f32[32,72]{1,0:T(8,128)S(1)} %add.147), channel_id=1, source_target_pairs={{0,2},{1,3},{2,0},{3,1},{4,6},{5,7},{6,4},{7,5},{8,10},{9,11},{10,... | collective-permute-start | bytes 27656 | tf_op jit(solution)/shard_map/ppermute | solution.py:140
  139.9 1.7 %collective-permute-done.36 = f32[32,72]{1,0:T(8,128)S(1)} collective-permute-done((f32[32,72]{1,0:T(8,128)S(1)}, f32[32,72]{1,0:T(8,128)S(1)}, u32[]{:S(2)}, u32[]{:S(2)}) %collective-permute-start.36) | collective-permute-done | bytes 9248 | tf_op jit(solution)/shard_map/ppermute | solution.py:140
  141.6 1.7 %collective-permute-start.37 = (f32[32,72]{1,0:T(8,128)S(1)}, f32[32,72]{1,0:T(8,128)S(1)}, u32[]{:S(2)}, u32[]{:S(2)}) collective-permute-start(f32[32,72]{1,0:T(8,128)S(1)} %add.148), channel_id=1, source_target_pairs={{0,4},{1,5},{2,6},{3,7},{4,0},{5,1},{6,2},{7,3},{8,12},{9,13},{10,... | collective-permute-start | bytes 27656 | tf_op jit(solution)/shard_map/ppermute | solution.py:140
  143.4 1.6 collective-permute-start.35
  146.9 7.0 %collective-permute-done.35.refs_1_ = bf16[2,2,48,768]{3,2,1,0:T(8,128)(2,1)S(1)} collective-permute-done((bf16[2,2,48,768]{3,2,1,0:T(8,128)(2,1)S(1)}, bf16[2,2,48,768]{3,2,1,0:T(8,128)(2,1)S(1)}, u32[]{:S(2)}, u32[]{:S(2)}) %collective-permute-start.35) | collective-permute-done | bytes 294944 | tf_op jit(solution)/shard_map/ppermute | solution.py:140
  154.0 1.9 %collective-permute-start.40 = (bf16[2,1,48,768]{3,2,1,0:T(8,128)(2,1)S(1)}, bf16[2,1,48,768]{3,2,1,0:T(8,128)(2,1)S(1)}, u32[]{:S(2)}, u32[]{:S(2)}) collective-permute-start(bf16[2,1,48,768]{3,2,1,0:T(8,128)(2,1)S(1)} %get-tuple-element.121), channel_id=1, source_target_pairs={{0,16},{1,17},{2,18},{3,19},{4,20},{5,21},{6,22},{7,23},{8,24},{9,... | collective-permute-start | bytes 442376 | tf_op jit(solution)/shard_map/ppermute | solution.py:140
  156.3 1.6 collective-permute-start.41
  158.0 3.7 %collective-permute-done.40 = bf16[2,1,48,768]{3,2,1,0:T(8,128)(2,1)S(1)} collective-permute-done((bf16[2,1,48,768]{3,2,1,0:T(8,128)(2,1)S(1)}, bf16[2,1,48,768]{3,2,1,0:T(8,128)(2,1)S(1)}, u32[]{:S(2)}, u32[]{:S(2)}) %collective-permute-start.40) | collective-permute-done | bytes 147488 | tf_op jit(solution)/shard_map/ppermute | solution.py:140
  (161 shorter events, 29.8 us)
Async XLA Ops:
  0.6 13.8 %copy-start = (bf16[2,128,1536]{2,1,0:T(8,128)(2,1)S(1)}, bf16[2,128,1536]{2,1,0:T(8,128)(2,1)}, u32[]{:S(2)}) copy-start(bf16[2,128,1536]{2,1,0:T(8,128)(2,1)} %features_ref) | copy-start | bytes 2359300
  1.6 11.1 %collective-permute-start = (bf16[2,1,48,768]{3,2,0,1:T(8,128)(2,1)S(1)}, bf16[2,1,48,768]{3,2,0,1:T(8,128)(2,1)S(1)}, u32[]{:S(2)}, u32[]{:S(2)}) collective-permute-start(bf16[2,1,48,768]{3,2,0,1:T(8,128)(2,1)S(1)} %get-tuple-element.151), channel_id=1, source_target_pairs={{0,16},{1,17},{2,18},{3,19},{4,20},{5,21},{6,22},{7,23},{8,24},{9,... | collective-permute-start | bytes 442376 | tf_op jit(solution)/shard_map/ppermute | solution.py:140
  7.5 5.2 %collective-permute-start.1 = (bf16[2,1,48,768]{3,2,1,0:T(8,128)(2,1)S(1)}, bf16[2,1,48,768]{3,2,1,0:T(8,128)(2,1)S(1)}, u32[]{:S(2)}, u32[]{:S(2)}) collective-permute-start(bf16[2,1,48,768]{3,2,1,0:T(8,128)(2,1)S(1)} %pad_maximum_fusion.refs_2_), channel_id=1, source_target_pairs={{0,2},{1,5},{2,0},{3,7},{4,6},{5,1},{6,4},{7,3},{8,10},{9,13},{10,... | collective-permute-start | bytes 442376 | tf_op jit(solution)/shard_map/ppermute | solution.py:140
  12.8 11.4 %collective-permute-start.2 = (bf16[2,2,48,768]{3,2,1,0:T(8,128)(2,1)S(1)}, bf16[2,2,48,768]{3,2,1,0:T(8,128)(2,1)S(1)}, u32[]{:S(2)}, u32[]{:S(2)}) collective-permute-start(bf16[2,2,48,768]{3,2,1,0:T(8,128)(2,1)S(1)} %get-tuple-element.65.refs_0_), channel_id=1, source_target_pairs={{0,8},{1,9},{2,10},{3,11},{4,12},{5,13},{6,14},{7,15},{8,0},{9,1},... | collective-permute-start | bytes 884744 | tf_op jit(solution)/shard_map/ppermute | solution.py:140
  14.5 4.7 %collective-permute-start.4 = (bf16[1,32,1536]{2,1,0:T(8,128)(2,1)S(1)}, bf16[1,32,1536]{2,1,0:T(8,128)(2,1)S(1)}, u32[]{:S(2)}, u32[]{:S(2)}) collective-permute-start(bf16[1,32,1536]{2,1,0:T(8,128)(2,1)S(1)} %get-tuple-element.146), channel_id=1, source_target_pairs={{0,1},{1,0},{2,3},{3,2},{4,5},{5,4},{6,7},{7,6},{8,9},{9,8},{10,11... | collective-permute-start | bytes 294920 | tf_op jit(solution)/shard_map/ppermute | solution.py:140
  14.6 5.3 %collective-permute-start.5 = (bf16[1,32,1536]{2,1,0:T(8,128)(2,1)S(1)}, bf16[1,32,1536]{2,1,0:T(8,128)(2,1)S(1)}, u32[]{:S(2)}, u32[]{:S(2)}) collective-permute-start(bf16[1,32,1536]{2,1,0:T(8,128)(2,1)S(1)} %get-tuple-element.144), channel_id=1, source_target_pairs={{0,1},{1,0},{2,3},{3,2},{4,5},{5,4},{6,7},{7,6},{8,9},{9,8},{10,11... | collective-permute-start | bytes 294920 | tf_op jit(solution)/shard_map/ppermute | solution.py:140
  15.2 5.4 %collective-permute-start.3 = (bf16[1,2,48,768]{3,2,1,0:T(8,128)(2,1)S(1)}, bf16[1,2,48,768]{3,2,1,0:T(8,128)(2,1)S(1)}, u32[]{:S(2)}, u32[]{:S(2)}) collective-permute-start(bf16[1,2,48,768]{3,2,1,0:T(8,128)(2,1)S(1)} %get-tuple-element.66.refs_0_), channel_id=1, source_target_pairs={{0,4},{1,3},{2,6},{3,1},{4,0},{5,7},{6,2},{7,5},{8,12},{9,11},{10,... | collective-permute-start | bytes 442376 | tf_op jit(solution)/shard_map/ppermute | solution.py:140
  16.7 7.5 %collective-permute-start.8 = (bf16[1,2,48,768]{3,2,1,0:T(8,128)(2,1)S(1)}, bf16[1,2,48,768]{3,2,1,0:T(8,128)(2,1)S(1)}, u32[]{:S(2)}, u32[]{:S(2)}) collective-permute-start(bf16[1,2,48,768]{3,2,1,0:T(8,128)(2,1)S(1)} %get-tuple-element.69.refs_2_), channel_id=1, source_target_pairs={{0,16},{1,17},{2,18},{3,19},{4,20},{5,21},{6,22},{7,23},{8,24},{9,... | collective-permute-start | bytes 442376 | tf_op jit(solution)/shard_map/ppermute | solution.py:140
  19.2 1.4 collective-permute-start.6
  19.9 0.7 collective-permute-start.7
  24.3 16.9 %collective-permute-start.9 = (bf16[2,4,48,768]{3,2,1,0:T(8,128)(2,1)S(1)}, bf16[2,4,48,768]{3,2,1,0:T(8,128)(2,1)S(1)}, u32[]{:S(2)}, u32[]{:S(2)}) collective-permute-start(bf16[2,4,48,768]{3,2,1,0:T(8,128)(2,1)S(1)} %get-tuple-element.72.refs_0_), channel_id=1, source_target_pairs={{0,2},{1,5},{2,0},{3,7},{4,6},{5,1},{6,4},{7,3},{8,10},{9,13},{10,... | collective-permute-start | bytes 1769480 | tf_op jit(solution)/shard_map/ppermute | solution.py:140
  28.9 12.2 %collective-permute-start.10 = (bf16[1,4,48,768]{3,2,1,0:T(8,128)(2,1)S(1)}, bf16[1,4,48,768]{3,2,1,0:T(8,128)(2,1)S(1)}, u32[]{:S(2)}, u32[]{:S(2)}) collective-permute-start(bf16[1,4,48,768]{3,2,1,0:T(8,128)(2,1)S(1)} %get-tuple-element.74.refs_2_), channel_id=1, source_target_pairs={{0,8},{1,9},{2,10},{3,11},{4,12},{5,13},{6,14},{7,15},{8,0},{9,1},... | collective-permute-start | bytes 884744 | tf_op jit(solution)/shard_map/ppermute | solution.py:140
  31.2 7.8 %collective-permute-start.11 = (bf16[1,2,48,768]{3,2,1,0:T(8,128)(2,1)S(1)}, bf16[1,2,48,768]{3,2,1,0:T(8,128)(2,1)S(1)}, u32[]{:S(2)}, u32[]{:S(2)}) collective-permute-start(bf16[1,2,48,768]{3,2,1,0:T(8,128)(2,1)S(1)} %get-tuple-element.66.refs_0_), channel_id=1, source_target_pairs={{0,16},{1,17},{2,18},{3,19},{4,20},{5,21},{6,22},{7,23},{8,24},{9,... | collective-permute-start | bytes 442376 | tf_op jit(solution)/shard_map/ppermute | solution.py:140
  41.3 23.9 %collective-permute-start.14 = (bf16[3,8,48,768]{3,2,1,0:T(8,128)(2,1)S(1)}, bf16[3,8,48,768]{3,2,1,0:T(8,128)(2,1)S(1)}, u32[]{:S(2)}, u32[]{:S(2)}) collective-permute-start(bf16[3,8,48,768]{3,2,1,0:T(8,128)(2,1)S(1)} %assemble.10.refs_0_), channel_id=1, source_target_pairs={{0,4},{1,3},{2,6},{3,1},{4,0},{5,7},{6,2},{7,5},{8,12},{9,11},{10,... | collective-permute-start | bytes 5308424 | tf_op jit(solution)/shard_map/ppermute | solution.py:140
  42.9 9.7 %collective-permute-start.12 = (bf16[1,2,48,768]{3,2,1,0:T(8,128)(2,1)S(1)}, bf16[1,2,48,768]{3,2,1,0:T(8,128)(2,1)S(1)}, u32[]{:S(2)}, u32[]{:S(2)}) collective-permute-start(bf16[1,2,48,768]{3,2,1,0:T(8,128)(2,1)S(1)} %collective-permute-done.3.refs_0_), channel_id=1, source_target_pairs={{0,16},{1,17},{2,18},{3,19},{4,20},{5,21},{6,22},{7,23},{8,24},{9,... | collective-permute-start | bytes 442376 | tf_op jit(solution)/shard_map/ppermute | solution.py:140
  44.1 21.7 %collective-permute-start.13 = (bf16[3,8,48,768]{3,2,1,0:T(8,128)(2,1)S(1)}, bf16[3,8,48,768]{3,2,1,0:T(8,128)(2,1)S(1)}, u32[]{:S(2)}, u32[]{:S(2)}) collective-permute-start(bf16[3,8,48,768]{3,2,1,0:T(8,128)(2,1)S(1)} %assemble.10.refs_0_), channel_id=1, source_target_pairs={{0,1},{1,0},{2,3},{3,2},{4,5},{5,4},{6,7},{7,6},{8,9},{9,8},{10,11... | collective-permute-start | bytes 5308424 | tf_op jit(solution)/shard_map/ppermute | solution.py:140
  44.2 13.0 %collective-permute-start.16 = (bf16[1,4,48,768]{3,2,1,0:T(8,128)(2,1)S(1)}, bf16[1,4,48,768]{3,2,1,0:T(8,128)(2,1)S(1)}, u32[]{:S(2)}, u32[]{:S(2)}) collective-permute-start(bf16[1,4,48,768]{3,2,1,0:T(8,128)(2,1)S(1)} %assemble.9.refs_0_), channel_id=1, source_target_pairs={{0,8},{1,9},{2,10},{3,11},{4,12},{5,13},{6,14},{7,15},{8,0},{9,1},... | collective-permute-start | bytes 884744 | tf_op jit(solution)/shard_map/ppermute | solution.py:140
  47.2 26.7 %copy-start.1 = (bf16[2,2,3,8,48,256]{5,4,3,2,1,0:T(8,128)(2,1)}, bf16[2,2,3,8,48,256]{5,4,3,2,1,0:T(8,128)(2,1)S(1)}, u32[]{:S(2)}) copy-start(bf16[2,2,3,8,48,256]{5,4,3,2,1,0:T(8,128)(2,1)S(1)} %get-tuple-element.77) | copy-start | bytes 7077892
  47.2 28.6 %copy-start.16 = (bf16[2,2,1,8,48,256]{5,4,3,2,1,0:T(8,128)(2,1)}, bf16[2,2,1,8,48,256]{5,4,3,2,1,0:T(8,128)(2,1)S(1)}, u32[]{:S(2)}) copy-start(bf16[2,2,1,8,48,256]{5,4,3,2,1,0:T(8,128)(2,1)S(1)} %get-tuple-element.84) | copy-start | bytes 2359300
  52.6 10.5 %collective-permute-start.15 = (bf16[1,4,48,768]{3,2,1,0:T(8,128)(2,1)S(1)}, bf16[1,4,48,768]{3,2,1,0:T(8,128)(2,1)S(1)}, u32[]{:S(2)}, u32[]{:S(2)}) collective-permute-start(bf16[1,4,48,768]{3,2,1,0:T(8,128)(2,1)S(1)} %assemble.11.refs_0_), channel_id=1, source_target_pairs={{0,8},{1,9},{2,10},{3,11},{4,12},{5,13},{6,14},{7,15},{8,0},{9,1},... | collective-permute-start | bytes 884744 | tf_op jit(solution)/shard_map/ppermute | solution.py:140
  57.2 6.0 %collective-permute-start.18 = (bf16[1,8,48,768]{3,2,1,0:T(8,128)(2,1)S(1)}, bf16[1,8,48,768]{3,2,1,0:T(8,128)(2,1)S(1)}, u32[]{:S(2)}, u32[]{:S(2)}) collective-permute-start(bf16[1,8,48,768]{3,2,1,0:T(8,128)(2,1)S(1)} %assemble.12.refs_0_), channel_id=1, source_target_pairs={{0,1},{1,0},{2,3},{3,2},{4,5},{5,4},{6,7},{7,6},{8,9},{9,8},{10,11... | collective-permute-start | bytes 1769480 | tf_op jit(solution)/shard_map/ppermute | solution.py:140
  63.1 2.1 %collective-permute-start.17 = (bf16[1,8,48,768]{3,2,1,0:T(8,128)(2,1)S(1)}, bf16[1,8,48,768]{3,2,1,0:T(8,128)(2,1)S(1)}, u32[]{:S(2)}, u32[]{:S(2)}) collective-permute-start(bf16[1,8,48,768]{3,2,1,0:T(8,128)(2,1)S(1)} %assemble.13.refs_1_), channel_id=1, source_target_pairs={{0,1},{1,0},{2,3},{3,2},{4,5},{5,4},{6,7},{7,6},{8,9},{9,8},{10,11... | collective-permute-start | bytes 1769480 | tf_op jit(solution)/shard_map/ppermute | solution.py:140
  65.2 3.8 %collective-permute-start.19 = (bf16[3,8,48,768]{3,2,1,0:T(8,128)(2,1)S(1)}, bf16[3,8,48,768]{3,2,1,0:T(8,128)(2,1)S(1)}, u32[]{:S(2)}, u32[]{:S(2)}) collective-permute-start(bf16[3,8,48,768]{3,2,1,0:T(8,128)(2,1)S(1)} %collective-permute-done.14.refs_1_), channel_id=1, source_target_pairs={{0,1},{1,0},{2,3},{3,2},{4,5},{5,4},{6,7},{7,6},{8,9},{9,8},{10,11... | collective-permute-start | bytes 5308424 | tf_op jit(solution)/shard_map/ppermute | solution.py:140
  73.8 6.6 %collective-permute-start.20 = (bf16[3,8,48,768]{3,2,1,0:T(8,128)(2,1)}, bf16[3,8,48,768]{3,2,1,0:T(8,128)(2,1)}, u32[]{:S(2)}, u32[]{:S(2)}) collective-permute-start(bf16[3,8,48,768]{3,2,1,0:T(8,128)(2,1)} %convolution_convert_fusion.1), channel_id=1, source_target_pairs={{0,1},{1,0},{2,3},{3,2},{4,5},{5,4},{6,7},{7,6},{8,9},{9,8},{10,11... | collective-permute-start | bytes 5308424 | tf_op jit(solution)/shard_map/ppermute | solution.py:140
  77.3 10.6 %collective-permute-start.21 = (bf16[2,8,48,768]{3,2,1,0:T(8,128)(2,1)}, bf16[2,8,48,768]{3,2,1,0:T(8,128)(2,1)}, u32[]{:S(2)}, u32[]{:S(2)}) collective-permute-start(bf16[2,8,48,768]{3,2,1,0:T(8,128)(2,1)} %convolution_convert_fusion.2), channel_id=1, source_target_pairs={{0,1},{1,0},{2,3},{3,2},{4,5},{5,4},{6,7},{7,6},{8,9},{9,8},{10,11... | collective-permute-start | bytes 3538952 | tf_op jit(solution)/shard_map/ppermute | solution.py:140
  77.7 19.2 %collective-permute-start.22 = (bf16[3,8,48,768]{3,2,1,0:T(8,128)(2,1)}, bf16[3,8,48,768]{3,2,1,0:T(8,128)(2,1)}, u32[]{:S(2)}, u32[]{:S(2)}) collective-permute-start(bf16[3,8,48,768]{3,2,1,0:T(8,128)(2,1)} %convolution_convert_fusion), channel_id=1, source_target_pairs={{0,1},{1,0},{2,3},{3,2},{4,5},{5,4},{6,7},{7,6},{8,9},{9,8},{10,11... | collective-permute-start | bytes 5308424 | tf_op jit(solution)/shard_map/ppermute | solution.py:140
  78.5 22.4 %collective-permute-start.25 = (bf16[2,32,768]{2,1,0:T(8,128)(2,1)}, bf16[2,32,768]{2,1,0:T(8,128)(2,1)S(1)}, u32[]{:S(2)}, u32[]{:S(2)}) collective-permute-start(bf16[2,32,768]{2,1,0:T(8,128)(2,1)} %get-tuple-element.142), channel_id=1, source_target_pairs={{0,1},{1,0},{2,3},{3,2},{4,5},{5,4},{6,7},{7,6},{8,9},{9,8},{10,11... | collective-permute-start | bytes 294920 | tf_op jit(solution)/shard_map/ppermute | solution.py:140
  78.9 22.1 %collective-permute-start.26 = (bf16[2,32,768]{2,1,0:T(8,128)(2,1)}, bf16[2,32,768]{2,1,0:T(8,128)(2,1)S(1)}, u32[]{:S(2)}, u32[]{:S(2)}) collective-permute-start(bf16[2,32,768]{2,1,0:T(8,128)(2,1)} %get-tuple-element.141), channel_id=1, source_target_pairs={{1,2},{2,1},{3,4},{4,3},{5,6},{6,5},{7,8},{8,7},{9,10},{10,9},{11,... | collective-permute-start | bytes 294920 | tf_op jit(solution)/shard_map/ppermute | solution.py:140
  84.1 36.4 %collective-permute-start.23 = (bf16[3,8,48,768]{3,2,1,0:T(8,128)(2,1)}, bf16[3,8,48,768]{3,2,1,0:T(8,128)(2,1)}, u32[]{:S(2)}, u32[]{:S(2)}) collective-permute-start(bf16[3,8,48,768]{3,2,1,0:T(8,128)(2,1)} %add_convert_fusion), channel_id=1, source_target_pairs={{0,4},{1,3},{2,6},{3,1},{4,0},{5,7},{6,2},{7,5},{8,12},{9,11},{10,... | collective-permute-start | bytes 5308424 | tf_op jit(solution)/shard_map/ppermute | solution.py:140
  89.8 17.4 %collective-permute-start.24 = (bf16[1,4,48,768]{3,2,1,0:T(8,128)(2,1)}, bf16[1,4,48,768]{3,2,1,0:T(8,128)(2,1)}, u32[]{:S(2)}, u32[]{:S(2)}) collective-permute-start(bf16[1,4,48,768]{3,2,1,0:T(8,128)(2,1)} %fusion.20), channel_id=1, source_target_pairs={{0,8},{1,9},{2,10},{3,11},{4,12},{5,13},{6,14},{7,15},{8,0},{9,1},... | collective-permute-start | bytes 884744 | tf_op jit(solution)/shard_map/ppermute | solution.py:140
  105.7 14.8 %copy-start.20 = (f32[1,4,48,768]{3,2,1,0:T(8,128)S(1)}, f32[1,4,48,768]{3,2,1,0:T(8,128)}, u32[]{:S(2)}) copy-start(f32[1,4,48,768]{3,2,1,0:T(8,128)} %fusion.16.refs_2_) | copy-start | bytes 1769476
  109.3 11.1 %collective-permute-start.27 = (bf16[1,4,48,768]{3,2,1,0:T(8,128)(2,1)S(1)}, bf16[1,4,48,768]{3,2,1,0:T(8,128)(2,1)S(1)}, u32[]{:S(2)}, u32[]{:S(2)}) collective-permute-start(bf16[1,4,48,768]{3,2,1,0:T(8,128)(2,1)S(1)} %copy-done.26), channel_id=1, source_target_pairs={{0,8},{1,9},{2,10},{3,11},{4,12},{5,13},{6,14},{7,15},{8,0},{9,1},... | collective-permute-start | bytes 884744 | tf_op jit(solution)/shard_map/ppermute | solution.py:140
  110.5 10.0 %collective-permute-start.30 = (bf16[1,2,48,768]{3,2,1,0:T(8,128)(2,1)S(1)}, bf16[1,2,48,768]{3,2,1,0:T(8,128)(2,1)S(1)}, u32[]{:S(2)}, u32[]{:S(2)}) collective-permute-start(bf16[1,2,48,768]{3,2,1,0:T(8,128)(2,1)S(1)} %get-tuple-element.96), channel_id=1, source_target_pairs={{0,16},{1,17},{2,18},{3,19},{4,20},{5,21},{6,22},{7,23},{8,24},{9,... | collective-permute-start | bytes 442376 | tf_op jit(solution)/shard_map/ppermute | solution.py:140
  112.4 1.2 collective-permute-start.28
  113.6 6.9 %collective-permute-start.29 = (f32[32,72]{1,0:T(8,128)S(1)}, f32[32,72]{1,0:T(8,128)S(1)}, u32[]{:S(2)}, u32[]{:S(2)}) collective-permute-start(f32[32,72]{1,0:T(8,128)S(1)} %add.145), channel_id=1, source_target_pairs={{0,8},{1,9},{2,10},{3,11},{4,12},{5,13},{6,14},{7,15},{8,0},{9,1},... | collective-permute-start | bytes 27656 | tf_op jit(solution)/shard_map/ppermute | solution.py:140
  122.5 9.1 %copy-start.19 = (bf16[1,8,48,768]{3,2,1,0:T(8,128)(2,1)S(1)}, bf16[1,8,48,768]{3,2,1,0:T(8,128)(2,1)}, u32[]{:S(2)}) copy-start(bf16[1,8,48,768]{3,2,1,0:T(8,128)(2,1)} %copy-done.18) | copy-start | bytes 1769476
  122.5 9.1 %copy-start.23 = (bf16[1,8,48,768]{3,2,1,0:T(8,128)(2,1)S(1)}, bf16[1,8,48,768]{3,2,1,0:T(8,128)(2,1)}, u32[]{:S(2)}) copy-start(bf16[1,8,48,768]{3,2,1,0:T(8,128)(2,1)} %copy-done.22) | copy-start | bytes 1769476
  125.9 10.2 %collective-permute-start.31 = (bf16[2,4,48,768]{3,2,1,0:T(8,128)(2,1)S(1)}, bf16[2,4,48,768]{3,2,1,0:T(8,128)(2,1)S(1)}, u32[]{:S(2)}, u32[]{:S(2)}) collective-permute-start(bf16[2,4,48,768]{3,2,1,0:T(8,128)(2,1)S(1)} %get-tuple-element.101), channel_id=1, source_target_pairs={{0,2},{1,5},{2,0},{3,7},{4,6},{5,1},{6,4},{7,3},{8,10},{9,13},{10,... | collective-permute-start | bytes 1769480 | tf_op jit(solution)/shard_map/ppermute | solution.py:140
  127.1 9.7 %collective-permute-start.33 = (bf16[1,4,48,768]{3,2,1,0:T(8,128)(2,1)S(1)}, bf16[1,4,48,768]{3,2,1,0:T(8,128)(2,1)S(1)}, u32[]{:S(2)}, u32[]{:S(2)}) collective-permute-start(bf16[1,4,48,768]{3,2,1,0:T(8,128)(2,1)S(1)} %get-tuple-element.108), channel_id=1, source_target_pairs={{0,8},{1,9},{2,10},{3,11},{4,12},{5,13},{6,14},{7,15},{8,0},{9,1},... | collective-permute-start | bytes 884744 | tf_op jit(solution)/shard_map/ppermute | solution.py:140
  128.7 7.4 %collective-permute-start.34 = (bf16[1,2,48,768]{3,2,1,0:T(8,128)(2,1)S(1)}, bf16[1,2,48,768]{3,2,1,0:T(8,128)(2,1)S(1)}, u32[]{:S(2)}, u32[]{:S(2)}) collective-permute-start(bf16[1,2,48,768]{3,2,1,0:T(8,128)(2,1)S(1)} %get-tuple-element.110), channel_id=1, source_target_pairs={{0,16},{1,17},{2,18},{3,19},{4,20},{5,21},{6,22},{7,23},{8,24},{9,... | collective-permute-start | bytes 442376 | tf_op jit(solution)/shard_map/ppermute | solution.py:140
  129.5 6.6 %collective-permute-start.32 = (f32[32,72]{1,0:T(8,128)S(1)}, f32[32,72]{1,0:T(8,128)S(1)}, u32[]{:S(2)}, u32[]{:S(2)}) collective-permute-start(f32[32,72]{1,0:T(8,128)S(1)} %add.146), channel_id=1, source_target_pairs={{0,16},{1,17},{2,18},{3,19},{4,20},{5,21},{6,22},{7,23},{8,24},{9,... | collective-permute-start | bytes 27656 | tf_op jit(solution)/shard_map/ppermute | solution.py:140
  137.0 4.6 %collective-permute-start.36 = (f32[32,72]{1,0:T(8,128)S(1)}, f32[32,72]{1,0:T(8,128)S(1)}, u32[]{:S(2)}, u32[]{:S(2)}) collective-permute-start(f32[32,72]{1,0:T(8,128)S(1)} %add.147), channel_id=1, source_target_pairs={{0,2},{1,3},{2,0},{3,1},{4,6},{5,7},{6,4},{7,5},{8,10},{9,11},{10,... | collective-permute-start | bytes 27656 | tf_op jit(solution)/shard_map/ppermute | solution.py:140
  141.6 4.7 %collective-permute-start.37 = (f32[32,72]{1,0:T(8,128)S(1)}, f32[32,72]{1,0:T(8,128)S(1)}, u32[]{:S(2)}, u32[]{:S(2)}) collective-permute-start(f32[32,72]{1,0:T(8,128)S(1)} %add.148), channel_id=1, source_target_pairs={{0,4},{1,5},{2,6},{3,7},{4,0},{5,1},{6,2},{7,3},{8,12},{9,13},{10,... | collective-permute-start | bytes 27656 | tf_op jit(solution)/shard_map/ppermute | solution.py:140
  143.4 10.5 %collective-permute-start.35 = (bf16[2,2,48,768]{3,2,1,0:T(8,128)(2,1)S(1)}, bf16[2,2,48,768]{3,2,1,0:T(8,128)(2,1)S(1)}, u32[]{:S(2)}, u32[]{:S(2)}) collective-permute-start(bf16[2,2,48,768]{3,2,1,0:T(8,128)(2,1)S(1)} %get-tuple-element.112), channel_id=1, source_target_pairs={{0,8},{1,9},{2,10},{3,11},{4,12},{5,13},{6,14},{7,15},{8,0},{9,1},... | collective-permute-start | bytes 884744 | tf_op jit(solution)/shard_map/ppermute | solution.py:140
  144.9 8.9 %collective-permute-start.39 = (bf16[1,2,48,768]{3,2,1,0:T(8,128)(2,1)S(1)}, bf16[1,2,48,768]{3,2,1,0:T(8,128)(2,1)S(1)}, u32[]{:S(2)}, u32[]{:S(2)}) collective-permute-start(bf16[1,2,48,768]{3,2,1,0:T(8,128)(2,1)S(1)} %copy-done.25), channel_id=1, source_target_pairs={{0,4},{1,3},{2,6},{3,1},{4,0},{5,7},{6,2},{7,5},{8,12},{9,11},{10,... | collective-permute-start | bytes 442376 | tf_op jit(solution)/shard_map/ppermute | solution.py:140
  146.1 7.8 %collective-permute-start.38 = (bf16[1,2,48,768]{3,2,1,0:T(8,128)(2,1)S(1)}, bf16[1,2,48,768]{3,2,1,0:T(8,128)(2,1)S(1)}, u32[]{:S(2)}, u32[]{:S(2)}) collective-permute-start(bf16[1,2,48,768]{3,2,1,0:T(8,128)(2,1)S(1)} %get-tuple-element.116), channel_id=1, source_target_pairs={{0,16},{1,17},{2,18},{3,19},{4,20},{5,21},{6,22},{7,23},{8,24},{9,... | collective-permute-start | bytes 442376 | tf_op jit(solution)/shard_map/ppermute | solution.py:140
  154.0 7.7 %collective-permute-start.40 = (bf16[2,1,48,768]{3,2,1,0:T(8,128)(2,1)S(1)}, bf16[2,1,48,768]{3,2,1,0:T(8,128)(2,1)S(1)}, u32[]{:S(2)}, u32[]{:S(2)}) collective-permute-start(bf16[2,1,48,768]{3,2,1,0:T(8,128)(2,1)S(1)} %get-tuple-element.121), channel_id=1, source_target_pairs={{0,16},{1,17},{2,18},{3,19},{4,20},{5,21},{6,22},{7,23},{8,24},{9,... | collective-permute-start | bytes 442376 | tf_op jit(solution)/shard_map/ppermute | solution.py:140
  156.3 5.4 %collective-permute-start.41 = (bf16[2,1,48,768]{3,2,1,0:T(8,128)(2,1)S(1)}, bf16[2,1,48,768]{3,2,1,0:T(8,128)(2,1)S(1)}, u32[]{:S(2)}, u32[]{:S(2)}) collective-permute-start(bf16[2,1,48,768]{3,2,1,0:T(8,128)(2,1)S(1)} %get-tuple-element.123), channel_id=1, source_target_pairs={{0,2},{1,5},{2,0},{3,7},{4,6},{5,1},{6,4},{7,3},{8,10},{9,13},{10,... | collective-permute-start | bytes 442376 | tf_op jit(solution)/shard_map/ppermute | solution.py:140
  (24 other events, 97.3 us)
